TPU v7x, 32 devices: a whole 2x2x4 slice. The times are simulated.
32 devices in a mesh: ctx: 4 (over z), head: 8 (over y, x, core).
Axes of the slice: x: 2, y: 2, z: 4, core: 2. Of those that a mesh axis runs over, the one named last changes fastest.
Arguments:
- queries: bfloat16 [1024, 8192], P('ctx', 'head'), may hold values from -6 to 6
- key_vectors: bfloat16 [1024, 1024], P('ctx'), may hold values from -6 to 6
- value_head_vectors: bfloat16 [1024, 1024], P('ctx'), may hold values from -6 to 6
- block_pattern: int32 [8, 8], replicated, may hold values from 0 to 1
- out_weight: bfloat16 [8192, 8192], P(None, 'head'), may hold values from -0.625 to 0.625
Outputs:
- layer_out: bfloat16 [1024, 8192], P('ctx', 'head')
All inputs are finite; a program needn't handle non-finite values.
Results may differ from a plain program's by a relative error of at most 0.013.
Values may be sent and summed in bfloat16 or wider, within the bound.
No kernel may reach another device: no remote copies, remote signals or barrier semaphores. Data moves between devices by JAX's collectives and lax.ppermute only.
A program may use at most 64 MiB of HBM per device.

v0:
```python
import math

import jax
import jax.numpy as jnp
from jax import lax
from jax.sharding import PartitionSpec as P

QUERY_HEADS = 64
KEY_VALUE_HEADS = 8
HEAD_SIZE = 128
BLOCK = 128


def passed_along(value, axis, steps):
    count = lax.axis_size(axis)
    pairs = [(source, (source + steps) % count) for source in range(count)]
    return lax.ppermute(value, axis, pairs)


def block_mask(active, query_block, key_start, key_count, tok_dev):
    blocks_dev = tok_dev // BLOCK
    block_total = active.shape[0]
    rows_table = lax.dynamic_slice_in_dim(active, query_block, blocks_dev, 0).astype(jnp.float32)
    key_block = (key_start + jnp.arange(key_count, dtype=jnp.int32)) // BLOCK
    one_hot = (key_block[:, None] == jnp.arange(block_total, dtype=jnp.int32)[None, :]).astype(
        jnp.float32
    )
    tile_mask = jnp.dot(rows_table, one_hot.T) > 0.5
    return jnp.repeat(tile_mask, BLOCK, axis=0)


def absorb(running, visiting, key_part, value_part, tile_mask):
    best, total, accum = running
    score_scale = 1.0 / math.sqrt(visiting.shape[-1])
    scores = (
        jnp.einsum("qgad,kgd->gaqk", visiting, key_part, preferred_element_type=jnp.float32)
        * score_scale
    )
    scores = jnp.where(tile_mask[None, None], scores, -jnp.inf)
    newest = jnp.maximum(best, jnp.max(scores, axis=-1))
    anchor = jnp.where(newest == -jnp.inf, 0.0, newest)
    factor = jnp.exp(best - anchor)
    weights = jnp.exp(scores - anchor[..., None])
    total = total * factor + jnp.sum(weights, axis=-1)
    rounded = weights.astype(jnp.bfloat16)
    accum = accum * factor[..., None] + jnp.einsum(
        "gaqk,kgd->gaqd", rounded, value_part, preferred_element_type=jnp.float32
    )
    return (newest, total, accum)


def visit(running, visiting, key_part, value_part, tile_mask):
    return absorb(running, visiting, key_part, value_part, tile_mask)


def on_device(queries, key_vectors, value_head_vectors, block_pattern, out_weight):
    tok_dev = queries.shape[0]
    heads_dev = queries.shape[1] // HEAD_SIZE
    query_group_count = QUERY_HEADS // KEY_VALUE_HEADS
    key_heads = max(1, heads_dev // query_group_count)
    query_per_key = heads_dev // key_heads
    blocks_dev = tok_dev // BLOCK
    context_size = lax.axis_size("ctx")
    context_index = lax.axis_index("ctx")
    head_index = lax.axis_index("head")
    block_total = block_pattern.shape[0]
    block_ids = jnp.arange(block_total, dtype=jnp.int32)
    active = ((block_pattern == 1) | (block_ids[:, None] == block_ids[None, :])).astype(jnp.int32)
    first_key_head = head_index * heads_dev // query_group_count
    own_keys = lax.dynamic_slice_in_dim(
        key_vectors, first_key_head * HEAD_SIZE, key_heads * HEAD_SIZE, 1
    )
    own_values = lax.dynamic_slice_in_dim(
        value_head_vectors, first_key_head * HEAD_SIZE, key_heads * HEAD_SIZE, 1
    )
    local_queries = queries.reshape(tok_dev, key_heads, query_per_key, HEAD_SIZE)
    stat_shape = (key_heads, query_per_key, tok_dev)
    initial = (
        jnp.full(stat_shape, -jnp.inf, jnp.float32),
        jnp.zeros(stat_shape, jnp.float32),
        jnp.zeros(stat_shape + (HEAD_SIZE,), jnp.float32),
    )
    keys_held = own_keys.reshape(tok_dev, key_heads, HEAD_SIZE)
    values_held = own_values.reshape(tok_dev, key_heads, HEAD_SIZE)

    def hop(hop_index, carried):
        visiting, running = carried
        root = (context_index - hop_index) % context_size
        tile_mask = block_mask(active, root * blocks_dev, context_index * tok_dev, tok_dev, tok_dev)
        best, total, accum = visit(running, visiting, keys_held, values_held, tile_mask)
        visiting = passed_along(visiting, "ctx", 1)
        moved = passed_along((best, total, accum), "ctx", 1)
        return (visiting, moved)

    arrived, running = lax.fori_loop(0, context_size, hop, (local_queries, initial))
    best, total, accum = running
    attended = accum / total[..., None]
    attended = (
        jnp.transpose(attended, (2, 0, 1, 3))
        .reshape(tok_dev, heads_dev * HEAD_SIZE)
        .astype(jnp.bfloat16)
    )
    mixed = jnp.dot(
        lax.all_gather(attended, "head", axis=1, tiled=True),
        out_weight,
        preferred_element_type=jnp.float32,
    )
    return mixed.astype(jnp.bfloat16)


def solution(mesh):
    return jax.shard_map(
        on_device,
        mesh=mesh,
        in_specs=(P("ctx", "head"), P("ctx", None), P("ctx", None), P(), P(None, "head")),
        out_specs=P("ctx", "head"),
        check_vma=False,
    )
```

profile of v0, /device:TPU:0, one launch (start us, length us, event | category | flops | bytes accessed | tf_op | source)
XLA Modules:
  0.0 221.5 jit_solution(5827685689468238781)
XLA Ops:
  6.5 0.0 all-gather.2.cloned.1.call-start
  6.5 1.3 copy.10
  7.8 0.3 copy.11
  8.1 0.0 copy-done
  8.1 0.9 dynamic-slice_bitcast_fusion
  9.0 0.1 broadcast_in_dim.75
  9.1 157.6 %while.21 = (s32[]{:T(128)}, bf16[256,1,8,128]{3,0,2,1:T(8,128)(2,1)S(1)}, f32[1,8,256]{2,1,0:T(8,128)S(1)}, f32[1,8,256]{2,1,0:T(8,128)S(1)}, f32[1,8,256,128]{...) while((s32[]{:T(128)}, ...), condition=%wide.region_3.4_spmd, body=%wide.region_0.3_spmd.sunk | while | flops 272663072 | bytes 16863716 | solution.py:95
  9.2 0.2 convolution_compare_fusion.2
  9.5 0.2 copy.15
  9.6 0.5 fusion.31
  10.1 0.8 fusion.35
  10.9 3.1 %collective-permute-start.3 = (f32[1,8,256,128]{3,2,1,0:T(8,128)S(1)}, f32[1,8,256,128]{3,2,1,0:T(8,128)S(1)}, u32[]{:S(2)}, u32[]{:S(2)}) collective-permute-start(f32[1,8,256,128]{3,2,1,0:T(8,128)S(1)} %fusion.35), channel_id=1, source_target_pairs={{0,8},{8,16},{16,24},{24,0},{1,9},{9,17},{17,25},{25,1},{2,10},{10... | collective-permute-start | bytes 3145736 | tf_op jit(solution)/shard_map/while/body/eval_jaxpr/ppermute | solution.py:17
  14.0 1.6 collective-permute-start
  15.6 1.6 collective-permute-start.1
  17.2 0.3 fusion.34
  17.5 0.1 collective-permute-start.2
  17.6 33.1 %collective-permute-done.1 = f32[1,8,256]{2,1,0:T(8,128)S(1)} collective-permute-done((f32[1,8,256]{2,1,0:T(8,128)S(1)}, f32[1,8,256]{2,1,0:T(8,128)S(1)}, u32[]{:S(2)}, u32[]{:S(2)}) %collective-permute-start.1) | collective-permute-done | bytes 8224 | tf_op jit(solution)/shard_map/while/body/eval_jaxpr/ppermute | solution.py:17
  50.7 0.1 collective-permute-done.2
  50.8 0.0 collective-permute-done
  50.8 0.0 collective-permute-done.3
  50.9 0.2 convolution_compare_fusion.2
  51.1 0.2 copy.15
  51.3 0.5 fusion.31
  51.8 0.8 fusion.35
  52.6 0.1 collective-permute-start.3
  52.6 1.3 collective-permute-start
  53.9 1.6 collective-permute-start.1
  55.5 0.3 fusion.34
  55.8 2.1 collective-permute-start.2
  57.9 32.3 %collective-permute-done.1 = f32[1,8,256]{2,1,0:T(8,128)S(1)} collective-permute-done((f32[1,8,256]{2,1,0:T(8,128)S(1)}, f32[1,8,256]{2,1,0:T(8,128)S(1)}, u32[]{:S(2)}, u32[]{:S(2)}) %collective-permute-start.1) | collective-permute-done | bytes 8224 | tf_op jit(solution)/shard_map/while/body/eval_jaxpr/ppermute | solution.py:17
  90.3 0.1 collective-permute-done.2
  90.3 0.0 collective-permute-done
  90.4 0.0 collective-permute-done.3
  90.4 0.2 convolution_compare_fusion.2
  90.7 0.2 copy.15
  90.9 0.5 fusion.31
  91.3 0.8 fusion.35
  92.1 0.1 collective-permute-start.3
  92.2 0.1 collective-permute-start
  92.3 0.7 collective-permute-start.1
  92.9 0.3 fusion.34
  93.3 4.2 %collective-permute-start.2 = (f32[1,8,256]{2,1,0:T(8,128)S(1)}, f32[1,8,256]{2,1,0:T(8,128)S(1)}, u32[]{:S(2)}, u32[]{:S(2)}) collective-permute-start(f32[1,8,256]{2,1,0:T(8,128)S(1)} %bitcast_add_fusion.2), channel_id=1, source_target_pairs={{0,8},{8,16},{16,24},{24,0},{1,9},{9,17},{17,25},{25,1},{2,10},{10... | collective-permute-start | bytes 24584 | tf_op jit(solution)/shard_map/while/body/eval_jaxpr/ppermute | solution.py:17
  97.5 31.4 %collective-permute-done.1 = f32[1,8,256]{2,1,0:T(8,128)S(1)} collective-permute-done((f32[1,8,256]{2,1,0:T(8,128)S(1)}, f32[1,8,256]{2,1,0:T(8,128)S(1)}, u32[]{:S(2)}, u32[]{:S(2)}) %collective-permute-start.1) | collective-permute-done | bytes 8224 | tf_op jit(solution)/shard_map/while/body/eval_jaxpr/ppermute | solution.py:17
  128.9 0.1 collective-permute-done.2
  129.0 0.0 collective-permute-done
  129.0 0.0 collective-permute-done.3
  129.1 0.2 convolution_compare_fusion.2
  129.3 0.2 copy.15
  129.5 0.5 fusion.31
  130.0 0.8 fusion.35
  130.8 0.1 collective-permute-start.3
  130.9 0.1 collective-permute-start
  130.9 0.6 collective-permute-start.1
  131.5 0.3 fusion.34
  131.8 4.3 %collective-permute-start.2 = (f32[1,8,256]{2,1,0:T(8,128)S(1)}, f32[1,8,256]{2,1,0:T(8,128)S(1)}, u32[]{:S(2)}, u32[]{:S(2)}) collective-permute-start(f32[1,8,256]{2,1,0:T(8,128)S(1)} %bitcast_add_fusion.2), channel_id=1, source_target_pairs={{0,8},{8,16},{16,24},{24,0},{1,9},{9,17},{17,25},{25,1},{2,10},{10... | collective-permute-start | bytes 24584 | tf_op jit(solution)/shard_map/while/body/eval_jaxpr/ppermute | solution.py:17
  136.2 30.5 %collective-permute-done.1 = f32[1,8,256]{2,1,0:T(8,128)S(1)} collective-permute-done((f32[1,8,256]{2,1,0:T(8,128)S(1)}, f32[1,8,256]{2,1,0:T(8,128)S(1)}, u32[]{:S(2)}, u32[]{:S(2)}) %collective-permute-start.1) | collective-permute-done | bytes 8224 | tf_op jit(solution)/shard_map/while/body/eval_jaxpr/ppermute | solution.py:17
  166.6 0.1 collective-permute-done.2
  166.7 0.0 collective-permute-done
  166.7 0.0 collective-permute-done.3
  166.7 0.3 copy.12
  167.1 0.9 divide_convert_fusion
  167.9 0.0 all-gather.2.cloned.1.call-update
  168.0 34.4 %all-gather.2.cloned.1.call-done = bf16[256,8192]{0,1:T(8,128)(2,1)} async-done(((bf16[256,1024]{0,1:T(8,128)(2,1)}), bf16[256,8192]{0,1:T(8,128)(2,1)}) %all-gather.2.cloned.1.call-update) | async-done | bytes 4194320 | tf_op jit(solution)/shard_map/all_gather | solution.py:104
  202.3 12.4 %convolution_convert_fusion = bf16[256,1024]{1,0:T(8,128)(2,1)} fusion(bf16[256,8192]{0,1:T(8,128)(2,1)} %all-gather.2.cloned.1.call-done, bf16[8192,1024]{1,0:T(8,128)(2,1)} %param.11), kind=kOutput, calls=%fused_computation.27 | convolution fusion | flops 4295229440 | bytes 21495808 | tf_op jit(solution)/shard_map/dot_general | solution.py:103
  (32 shorter events, 0.4 us)
Async XLA Ops:
  6.5 1.5 copy-start
  6.5 195.8 %all-gather.2.cloned.1.call-start = ((), (), s32[]{:S(2)}) async-start(), calls=%async_computation | async-start | bytes 4718592 | tf_op jit(solution)/shard_map/all_gather | solution.py:104
  10.9 39.9 %collective-permute-start.3 = (f32[1,8,256,128]{3,2,1,0:T(8,128)S(1)}, f32[1,8,256,128]{3,2,1,0:T(8,128)S(1)}, u32[]{:S(2)}, u32[]{:S(2)}) collective-permute-start(f32[1,8,256,128]{3,2,1,0:T(8,128)S(1)} %fusion.35), channel_id=1, source_target_pairs={{0,8},{8,16},{16,24},{24,0},{1,9},{9,17},{17,25},{25,1},{2,10},{10... | collective-permute-start | bytes 3145736 | tf_op jit(solution)/shard_map/while/body/eval_jaxpr/ppermute | solution.py:17
  14.0 36.8 %collective-permute-start = (bf16[256,1,8,128]{3,0,2,1:T(8,128)(2,1)S(1)}, bf16[256,1,8,128]{3,0,2,1:T(8,128)(2,1)S(1)}, u32[]{:S(2)}, u32[]{:S(2)}) collective-permute-start(bf16[256,1,8,128]{3,0,2,1:T(8,128)(2,1)S(1)} %copy.22), channel_id=1, source_target_pairs={{0,8},{8,16},{16,24},{24,0},{1,9},{9,17},{17,25},{25,1},{2,10},{10... | collective-permute-start | bytes 1572872 | tf_op jit(solution)/shard_map/while/body/eval_jaxpr/ppermute | solution.py:17
  15.6 35.1 %collective-permute-start.1 = (f32[1,8,256]{2,1,0:T(8,128)S(1)}, f32[1,8,256]{2,1,0:T(8,128)S(1)}, u32[]{:S(2)}, u32[]{:S(2)}) collective-permute-start(f32[1,8,256]{2,1,0:T(8,128)S(1)} %get-tuple-element.339), channel_id=1, source_target_pairs={{0,8},{8,16},{16,24},{24,0},{1,9},{9,17},{17,25},{25,1},{2,10},{10... | collective-permute-start | bytes 24584 | tf_op jit(solution)/shard_map/while/body/eval_jaxpr/ppermute | solution.py:17
  17.5 33.3 %collective-permute-start.2 = (f32[1,8,256]{2,1,0:T(8,128)S(1)}, f32[1,8,256]{2,1,0:T(8,128)S(1)}, u32[]{:S(2)}, u32[]{:S(2)}) collective-permute-start(f32[1,8,256]{2,1,0:T(8,128)S(1)} %bitcast_add_fusion.2), channel_id=1, source_target_pairs={{0,8},{8,16},{16,24},{24,0},{1,9},{9,17},{17,25},{25,1},{2,10},{10... | collective-permute-start | bytes 24584 | tf_op jit(solution)/shard_map/while/body/eval_jaxpr/ppermute | solution.py:17
  52.6 37.8 %collective-permute-start.3 = (f32[1,8,256,128]{3,2,1,0:T(8,128)S(1)}, f32[1,8,256,128]{3,2,1,0:T(8,128)S(1)}, u32[]{:S(2)}, u32[]{:S(2)}) collective-permute-start(f32[1,8,256,128]{3,2,1,0:T(8,128)S(1)} %fusion.35), channel_id=1, source_target_pairs={{0,8},{8,16},{16,24},{24,0},{1,9},{9,17},{17,25},{25,1},{2,10},{10... | collective-permute-start | bytes 3145736 | tf_op jit(solution)/shard_map/while/body/eval_jaxpr/ppermute | solution.py:17
  52.6 37.7 %collective-permute-start = (bf16[256,1,8,128]{3,0,2,1:T(8,128)(2,1)S(1)}, bf16[256,1,8,128]{3,0,2,1:T(8,128)(2,1)S(1)}, u32[]{:S(2)}, u32[]{:S(2)}) collective-permute-start(bf16[256,1,8,128]{3,0,2,1:T(8,128)(2,1)S(1)} %copy.22), channel_id=1, source_target_pairs={{0,8},{8,16},{16,24},{24,0},{1,9},{9,17},{17,25},{25,1},{2,10},{10... | collective-permute-start | bytes 1572872 | tf_op jit(solution)/shard_map/while/body/eval_jaxpr/ppermute | solution.py:17
  53.9 36.3 %collective-permute-start.1 = (f32[1,8,256]{2,1,0:T(8,128)S(1)}, f32[1,8,256]{2,1,0:T(8,128)S(1)}, u32[]{:S(2)}, u32[]{:S(2)}) collective-permute-start(f32[1,8,256]{2,1,0:T(8,128)S(1)} %get-tuple-element.339), channel_id=1, source_target_pairs={{0,8},{8,16},{16,24},{24,0},{1,9},{9,17},{17,25},{25,1},{2,10},{10... | collective-permute-start | bytes 24584 | tf_op jit(solution)/shard_map/while/body/eval_jaxpr/ppermute | solution.py:17
  55.8 34.5 %collective-permute-start.2 = (f32[1,8,256]{2,1,0:T(8,128)S(1)}, f32[1,8,256]{2,1,0:T(8,128)S(1)}, u32[]{:S(2)}, u32[]{:S(2)}) collective-permute-start(f32[1,8,256]{2,1,0:T(8,128)S(1)} %bitcast_add_fusion.2), channel_id=1, source_target_pairs={{0,8},{8,16},{16,24},{24,0},{1,9},{9,17},{17,25},{25,1},{2,10},{10... | collective-permute-start | bytes 24584 | tf_op jit(solution)/shard_map/while/body/eval_jaxpr/ppermute | solution.py:17
  92.1 36.9 %collective-permute-start.3 = (f32[1,8,256,128]{3,2,1,0:T(8,128)S(1)}, f32[1,8,256,128]{3,2,1,0:T(8,128)S(1)}, u32[]{:S(2)}, u32[]{:S(2)}) collective-permute-start(f32[1,8,256,128]{3,2,1,0:T(8,128)S(1)} %fusion.35), channel_id=1, source_target_pairs={{0,8},{8,16},{16,24},{24,0},{1,9},{9,17},{17,25},{25,1},{2,10},{10... | collective-permute-start | bytes 3145736 | tf_op jit(solution)/shard_map/while/body/eval_jaxpr/ppermute | solution.py:17
  92.2 36.8 %collective-permute-start = (bf16[256,1,8,128]{3,0,2,1:T(8,128)(2,1)S(1)}, bf16[256,1,8,128]{3,0,2,1:T(8,128)(2,1)S(1)}, u32[]{:S(2)}, u32[]{:S(2)}) collective-permute-start(bf16[256,1,8,128]{3,0,2,1:T(8,128)(2,1)S(1)} %copy.22), channel_id=1, source_target_pairs={{0,8},{8,16},{16,24},{24,0},{1,9},{9,17},{17,25},{25,1},{2,10},{10... | collective-permute-start | bytes 1572872 | tf_op jit(solution)/shard_map/while/body/eval_jaxpr/ppermute | solution.py:17
  92.3 36.6 %collective-permute-start.1 = (f32[1,8,256]{2,1,0:T(8,128)S(1)}, f32[1,8,256]{2,1,0:T(8,128)S(1)}, u32[]{:S(2)}, u32[]{:S(2)}) collective-permute-start(f32[1,8,256]{2,1,0:T(8,128)S(1)} %get-tuple-element.339), channel_id=1, source_target_pairs={{0,8},{8,16},{16,24},{24,0},{1,9},{9,17},{17,25},{25,1},{2,10},{10... | collective-permute-start | bytes 24584 | tf_op jit(solution)/shard_map/while/body/eval_jaxpr/ppermute | solution.py:17
  93.3 35.7 %collective-permute-start.2 = (f32[1,8,256]{2,1,0:T(8,128)S(1)}, f32[1,8,256]{2,1,0:T(8,128)S(1)}, u32[]{:S(2)}, u32[]{:S(2)}) collective-permute-start(f32[1,8,256]{2,1,0:T(8,128)S(1)} %bitcast_add_fusion.2), channel_id=1, source_target_pairs={{0,8},{8,16},{16,24},{24,0},{1,9},{9,17},{17,25},{25,1},{2,10},{10... | collective-permute-start | bytes 24584 | tf_op jit(solution)/shard_map/while/body/eval_jaxpr/ppermute | solution.py:17
  130.8 35.9 %collective-permute-start.3 = (f32[1,8,256,128]{3,2,1,0:T(8,128)S(1)}, f32[1,8,256,128]{3,2,1,0:T(8,128)S(1)}, u32[]{:S(2)}, u32[]{:S(2)}) collective-permute-start(f32[1,8,256,128]{3,2,1,0:T(8,128)S(1)} %fusion.35), channel_id=1, source_target_pairs={{0,8},{8,16},{16,24},{24,0},{1,9},{9,17},{17,25},{25,1},{2,10},{10... | collective-permute-start | bytes 3145736 | tf_op jit(solution)/shard_map/while/body/eval_jaxpr/ppermute | solution.py:17
  130.9 35.9 %collective-permute-start = (bf16[256,1,8,128]{3,0,2,1:T(8,128)(2,1)S(1)}, bf16[256,1,8,128]{3,0,2,1:T(8,128)(2,1)S(1)}, u32[]{:S(2)}, u32[]{:S(2)}) collective-permute-start(bf16[256,1,8,128]{3,0,2,1:T(8,128)(2,1)S(1)} %copy.22), channel_id=1, source_target_pairs={{0,8},{8,16},{16,24},{24,0},{1,9},{9,17},{17,25},{25,1},{2,10},{10... | collective-permute-start | bytes 1572872 | tf_op jit(solution)/shard_map/while/body/eval_jaxpr/ppermute | solution.py:17
  130.9 35.7 %collective-permute-start.1 = (f32[1,8,256]{2,1,0:T(8,128)S(1)}, f32[1,8,256]{2,1,0:T(8,128)S(1)}, u32[]{:S(2)}, u32[]{:S(2)}) collective-permute-start(f32[1,8,256]{2,1,0:T(8,128)S(1)} %get-tuple-element.339), channel_id=1, source_target_pairs={{0,8},{8,16},{16,24},{24,0},{1,9},{9,17},{17,25},{25,1},{2,10},{10... | collective-permute-start | bytes 24584 | tf_op jit(solution)/shard_map/while/body/eval_jaxpr/ppermute | solution.py:17
  131.8 34.9 %collective-permute-start.2 = (f32[1,8,256]{2,1,0:T(8,128)S(1)}, f32[1,8,256]{2,1,0:T(8,128)S(1)}, u32[]{:S(2)}, u32[]{:S(2)}) collective-permute-start(f32[1,8,256]{2,1,0:T(8,128)S(1)} %bitcast_add_fusion.2), channel_id=1, source_target_pairs={{0,8},{8,16},{16,24},{24,0},{1,9},{9,17},{17,25},{25,1},{2,10},{10... | collective-permute-start | bytes 24584 | tf_op jit(solution)/shard_map/while/body/eval_jaxpr/ppermute | solution.py:17
Sparse Core Ops, SparseCore 0:
  168.1 34.1 all-gather.1
where the time goes:
time: 222 us
  waiting for transfers between devices  162 us (73%)
  starting transfers between devices  21.5 us (10%)
  matrix products  18.2 us (8%)
  between operations  13.5 us (6%)
  local copies, waits for them, and re-layouts  3.77 us (2%)
    ppermute x16, waiting for transfers between devices, passed_along(): return lax.ppermute(value, axis, pairs)  128 us
    all_gather x1, waiting for transfers between devices, on_device(): lax.all_gather(attended, 'head', axis=1, tiled=True)  34.4 us
    ppermute x16, starting transfers between devices, passed_along(): return lax.ppermute(value, axis, pairs)  21.5 us
    dot_general x1, matrix products, on_device(): jnp.dot(lax.all_gather(attended, 'head', axis=1, tiled=True), out_weight,...  12.4 us
  transfers between devices with their start and end apart: 17, of which 9 were waited for; matrix products, arithmetic and copies ran while one was open for 1% of the time, Pallas kernels for 0%

commit v1 on v0

v1 whole, which is shorter than its diff:
```python
import functools
import math

import jax
import jax.numpy as jnp
from jax import lax
from jax.experimental import pallas as pl
from jax.experimental.pallas import tpu as pltpu
from jax.sharding import PartitionSpec as P

QUERY_HEADS = 64
KEY_VALUE_HEADS = 8
HEAD_SIZE = 128
BLOCK = 128
FAR = -1e30


def shifted(value, axis, steps):
    count = lax.axis_size(axis)
    return lax.ppermute(value, axis, [(source, (source + steps) % count) for source in range(count)])


def swapped(value, axis, bits):
    count = lax.axis_size(axis)
    return lax.ppermute(value, axis, [(source, source ^ bits) for source in range(count)])


def attention_kernel(chunks, sources_ref, pattern_ref, q_ref, *refs):
    kv_refs, out_ref = refs[:-1], refs[-1]
    tok_dev, width = q_ref.shape
    heads = width // HEAD_SIZE
    blocks_dev = tok_dev // BLOCK
    group = min(heads, 4)
    exponent_scale = math.log2(math.e) / math.sqrt(HEAD_SIZE)
    keys = jnp.concatenate([ref[:, :HEAD_SIZE] for ref in kv_refs], axis=0)
    values = jnp.concatenate([ref[:, HEAD_SIZE:] for ref in kv_refs], axis=0)
    values = jnp.concatenate([values, jnp.ones_like(values)], axis=1)
    own = sources_ref[chunks]
    for a in range(blocks_dev):
        query_block = own * blocks_dev + a
        pieces = []
        for s in range(chunks):
            for j in range(blocks_dev):
                key_block = sources_ref[s] * blocks_dev + j
                on = (pattern_ref[query_block, key_block] == 1) | (query_block == key_block)
                pieces.append(jnp.full((1, BLOCK), jnp.where(on, 0.0, FAR), jnp.float32))
        bias = jnp.concatenate(pieces, axis=1)
        rows = slice(a * BLOCK, (a + 1) * BLOCK)
        for first in range(0, heads, group):
            ids = range(first, first + group)
            q = jnp.concatenate(
                [q_ref[rows, h * HEAD_SIZE : (h + 1) * HEAD_SIZE] for h in ids], axis=0
            )
            scores = lax.dot_general(
                q, keys, (((1,), (1,)), ((), ())), preferred_element_type=jnp.float32
            )
            scores = scores + bias
            top = jnp.max(scores, axis=1, keepdims=True)
            weights = jnp.exp2((scores - top) * exponent_scale).astype(jnp.bfloat16)
            summed = jnp.dot(weights, values, preferred_element_type=jnp.float32)
            result = (summed[:, :HEAD_SIZE] / summed[:, HEAD_SIZE:]).astype(jnp.bfloat16)
            for i, h in enumerate(ids):
                out_ref[rows, h * HEAD_SIZE : (h + 1) * HEAD_SIZE] = result[
                    i * BLOCK : (i + 1) * BLOCK
                ]


def attend(queries, kv_parts, sources, block_pattern):
    chunks = len(kv_parts)
    smem = pl.BlockSpec(memory_space=pltpu.SMEM)
    vmem = pl.BlockSpec(memory_space=pltpu.VMEM)
    return pl.pallas_call(
        functools.partial(attention_kernel, chunks),
        out_shape=jax.ShapeDtypeStruct(queries.shape, jnp.bfloat16),
        in_specs=[smem, smem, vmem] + [vmem] * chunks,
        out_specs=vmem,
        compiler_params=pltpu.CompilerParams(vmem_limit_bytes=40 << 20),
    )(sources, block_pattern, queries, *kv_parts)


def gathered_over_ctx(kv):
    count = lax.axis_size("ctx")
    me = lax.axis_index("ctx")
    if count == 4:
        parts = [kv, shifted(kv, "ctx", 2), shifted(kv, "ctx", 1), shifted(kv, "ctx", 3)]
        steps = jnp.array([0, 2, 1, 3, 0], jnp.int32)
        return parts, (me - steps + count) % count
    whole = lax.all_gather(kv, "ctx")
    sources = jnp.concatenate([jnp.arange(count, dtype=jnp.int32), me[None].astype(jnp.int32)])
    return [whole[i] for i in range(count)], sources


def weight_rows(out_weight, device, rows, first=0):
    return lax.dynamic_slice_in_dim(out_weight, device * rows + first, rows if not first else first, 0)


def on_device(queries, key_vectors, value_head_vectors, block_pattern, out_weight):
    heads_dev = queries.shape[1] // HEAD_SIZE
    query_group_count = QUERY_HEADS // KEY_VALUE_HEADS
    head_count = lax.axis_size("head")
    me = lax.axis_index("head")
    key_head = me * heads_dev // query_group_count
    start = key_head * HEAD_SIZE
    kv = jnp.concatenate(
        [
            lax.dynamic_slice_in_dim(key_vectors, start, HEAD_SIZE, 1),
            lax.dynamic_slice_in_dim(value_head_vectors, start, HEAD_SIZE, 1),
        ],
        axis=1,
    )
    kv_parts, sources = gathered_over_ctx(kv)
    att = attend(queries, kv_parts, sources, block_pattern)

    width = att.shape[1]

    def times(part, owner, first=0):
        rows = lax.dynamic_slice_in_dim(out_weight, owner * width + first, part.shape[1], 0)
        return jnp.dot(part, rows, preferred_element_type=jnp.float32)

    if head_count == 8:
        half = width // 2
        x = swapped(att, "head", 2)
        y = swapped(att, "head", 4)
        sib = swapped(att, "head", 1)
        mixed = times(att, me) + times(sib, me ^ 1)
        xs = swapped(x, "head", 1)
        da = swapped(x[:, :half], "head", 4)
        mixed = mixed + times(x, me ^ 2) + times(xs, me ^ 3)
        ys = swapped(y, "head", 1)
        db = swapped(y[:, half:], "head", 2)
        mixed = mixed + times(y, me ^ 4) + times(ys, me ^ 5)
        das = swapped(da, "head", 1)
        mixed = mixed + times(da, me ^ 6) + times(das, me ^ 7)
        dbs = swapped(db, "head", 1)
        mixed = mixed + times(db, me ^ 6, half) + times(dbs, me ^ 7, half)
    else:
        mixed = jnp.dot(
            lax.all_gather(att, "head", axis=1, tiled=True),
            out_weight,
            preferred_element_type=jnp.float32,
        )
    return mixed.astype(jnp.bfloat16)


def solution(mesh):
    return jax.shard_map(
        on_device,
        mesh=mesh,
        in_specs=(P("ctx", "head"), P("ctx", None), P("ctx", None), P(), P(None, "head")),
        out_specs=P("ctx", "head"),
        check_vma=False,
    )
```

time: 222 us -> 53.5 us (0.24)
  the two profiles are of different devices: /device:TPU:0 before, /device:TPU:17 now
where the time goes in v1:
time: 53.5 us; the launch traced here: 53.2 us
  waiting for transfers between devices  21.1 us (39%)
  matrix products  13.3 us (25%)
  starting transfers between devices  11.4 us (21%)
  Pallas kernels  3.84 us (7%)
  local copies, waits for them, and re-layouts  2.65 us (5%)
  other arithmetic  0.68 us (1%)
    dot_general x10, matrix products, times(): return jnp.dot(part, rows, preferred_element_type=jnp.float32)  13.3 us
    ppermute x3, waiting for transfers between devices, shifted(): lax.ppermute(value, axis, [(source, (source + steps) % count) for source...  11.6 us
    ppermute x9, waiting for transfers between devices, swapped(): lax.ppermute(value, axis, [(source, source ^ bits) for source in range(co...  9.51 us
    ppermute x9, starting transfers between devices, swapped(): lax.ppermute(value, axis, [(source, source ^ bits) for source in range(co...  8.83 us
    pallas_call x1, Pallas kernels, attend(): pl.pallas_call(functools.partial(attention_kernel, chunks), out_shape=jax...  3.84 us
    ppermute x3, starting transfers between devices, shifted(): lax.ppermute(value, axis, [(source, (source + steps) % count) for source...  2.54 us
    unnamed x6, local copies, waits for them, and re-layouts  1.73 us
  transfers between devices with their start and end apart: 12, of which 3 were waited for; matrix products, arithmetic and copies ran while one was open for 24% of the time, Pallas kernels for 0%

profile of v1, /device:TPU:17, one launch (start us, length us, event | category | flops | bytes accessed | tf_op | source)
XLA Modules:
  0.0 53.2 jit_solution(2391074949913499228)
XLA Ops:
  0.0 0.9 %constant_dynamic-slice_fusion = (bf16[256,128]{1,0:T(8,128)(2,1)S(1)}, bf16[256,128]{1,0:T(8,128)(2,1)S(1)}) fusion(bf16[256,1024]{1,0:T(8,128)(2,1)} %param.8, s32[]{:T(128)S(6)} %select_n.47, bf16[256,1024]{1,0:T(8,128)(2,1)} %param.7), kind=kLoop, calls=%fused_computation.39 | loop fusion | bytes 262148 | tf_op jit(solution)/shard_map/dynamic_slice | solution.py:107
  0.9 0.1 collective-permute-start
  1.0 1.3 %collective-permute-start.1 = (bf16[256,256]{1,0:T(8,128)(2,1)S(1)}, bf16[256,256]{1,0:T(8,128)(2,1)S(1)}, u32[]{:S(2)}, u32[]{:S(2)}) collective-permute-start(bf16[256,256]{1,0:T(8,128)(2,1)S(1)} %pad_maximum_fusion.refs_0_), channel_id=1, source_target_pairs={{0,8},{8,16},{16,24},{24,0},{1,9},{9,17},{17,25},{25,1},{2,10},{10... | collective-permute-start | bytes 393224 | tf_op jit(solution)/shard_map/ppermute | solution.py:20
  2.3 1.1 %collective-permute-start.2 = (bf16[256,256]{1,0:T(8,128)(2,1)S(1)}, bf16[256,256]{1,0:T(8,128)(2,1)S(1)}, u32[]{:S(2)}, u32[]{:S(2)}) collective-permute-start(bf16[256,256]{1,0:T(8,128)(2,1)S(1)} %pad_maximum_fusion.refs_0_), channel_id=1, source_target_pairs={{0,24},{8,0},{16,8},{24,16},{1,25},{9,1},{17,9},{25,17},{2,26},{10... | collective-permute-start | bytes 393224 | tf_op jit(solution)/shard_map/ppermute | solution.py:20
  3.5 0.7 %and_select_fusion.sources_ref = s32[5]{0:T(128)S(1)} fusion(s32[5]{0:T(128)} %constant.63, s32[]{:T(128)S(6)} %axis_index.23), kind=kLoop, calls=%fused_computation.43 | loop fusion | flops 65 | bytes 44 | tf_op jit(solution)/shard_map/jit(remainder)/select_n | solution.py:87
  4.1 4.6 %collective-permute-done.refs_1_ = bf16[256,256]{1,0:T(8,128)(2,1)S(1)} collective-permute-done((bf16[256,256]{1,0:T(8,128)(2,1)S(1)}, bf16[256,256]{1,0:T(8,128)(2,1)S(1)}, u32[]{:S(2)}, u32[]{:S(2)}) %collective-permute-start) | collective-permute-done | bytes 131104 | tf_op jit(solution)/shard_map/ppermute | solution.py:20
  8.7 7.0 %collective-permute-done.1.refs_2_ = bf16[256,256]{1,0:T(8,128)(2,1)S(1)} collective-permute-done((bf16[256,256]{1,0:T(8,128)(2,1)S(1)}, bf16[256,256]{1,0:T(8,128)(2,1)S(1)}, u32[]{:S(2)}, u32[]{:S(2)}) %collective-permute-start.1) | collective-permute-done | bytes 131104 | tf_op jit(solution)/shard_map/ppermute | solution.py:20
  15.7 0.0 collective-permute-done.2.refs_3_
  15.7 0.0 copy-start
  15.7 1.0 %copy-done = bf16[256,1024]{1,0:T(8,128)(2,1)S(1)} copy-done((bf16[256,1024]{1,0:T(8,128)(2,1)S(1)}, bf16[256,1024]{1,0:T(8,128)(2,1)}, u32[]{:S(2)}) %copy-start) | copy-done | bytes 524312
  16.8 0.0 copy-start.1
  16.8 0.7 %copy-done.1 = s32[8,8]{1,0:T(8,128)S(1)} copy-done((s32[8,8]{1,0:T(8,128)S(1)}, s32[8,8]{1,0:T(8,128)}, u32[]{:S(2)}) %copy-start.1) | copy-done | bytes 280
  17.5 3.8 %shard_map.64 = bf16[256,1024]{1,0:T(8,128)(2,1)S(1)} custom-call(s32[5]{0:T(128)S(1)} %and_select_fusion.sources_ref, s32[8,8]{1,0:T(8,128)S(1)} %copy-done.1, bf16[256,1024]{1,0:T(8,128)(2,1)S(1)} %copy-done, bf16[256,256]{1,0:T(8,128)(2,1)S(1)} %pad_maximum_fusion.refs_0_, bf16[256,256]{1,0:T(8,128)(2,1)S(1)} %collective-permute-done.refs_1_, ...), custom_call_target="tpu_custom_call" | custom-call | tf_op jit(solution)/shard_map/pallas_call | solution.py:72
  21.3 1.3 %collective-permute-start.4 = (bf16[256,1024]{1,0:T(8,128)(2,1)S(1)}, bf16[256,1024]{1,0:T(8,128)(2,1)S(1)}, u32[]{:S(2)}, u32[]{:S(2)}) collective-permute-start(bf16[256,1024]{1,0:T(8,128)(2,1)S(1)} %shard_map.64), channel_id=1, source_target_pairs={{0,2},{1,3},{2,0},{3,1},{4,6},{5,7},{6,4},{7,5},{8,10},{9,11},{10,... | collective-permute-start | bytes 1572872 | tf_op jit(solution)/shard_map/ppermute | solution.py:25
  22.6 1.2 %collective-permute-start.6 = (bf16[256,1024]{1,0:T(8,128)(2,1)S(1)}, bf16[256,1024]{1,0:T(8,128)(2,1)S(1)}, u32[]{:S(2)}, u32[]{:S(2)}) collective-permute-start(bf16[256,1024]{1,0:T(8,128)(2,1)S(1)} %shard_map.64), channel_id=1, source_target_pairs={{0,4},{1,5},{2,6},{3,7},{4,0},{5,1},{6,2},{7,3},{8,12},{9,13},{10,... | collective-permute-start | bytes 1572872 | tf_op jit(solution)/shard_map/ppermute | solution.py:25
  23.8 1.1 %collective-permute-start.3 = (bf16[256,1024]{1,0:T(8,128)(2,1)S(1)}, bf16[256,1024]{1,0:T(8,128)(2,1)S(1)}, u32[]{:S(2)}, u32[]{:S(2)}) collective-permute-start(bf16[256,1024]{1,0:T(8,128)(2,1)S(1)} %shard_map.64), channel_id=1, source_target_pairs={{0,1},{1,0},{2,3},{3,2},{4,5},{5,4},{6,7},{7,6},{8,9},{9,8},{10,11... | collective-permute-start | bytes 1572872 | tf_op jit(solution)/shard_map/ppermute | solution.py:25
  24.9 0.0 copy-start.2
  24.9 9.5 %collective-permute-done.4 = bf16[256,1024]{1,0:T(8,128)(2,1)S(1)} collective-permute-done((bf16[256,1024]{1,0:T(8,128)(2,1)S(1)}, bf16[256,1024]{1,0:T(8,128)(2,1)S(1)}, u32[]{:S(2)}, u32[]{:S(2)}) %collective-permute-start.4) | collective-permute-done | bytes 524320 | tf_op jit(solution)/shard_map/ppermute | solution.py:25
  34.4 1.3 %collective-permute-start.8 = (bf16[256,512]{1,0:T(8,128)(2,1)S(1)}, bf16[256,512]{1,0:T(8,128)(2,1)S(1)}, u32[]{:S(2)}, u32[]{:S(2)}) collective-permute-start(bf16[256,512]{1,0:T(8,128)(2,1)S(1)} %slice.8), channel_id=1, source_target_pairs={{0,4},{1,5},{2,6},{3,7},{4,0},{5,1},{6,2},{7,3},{8,12},{9,13},{10,... | collective-permute-start | bytes 786440 | tf_op jit(solution)/shard_map/ppermute | solution.py:25
  35.7 0.0 collective-permute-done.6
  35.7 1.3 %collective-permute-start.10 = (bf16[256,512]{1,0:T(8,128)(2,1)S(1)}, bf16[256,512]{1,0:T(8,128)(2,1)S(1)}, u32[]{:S(2)}, u32[]{:S(2)}) collective-permute-start(bf16[256,512]{1,0:T(8,128)(2,1)S(1)} %slice.9), channel_id=1, source_target_pairs={{0,2},{1,3},{2,0},{3,1},{4,6},{5,7},{6,4},{7,5},{8,10},{9,11},{10,... | collective-permute-start | bytes 786440 | tf_op jit(solution)/shard_map/ppermute | solution.py:25
  37.0 2.3 %fusion.6 = f32[256,1024]{1,0:T(8,128)S(1)} fusion(bf16[256,1024]{1,0:T(8,128)(2,1)S(1)} %collective-permute-done.4, bf16[8192,1024]{1,0:T(8,128)(2,1)} %param.10, s32[]{:T(128)S(6)} %select_n.50), kind=kOutput, calls=%fused_computation.6 | convolution fusion | flops 536870912 | bytes 3670020 | tf_op jit(solution)/shard_map/dot_general | solution.py:118
  39.3 0.0 collective-permute-done.3
  39.3 2.3 %fusion.8 = f32[256,1024]{1,0:T(8,128)S(1)} fusion(bf16[256,1024]{1,0:T(8,128)(2,1)S(1)} %collective-permute-done.3, bf16[8192,1024]{1,0:T(8,128)(2,1)} %param.10, s32[]{:T(128)S(6)} %select_n.49), kind=kOutput, calls=%fused_computation.8 | convolution fusion | flops 536870912 | bytes 3670020 | tf_op jit(solution)/shard_map/dot_general | solution.py:118
  41.6 2.4 %fusion.15 = f32[256,1024]{1,0:T(8,128)S(1)} fusion(f32[256,1024]{1,0:T(8,128)S(1)} %fusion.6, f32[256,1024]{1,0:T(8,128)S(1)} %fusion.8, bf16[256,1024]{1,0:T(8,128)(2,1)S(1)} %shard_map.64, bf16[8192,1024]{1,0:T(8,128)(2,1)} %param.10, s32[]{:T(128)S(6)} %select_n.48), kind=kOutput, calls=%fused_computation.13 | convolution fusion | flops 537395200 | bytes 5767172 | tf_op jit(solution)/shard_map/dot_general | solution.py:118
  44.0 2.0 %collective-permute-start.7 = (bf16[256,1024]{1,0:T(8,128)(2,1)S(1)}, bf16[256,1024]{1,0:T(8,128)(2,1)S(1)}, u32[]{:S(2)}, u32[]{:S(2)}) collective-permute-start(bf16[256,1024]{1,0:T(8,128)(2,1)S(1)} %collective-permute-done.6), channel_id=1, source_target_pairs={{0,1},{1,0},{2,3},{3,2},{4,5},{5,4},{6,7},{7,6},{8,9},{9,8},{10,11... | collective-permute-start | bytes 1572872 | tf_op jit(solution)/shard_map/ppermute | solution.py:25
  46.0 0.1 collective-permute-start.5
  46.0 2.3 %fusion.2 = f32[256,1024]{1,0:T(8,128)S(1)} fusion(bf16[256,1024]{1,0:T(8,128)(2,1)S(1)} %collective-permute-done.6, bf16[8192,1024]{1,0:T(8,128)(2,1)} %param.10, s32[]{:T(128)S(6)} %select_n.52), kind=kOutput, calls=%fused_computation.2 | convolution fusion | flops 536870912 | bytes 3670020 | tf_op jit(solution)/shard_map/dot_general | solution.py:118
  48.3 0.0 collective-permute-done.8
  48.4 0.5 collective-permute-start.9
  48.9 0.0 copy-done.2
  48.9 0.4 fusion.36
  49.3 0.0 collective-permute-done.10
  49.3 0.1 collective-permute-start.11
  49.5 0.4 fusion.33
  49.9 0.0 collective-permute-done.7
  49.9 0.7 %fusion = f32[256,1024]{1,0:T(8,128)S(1)} fusion(bf16[256,1024]{1,0:T(8,128)(2,1)S(1)} %collective-permute-done.7, bf16[8192,1024]{1,0:T(8,128)(2,1)S(1)} %copy-done.2, s32[]{:T(128)S(6)} %select_n.53), kind=kOutput, calls=%fused_computation | convolution fusion | flops 536870912 | bytes 3670020 | tf_op jit(solution)/shard_map/dot_general | solution.py:118
  50.6 0.0 collective-permute-done.5
  50.6 0.8 %fusion.28 = f32[256,1024]{1,0:T(8,128)S(1)} fusion(f32[256,1024]{1,0:T(8,128)S(1)} %fusion.36, f32[256,1024]{1,0:T(8,128)S(1)} %fusion, f32[256,1024]{1,0:T(8,128)S(1)} %fusion.2, f32[256,1024]{1,0:T(8,128)S(1)} %fusion.15, bf16[256,1024]{1,0:T(8,128)(2,1)S(1)} %collective-permute-done.5, bf16[8192,1024]{1,0:T(8,128)(2,1)S(1)} %copy-done.2, s32[]{:T(128)S(6)} %select_n.51), kind=kOutput, calls=%fused_computation.20 | convolution fusion | flops 537919488 | bytes 7864324 | tf_op jit(solution)/shard_map/dot_general | solution.py:118
  51.5 0.0 collective-permute-done.9
  51.5 0.4 fusion.24
  51.9 0.0 collective-permute-done.11
  51.9 1.2 %fusion.31 = bf16[256,1024]{1,0:T(8,128)(2,1)} fusion(f32[256,1024]{1,0:T(8,128)S(1)} %fusion.24, bf16[256,512]{1,0:T(8,128)(2,1)S(1)} %collective-permute-done.11, bf16[8192,1024]{1,0:T(8,128)(2,1)S(1)} %copy-done.2, s32[]{:T(128)S(6)} %select_n.57), kind=kOutput, calls=%fused_computation.21 | convolution fusion | flops 268959744 | bytes 2883588 | tf_op jit(solution)/shard_map/dot_general | solution.py:118
  (3 shorter events, 0.1 us)
Async XLA Ops:
  0.9 7.8 %collective-permute-start = (bf16[256,256]{1,0:T(8,128)(2,1)S(1)}, bf16[256,256]{1,0:T(8,128)(2,1)S(1)}, u32[]{:S(2)}, u32[]{:S(2)}) collective-permute-start(bf16[256,256]{1,0:T(8,128)(2,1)S(1)} %pad_maximum_fusion.refs_0_), channel_id=1, source_target_pairs={{0,16},{8,24},{16,0},{24,8},{1,17},{9,25},{17,1},{25,9},{2,18},{10... | collective-permute-start | bytes 393224 | tf_op jit(solution)/shard_map/ppermute | solution.py:20
  1.0 14.7 %collective-permute-start.1 = (bf16[256,256]{1,0:T(8,128)(2,1)S(1)}, bf16[256,256]{1,0:T(8,128)(2,1)S(1)}, u32[]{:S(2)}, u32[]{:S(2)}) collective-permute-start(bf16[256,256]{1,0:T(8,128)(2,1)S(1)} %pad_maximum_fusion.refs_0_), channel_id=1, source_target_pairs={{0,8},{8,16},{16,24},{24,0},{1,9},{9,17},{17,25},{25,1},{2,10},{10... | collective-permute-start | bytes 393224 | tf_op jit(solution)/shard_map/ppermute | solution.py:20
  2.3 13.4 %collective-permute-start.2 = (bf16[256,256]{1,0:T(8,128)(2,1)S(1)}, bf16[256,256]{1,0:T(8,128)(2,1)S(1)}, u32[]{:S(2)}, u32[]{:S(2)}) collective-permute-start(bf16[256,256]{1,0:T(8,128)(2,1)S(1)} %pad_maximum_fusion.refs_0_), channel_id=1, source_target_pairs={{0,24},{8,0},{16,8},{24,16},{1,25},{9,1},{17,9},{25,17},{2,26},{10... | collective-permute-start | bytes 393224 | tf_op jit(solution)/shard_map/ppermute | solution.py:20
  15.7 1.0 %copy-start = (bf16[256,1024]{1,0:T(8,128)(2,1)S(1)}, bf16[256,1024]{1,0:T(8,128)(2,1)}, u32[]{:S(2)}) copy-start(bf16[256,1024]{1,0:T(8,128)(2,1)} %q_ref.1) | copy-start | bytes 1572868
  16.8 0.7 %copy-start.1 = (s32[8,8]{1,0:T(8,128)S(1)}, s32[8,8]{1,0:T(8,128)}, u32[]{:S(2)}) copy-start(s32[8,8]{1,0:T(8,128)} %pattern_ref.1) | copy-start | bytes 772
  21.3 13.1 %collective-permute-start.4 = (bf16[256,1024]{1,0:T(8,128)(2,1)S(1)}, bf16[256,1024]{1,0:T(8,128)(2,1)S(1)}, u32[]{:S(2)}, u32[]{:S(2)}) collective-permute-start(bf16[256,1024]{1,0:T(8,128)(2,1)S(1)} %shard_map.64), channel_id=1, source_target_pairs={{0,2},{1,3},{2,0},{3,1},{4,6},{5,7},{6,4},{7,5},{8,10},{9,11},{10,... | collective-permute-start | bytes 1572872 | tf_op jit(solution)/shard_map/ppermute | solution.py:25
  22.6 13.1 %collective-permute-start.6 = (bf16[256,1024]{1,0:T(8,128)(2,1)S(1)}, bf16[256,1024]{1,0:T(8,128)(2,1)S(1)}, u32[]{:S(2)}, u32[]{:S(2)}) collective-permute-start(bf16[256,1024]{1,0:T(8,128)(2,1)S(1)} %shard_map.64), channel_id=1, source_target_pairs={{0,4},{1,5},{2,6},{3,7},{4,0},{5,1},{6,2},{7,3},{8,12},{9,13},{10,... | collective-permute-start | bytes 1572872 | tf_op jit(solution)/shard_map/ppermute | solution.py:25
  23.8 15.5 %collective-permute-start.3 = (bf16[256,1024]{1,0:T(8,128)(2,1)S(1)}, bf16[256,1024]{1,0:T(8,128)(2,1)S(1)}, u32[]{:S(2)}, u32[]{:S(2)}) collective-permute-start(bf16[256,1024]{1,0:T(8,128)(2,1)S(1)} %shard_map.64), channel_id=1, source_target_pairs={{0,1},{1,0},{2,3},{3,2},{4,5},{5,4},{6,7},{7,6},{8,9},{9,8},{10,11... | collective-permute-start | bytes 1572872 | tf_op jit(solution)/shard_map/ppermute | solution.py:25
  24.9 24.0 %copy-start.2 = (bf16[8192,1024]{1,0:T(8,128)(2,1)S(1)}, bf16[8192,1024]{1,0:T(8,128)(2,1)}, u32[]{:S(2)}) copy-start(bf16[8192,1024]{1,0:T(8,128)(2,1)} %param.10) | copy-start | bytes 50331652
  34.4 14.0 %collective-permute-start.8 = (bf16[256,512]{1,0:T(8,128)(2,1)S(1)}, bf16[256,512]{1,0:T(8,128)(2,1)S(1)}, u32[]{:S(2)}, u32[]{:S(2)}) collective-permute-start(bf16[256,512]{1,0:T(8,128)(2,1)S(1)} %slice.8), channel_id=1, source_target_pairs={{0,4},{1,5},{2,6},{3,7},{4,0},{5,1},{6,2},{7,3},{8,12},{9,13},{10,... | collective-permute-start | bytes 786440 | tf_op jit(solution)/shard_map/ppermute | solution.py:25
  35.7 13.6 %collective-permute-start.10 = (bf16[256,512]{1,0:T(8,128)(2,1)S(1)}, bf16[256,512]{1,0:T(8,128)(2,1)S(1)}, u32[]{:S(2)}, u32[]{:S(2)}) collective-permute-start(bf16[256,512]{1,0:T(8,128)(2,1)S(1)} %slice.9), channel_id=1, source_target_pairs={{0,2},{1,3},{2,0},{3,1},{4,6},{5,7},{6,4},{7,5},{8,10},{9,11},{10,... | collective-permute-start | bytes 786440 | tf_op jit(solution)/shard_map/ppermute | solution.py:25
  44.0 5.9 %collective-permute-start.7 = (bf16[256,1024]{1,0:T(8,128)(2,1)S(1)}, bf16[256,1024]{1,0:T(8,128)(2,1)S(1)}, u32[]{:S(2)}, u32[]{:S(2)}) collective-permute-start(bf16[256,1024]{1,0:T(8,128)(2,1)S(1)} %collective-permute-done.6), channel_id=1, source_target_pairs={{0,1},{1,0},{2,3},{3,2},{4,5},{5,4},{6,7},{7,6},{8,9},{9,8},{10,11... | collective-permute-start | bytes 1572872 | tf_op jit(solution)/shard_map/ppermute | solution.py:25
  46.0 4.7 %collective-permute-start.5 = (bf16[256,1024]{1,0:T(8,128)(2,1)S(1)}, bf16[256,1024]{1,0:T(8,128)(2,1)S(1)}, u32[]{:S(2)}, u32[]{:S(2)}) collective-permute-start(bf16[256,1024]{1,0:T(8,128)(2,1)S(1)} %collective-permute-done.4), channel_id=1, source_target_pairs={{0,1},{1,0},{2,3},{3,2},{4,5},{5,4},{6,7},{7,6},{8,9},{9,8},{10,11... | collective-permute-start | bytes 1572872 | tf_op jit(solution)/shard_map/ppermute | solution.py:25
  48.4 3.1 %collective-permute-start.9 = (bf16[256,512]{1,0:T(8,128)(2,1)S(1)}, bf16[256,512]{1,0:T(8,128)(2,1)S(1)}, u32[]{:S(2)}, u32[]{:S(2)}) collective-permute-start(bf16[256,512]{1,0:T(8,128)(2,1)S(1)} %collective-permute-done.8), channel_id=1, source_target_pairs={{0,1},{1,0},{2,3},{3,2},{4,5},{5,4},{6,7},{7,6},{8,9},{9,8},{10,11... | collective-permute-start | bytes 786440 | tf_op jit(solution)/shard_map/ppermute | solution.py:25
  49.3 2.6 %collective-permute-start.11 = (bf16[256,512]{1,0:T(8,128)(2,1)S(1)}, bf16[256,512]{1,0:T(8,128)(2,1)S(1)}, u32[]{:S(2)}, u32[]{:S(2)}) collective-permute-start(bf16[256,512]{1,0:T(8,128)(2,1)S(1)} %collective-permute-done.10), channel_id=1, source_target_pairs={{0,1},{1,0},{2,3},{3,2},{4,5},{5,4},{6,7},{7,6},{8,9},{9,8},{10,11... | collective-permute-start | bytes 786440 | tf_op jit(solution)/shard_map/ppermute | solution.py:25

commit v2 on v1

v2 whole, which is shorter than its diff:
```python
import functools
import math

import jax
import jax.numpy as jnp
from jax import lax
from jax.experimental import pallas as pl
from jax.experimental.pallas import tpu as pltpu
from jax.sharding import PartitionSpec as P

QUERY_HEADS = 64
KEY_VALUE_HEADS = 8
HEAD_SIZE = 128
BLOCK = 128
FAR = -1e30

SMEM = pl.BlockSpec(memory_space=pltpu.SMEM)
VMEM = pl.BlockSpec(memory_space=pltpu.VMEM)
HBM = pl.BlockSpec(memory_space=pltpu.HBM)


def params(mib):
    return pltpu.CompilerParams(vmem_limit_bytes=mib << 20)


def cost(flops, moved):
    return pl.CostEstimate(flops=flops, bytes_accessed=moved, transcendentals=0)


def shifted(value, axis, steps):
    count = lax.axis_size(axis)
    return lax.ppermute(value, axis, [(source, (source + steps) % count) for source in range(count)])


def swapped(value, axis, bits):
    count = lax.axis_size(axis)
    return lax.ppermute(value, axis, [(source, source ^ bits) for source in range(count)])


def staging(places, depth, table_ref, staged_ref, sems):
    me = lax.axis_index("head")
    copies = []
    for slot, (bits, half) in enumerate(places):
        row = pl.multiple_of((me ^ bits) * (2 * depth) + half * depth, depth)
        copies.append(
            pltpu.make_async_copy(
                table_ref.at[pl.ds(row, depth)],
                staged_ref.at[pl.ds(slot * depth, depth)],
                sems.at[slot],
            )
        )
    for copy in copies:
        copy.start()
    return copies


def weights_kernel(steps, count, upcoming, depth, pattern_ref, q_ref, *refs):
    copies = []
    if upcoming:
        *key_refs, table_ref, out_ref, staged_ref, sems = refs
        copies = staging(upcoming, depth, table_ref, staged_ref, sems)
    else:
        *key_refs, out_ref = refs
    tok_dev, width = q_ref.shape
    heads = width // HEAD_SIZE
    blocks_dev = tok_dev // BLOCK
    group = min(heads, 4)
    exponent_scale = math.log2(math.e) / math.sqrt(HEAD_SIZE)
    keys = jnp.concatenate([ref[...] for ref in key_refs], axis=0)
    me = lax.axis_index("ctx")
    for a in range(blocks_dev):
        query_block = me * blocks_dev + a
        pieces = []
        for step in steps:
            source = step if count is None else lax.rem(me + (count - step), count)
            for j in range(blocks_dev):
                key_block = source * blocks_dev + j
                on = (pattern_ref[query_block, key_block] == 1) | (query_block == key_block)
                pieces.append(jnp.full((1, BLOCK), jnp.where(on, 0.0, FAR), jnp.float32))
        bias = jnp.concatenate(pieces, axis=1)
        rows = slice(a * BLOCK, (a + 1) * BLOCK)
        for first in range(0, heads, group):
            q = jnp.concatenate(
                [
                    q_ref[rows, h * HEAD_SIZE : (h + 1) * HEAD_SIZE]
                    for h in range(first, first + group)
                ],
                axis=0,
            )
            scores = lax.dot_general(
                q, keys, (((1,), (1,)), ((), ())), preferred_element_type=jnp.float32
            )
            scores = scores + bias
            top = jnp.max(scores, axis=1, keepdims=True)
            out_ref[a, first * BLOCK : (first + group) * BLOCK, :] = jnp.exp2(
                (scores - top) * exponent_scale
            ).astype(jnp.bfloat16)
    for copy in copies:
        copy.wait()


def weights_of(queries, key_parts, steps, count, block_pattern, table=None, upcoming=()):
    tok_dev, width = queries.shape
    blocks_dev, heads = tok_dev // BLOCK, width // HEAD_SIZE
    keys = sum(part.shape[0] for part in key_parts)
    out_shape = [jax.ShapeDtypeStruct((blocks_dev, heads * BLOCK, keys), jnp.bfloat16)]
    more, scratch = [], []
    depth = width // 2
    if upcoming:
        out_shape.append(
            jax.ShapeDtypeStruct((depth * len(upcoming), table.shape[1]), table.dtype)
        )
        more = [table]
        scratch = [pltpu.SemaphoreType.DMA((len(upcoming),))]
    return pl.pallas_call(
        functools.partial(weights_kernel, steps, count, upcoming, depth),
        out_shape=out_shape,
        in_specs=[SMEM, VMEM] + [VMEM] * len(key_parts) + [HBM] * len(more),
        out_specs=[VMEM] * len(out_shape),
        scratch_shapes=scratch,
        compiler_params=params(32),
        cost_estimate=cost(8 * tok_dev * heads * keys * HEAD_SIZE, 4 << 20),
    )(block_pattern, queries, *key_parts, *more)


def values_kernel(first, group, weights_ref, *refs):
    value_refs, out_ref = refs[:-1], refs[-1]
    values = jnp.concatenate([ref[...] for ref in value_refs], axis=0)
    values = jnp.concatenate([values, jnp.ones_like(values)], axis=1)
    for a in range(weights_ref.shape[0]):
        summed = jnp.dot(
            weights_ref[a, first * BLOCK : (first + group) * BLOCK, :],
            values,
            preferred_element_type=jnp.float32,
        )
        result = (summed[:, :HEAD_SIZE] / summed[:, HEAD_SIZE:]).astype(jnp.bfloat16)
        for i in range(group):
            out_ref[a * BLOCK : (a + 1) * BLOCK, i * HEAD_SIZE : (i + 1) * HEAD_SIZE] = result[
                i * BLOCK : (i + 1) * BLOCK
            ]


def attended_of(weights, value_parts, first, group):
    blocks_dev, _, keys = weights.shape
    return pl.pallas_call(
        functools.partial(values_kernel, first, group),
        out_shape=jax.ShapeDtypeStruct((blocks_dev * BLOCK, group * HEAD_SIZE), jnp.bfloat16),
        in_specs=[VMEM] * (1 + len(value_parts)),
        out_specs=VMEM,
        compiler_params=params(20),
        cost_estimate=cost(4 * blocks_dev * BLOCK * group * keys * HEAD_SIZE, 1 << 20),
    )(weights, *value_parts)


def projection_kernel(count, fresh, upcoming, weight_ref, *refs):
    refs = list(refs)
    total = None if fresh else refs.pop(0)[...]
    parts = refs[:count]
    depth = parts[0].shape[1]
    copies = []
    if upcoming:
        table_ref, out_ref, staged_ref, sems = refs[count:]
        copies = staging(upcoming, depth, table_ref, staged_ref, sems)
    else:
        (out_ref,) = refs[count:]
    for slot, part in enumerate(parts):
        term = jnp.dot(
            part[...],
            weight_ref[slot * depth : (slot + 1) * depth, :],
            preferred_element_type=jnp.float32,
        )
        total = term if total is None else total + term
    out_ref[...] = total.astype(out_ref.dtype)
    for copy in copies:
        copy.wait()


def projected(total, weight, parts, table=None, upcoming=()):
    rows, depth = parts[0].shape
    columns = weight.shape[1]
    fresh = total is None
    operands = [weight] + ([] if fresh else [total]) + parts
    out_shape = [jax.ShapeDtypeStruct((rows, columns), jnp.float32 if upcoming else jnp.bfloat16)]
    more, scratch = [], []
    if upcoming:
        out_shape.append(jax.ShapeDtypeStruct((depth * len(upcoming), columns), weight.dtype))
        more = [table]
        scratch = [pltpu.SemaphoreType.DMA((len(upcoming),))]
    return pl.pallas_call(
        functools.partial(projection_kernel, len(parts), fresh, upcoming),
        out_shape=out_shape,
        in_specs=[VMEM] * len(operands) + [HBM] * len(more),
        out_specs=[VMEM] * len(out_shape),
        scratch_shapes=scratch,
        compiler_params=params(24),
        cost_estimate=cost(16 * rows * depth * columns * len(parts), 1 << 20),
    )(*operands, *more)


def gathered_over_ctx(part):
    if lax.axis_size("ctx") == 4:
        return [part] + [shifted(part, "ctx", step) for step in (2, 1, 3)], (0, 2, 1, 3), 4
    whole = lax.all_gather(part, "ctx")
    count = whole.shape[0]
    return [whole[i] for i in range(count)], tuple(range(count)), None


def on_device(queries, key_vectors, value_head_vectors, block_pattern, out_weight):
    heads_dev = queries.shape[1] // HEAD_SIZE
    query_group_count = QUERY_HEADS // KEY_VALUE_HEADS
    head_count = lax.axis_size("head")
    me = lax.axis_index("head")
    start = (me * heads_dev // query_group_count) * HEAD_SIZE
    keys = lax.dynamic_slice_in_dim(key_vectors, start, HEAD_SIZE, 1)
    values = lax.dynamic_slice_in_dim(value_head_vectors, start, HEAD_SIZE, 1)
    key_parts, steps, count = gathered_over_ctx(keys)
    value_parts, _, _ = gathered_over_ctx(values)
    if head_count != 8:
        (weights,) = weights_of(queries, key_parts, steps, count, block_pattern)
        att = attended_of(weights, value_parts, 0, heads_dev)
        mixed = jnp.dot(
            lax.all_gather(att, "head", axis=1, tiled=True),
            out_weight,
            preferred_element_type=jnp.float32,
        )
        return mixed.astype(jnp.bfloat16)

    own = ((0, 0), (0, 1), (1, 0), (1, 1))
    early = ((2, 0), (3, 0), (4, 1), (5, 1))
    late = ((2, 1), (3, 1), (4, 0), (5, 0))
    across = ((6, 0), (7, 0), (6, 1), (7, 1))
    weights, rows = weights_of(
        queries, key_parts, steps, count, block_pattern, out_weight, own
    )
    half = heads_dev // 2
    a = attended_of(weights, value_parts, 0, half)
    b = attended_of(weights, value_parts, half, half)
    xa = swapped(a, "head", 2)
    yb = swapped(b, "head", 4)
    xb = swapped(b, "head", 2)
    ya = swapped(a, "head", 4)
    sa = swapped(a, "head", 1)
    sb = swapped(b, "head", 1)
    mixed, rows = projected(None, rows, [a, b, sa, sb], out_weight, early)
    da = swapped(xa, "head", 4)
    db = swapped(yb, "head", 2)
    xas, xbs, yas, ybs = [swapped(part, "head", 1) for part in (xa, xb, ya, yb)]
    mixed, rows = projected(mixed, rows, [xa, xas, yb, ybs], out_weight, late)
    mixed, rows = projected(mixed, rows, [xb, xbs, ya, yas], out_weight, across)
    das = swapped(da, "head", 1)
    dbs = swapped(db, "head", 1)
    (mixed,) = projected(mixed, rows, [da, das, db, dbs])
    return mixed


def solution(mesh):
    return jax.shard_map(
        on_device,
        mesh=mesh,
        in_specs=(P("ctx", "head"), P("ctx", None), P("ctx", None), P(), P(None, "head")),
        out_specs=P("ctx", "head"),
        check_vma=False,
    )
```

time: 53.5 us -> 52.4 us (0.979)
  the two profiles are of different devices: /device:TPU:17 before, /device:TPU:0 now
where the time goes in v2:
time: 52.4 us; the launch traced here: 52 us
  starting transfers between devices  19.2 us (37%)
  Pallas kernels  12.5 us (24%)
  waiting for transfers between devices  10.7 us (20%)
  local copies, waits for them, and re-layouts  9.4 us (18%)
    ppermute x6, starting transfers between devices, shifted(): lax.ppermute(value, axis, [(source, (source + steps) % count) for source...  11.8 us
    ppermute x14, waiting for transfers between devices, swapped(): lax.ppermute(value, axis, [(source, source ^ bits) for source in range(co...  10.7 us
    unnamed x8, local copies, waits for them, and re-layouts  8.54 us
    ppermute x14, starting transfers between devices, swapped(): lax.ppermute(value, axis, [(source, source ^ bits) for source in range(co...  7.49 us
    pallas_call x4, Pallas kernels, projected(): pl.pallas_call(functools.partial(projection_kernel, len(parts), fresh, up...  6.9 us
    pallas_call x1, Pallas kernels, weights_of(): pl.pallas_call(functools.partial(weights_kernel, steps, count, upcoming,...  4.16 us
    pallas_call x2, Pallas kernels, attended_of(): pl.pallas_call(functools.partial(values_kernel, first, group), out_shape=...  1.43 us
  transfers between devices with their start and end apart: 20, of which 3 were waited for; matrix products, arithmetic and copies ran while one was open for 2% of the time, Pallas kernels for 19%

profile of v2, /device:TPU:0, one launch (start us, length us, event | category | flops | bytes accessed | tf_op | source)
XLA Modules:
  0.0 52.0 jit_solution(7753378431397319017)
XLA Ops:
  0.0 0.0 copy-start
  0.0 1.0 %copy-done = bf16[256,1024]{1,0:T(8,128)(2,1)S(1)} copy-done((bf16[256,1024]{1,0:T(8,128)(2,1)S(1)}, bf16[256,1024]{1,0:T(8,128)(2,1)}, u32[]{:S(2)}) %copy-start) | copy-done | bytes 524312
  1.1 4.1 %collective-permute-start = (bf16[256,128]{1,0:T(8,128)(2,1)S(1)}, bf16[256,128]{1,0:T(8,128)(2,1)S(1)}, u32[]{:S(2)}, u32[]{:S(2)}) collective-permute-start(bf16[256,128]{1,0:T(8,128)(2,1)S(1)} %constant_dynamic-slice_fusion.1.refs_0_), channel_id=1, source_target_pairs={{0,16},{8,24},{16,0},{24,8},{1,17},{9,25},{17,1},{25,9},{2,18},{10... | collective-permute-start | bytes 196616 | tf_op jit(solution)/shard_map/ppermute | solution.py:32
  5.2 1.6 %collective-permute-start.1 = (bf16[256,128]{1,0:T(8,128)(2,1)S(1)}, bf16[256,128]{1,0:T(8,128)(2,1)S(1)}, u32[]{:S(2)}, u32[]{:S(2)}) collective-permute-start(bf16[256,128]{1,0:T(8,128)(2,1)S(1)} %constant_dynamic-slice_fusion.1.refs_0_), channel_id=1, source_target_pairs={{0,8},{8,16},{16,24},{24,0},{1,9},{9,17},{17,25},{25,1},{2,10},{10... | collective-permute-start | bytes 196616 | tf_op jit(solution)/shard_map/ppermute | solution.py:32
  6.7 2.2 %collective-permute-start.2 = (bf16[256,128]{1,0:T(8,128)(2,1)S(1)}, bf16[256,128]{1,0:T(8,128)(2,1)S(1)}, u32[]{:S(2)}, u32[]{:S(2)}) collective-permute-start(bf16[256,128]{1,0:T(8,128)(2,1)S(1)} %constant_dynamic-slice_fusion.1.refs_0_), channel_id=1, source_target_pairs={{0,24},{8,0},{16,8},{24,16},{1,25},{9,1},{17,9},{25,17},{2,26},{10... | collective-permute-start | bytes 196616 | tf_op jit(solution)/shard_map/ppermute | solution.py:32
  9.0 0.8 %constant_dynamic-slice_fusion.refs_0_ = bf16[256,128]{1,0:T(8,128)(2,1)S(1)} fusion(bf16[256,1024]{1,0:T(8,128)(2,1)} %param.7, s32[]{:T(128)S(6)} %select_n.10), kind=kLoop, calls=%fused_computation | loop fusion | bytes 131076 | tf_op jit(solution)/shard_map/dynamic_slice | solution.py:215
  9.8 0.0 collective-permute-start.3
  9.8 0.6 %collective-permute-start.4 = (bf16[256,128]{1,0:T(8,128)(2,1)S(1)}, bf16[256,128]{1,0:T(8,128)(2,1)S(1)}, u32[]{:S(2)}, u32[]{:S(2)}) collective-permute-start(bf16[256,128]{1,0:T(8,128)(2,1)S(1)} %constant_dynamic-slice_fusion.refs_0_), channel_id=1, source_target_pairs={{0,8},{8,16},{16,24},{24,0},{1,9},{9,17},{17,25},{25,1},{2,10},{10... | collective-permute-start | bytes 196616 | tf_op jit(solution)/shard_map/ppermute | solution.py:32
  10.4 0.0 collective-permute-done.refs_1_
  10.4 3.3 %collective-permute-start.5 = (bf16[256,128]{1,0:T(8,128)(2,1)S(1)}, bf16[256,128]{1,0:T(8,128)(2,1)S(1)}, u32[]{:S(2)}, u32[]{:S(2)}) collective-permute-start(bf16[256,128]{1,0:T(8,128)(2,1)S(1)} %constant_dynamic-slice_fusion.refs_0_), channel_id=1, source_target_pairs={{0,24},{8,0},{16,8},{24,16},{1,25},{9,1},{17,9},{25,17},{2,26},{10... | collective-permute-start | bytes 196616 | tf_op jit(solution)/shard_map/ppermute | solution.py:32
  13.7 0.0 collective-permute-done.1.refs_2_
  13.7 0.0 collective-permute-done.2.refs_3_
  13.7 0.0 copy-start.2
  13.7 1.0 %copy-done.2 = bf16[256,1024]{1,0:T(8,128)(2,1)S(1)} copy-done((bf16[256,1024]{1,0:T(8,128)(2,1)S(1)}, bf16[256,1024]{1,0:T(8,128)(2,1)}, u32[]{:S(2)}) %copy-start.2) | copy-done | bytes 524312
  14.7 0.0 copy-start.3
  14.7 0.7 %copy-done.3 = s32[8,8]{1,0:T(8,128)S(1)} copy-done((s32[8,8]{1,0:T(8,128)S(1)}, s32[8,8]{1,0:T(8,128)}, u32[]{:S(2)}) %copy-start.3) | copy-done | bytes 280
  15.4 4.2 %shard_map.55 = (bf16[2,1024,1024]{2,1,0:T(8,128)(2,1)S(1)}, bf16[2048,1024]{1,0:T(8,128)(2,1)S(1)}) custom-call(s32[8,8]{1,0:T(8,128)S(1)} %copy-done.3, bf16[256,1024]{1,0:T(8,128)(2,1)S(1)} %copy-done.2, bf16[256,128]{1,0:T(8,128)(2,1)S(1)} %constant_dynamic-slice_fusion.1.refs_0_, bf16[256,128]{1,0:T(8,128)(2,1)S(1)} %collective-permute-done.refs_1_, ...), custom_call_target="tpu_custom_call" | custom-call | flops 2147483648 | bytes 4194304 | tf_op jit(solution)/shard_map/pallas_call | solution.py:115
  19.6 0.0 collective-permute-done.3.refs_1_
  19.6 0.0 collective-permute-done.4.refs_2_
  19.6 0.0 collective-permute-done.5.refs_3_
  19.6 0.7 %shard_map.57.refs_1_ = bf16[256,512]{1,0:T(8,128)(2,1)S(1)} custom-call(bf16[2,1024,1024]{2,1,0:T(8,128)(2,1)S(1)} %get-tuple-element.14.weights_ref, bf16[256,128]{1,0:T(8,128)(2,1)S(1)} %constant_dynamic-slice_fusion.refs_0_, bf16[256,128]{1,0:T(8,128)(2,1)S(1)} %collective-permute-done.3.refs_1_, bf16[256,128]{1,0:T(8,128)(2,1)S(1)} %collective-permute-done.4.refs_2_, ...), custom_call_target="tpu_custom_call" | custom-call | flops 536870912 | bytes 1048576 | tf_op jit(solution)/shard_map/pallas_call | solution.py:145
  20.3 0.1 collective-permute-start.7
  20.4 1.6 %collective-permute-start.10 = (bf16[256,512]{1,0:T(8,128)(2,1)S(1)}, bf16[256,512]{1,0:T(8,128)(2,1)S(1)}, u32[]{:S(2)}, u32[]{:S(2)}) collective-permute-start(bf16[256,512]{1,0:T(8,128)(2,1)S(1)} %shard_map.57.refs_1_), channel_id=1, source_target_pairs={{0,4},{1,5},{2,6},{3,7},{4,0},{5,1},{6,2},{7,3},{8,12},{9,13},{10,... | collective-permute-start | bytes 786440 | tf_op jit(solution)/shard_map/ppermute | solution.py:37
  22.0 0.7 %shard_map.56.refs_0_ = bf16[256,512]{1,0:T(8,128)(2,1)S(1)} custom-call(bf16[2,1024,1024]{2,1,0:T(8,128)(2,1)S(1)} %get-tuple-element.14.weights_ref, bf16[256,128]{1,0:T(8,128)(2,1)S(1)} %constant_dynamic-slice_fusion.refs_0_, bf16[256,128]{1,0:T(8,128)(2,1)S(1)} %collective-permute-done.3.refs_1_, bf16[256,128]{1,0:T(8,128)(2,1)S(1)} %collective-permute-done.4.refs_2_, ...), custom_call_target="tpu_custom_call" | custom-call | flops 536870912 | bytes 1048576 | tf_op jit(solution)/shard_map/pallas_call | solution.py:145
  22.7 0.2 collective-permute-start.6
  22.9 1.5 %collective-permute-start.8 = (bf16[256,512]{1,0:T(8,128)(2,1)S(1)}, bf16[256,512]{1,0:T(8,128)(2,1)S(1)}, u32[]{:S(2)}, u32[]{:S(2)}) collective-permute-start(bf16[256,512]{1,0:T(8,128)(2,1)S(1)} %shard_map.56.refs_0_), channel_id=1, source_target_pairs={{0,2},{1,3},{2,0},{3,1},{4,6},{5,7},{6,4},{7,5},{8,10},{9,11},{10,... | collective-permute-start | bytes 786440 | tf_op jit(solution)/shard_map/ppermute | solution.py:37
  24.4 0.5 %collective-permute-start.12 = (bf16[256,512]{1,0:T(8,128)(2,1)S(1)}, bf16[256,512]{1,0:T(8,128)(2,1)S(1)}, u32[]{:S(2)}, u32[]{:S(2)}) collective-permute-start(bf16[256,512]{1,0:T(8,128)(2,1)S(1)} %shard_map.57.refs_1_), channel_id=1, source_target_pairs={{0,2},{1,3},{2,0},{3,1},{4,6},{5,7},{6,4},{7,5},{8,10},{9,11},{10,... | collective-permute-start | bytes 786440 | tf_op jit(solution)/shard_map/ppermute | solution.py:37
  25.0 0.0 collective-permute-done.7.refs_3_
  25.0 0.5 collective-permute-start.14
  25.5 4.1 %collective-permute-done.10.refs_3_ = bf16[256,512]{1,0:T(8,128)(2,1)S(1)} collective-permute-done((bf16[256,512]{1,0:T(8,128)(2,1)S(1)}, bf16[256,512]{1,0:T(8,128)(2,1)S(1)}, u32[]{:S(2)}, u32[]{:S(2)}) %collective-permute-start.10) | collective-permute-done | bytes 262176 | tf_op jit(solution)/shard_map/ppermute | solution.py:37
  29.6 0.0 collective-permute-start.11
  29.6 0.0 collective-permute-done.6.refs_2_
  29.6 1.5 %collective-permute-start.18 = (bf16[256,512]{1,0:T(8,128)(2,1)S(1)}, bf16[256,512]{1,0:T(8,128)(2,1)S(1)}, u32[]{:S(2)}, u32[]{:S(2)}) collective-permute-start(bf16[256,512]{1,0:T(8,128)(2,1)S(1)} %collective-permute-done.10.refs_3_), channel_id=1, source_target_pairs={{0,2},{1,3},{2,0},{3,1},{4,6},{5,7},{6,4},{7,5},{8,10},{9,11},{10,... | collective-permute-start | bytes 786440 | tf_op jit(solution)/shard_map/ppermute | solution.py:37
  31.1 1.0 %collective-permute-done.8.refs_1_ = bf16[256,512]{1,0:T(8,128)(2,1)S(1)} collective-permute-done((bf16[256,512]{1,0:T(8,128)(2,1)S(1)}, bf16[256,512]{1,0:T(8,128)(2,1)S(1)}, u32[]{:S(2)}, u32[]{:S(2)}) %collective-permute-start.8) | collective-permute-done | bytes 262176 | tf_op jit(solution)/shard_map/ppermute | solution.py:37
  32.1 0.0 collective-permute-start.9
  32.1 5.6 %collective-permute-done.12.refs_1_ = bf16[256,512]{1,0:T(8,128)(2,1)S(1)} collective-permute-done((bf16[256,512]{1,0:T(8,128)(2,1)S(1)}, bf16[256,512]{1,0:T(8,128)(2,1)S(1)}, u32[]{:S(2)}, u32[]{:S(2)}) %collective-permute-start.12) | collective-permute-done | bytes 262176 | tf_op jit(solution)/shard_map/ppermute | solution.py:37
  37.7 0.5 collective-permute-start.16
  38.2 0.0 copy-start.1
  38.2 5.8 %copy-done.1 = bf16[8192,1024]{1,0:T(8,128)(2,1)S(1)} copy-done((bf16[8192,1024]{1,0:T(8,128)(2,1)S(1)}, bf16[8192,1024]{1,0:T(8,128)(2,1)}, u32[]{:S(2)}) %copy-start.1) | copy-done | bytes 16777240
  44.0 1.6 %shard_map.58 = (f32[256,1024]{1,0:T(8,128)S(1)}, bf16[2048,1024]{1,0:T(8,128)(2,1)S(1)}) custom-call(bf16[2048,1024]{1,0:T(8,128)(2,1)S(1)} %get-tuple-element.13.weight_ref, bf16[256,512]{1,0:T(8,128)(2,1)S(1)} %shard_map.56.refs_0_, bf16[256,512]{1,0:T(8,128)(2,1)S(1)} %shard_map.57.refs_1_, bf16[256,512]{1,0:T(8,128)(2,1)S(1)} %collective-permute-done.6.refs_2_, ...), custom_call_target="tpu_custom_call" | custom-call | flops 8589934592 | bytes 1048576 | tf_op jit(solution)/shard_map/pallas_call | solution.py:189
  45.5 0.0 collective-permute-done.14.refs_3_
  45.5 0.1 collective-permute-start.13
  45.6 0.0 collective-permute-done.11.refs_4_
  45.6 0.5 collective-permute-start.15
  46.1 0.0 collective-permute-done.18.refs_3_
  46.1 0.1 collective-permute-start.19
  46.2 0.0 collective-permute-done.16.refs_1_
  46.2 0.4 collective-permute-start.17
  46.6 0.0 collective-permute-done.9.refs_2_
  46.7 1.6 %shard_map.59 = (f32[256,1024]{1,0:T(8,128)S(1)}, bf16[2048,1024]{1,0:T(8,128)(2,1)S(1)}) custom-call(bf16[2048,1024]{1,0:T(8,128)(2,1)S(1)} %get-tuple-element.15.weight_ref, f32[256,1024]{1,0:T(8,128)S(1)} %get-tuple-element.16.refs_0_, bf16[256,512]{1,0:T(8,128)(2,1)S(1)} %collective-permute-done.8.refs_1_, ...), custom_call_target="tpu_custom_call" | custom-call | flops 8589934592 | bytes 1048576 | tf_op jit(solution)/shard_map/pallas_call | solution.py:189
  48.3 0.0 collective-permute-done.13.refs_2_
  48.3 0.0 collective-permute-done.15.refs_4_
  48.3 1.6 %shard_map.60 = (f32[256,1024]{1,0:T(8,128)S(1)}, bf16[2048,1024]{1,0:T(8,128)(2,1)S(1)}) custom-call(bf16[2048,1024]{1,0:T(8,128)(2,1)S(1)} %get-tuple-element.17.weight_ref, f32[256,1024]{1,0:T(8,128)S(1)} %get-tuple-element.18.refs_0_, bf16[256,512]{1,0:T(8,128)(2,1)S(1)} %collective-permute-done.12.refs_1_, ...), custom_call_target="tpu_custom_call" | custom-call | flops 8589934592 | bytes 1048576 | tf_op jit(solution)/shard_map/pallas_call | solution.py:189
  50.0 0.0 collective-permute-done.19.refs_4_
  50.0 0.0 collective-permute-done.17.refs_2_
  50.0 2.1 %shard_map.61 = bf16[256,1024]{1,0:T(8,128)(2,1)} custom-call(bf16[2048,1024]{1,0:T(8,128)(2,1)S(1)} %get-tuple-element.19.weight_ref, f32[256,1024]{1,0:T(8,128)S(1)} %get-tuple-element.20.refs_0_, bf16[256,512]{1,0:T(8,128)(2,1)S(1)} %collective-permute-done.16.refs_1_, bf16[256,512]{1,0:T(8,128)(2,1)S(1)} %collective-permute-done.17.refs_2_, ...), custom_call_target="tpu_custom_call" | custom-call | flops 8589934592 | bytes 1048576 | tf_op jit(solution)/shard_map/pallas_call | solution.py:189
  (1 shorter events, 0.0 us)
Async XLA Ops:
  0.0 1.0 %copy-start = (bf16[256,1024]{1,0:T(8,128)(2,1)S(1)}, bf16[256,1024]{1,0:T(8,128)(2,1)}, u32[]{:S(2)}) copy-start(bf16[256,1024]{1,0:T(8,128)(2,1)} %param.6) | copy-start | bytes 1572868
  1.1 9.3 %collective-permute-start = (bf16[256,128]{1,0:T(8,128)(2,1)S(1)}, bf16[256,128]{1,0:T(8,128)(2,1)S(1)}, u32[]{:S(2)}, u32[]{:S(2)}) collective-permute-start(bf16[256,128]{1,0:T(8,128)(2,1)S(1)} %constant_dynamic-slice_fusion.1.refs_0_), channel_id=1, source_target_pairs={{0,16},{8,24},{16,0},{24,8},{1,17},{9,25},{17,1},{25,9},{2,18},{10... | collective-permute-start | bytes 196616 | tf_op jit(solution)/shard_map/ppermute | solution.py:32
  5.2 8.5 %collective-permute-start.1 = (bf16[256,128]{1,0:T(8,128)(2,1)S(1)}, bf16[256,128]{1,0:T(8,128)(2,1)S(1)}, u32[]{:S(2)}, u32[]{:S(2)}) collective-permute-start(bf16[256,128]{1,0:T(8,128)(2,1)S(1)} %constant_dynamic-slice_fusion.1.refs_0_), channel_id=1, source_target_pairs={{0,8},{8,16},{16,24},{24,0},{1,9},{9,17},{17,25},{25,1},{2,10},{10... | collective-permute-start | bytes 196616 | tf_op jit(solution)/shard_map/ppermute | solution.py:32
  6.7 6.9 %collective-permute-start.2 = (bf16[256,128]{1,0:T(8,128)(2,1)S(1)}, bf16[256,128]{1,0:T(8,128)(2,1)S(1)}, u32[]{:S(2)}, u32[]{:S(2)}) collective-permute-start(bf16[256,128]{1,0:T(8,128)(2,1)S(1)} %constant_dynamic-slice_fusion.1.refs_0_), channel_id=1, source_target_pairs={{0,24},{8,0},{16,8},{24,16},{1,25},{9,1},{17,9},{25,17},{2,26},{10... | collective-permute-start | bytes 196616 | tf_op jit(solution)/shard_map/ppermute | solution.py:32
  9.8 9.7 %collective-permute-start.3 = (bf16[256,128]{1,0:T(8,128)(2,1)S(1)}, bf16[256,128]{1,0:T(8,128)(2,1)S(1)}, u32[]{:S(2)}, u32[]{:S(2)}) collective-permute-start(bf16[256,128]{1,0:T(8,128)(2,1)S(1)} %constant_dynamic-slice_fusion.refs_0_), channel_id=1, source_target_pairs={{0,16},{8,24},{16,0},{24,8},{1,17},{9,25},{17,1},{25,9},{2,18},{10... | collective-permute-start | bytes 196616 | tf_op jit(solution)/shard_map/ppermute | solution.py:32
  9.8 9.8 %collective-permute-start.4 = (bf16[256,128]{1,0:T(8,128)(2,1)S(1)}, bf16[256,128]{1,0:T(8,128)(2,1)S(1)}, u32[]{:S(2)}, u32[]{:S(2)}) collective-permute-start(bf16[256,128]{1,0:T(8,128)(2,1)S(1)} %constant_dynamic-slice_fusion.refs_0_), channel_id=1, source_target_pairs={{0,8},{8,16},{16,24},{24,0},{1,9},{9,17},{17,25},{25,1},{2,10},{10... | collective-permute-start | bytes 196616 | tf_op jit(solution)/shard_map/ppermute | solution.py:32
  10.4 9.2 %collective-permute-start.5 = (bf16[256,128]{1,0:T(8,128)(2,1)S(1)}, bf16[256,128]{1,0:T(8,128)(2,1)S(1)}, u32[]{:S(2)}, u32[]{:S(2)}) collective-permute-start(bf16[256,128]{1,0:T(8,128)(2,1)S(1)} %constant_dynamic-slice_fusion.refs_0_), channel_id=1, source_target_pairs={{0,24},{8,0},{16,8},{24,16},{1,25},{9,1},{17,9},{25,17},{2,26},{10... | collective-permute-start | bytes 196616 | tf_op jit(solution)/shard_map/ppermute | solution.py:32
  13.7 1.0 %copy-start.2 = (bf16[256,1024]{1,0:T(8,128)(2,1)S(1)}, bf16[256,1024]{1,0:T(8,128)(2,1)}, u32[]{:S(2)}) copy-start(bf16[256,1024]{1,0:T(8,128)(2,1)} %q_ref.1) | copy-start | bytes 1572868
  14.7 0.7 %copy-start.3 = (s32[8,8]{1,0:T(8,128)S(1)}, s32[8,8]{1,0:T(8,128)}, u32[]{:S(2)}) copy-start(s32[8,8]{1,0:T(8,128)} %pattern_ref.1) | copy-start | bytes 772
  20.3 4.6 %collective-permute-start.7 = (bf16[256,512]{1,0:T(8,128)(2,1)S(1)}, bf16[256,512]{1,0:T(8,128)(2,1)S(1)}, u32[]{:S(2)}, u32[]{:S(2)}) collective-permute-start(bf16[256,512]{1,0:T(8,128)(2,1)S(1)} %shard_map.57.refs_1_), channel_id=1, source_target_pairs={{0,1},{1,0},{2,3},{3,2},{4,5},{5,4},{6,7},{7,6},{8,9},{9,8},{10,11... | collective-permute-start | bytes 786440 | tf_op jit(solution)/shard_map/ppermute | solution.py:37
  20.4 9.2 %collective-permute-start.10 = (bf16[256,512]{1,0:T(8,128)(2,1)S(1)}, bf16[256,512]{1,0:T(8,128)(2,1)S(1)}, u32[]{:S(2)}, u32[]{:S(2)}) collective-permute-start(bf16[256,512]{1,0:T(8,128)(2,1)S(1)} %shard_map.57.refs_1_), channel_id=1, source_target_pairs={{0,4},{1,5},{2,6},{3,7},{4,0},{5,1},{6,2},{7,3},{8,12},{9,13},{10,... | collective-permute-start | bytes 786440 | tf_op jit(solution)/shard_map/ppermute | solution.py:37
  22.7 6.9 %collective-permute-start.6 = (bf16[256,512]{1,0:T(8,128)(2,1)S(1)}, bf16[256,512]{1,0:T(8,128)(2,1)S(1)}, u32[]{:S(2)}, u32[]{:S(2)}) collective-permute-start(bf16[256,512]{1,0:T(8,128)(2,1)S(1)} %shard_map.56.refs_0_), channel_id=1, source_target_pairs={{0,1},{1,0},{2,3},{3,2},{4,5},{5,4},{6,7},{7,6},{8,9},{9,8},{10,11... | collective-permute-start | bytes 786440 | tf_op jit(solution)/shard_map/ppermute | solution.py:37
  22.9 9.1 %collective-permute-start.8 = (bf16[256,512]{1,0:T(8,128)(2,1)S(1)}, bf16[256,512]{1,0:T(8,128)(2,1)S(1)}, u32[]{:S(2)}, u32[]{:S(2)}) collective-permute-start(bf16[256,512]{1,0:T(8,128)(2,1)S(1)} %shard_map.56.refs_0_), channel_id=1, source_target_pairs={{0,2},{1,3},{2,0},{3,1},{4,6},{5,7},{6,4},{7,5},{8,10},{9,11},{10,... | collective-permute-start | bytes 786440 | tf_op jit(solution)/shard_map/ppermute | solution.py:37
  24.4 13.2 %collective-permute-start.12 = (bf16[256,512]{1,0:T(8,128)(2,1)S(1)}, bf16[256,512]{1,0:T(8,128)(2,1)S(1)}, u32[]{:S(2)}, u32[]{:S(2)}) collective-permute-start(bf16[256,512]{1,0:T(8,128)(2,1)S(1)} %shard_map.57.refs_1_), channel_id=1, source_target_pairs={{0,2},{1,3},{2,0},{3,1},{4,6},{5,7},{6,4},{7,5},{8,10},{9,11},{10,... | collective-permute-start | bytes 786440 | tf_op jit(solution)/shard_map/ppermute | solution.py:37
  25.0 20.6 %collective-permute-start.14 = (bf16[256,512]{1,0:T(8,128)(2,1)S(1)}, bf16[256,512]{1,0:T(8,128)(2,1)S(1)}, u32[]{:S(2)}, u32[]{:S(2)}) collective-permute-start(bf16[256,512]{1,0:T(8,128)(2,1)S(1)} %shard_map.56.refs_0_), channel_id=1, source_target_pairs={{0,4},{1,5},{2,6},{3,7},{4,0},{5,1},{6,2},{7,3},{8,12},{9,13},{10,... | collective-permute-start | bytes 786440 | tf_op jit(solution)/shard_map/ppermute | solution.py:37
  29.6 16.1 %collective-permute-start.11 = (bf16[256,512]{1,0:T(8,128)(2,1)S(1)}, bf16[256,512]{1,0:T(8,128)(2,1)S(1)}, u32[]{:S(2)}, u32[]{:S(2)}) collective-permute-start(bf16[256,512]{1,0:T(8,128)(2,1)S(1)} %collective-permute-done.10.refs_3_), channel_id=1, source_target_pairs={{0,1},{1,0},{2,3},{3,2},{4,5},{5,4},{6,7},{7,6},{8,9},{9,8},{10,11... | collective-permute-start | bytes 786440 | tf_op jit(solution)/shard_map/ppermute | solution.py:37
  29.6 16.5 %collective-permute-start.18 = (bf16[256,512]{1,0:T(8,128)(2,1)S(1)}, bf16[256,512]{1,0:T(8,128)(2,1)S(1)}, u32[]{:S(2)}, u32[]{:S(2)}) collective-permute-start(bf16[256,512]{1,0:T(8,128)(2,1)S(1)} %collective-permute-done.10.refs_3_), channel_id=1, source_target_pairs={{0,2},{1,3},{2,0},{3,1},{4,6},{5,7},{6,4},{7,5},{8,10},{9,11},{10,... | collective-permute-start | bytes 786440 | tf_op jit(solution)/shard_map/ppermute | solution.py:37
  32.1 14.6 %collective-permute-start.9 = (bf16[256,512]{1,0:T(8,128)(2,1)S(1)}, bf16[256,512]{1,0:T(8,128)(2,1)S(1)}, u32[]{:S(2)}, u32[]{:S(2)}) collective-permute-start(bf16[256,512]{1,0:T(8,128)(2,1)S(1)} %collective-permute-done.8.refs_1_), channel_id=1, source_target_pairs={{0,1},{1,0},{2,3},{3,2},{4,5},{5,4},{6,7},{7,6},{8,9},{9,8},{10,11... | collective-permute-start | bytes 786440 | tf_op jit(solution)/shard_map/ppermute | solution.py:37
  37.7 8.5 %collective-permute-start.16 = (bf16[256,512]{1,0:T(8,128)(2,1)S(1)}, bf16[256,512]{1,0:T(8,128)(2,1)S(1)}, u32[]{:S(2)}, u32[]{:S(2)}) collective-permute-start(bf16[256,512]{1,0:T(8,128)(2,1)S(1)} %collective-permute-done.8.refs_1_), channel_id=1, source_target_pairs={{0,4},{1,5},{2,6},{3,7},{4,0},{5,1},{6,2},{7,3},{8,12},{9,13},{10,... | collective-permute-start | bytes 786440 | tf_op jit(solution)/shard_map/ppermute | solution.py:37
  38.2 5.8 %copy-start.1 = (bf16[8192,1024]{1,0:T(8,128)(2,1)S(1)}, bf16[8192,1024]{1,0:T(8,128)(2,1)}, u32[]{:S(2)}) copy-start(bf16[8192,1024]{1,0:T(8,128)(2,1)} %refs_5_.3) | copy-start | bytes 50331652
  45.5 2.7 %collective-permute-start.13 = (bf16[256,512]{1,0:T(8,128)(2,1)S(1)}, bf16[256,512]{1,0:T(8,128)(2,1)S(1)}, u32[]{:S(2)}, u32[]{:S(2)}) collective-permute-start(bf16[256,512]{1,0:T(8,128)(2,1)S(1)} %collective-permute-done.12.refs_1_), channel_id=1, source_target_pairs={{0,1},{1,0},{2,3},{3,2},{4,5},{5,4},{6,7},{7,6},{8,9},{9,8},{10,11... | collective-permute-start | bytes 786440 | tf_op jit(solution)/shard_map/ppermute | solution.py:37
  45.6 2.7 %collective-permute-start.15 = (bf16[256,512]{1,0:T(8,128)(2,1)S(1)}, bf16[256,512]{1,0:T(8,128)(2,1)S(1)}, u32[]{:S(2)}, u32[]{:S(2)}) collective-permute-start(bf16[256,512]{1,0:T(8,128)(2,1)S(1)} %collective-permute-done.14.refs_3_), channel_id=1, source_target_pairs={{0,1},{1,0},{2,3},{3,2},{4,5},{5,4},{6,7},{7,6},{8,9},{9,8},{10,11... | collective-permute-start | bytes 786440 | tf_op jit(solution)/shard_map/ppermute | solution.py:37
  46.1 3.8 %collective-permute-start.19 = (bf16[256,512]{1,0:T(8,128)(2,1)S(1)}, bf16[256,512]{1,0:T(8,128)(2,1)S(1)}, u32[]{:S(2)}, u32[]{:S(2)}) collective-permute-start(bf16[256,512]{1,0:T(8,128)(2,1)S(1)} %collective-permute-done.18.refs_3_), channel_id=1, source_target_pairs={{0,1},{1,0},{2,3},{3,2},{4,5},{5,4},{6,7},{7,6},{8,9},{9,8},{10,11... | collective-permute-start | bytes 786440 | tf_op jit(solution)/shard_map/ppermute | solution.py:37
  46.2 3.8 %collective-permute-start.17 = (bf16[256,512]{1,0:T(8,128)(2,1)S(1)}, bf16[256,512]{1,0:T(8,128)(2,1)S(1)}, u32[]{:S(2)}, u32[]{:S(2)}) collective-permute-start(bf16[256,512]{1,0:T(8,128)(2,1)S(1)} %collective-permute-done.16.refs_1_), channel_id=1, source_target_pairs={{0,1},{1,0},{2,3},{3,2},{4,5},{5,4},{6,7},{7,6},{8,9},{9,8},{10,11... | collective-permute-start | bytes 786440 | tf_op jit(solution)/shard_map/ppermute | solution.py:37

commit v3 on v2

--- a/solution.py
+++ b/solution.py
@@ -54,58 +54,105 @@
     return copies
 
 
-def weights_kernel(steps, count, upcoming, depth, pattern_ref, q_ref, *refs):
+def own_slices(key_vectors, value_vectors, width):
+    heads_dev = width // HEAD_SIZE
+    head = lax.axis_index("head") * heads_dev // (QUERY_HEADS // KEY_VALUE_HEADS)
+    return lax.optimization_barrier(
+        tuple(
+            lax.dynamic_slice_in_dim(vectors, head * HEAD_SIZE, HEAD_SIZE, 1)
+            for vectors in (key_vectors, value_vectors)
+        )
+    )
+
+
+def first_lane(shape):
+    return lax.broadcasted_iota(jnp.int32, shape, 1) == 0
+
+
+def stack_kernel(steps, count, pattern_ref, q_ref, stacked_ref, mask_ref, sems):
+    tok_dev, width = q_ref.shape
+    heads = width // HEAD_SIZE
+    blocks_dev = tok_dev // BLOCK
+    copies = []
+    for a in range(blocks_dev):
+        for h in range(heads):
+            copies.append(
+                pltpu.make_async_copy(
+                    q_ref.at[pl.ds(a * BLOCK, BLOCK), pl.ds(h * HEAD_SIZE, HEAD_SIZE)],
+                    stacked_ref.at[a, pl.ds(h * BLOCK, BLOCK)],
+                    sems.at[a, h],
+                )
+            )
+    for copy in copies:
+        copy.start()
+    me = lax.axis_index("ctx")
+    lane = first_lane((BLOCK, BLOCK))
+    for a in range(blocks_dev):
+        query_block = me * blocks_dev + a
+        row = 0
+        for step in steps:
+            source = step if count is None else lax.rem(me + (count - step), count)
+            for j in range(blocks_dev):
+                key_block = source * blocks_dev + j
+                on = (pattern_ref[query_block, key_block] == 1) | (query_block == key_block)
+                mask_ref[a, row : row + BLOCK, :] = jnp.where(
+                    lane, jnp.where(on, 0.0, FAR), 0.0
+                ).astype(jnp.bfloat16)
+                row += BLOCK
+    for copy in copies:
+        copy.wait()
+
+
+def stacked_of(queries, steps, count, block_pattern):
+    tok_dev, width = queries.shape
+    blocks_dev, heads = tok_dev // BLOCK, width // HEAD_SIZE
+    return pl.pallas_call(
+        functools.partial(stack_kernel, steps, count),
+        out_shape=[
+            jax.ShapeDtypeStruct((blocks_dev, heads * BLOCK, HEAD_SIZE), jnp.bfloat16),
+            jax.ShapeDtypeStruct((blocks_dev, len(steps) * tok_dev, BLOCK), jnp.bfloat16),
+        ],
+        in_specs=[SMEM, HBM],
+        out_specs=[VMEM, VMEM],
+        scratch_shapes=[pltpu.SemaphoreType.DMA((blocks_dev, heads))],
+        compiler_params=params(40),
+        cost_estimate=cost(0, 1 << 20),
+    )(block_pattern, queries)
+
+
+def weights_kernel(upcoming, depth, q_ref, mask_ref, *refs):
     copies = []
     if upcoming:
         *key_refs, table_ref, out_ref, staged_ref, sems = refs
         copies = staging(upcoming, depth, table_ref, staged_ref, sems)
     else:
         *key_refs, out_ref = refs
-    tok_dev, width = q_ref.shape
-    heads = width // HEAD_SIZE
-    blocks_dev = tok_dev // BLOCK
-    group = min(heads, 4)
+    blocks_dev, rows, _ = q_ref.shape
+    group = min(rows, 512)
     exponent_scale = math.log2(math.e) / math.sqrt(HEAD_SIZE)
     keys = jnp.concatenate([ref[...] for ref in key_refs], axis=0)
-    me = lax.axis_index("ctx")
+    lane = jnp.where(first_lane((group, BLOCK)), 1.0, 0.0).astype(jnp.bfloat16)
     for a in range(blocks_dev):
-        query_block = me * blocks_dev + a
-        pieces = []
-        for step in steps:
-            source = step if count is None else lax.rem(me + (count - step), count)
-            for j in range(blocks_dev):
-                key_block = source * blocks_dev + j
-                on = (pattern_ref[query_block, key_block] == 1) | (query_block == key_block)
-                pieces.append(jnp.full((1, BLOCK), jnp.where(on, 0.0, FAR), jnp.float32))
-        bias = jnp.concatenate(pieces, axis=1)
-        rows = slice(a * BLOCK, (a + 1) * BLOCK)
-        for first in range(0, heads, group):
-            q = jnp.concatenate(
-                [
-                    q_ref[rows, h * HEAD_SIZE : (h + 1) * HEAD_SIZE]
-                    for h in range(first, first + group)
-                ],
-                axis=0,
+        wide_keys = jnp.concatenate([keys, mask_ref[a]], axis=1)
+        for first in range(0, rows, group):
+            wide = jnp.concatenate([q_ref[a, first : first + group, :], lane], axis=1)
+            scores = lax.dot_general(
+                wide, wide_keys, (((1,), (1,)), ((), ())), preferred_element_type=jnp.float32
             )
-            scores = lax.dot_general(
-                q, keys, (((1,), (1,)), ((), ())), preferred_element_type=jnp.float32
-            )
-            scores = scores + bias
             top = jnp.max(scores, axis=1, keepdims=True)
-            out_ref[a, first * BLOCK : (first + group) * BLOCK, :] = jnp.exp2(
+            out_ref[a, first : first + group, :] = jnp.exp2(
                 (scores - top) * exponent_scale
             ).astype(jnp.bfloat16)
     for copy in copies:
         copy.wait()
 
 
-def weights_of(queries, key_parts, steps, count, block_pattern, table=None, upcoming=()):
-    tok_dev, width = queries.shape
-    blocks_dev, heads = tok_dev // BLOCK, width // HEAD_SIZE
-    keys = sum(part.shape[0] for part in key_parts)
-    out_shape = [jax.ShapeDtypeStruct((blocks_dev, heads * BLOCK, keys), jnp.bfloat16)]
+def weights_of(stacked, mask, key_parts, table=None, upcoming=()):
+    blocks_dev, rows, _ = stacked.shape
+    keys = mask.shape[1]
+    out_shape = [jax.ShapeDtypeStruct((blocks_dev, rows, keys), jnp.bfloat16)]
     more, scratch = [], []
-    depth = width // 2
+    depth = rows // 2
     if upcoming:
         out_shape.append(
             jax.ShapeDtypeStruct((depth * len(upcoming), table.shape[1]), table.dtype)
@@ -113,14 +160,14 @@
         more = [table]
         scratch = [pltpu.SemaphoreType.DMA((len(upcoming),))]
     return pl.pallas_call(
-        functools.partial(weights_kernel, steps, count, upcoming, depth),
+        functools.partial(weights_kernel, upcoming, depth),
         out_shape=out_shape,
-        in_specs=[SMEM, VMEM] + [VMEM] * len(key_parts) + [HBM] * len(more),
+        in_specs=[VMEM] * (2 + len(key_parts)) + [HBM] * len(more),
         out_specs=[VMEM] * len(out_shape),
         scratch_shapes=scratch,
-        compiler_params=params(32),
-        cost_estimate=cost(8 * tok_dev * heads * keys * HEAD_SIZE, 4 << 20),
-    )(block_pattern, queries, *key_parts, *more)
+        compiler_params=params(40),
+        cost_estimate=cost(8 * blocks_dev * rows * keys * HEAD_SIZE, 4 << 20),
+    )(stacked, mask, *key_parts, *more)
 
 
 def values_kernel(first, group, weights_ref, *refs):
@@ -147,7 +194,7 @@
         out_shape=jax.ShapeDtypeStruct((blocks_dev * BLOCK, group * HEAD_SIZE), jnp.bfloat16),
         in_specs=[VMEM] * (1 + len(value_parts)),
         out_specs=VMEM,
-        compiler_params=params(20),
+        compiler_params=params(40),
         cost_estimate=cost(4 * blocks_dev * BLOCK * group * keys * HEAD_SIZE, 1 << 20),
     )(weights, *value_parts)
 
@@ -163,13 +210,12 @@
         copies = staging(upcoming, depth, table_ref, staged_ref, sems)
     else:
         (out_ref,) = refs[count:]
-    for slot, part in enumerate(parts):
-        term = jnp.dot(
-            part[...],
-            weight_ref[slot * depth : (slot + 1) * depth, :],
-            preferred_element_type=jnp.float32,
-        )
-        total = term if total is None else total + term
+    term = jnp.dot(
+        jnp.concatenate([part[...] for part in parts], axis=1),
+        weight_ref[...],
+        preferred_element_type=jnp.float32,
+    )
+    total = term if total is None else total + term
     out_ref[...] = total.astype(out_ref.dtype)
     for copy in copies:
         copy.wait()
@@ -192,7 +238,7 @@
         in_specs=[VMEM] * len(operands) + [HBM] * len(more),
         out_specs=[VMEM] * len(out_shape),
         scratch_shapes=scratch,
-        compiler_params=params(24),
+        compiler_params=params(40),
         cost_estimate=cost(16 * rows * depth * columns * len(parts), 1 << 20),
     )(*operands, *more)
 
@@ -207,16 +253,12 @@
 
 def on_device(queries, key_vectors, value_head_vectors, block_pattern, out_weight):
     heads_dev = queries.shape[1] // HEAD_SIZE
-    query_group_count = QUERY_HEADS // KEY_VALUE_HEADS
-    head_count = lax.axis_size("head")
-    me = lax.axis_index("head")
-    start = (me * heads_dev // query_group_count) * HEAD_SIZE
-    keys = lax.dynamic_slice_in_dim(key_vectors, start, HEAD_SIZE, 1)
-    values = lax.dynamic_slice_in_dim(value_head_vectors, start, HEAD_SIZE, 1)
+    keys, values = own_slices(key_vectors, value_head_vectors, queries.shape[1])
     key_parts, steps, count = gathered_over_ctx(keys)
     value_parts, _, _ = gathered_over_ctx(values)
-    if head_count != 8:
-        (weights,) = weights_of(queries, key_parts, steps, count, block_pattern)
+    stacked, mask = stacked_of(queries, steps, count, block_pattern)
+    if lax.axis_size("head") != 8:
+        (weights,) = weights_of(stacked, mask, key_parts)
         att = attended_of(weights, value_parts, 0, heads_dev)
         mixed = jnp.dot(
             lax.all_gather(att, "head", axis=1, tiled=True),
@@ -229,9 +271,7 @@
     early = ((2, 0), (3, 0), (4, 1), (5, 1))
     late = ((2, 1), (3, 1), (4, 0), (5, 0))
     across = ((6, 0), (7, 0), (6, 1), (7, 1))
-    weights, rows = weights_of(
-        queries, key_parts, steps, count, block_pattern, out_weight, own
-    )
+    weights, rows = weights_of(stacked, mask, key_parts, out_weight, own)
     half = heads_dev // 2
     a = attended_of(weights, value_parts, 0, half)
     b = attended_of(weights, value_parts, half, half)
@@ -242,7 +282,9 @@
     sa = swapped(a, "head", 1)
     sb = swapped(b, "head", 1)
     mixed, rows = projected(None, rows, [a, b, sa, sb], out_weight, early)
+    xa, mixed = lax.optimization_barrier((xa, mixed))
     da = swapped(xa, "head", 4)
+    yb, mixed = lax.optimization_barrier((yb, mixed))
     db = swapped(yb, "head", 2)
     xas, xbs, yas, ybs = [swapped(part, "head", 1) for part in (xa, xb, ya, yb)]
     mixed, rows = projected(mixed, rows, [xa, xas, yb, ybs], out_weight, late)

time: 52.4 us -> 50.7 us (0.968)
  local copies, waits for them, and re-layouts: 9.4 us -> 2.61 us
  Pallas kernels: 12.5 us -> 17.6 us
    unnamed x8 -> x4, local copies, waits for them, and re-layouts: 8.54 us -> 1.73 us
    pallas_call x4, Pallas kernels: 6.9 us -> 11.5 us  [projected(): pl.pallas_call(functools.partial(projection_kernel, len(parts), fresh, up...]
    pallas_call x1 -> x2, Pallas kernels: 4.16 us -> 4.7 us  [the longest x1 3.72 us: weights_of(): pl.pallas_call(functools.partial(weights_kernel, upcoming, depth), out_sh...]
  transfers between devices with their start and end apart: 20 -> 20, of which waited for: 3 -> 6; matrix products, arithmetic and copies ran while one was open for 2% -> 0% of each run, Pallas kernels for 19% -> 30%
where the time goes in v3:
time: 50.7 us; the launch traced here: 50.3 us
  starting transfers between devices  19.1 us (38%)
  Pallas kernels  17.6 us (35%)
  waiting for transfers between devices  10.9 us (21%)
  local copies, waits for them, and re-layouts  2.61 us (5%)
    ppermute x6, starting transfers between devices, shifted(): lax.ppermute(value, axis, [(source, (source + steps) % count) for source...  11.8 us
    pallas_call x4, Pallas kernels, projected(): pl.pallas_call(functools.partial(projection_kernel, len(parts), fresh, up...  11.5 us
    ppermute x14, waiting for transfers between devices, swapped(): lax.ppermute(value, axis, [(source, source ^ bits) for source in range(co...  10.9 us
    ppermute x14, starting transfers between devices, swapped(): lax.ppermute(value, axis, [(source, source ^ bits) for source in range(co...  7.26 us
    pallas_call x1, Pallas kernels, weights_of(): pl.pallas_call(functools.partial(weights_kernel, upcoming, depth), out_sh...  3.72 us
    unnamed x4, local copies, waits for them, and re-layouts  1.73 us
    pallas_call x2, Pallas kernels, attended_of(): pl.pallas_call(functools.partial(values_kernel, first, group), out_shape=...  1.43 us
  transfers between devices with their start and end apart: 20, of which 6 were waited for; matrix products, arithmetic and copies ran while one was open for 0% of the time, Pallas kernels for 30%

profile of v3, /device:TPU:0, one launch (start us, length us, event | category | flops | bytes accessed | tf_op | source)
XLA Modules:
  0.0 50.3 jit_solution(3323517725019585219)
XLA Ops:
  0.0 0.9 %constant_dynamic-slice_fusion = (bf16[256,128]{1,0:T(8,128)(2,1)S(1)}, bf16[256,128]{1,0:T(8,128)(2,1)S(1)}) fusion(bf16[256,1024]{1,0:T(8,128)(2,1)} %param.7, s32[]{:T(128)S(6)} %select_n.10, bf16[256,1024]{1,0:T(8,128)(2,1)} %param.6), kind=kLoop, calls=%fused_computation | loop fusion | bytes 262148 | tf_op jit(solution)/shard_map/dynamic_slice | solution.py:62
  0.9 4.1 %collective-permute-start = (bf16[256,128]{1,0:T(8,128)(2,1)S(1)}, bf16[256,128]{1,0:T(8,128)(2,1)S(1)}, u32[]{:S(2)}, u32[]{:S(2)}) collective-permute-start(bf16[256,128]{1,0:T(8,128)(2,1)S(1)} %get-tuple-element.23.refs_0_), channel_id=1, source_target_pairs={{0,16},{8,24},{16,0},{24,8},{1,17},{9,25},{17,1},{25,9},{2,18},{10... | collective-permute-start | bytes 196616 | tf_op jit(solution)/shard_map/ppermute | solution.py:32
  5.0 1.6 %collective-permute-start.1 = (bf16[256,128]{1,0:T(8,128)(2,1)S(1)}, bf16[256,128]{1,0:T(8,128)(2,1)S(1)}, u32[]{:S(2)}, u32[]{:S(2)}) collective-permute-start(bf16[256,128]{1,0:T(8,128)(2,1)S(1)} %get-tuple-element.23.refs_0_), channel_id=1, source_target_pairs={{0,8},{8,16},{16,24},{24,0},{1,9},{9,17},{17,25},{25,1},{2,10},{10... | collective-permute-start | bytes 196616 | tf_op jit(solution)/shard_map/ppermute | solution.py:32
  6.6 2.2 %collective-permute-start.2 = (bf16[256,128]{1,0:T(8,128)(2,1)S(1)}, bf16[256,128]{1,0:T(8,128)(2,1)S(1)}, u32[]{:S(2)}, u32[]{:S(2)}) collective-permute-start(bf16[256,128]{1,0:T(8,128)(2,1)S(1)} %get-tuple-element.23.refs_0_), channel_id=1, source_target_pairs={{0,24},{8,0},{16,8},{24,16},{1,25},{9,1},{17,9},{25,17},{2,26},{10... | collective-permute-start | bytes 196616 | tf_op jit(solution)/shard_map/ppermute | solution.py:32
  8.8 0.0 collective-permute-start.3
  8.8 0.6 %collective-permute-start.4 = (bf16[256,128]{1,0:T(8,128)(2,1)S(1)}, bf16[256,128]{1,0:T(8,128)(2,1)S(1)}, u32[]{:S(2)}, u32[]{:S(2)}) collective-permute-start(bf16[256,128]{1,0:T(8,128)(2,1)S(1)} %get-tuple-element.26.refs_0_), channel_id=1, source_target_pairs={{0,8},{8,16},{16,24},{24,0},{1,9},{9,17},{17,25},{25,1},{2,10},{10... | collective-permute-start | bytes 196616 | tf_op jit(solution)/shard_map/ppermute | solution.py:32
  9.4 0.0 copy-start
  9.4 1.0 %copy-done = bf16[256,1024]{1,0:T(8,128)(2,1)S(1)} copy-done((bf16[256,1024]{1,0:T(8,128)(2,1)S(1)}, bf16[256,1024]{1,0:T(8,128)(2,1)}, u32[]{:S(2)}) %copy-start) | copy-done | bytes 524312
  10.4 0.0 copy-start.1
  10.4 0.7 %copy-done.1 = s32[8,8]{1,0:T(8,128)S(1)} copy-done((s32[8,8]{1,0:T(8,128)S(1)}, s32[8,8]{1,0:T(8,128)}, u32[]{:S(2)}) %copy-start.1) | copy-done | bytes 280
  11.1 1.0 %shard_map.55 = (bf16[2,1024,128]{2,1,0:T(8,128)(2,1)S(1)}, bf16[2,1024,128]{2,1,0:T(8,128)(2,1)S(1)}) custom-call(s32[8,8]{1,0:T(8,128)S(1)} %copy-done.1, bf16[256,1024]{1,0:T(8,128)(2,1)S(1)} %copy-done), custom_call_target="tpu_custom_call" | custom-call | bytes 1048576 | tf_op jit(solution)/shard_map/pallas_call | solution.py:109
  12.1 0.0 collective-permute-done.refs_1_
  12.1 3.3 %collective-permute-start.5 = (bf16[256,128]{1,0:T(8,128)(2,1)S(1)}, bf16[256,128]{1,0:T(8,128)(2,1)S(1)}, u32[]{:S(2)}, u32[]{:S(2)}) collective-permute-start(bf16[256,128]{1,0:T(8,128)(2,1)S(1)} %get-tuple-element.26.refs_0_), channel_id=1, source_target_pairs={{0,24},{8,0},{16,8},{24,16},{1,25},{9,1},{17,9},{25,17},{2,26},{10... | collective-permute-start | bytes 196616 | tf_op jit(solution)/shard_map/ppermute | solution.py:32
  15.4 0.0 collective-permute-done.1.refs_2_
  15.4 0.0 collective-permute-done.2.refs_3_
  15.4 3.7 %shard_map.56 = (bf16[2,1024,1024]{2,1,0:T(8,128)(2,1)S(1)}, bf16[2048,1024]{1,0:T(8,128)(2,1)S(1)}) custom-call(bf16[2,1024,128]{2,1,0:T(8,128)(2,1)S(1)} %get-tuple-element.21.q_ref, bf16[2,1024,128]{2,1,0:T(8,128)(2,1)S(1)} %get-tuple-element.22.mask_ref, bf16[256,128]{1,0:T(8,128)(2,1)S(1)} %get-tuple-element.23.refs_0_, ...), custom_call_target="tpu_custom_call" | custom-call | flops 2147483648 | bytes 4194304 | tf_op jit(solution)/shard_map/pallas_call | solution.py:162
  19.2 0.0 collective-permute-done.3.refs_1_
  19.2 0.0 collective-permute-done.4.refs_2_
  19.2 0.0 collective-permute-done.5.refs_3_
  19.2 0.7 %shard_map.58.refs_1_ = bf16[256,512]{1,0:T(8,128)(2,1)S(1)} custom-call(bf16[2,1024,1024]{2,1,0:T(8,128)(2,1)S(1)} %get-tuple-element.25.weights_ref, bf16[256,128]{1,0:T(8,128)(2,1)S(1)} %get-tuple-element.26.refs_0_, bf16[256,128]{1,0:T(8,128)(2,1)S(1)} %collective-permute-done.3.refs_1_, bf16[256,128]{1,0:T(8,128)(2,1)S(1)} %collective-permute-done.4.refs_2_, ...), custom_call_target="tpu_custom_call" | custom-call | flops 536870912 | bytes 1048576 | tf_op jit(solution)/shard_map/pallas_call | solution.py:192
  19.9 0.1 collective-permute-start.7
  20.0 0.7 %shard_map.57.refs_0_ = bf16[256,512]{1,0:T(8,128)(2,1)S(1)} custom-call(bf16[2,1024,1024]{2,1,0:T(8,128)(2,1)S(1)} %get-tuple-element.25.weights_ref, bf16[256,128]{1,0:T(8,128)(2,1)S(1)} %get-tuple-element.26.refs_0_, bf16[256,128]{1,0:T(8,128)(2,1)S(1)} %collective-permute-done.3.refs_1_, bf16[256,128]{1,0:T(8,128)(2,1)S(1)} %collective-permute-done.4.refs_2_, ...), custom_call_target="tpu_custom_call" | custom-call | flops 536870912 | bytes 1048576 | tf_op jit(solution)/shard_map/pallas_call | solution.py:192
  20.7 0.6 %collective-permute-start.6 = (bf16[256,512]{1,0:T(8,128)(2,1)S(1)}, bf16[256,512]{1,0:T(8,128)(2,1)S(1)}, u32[]{:S(2)}, u32[]{:S(2)}) collective-permute-start(bf16[256,512]{1,0:T(8,128)(2,1)S(1)} %shard_map.57.refs_0_), channel_id=1, source_target_pairs={{0,1},{1,0},{2,3},{3,2},{4,5},{5,4},{6,7},{7,6},{8,9},{9,8},{10,11... | collective-permute-start | bytes 786440 | tf_op jit(solution)/shard_map/ppermute | solution.py:37
  21.3 1.5 %collective-permute-start.9 = (bf16[256,512]{1,0:T(8,128)(2,1)S(1)}, bf16[256,512]{1,0:T(8,128)(2,1)S(1)}, u32[]{:S(2)}, u32[]{:S(2)}) collective-permute-start(bf16[256,512]{1,0:T(8,128)(2,1)S(1)} %shard_map.57.refs_0_), channel_id=1, source_target_pairs={{0,2},{1,3},{2,0},{3,1},{4,6},{5,7},{6,4},{7,5},{8,10},{9,11},{10,... | collective-permute-start | bytes 786440 | tf_op jit(solution)/shard_map/ppermute | solution.py:37
  22.8 1.5 %collective-permute-start.8 = (bf16[256,512]{1,0:T(8,128)(2,1)S(1)}, bf16[256,512]{1,0:T(8,128)(2,1)S(1)}, u32[]{:S(2)}, u32[]{:S(2)}) collective-permute-start(bf16[256,512]{1,0:T(8,128)(2,1)S(1)} %shard_map.58.refs_1_), channel_id=1, source_target_pairs={{0,4},{1,5},{2,6},{3,7},{4,0},{5,1},{6,2},{7,3},{8,12},{9,13},{10,... | collective-permute-start | bytes 786440 | tf_op jit(solution)/shard_map/ppermute | solution.py:37
  24.3 0.5 %collective-permute-start.12 = (bf16[256,512]{1,0:T(8,128)(2,1)S(1)}, bf16[256,512]{1,0:T(8,128)(2,1)S(1)}, u32[]{:S(2)}, u32[]{:S(2)}) collective-permute-start(bf16[256,512]{1,0:T(8,128)(2,1)S(1)} %shard_map.58.refs_1_), channel_id=1, source_target_pairs={{0,2},{1,3},{2,0},{3,1},{4,6},{5,7},{6,4},{7,5},{8,10},{9,11},{10,... | collective-permute-start | bytes 786440 | tf_op jit(solution)/shard_map/ppermute | solution.py:37
  24.8 0.0 collective-permute-done.7.refs_3_
  24.8 0.5 %collective-permute-start.14 = (bf16[256,512]{1,0:T(8,128)(2,1)S(1)}, bf16[256,512]{1,0:T(8,128)(2,1)S(1)}, u32[]{:S(2)}, u32[]{:S(2)}) collective-permute-start(bf16[256,512]{1,0:T(8,128)(2,1)S(1)} %shard_map.57.refs_0_), channel_id=1, source_target_pairs={{0,4},{1,5},{2,6},{3,7},{4,0},{5,1},{6,2},{7,3},{8,12},{9,13},{10,... | collective-permute-start | bytes 786440 | tf_op jit(solution)/shard_map/ppermute | solution.py:37
  25.3 0.0 collective-permute-done.6.refs_2_
  25.3 3.2 %shard_map.59 = (f32[256,1024]{1,0:T(8,128)S(1)}, bf16[2048,1024]{1,0:T(8,128)(2,1)S(1)}) custom-call(bf16[2048,1024]{1,0:T(8,128)(2,1)S(1)} %get-tuple-element.24.weight_ref, bf16[256,512]{1,0:T(8,128)(2,1)S(1)} %shard_map.57.refs_0_, bf16[256,512]{1,0:T(8,128)(2,1)S(1)} %shard_map.58.refs_1_, bf16[256,512]{1,0:T(8,128)(2,1)S(1)} %collective-permute-done.6.refs_2_, ...), custom_call_target="tpu_custom_call" | custom-call | flops 8589934592 | bytes 1048576 | tf_op jit(solution)/shard_map/pallas_call | solution.py:235
  28.6 1.9 %collective-permute-done.9.refs_1_ = bf16[256,512]{1,0:T(8,128)(2,1)S(1)} collective-permute-done((bf16[256,512]{1,0:T(8,128)(2,1)S(1)}, bf16[256,512]{1,0:T(8,128)(2,1)S(1)}, u32[]{:S(2)}, u32[]{:S(2)}) %collective-permute-start.9) | collective-permute-done | bytes 262176 | tf_op jit(solution)/shard_map/ppermute | solution.py:37
  30.4 1.5 %collective-permute-done.8.refs_3_ = bf16[256,512]{1,0:T(8,128)(2,1)S(1)} collective-permute-done((bf16[256,512]{1,0:T(8,128)(2,1)S(1)}, bf16[256,512]{1,0:T(8,128)(2,1)S(1)}, u32[]{:S(2)}, u32[]{:S(2)}) %collective-permute-start.8) | collective-permute-done | bytes 262176 | tf_op jit(solution)/shard_map/ppermute | solution.py:37
  32.0 0.0 collective-permute-start.11
  32.0 0.5 %collective-permute-start.18 = (bf16[256,512]{1,0:T(8,128)(2,1)S(1)}, bf16[256,512]{1,0:T(8,128)(2,1)S(1)}, u32[]{:S(2)}, u32[]{:S(2)}) collective-permute-start(bf16[256,512]{1,0:T(8,128)(2,1)S(1)} %collective-permute-done.8.refs_3_), channel_id=1, source_target_pairs={{0,2},{1,3},{2,0},{3,1},{4,6},{5,7},{6,4},{7,5},{8,10},{9,11},{10,... | collective-permute-start | bytes 786440 | tf_op jit(solution)/shard_map/ppermute | solution.py:37
  32.5 1.5 %collective-permute-start.16 = (bf16[256,512]{1,0:T(8,128)(2,1)S(1)}, bf16[256,512]{1,0:T(8,128)(2,1)S(1)}, u32[]{:S(2)}, u32[]{:S(2)}) collective-permute-start(bf16[256,512]{1,0:T(8,128)(2,1)S(1)} %collective-permute-done.9.refs_1_), channel_id=1, source_target_pairs={{0,4},{1,5},{2,6},{3,7},{4,0},{5,1},{6,2},{7,3},{8,12},{9,13},{10,... | collective-permute-start | bytes 786440 | tf_op jit(solution)/shard_map/ppermute | solution.py:37
  34.0 1.2 %collective-permute-done.12.refs_1_ = bf16[256,512]{1,0:T(8,128)(2,1)S(1)} collective-permute-done((bf16[256,512]{1,0:T(8,128)(2,1)S(1)}, bf16[256,512]{1,0:T(8,128)(2,1)S(1)}, u32[]{:S(2)}, u32[]{:S(2)}) %collective-permute-start.12) | collective-permute-done | bytes 262176 | tf_op jit(solution)/shard_map/ppermute | solution.py:37
  35.2 0.0 collective-permute-start.10
  35.2 2.2 %collective-permute-done.14.refs_3_ = bf16[256,512]{1,0:T(8,128)(2,1)S(1)} collective-permute-done((bf16[256,512]{1,0:T(8,128)(2,1)S(1)}, bf16[256,512]{1,0:T(8,128)(2,1)S(1)}, u32[]{:S(2)}, u32[]{:S(2)}) %collective-permute-start.14) | collective-permute-done | bytes 262176 | tf_op jit(solution)/shard_map/ppermute | solution.py:37
  37.4 0.0 collective-permute-start.13
  37.4 0.0 collective-permute-done.11.refs_4_
  37.4 0.5 %collective-permute-start.15 = (bf16[256,512]{1,0:T(8,128)(2,1)S(1)}, bf16[256,512]{1,0:T(8,128)(2,1)S(1)}, u32[]{:S(2)}, u32[]{:S(2)}) collective-permute-start(bf16[256,512]{1,0:T(8,128)(2,1)S(1)} %collective-permute-done.14.refs_3_), channel_id=1, source_target_pairs={{0,1},{1,0},{2,3},{3,2},{4,5},{5,4},{6,7},{7,6},{8,9},{9,8},{10,11... | collective-permute-start | bytes 786440 | tf_op jit(solution)/shard_map/ppermute | solution.py:37
  37.9 2.9 %collective-permute-done.18.refs_3_ = bf16[256,512]{1,0:T(8,128)(2,1)S(1)} collective-permute-done((bf16[256,512]{1,0:T(8,128)(2,1)S(1)}, bf16[256,512]{1,0:T(8,128)(2,1)S(1)}, u32[]{:S(2)}, u32[]{:S(2)}) %collective-permute-start.18) | collective-permute-done | bytes 262176 | tf_op jit(solution)/shard_map/ppermute | solution.py:37
  40.8 0.0 collective-permute-start.19
  40.8 1.2 %collective-permute-done.16.refs_1_ = bf16[256,512]{1,0:T(8,128)(2,1)S(1)} collective-permute-done((bf16[256,512]{1,0:T(8,128)(2,1)S(1)}, bf16[256,512]{1,0:T(8,128)(2,1)S(1)}, u32[]{:S(2)}, u32[]{:S(2)}) %collective-permute-start.16) | collective-permute-done | bytes 262176 | tf_op jit(solution)/shard_map/ppermute | solution.py:37
  42.0 0.0 collective-permute-start.17
  42.0 0.0 collective-permute-done.10.refs_2_
  42.0 3.0 %shard_map.60 = (f32[256,1024]{1,0:T(8,128)S(1)}, bf16[2048,1024]{1,0:T(8,128)(2,1)S(1)}) custom-call(bf16[2048,1024]{1,0:T(8,128)(2,1)S(1)} %get-tuple-element.27.weight_ref, f32[256,1024]{1,0:T(8,128)S(1)} %get-tuple-element.30.refs_0_, bf16[256,512]{1,0:T(8,128)(2,1)S(1)} %collective-permute-done.9.refs_1_, ...), custom_call_target="tpu_custom_call" | custom-call | flops 8589934592 | bytes 1048576 | tf_op jit(solution)/shard_map/pallas_call | solution.py:235
  45.0 0.0 collective-permute-done.13.refs_2_
  45.0 0.0 collective-permute-done.15.refs_4_
  45.0 3.2 %shard_map.61 = (f32[256,1024]{1,0:T(8,128)S(1)}, bf16[2048,1024]{1,0:T(8,128)(2,1)S(1)}) custom-call(bf16[2048,1024]{1,0:T(8,128)(2,1)S(1)} %get-tuple-element.33.weight_ref, f32[256,1024]{1,0:T(8,128)S(1)} %get-tuple-element.34.refs_0_, bf16[256,512]{1,0:T(8,128)(2,1)S(1)} %collective-permute-done.12.refs_1_, ...), custom_call_target="tpu_custom_call" | custom-call | flops 8589934592 | bytes 1048576 | tf_op jit(solution)/shard_map/pallas_call | solution.py:235
  48.3 0.0 collective-permute-done.19.refs_4_
  48.3 0.0 collective-permute-done.17.refs_2_
  48.3 2.1 %shard_map.62 = bf16[256,1024]{1,0:T(8,128)(2,1)} custom-call(bf16[2048,1024]{1,0:T(8,128)(2,1)S(1)} %get-tuple-element.35.weight_ref, f32[256,1024]{1,0:T(8,128)S(1)} %get-tuple-element.36.refs_0_, bf16[256,512]{1,0:T(8,128)(2,1)S(1)} %collective-permute-done.16.refs_1_, bf16[256,512]{1,0:T(8,128)(2,1)S(1)} %collective-permute-done.17.refs_2_, ...), custom_call_target="tpu_custom_call" | custom-call | flops 8589934592 | bytes 1048576 | tf_op jit(solution)/shard_map/pallas_call | solution.py:235
Async XLA Ops:
  0.9 11.2 %collective-permute-start = (bf16[256,128]{1,0:T(8,128)(2,1)S(1)}, bf16[256,128]{1,0:T(8,128)(2,1)S(1)}, u32[]{:S(2)}, u32[]{:S(2)}) collective-permute-start(bf16[256,128]{1,0:T(8,128)(2,1)S(1)} %get-tuple-element.23.refs_0_), channel_id=1, source_target_pairs={{0,16},{8,24},{16,0},{24,8},{1,17},{9,25},{17,1},{25,9},{2,18},{10... | collective-permute-start | bytes 196616 | tf_op jit(solution)/shard_map/ppermute | solution.py:32
  5.0 10.4 %collective-permute-start.1 = (bf16[256,128]{1,0:T(8,128)(2,1)S(1)}, bf16[256,128]{1,0:T(8,128)(2,1)S(1)}, u32[]{:S(2)}, u32[]{:S(2)}) collective-permute-start(bf16[256,128]{1,0:T(8,128)(2,1)S(1)} %get-tuple-element.23.refs_0_), channel_id=1, source_target_pairs={{0,8},{8,16},{16,24},{24,0},{1,9},{9,17},{17,25},{25,1},{2,10},{10... | collective-permute-start | bytes 196616 | tf_op jit(solution)/shard_map/ppermute | solution.py:32
  6.6 8.9 %collective-permute-start.2 = (bf16[256,128]{1,0:T(8,128)(2,1)S(1)}, bf16[256,128]{1,0:T(8,128)(2,1)S(1)}, u32[]{:S(2)}, u32[]{:S(2)}) collective-permute-start(bf16[256,128]{1,0:T(8,128)(2,1)S(1)} %get-tuple-element.23.refs_0_), channel_id=1, source_target_pairs={{0,24},{8,0},{16,8},{24,16},{1,25},{9,1},{17,9},{25,17},{2,26},{10... | collective-permute-start | bytes 196616 | tf_op jit(solution)/shard_map/ppermute | solution.py:32
  8.8 10.3 %collective-permute-start.3 = (bf16[256,128]{1,0:T(8,128)(2,1)S(1)}, bf16[256,128]{1,0:T(8,128)(2,1)S(1)}, u32[]{:S(2)}, u32[]{:S(2)}) collective-permute-start(bf16[256,128]{1,0:T(8,128)(2,1)S(1)} %get-tuple-element.26.refs_0_), channel_id=1, source_target_pairs={{0,16},{8,24},{16,0},{24,8},{1,17},{9,25},{17,1},{25,9},{2,18},{10... | collective-permute-start | bytes 196616 | tf_op jit(solution)/shard_map/ppermute | solution.py:32
  8.8 10.3 %collective-permute-start.4 = (bf16[256,128]{1,0:T(8,128)(2,1)S(1)}, bf16[256,128]{1,0:T(8,128)(2,1)S(1)}, u32[]{:S(2)}, u32[]{:S(2)}) collective-permute-start(bf16[256,128]{1,0:T(8,128)(2,1)S(1)} %get-tuple-element.26.refs_0_), channel_id=1, source_target_pairs={{0,8},{8,16},{16,24},{24,0},{1,9},{9,17},{17,25},{25,1},{2,10},{10... | collective-permute-start | bytes 196616 | tf_op jit(solution)/shard_map/ppermute | solution.py:32
  9.4 1.0 %copy-start = (bf16[256,1024]{1,0:T(8,128)(2,1)S(1)}, bf16[256,1024]{1,0:T(8,128)(2,1)}, u32[]{:S(2)}) copy-start(bf16[256,1024]{1,0:T(8,128)(2,1)} %q_ref.1) | copy-start | bytes 1572868
  10.4 0.7 %copy-start.1 = (s32[8,8]{1,0:T(8,128)S(1)}, s32[8,8]{1,0:T(8,128)}, u32[]{:S(2)}) copy-start(s32[8,8]{1,0:T(8,128)} %pattern_ref.1) | copy-start | bytes 772
  12.1 7.1 %collective-permute-start.5 = (bf16[256,128]{1,0:T(8,128)(2,1)S(1)}, bf16[256,128]{1,0:T(8,128)(2,1)S(1)}, u32[]{:S(2)}, u32[]{:S(2)}) collective-permute-start(bf16[256,128]{1,0:T(8,128)(2,1)S(1)} %get-tuple-element.26.refs_0_), channel_id=1, source_target_pairs={{0,24},{8,0},{16,8},{24,16},{1,25},{9,1},{17,9},{25,17},{2,26},{10... | collective-permute-start | bytes 196616 | tf_op jit(solution)/shard_map/ppermute | solution.py:32
  19.9 4.9 %collective-permute-start.7 = (bf16[256,512]{1,0:T(8,128)(2,1)S(1)}, bf16[256,512]{1,0:T(8,128)(2,1)S(1)}, u32[]{:S(2)}, u32[]{:S(2)}) collective-permute-start(bf16[256,512]{1,0:T(8,128)(2,1)S(1)} %shard_map.58.refs_1_), channel_id=1, source_target_pairs={{0,1},{1,0},{2,3},{3,2},{4,5},{5,4},{6,7},{7,6},{8,9},{9,8},{10,11... | collective-permute-start | bytes 786440 | tf_op jit(solution)/shard_map/ppermute | solution.py:37
  20.7 4.6 %collective-permute-start.6 = (bf16[256,512]{1,0:T(8,128)(2,1)S(1)}, bf16[256,512]{1,0:T(8,128)(2,1)S(1)}, u32[]{:S(2)}, u32[]{:S(2)}) collective-permute-start(bf16[256,512]{1,0:T(8,128)(2,1)S(1)} %shard_map.57.refs_0_), channel_id=1, source_target_pairs={{0,1},{1,0},{2,3},{3,2},{4,5},{5,4},{6,7},{7,6},{8,9},{9,8},{10,11... | collective-permute-start | bytes 786440 | tf_op jit(solution)/shard_map/ppermute | solution.py:37
  21.3 9.2 %collective-permute-start.9 = (bf16[256,512]{1,0:T(8,128)(2,1)S(1)}, bf16[256,512]{1,0:T(8,128)(2,1)S(1)}, u32[]{:S(2)}, u32[]{:S(2)}) collective-permute-start(bf16[256,512]{1,0:T(8,128)(2,1)S(1)} %shard_map.57.refs_0_), channel_id=1, source_target_pairs={{0,2},{1,3},{2,0},{3,1},{4,6},{5,7},{6,4},{7,5},{8,10},{9,11},{10,... | collective-permute-start | bytes 786440 | tf_op jit(solution)/shard_map/ppermute | solution.py:37
  22.8 9.2 %collective-permute-start.8 = (bf16[256,512]{1,0:T(8,128)(2,1)S(1)}, bf16[256,512]{1,0:T(8,128)(2,1)S(1)}, u32[]{:S(2)}, u32[]{:S(2)}) collective-permute-start(bf16[256,512]{1,0:T(8,128)(2,1)S(1)} %shard_map.58.refs_1_), channel_id=1, source_target_pairs={{0,4},{1,5},{2,6},{3,7},{4,0},{5,1},{6,2},{7,3},{8,12},{9,13},{10,... | collective-permute-start | bytes 786440 | tf_op jit(solution)/shard_map/ppermute | solution.py:37
  24.3 10.9 %collective-permute-start.12 = (bf16[256,512]{1,0:T(8,128)(2,1)S(1)}, bf16[256,512]{1,0:T(8,128)(2,1)S(1)}, u32[]{:S(2)}, u32[]{:S(2)}) collective-permute-start(bf16[256,512]{1,0:T(8,128)(2,1)S(1)} %shard_map.58.refs_1_), channel_id=1, source_target_pairs={{0,2},{1,3},{2,0},{3,1},{4,6},{5,7},{6,4},{7,5},{8,10},{9,11},{10,... | collective-permute-start | bytes 786440 | tf_op jit(solution)/shard_map/ppermute | solution.py:37
  24.8 12.6 %collective-permute-start.14 = (bf16[256,512]{1,0:T(8,128)(2,1)S(1)}, bf16[256,512]{1,0:T(8,128)(2,1)S(1)}, u32[]{:S(2)}, u32[]{:S(2)}) collective-permute-start(bf16[256,512]{1,0:T(8,128)(2,1)S(1)} %shard_map.57.refs_0_), channel_id=1, source_target_pairs={{0,4},{1,5},{2,6},{3,7},{4,0},{5,1},{6,2},{7,3},{8,12},{9,13},{10,... | collective-permute-start | bytes 786440 | tf_op jit(solution)/shard_map/ppermute | solution.py:37
  32.0 5.4 %collective-permute-start.11 = (bf16[256,512]{1,0:T(8,128)(2,1)S(1)}, bf16[256,512]{1,0:T(8,128)(2,1)S(1)}, u32[]{:S(2)}, u32[]{:S(2)}) collective-permute-start(bf16[256,512]{1,0:T(8,128)(2,1)S(1)} %collective-permute-done.8.refs_3_), channel_id=1, source_target_pairs={{0,1},{1,0},{2,3},{3,2},{4,5},{5,4},{6,7},{7,6},{8,9},{9,8},{10,11... | collective-permute-start | bytes 786440 | tf_op jit(solution)/shard_map/ppermute | solution.py:37
  32.0 8.8 %collective-permute-start.18 = (bf16[256,512]{1,0:T(8,128)(2,1)S(1)}, bf16[256,512]{1,0:T(8,128)(2,1)S(1)}, u32[]{:S(2)}, u32[]{:S(2)}) collective-permute-start(bf16[256,512]{1,0:T(8,128)(2,1)S(1)} %collective-permute-done.8.refs_3_), channel_id=1, source_target_pairs={{0,2},{1,3},{2,0},{3,1},{4,6},{5,7},{6,4},{7,5},{8,10},{9,11},{10,... | collective-permute-start | bytes 786440 | tf_op jit(solution)/shard_map/ppermute | solution.py:37
  32.5 9.5 %collective-permute-start.16 = (bf16[256,512]{1,0:T(8,128)(2,1)S(1)}, bf16[256,512]{1,0:T(8,128)(2,1)S(1)}, u32[]{:S(2)}, u32[]{:S(2)}) collective-permute-start(bf16[256,512]{1,0:T(8,128)(2,1)S(1)} %collective-permute-done.9.refs_1_), channel_id=1, source_target_pairs={{0,4},{1,5},{2,6},{3,7},{4,0},{5,1},{6,2},{7,3},{8,12},{9,13},{10,... | collective-permute-start | bytes 786440 | tf_op jit(solution)/shard_map/ppermute | solution.py:37
  35.2 6.8 %collective-permute-start.10 = (bf16[256,512]{1,0:T(8,128)(2,1)S(1)}, bf16[256,512]{1,0:T(8,128)(2,1)S(1)}, u32[]{:S(2)}, u32[]{:S(2)}) collective-permute-start(bf16[256,512]{1,0:T(8,128)(2,1)S(1)} %collective-permute-done.9.refs_1_), channel_id=1, source_target_pairs={{0,1},{1,0},{2,3},{3,2},{4,5},{5,4},{6,7},{7,6},{8,9},{9,8},{10,11... | collective-permute-start | bytes 786440 | tf_op jit(solution)/shard_map/ppermute | solution.py:37
  37.4 7.6 %collective-permute-start.13 = (bf16[256,512]{1,0:T(8,128)(2,1)S(1)}, bf16[256,512]{1,0:T(8,128)(2,1)S(1)}, u32[]{:S(2)}, u32[]{:S(2)}) collective-permute-start(bf16[256,512]{1,0:T(8,128)(2,1)S(1)} %collective-permute-done.12.refs_1_), channel_id=1, source_target_pairs={{0,1},{1,0},{2,3},{3,2},{4,5},{5,4},{6,7},{7,6},{8,9},{9,8},{10,11... | collective-permute-start | bytes 786440 | tf_op jit(solution)/shard_map/ppermute | solution.py:37
  37.4 7.6 %collective-permute-start.15 = (bf16[256,512]{1,0:T(8,128)(2,1)S(1)}, bf16[256,512]{1,0:T(8,128)(2,1)S(1)}, u32[]{:S(2)}, u32[]{:S(2)}) collective-permute-start(bf16[256,512]{1,0:T(8,128)(2,1)S(1)} %collective-permute-done.14.refs_3_), channel_id=1, source_target_pairs={{0,1},{1,0},{2,3},{3,2},{4,5},{5,4},{6,7},{7,6},{8,9},{9,8},{10,11... | collective-permute-start | bytes 786440 | tf_op jit(solution)/shard_map/ppermute | solution.py:37
  40.8 7.5 %collective-permute-start.19 = (bf16[256,512]{1,0:T(8,128)(2,1)S(1)}, bf16[256,512]{1,0:T(8,128)(2,1)S(1)}, u32[]{:S(2)}, u32[]{:S(2)}) collective-permute-start(bf16[256,512]{1,0:T(8,128)(2,1)S(1)} %collective-permute-done.18.refs_3_), channel_id=1, source_target_pairs={{0,1},{1,0},{2,3},{3,2},{4,5},{5,4},{6,7},{7,6},{8,9},{9,8},{10,11... | collective-permute-start | bytes 786440 | tf_op jit(solution)/shard_map/ppermute | solution.py:37
  42.0 6.3 %collective-permute-start.17 = (bf16[256,512]{1,0:T(8,128)(2,1)S(1)}, bf16[256,512]{1,0:T(8,128)(2,1)S(1)}, u32[]{:S(2)}, u32[]{:S(2)}) collective-permute-start(bf16[256,512]{1,0:T(8,128)(2,1)S(1)} %collective-permute-done.16.refs_1_), channel_id=1, source_target_pairs={{0,1},{1,0},{2,3},{3,2},{4,5},{5,4},{6,7},{7,6},{8,9},{9,8},{10,11... | collective-permute-start | bytes 786440 | tf_op jit(solution)/shard_map/ppermute | solution.py:37

commit v4 on v3

v4 whole, which is shorter than its diff:
```python
import functools
import math

import jax
import jax.numpy as jnp
from jax import lax
from jax.experimental import pallas as pl
from jax.experimental.pallas import tpu as pltpu
from jax.sharding import PartitionSpec as P

QUERY_HEADS = 64
KEY_VALUE_HEADS = 8
HEAD_SIZE = 128
BLOCK = 128
FAR = -1e30

SMEM = pl.BlockSpec(memory_space=pltpu.SMEM)
VMEM = pl.BlockSpec(memory_space=pltpu.VMEM)
HBM = pl.BlockSpec(memory_space=pltpu.HBM)


def params(mib):
    return pltpu.CompilerParams(vmem_limit_bytes=mib << 20)


def held(shape, dtype=jnp.bfloat16):
    return pltpu.VMEM(shape, dtype)


def cost(flops, moved):
    return pl.CostEstimate(flops=flops, bytes_accessed=moved, transcendentals=0)


def shifted(value, axis, steps):
    count = lax.axis_size(axis)
    return lax.ppermute(value, axis, [(source, (source + steps) % count) for source in range(count)])


def swapped(value, axis, bits):
    count = lax.axis_size(axis)
    return lax.ppermute(value, axis, [(source, source ^ bits) for source in range(count)])


def first_lane(shape):
    return lax.broadcasted_iota(jnp.int32, shape, 1) == 0


def prepare_kernel(steps, count, keys_ref, values_ref, q_ref, pattern_ref, *refs):
    own_keys_ref, own_values_ref, stacked_ref, mask_ref, table_ref, sems, stack_sems = refs
    tok_dev, width = q_ref.shape
    heads = width // HEAD_SIZE
    blocks_dev = tok_dev // BLOCK
    head = lax.div(lax.axis_index("head") * heads, QUERY_HEADS // KEY_VALUE_HEADS)
    columns = pl.ds(pl.multiple_of(head * HEAD_SIZE, HEAD_SIZE), HEAD_SIZE)
    table = pltpu.make_async_copy(pattern_ref, table_ref, sems.at[2])
    copies = [
        pltpu.make_async_copy(keys_ref.at[:, columns], own_keys_ref, sems.at[0]),
        pltpu.make_async_copy(values_ref.at[:, columns], own_values_ref, sems.at[1]),
    ]
    for a in range(blocks_dev):
        for h in range(heads):
            copies.append(
                pltpu.make_async_copy(
                    q_ref.at[pl.ds(a * BLOCK, BLOCK), pl.ds(h * HEAD_SIZE, HEAD_SIZE)],
                    stacked_ref.at[a, pl.ds(h * BLOCK, BLOCK)],
                    stack_sems.at[a, h],
                )
            )
    table.start()
    for copy in copies:
        copy.start()
    table.wait()
    me = lax.axis_index("ctx")
    lane = first_lane((BLOCK, BLOCK))
    for a in range(blocks_dev):
        query_block = me * blocks_dev + a
        row = 0
        for step in steps:
            source = step if count is None else lax.rem(me + (count - step), count)
            for j in range(blocks_dev):
                key_block = source * blocks_dev + j
                on = (table_ref[query_block, key_block] == 1) | (query_block == key_block)
                mask_ref[a, row : row + BLOCK, :] = jnp.where(
                    lane, jnp.where(on, 0.0, FAR), 0.0
                ).astype(jnp.bfloat16)
                row += BLOCK
    for copy in copies:
        copy.wait()


def prepared(key_vectors, value_vectors, queries, block_pattern, steps, count):
    tok_dev, width = queries.shape
    blocks_dev, heads = tok_dev // BLOCK, width // HEAD_SIZE
    own = held((tok_dev, HEAD_SIZE))
    return pl.pallas_call(
        functools.partial(prepare_kernel, steps, count),
        out_shape=[
            own,
            own,
            held((blocks_dev, heads * BLOCK, HEAD_SIZE)),
            held((blocks_dev, len(steps) * tok_dev, BLOCK)),
        ],
        in_specs=[HBM] * 4,
        out_specs=[VMEM] * 4,
        scratch_shapes=[
            pltpu.SMEM(block_pattern.shape, jnp.int32),
            pltpu.SemaphoreType.DMA((3,)),
            pltpu.SemaphoreType.DMA((blocks_dev, heads)),
        ],
        compiler_params=params(8),
        cost_estimate=cost(0, 1 << 20),
    )(
        *[
            pltpu.with_memory_space_constraint(operand, pltpu.HBM)
            for operand in (key_vectors, value_vectors, queries, block_pattern)
        ]
    )


def weights_kernel(q_ref, mask_ref, *refs):
    *key_refs, out_ref = refs
    blocks_dev, rows, _ = q_ref.shape
    group = min(rows, 512)
    exponent_scale = math.log2(math.e) / math.sqrt(HEAD_SIZE)
    keys = jnp.concatenate([ref[...] for ref in key_refs], axis=0)
    lane = jnp.where(first_lane((group, BLOCK)), 1.0, 0.0).astype(jnp.bfloat16)
    for a in range(blocks_dev):
        wide_keys = jnp.concatenate([keys, mask_ref[a]], axis=1)
        for first in range(0, rows, group):
            wide = jnp.concatenate([q_ref[a, first : first + group, :], lane], axis=1)
            scores = lax.dot_general(
                wide, wide_keys, (((1,), (1,)), ((), ())), preferred_element_type=jnp.float32
            )
            top = jnp.max(scores, axis=1, keepdims=True)
            out_ref[a, first : first + group, :] = jnp.exp2(
                (scores - top) * exponent_scale
            ).astype(jnp.bfloat16)


def weights_of(stacked, mask, key_parts):
    blocks_dev, rows, _ = stacked.shape
    keys = mask.shape[1]
    return pl.pallas_call(
        weights_kernel,
        out_shape=held((blocks_dev, rows, keys)),
        in_specs=[VMEM] * (2 + len(key_parts)),
        out_specs=VMEM,
        compiler_params=params(8 + (min(rows, 512) * keys * 16 >> 20)),
        cost_estimate=cost(8 * blocks_dev * rows * keys * HEAD_SIZE, 4 << 20),
    )(stacked, mask, *key_parts)


def values_kernel(first, group, weights_ref, *refs):
    value_refs, out_ref = refs[:-1], refs[-1]
    values = jnp.concatenate([ref[...] for ref in value_refs], axis=0)
    values = jnp.concatenate([values, jnp.ones_like(values)], axis=1)
    for a in range(weights_ref.shape[0]):
        summed = jnp.dot(
            weights_ref[a, first * BLOCK : (first + group) * BLOCK, :],
            values,
            preferred_element_type=jnp.float32,
        )
        result = (summed[:, :HEAD_SIZE] / summed[:, HEAD_SIZE:]).astype(jnp.bfloat16)
        for i in range(group):
            out_ref[a * BLOCK : (a + 1) * BLOCK, i * HEAD_SIZE : (i + 1) * HEAD_SIZE] = result[
                i * BLOCK : (i + 1) * BLOCK
            ]


def attended_of(weights, value_parts, first, group):
    blocks_dev, _, keys = weights.shape
    return pl.pallas_call(
        functools.partial(values_kernel, first, group),
        out_shape=held((blocks_dev * BLOCK, group * HEAD_SIZE)),
        in_specs=[VMEM] * (1 + len(value_parts)),
        out_specs=VMEM,
        compiler_params=params(16),
        cost_estimate=cost(4 * blocks_dev * BLOCK * group * keys * HEAD_SIZE, 1 << 20),
    )(weights, *value_parts)


def projection_kernel(places, fresh, weight_ref, *refs):
    *parts, out_ref = refs
    total = None if fresh else parts.pop(0)[...]
    me = lax.axis_index("head")
    for (bits, half), part in zip(places, parts):
        depth = part.shape[1]
        row = pl.multiple_of((me ^ bits) * (2 * depth) + half * depth, depth)
        term = jnp.dot(
            part[...], weight_ref[pl.ds(row, depth), :], preferred_element_type=jnp.float32
        )
        total = term if total is None else total + term
    out_ref[...] = total.astype(out_ref.dtype)


def projected(total, weight, places, parts, last=False):
    rows, depth = parts[0].shape
    columns = weight.shape[1]
    fresh = total is None
    operands = ([] if fresh else [total]) + parts
    shape = (rows, columns)
    return pl.pallas_call(
        functools.partial(projection_kernel, places, fresh),
        out_shape=jax.ShapeDtypeStruct(shape, jnp.bfloat16) if last else held(shape, jnp.float32),
        in_specs=[VMEM] * (1 + len(operands)),
        out_specs=VMEM,
        compiler_params=params(8),
        cost_estimate=cost(8 * rows * depth * columns * len(parts), 1 << 20),
    )(weight, *operands)


def gathered_over_ctx(part, steps):
    if len(steps) == 4:
        return [part] + [shifted(part, "ctx", step) for step in steps[1:]]
    whole = lax.all_gather(part, "ctx")
    return [whole[i] for i in range(len(steps))]


def on_device(queries, key_vectors, value_head_vectors, block_pattern, out_weight):
    heads_dev = queries.shape[1] // HEAD_SIZE
    count = lax.axis_size("ctx")
    steps = (0, 2, 1, 3) if count == 4 else tuple(range(count))
    keys, values, stacked, mask = prepared(
        key_vectors,
        value_head_vectors,
        queries,
        block_pattern,
        steps,
        count if count == 4 else None,
    )
    key_parts = gathered_over_ctx(keys, steps)
    value_parts = gathered_over_ctx(values, steps)
    weights = weights_of(stacked, mask, key_parts)
    if lax.axis_size("head") != 8:
        att = attended_of(weights, value_parts, 0, heads_dev)
        mixed = jnp.dot(
            lax.all_gather(att, "head", axis=1, tiled=True),
            out_weight,
            preferred_element_type=jnp.float32,
        )
        return mixed.astype(jnp.bfloat16)

    barrier = lax.optimization_barrier
    weight = pltpu.with_memory_space_constraint(out_weight, pltpu.VMEM)
    half = heads_dev // 2
    a = attended_of(weights, value_parts, 0, half)
    b = attended_of(weights, value_parts, half, half)
    xa = swapped(a, "head", 2)
    yb = swapped(b, "head", 4)
    xb = swapped(b, "head", 2)
    ya = swapped(a, "head", 4)
    a, b = barrier((a, b))
    sa = swapped(a, "head", 1)
    sb = swapped(b, "head", 1)
    mixed = projected(None, weight, ((0, 0), (0, 1), (1, 0), (1, 1)), [a, b, sa, sb])
    xa, mixed = barrier((xa, mixed))
    da = swapped(xa, "head", 4)
    yb, mixed = barrier((yb, mixed))
    db = swapped(yb, "head", 2)
    xas, ybs = swapped(xa, "head", 1), swapped(yb, "head", 1)
    mixed = projected(mixed, weight, ((2, 0), (3, 0), (4, 1), (5, 1)), [xa, xas, yb, ybs])

    xbs, yas = swapped(xb, "head", 1), swapped(ya, "head", 1)
    mixed = projected(mixed, weight, ((2, 1), (3, 1), (4, 0), (5, 0)), [xb, xbs, ya, yas])
    da, mixed = barrier((da, mixed))
    das = swapped(da, "head", 1)
    mixed = projected(mixed, weight, ((6, 0), (7, 0)), [da, das])
    dbs = swapped(db, "head", 1)
    return projected(mixed, weight, ((6, 1), (7, 1)), [db, dbs], True)


def solution(mesh):
    return jax.shard_map(
        on_device,
        mesh=mesh,
        in_specs=(P("ctx", "head"), P("ctx", None), P("ctx", None), P(), P(None, "head")),
        out_specs=P("ctx", "head"),
        check_vma=False,
    )
```

time: 50.7 us -> 43.7 us (0.86)
  Pallas kernels: 17.6 us -> 10.7 us
  local copies, waits for them, and re-layouts: 2.61 us -> 0.01 us
  starting transfers between devices: 19.1 us -> 20.7 us
  waiting for transfers between devices: 10.9 us -> 12 us
    pallas_call x6 -> x7, Pallas kernels: 16.2 us -> 9.28 us  [the longest x5 5.96 us: projected(): pl.pallas_call(functools.partial(projection_kernel, places, fresh), out_s...]
    unnamed x4 -> x2, local copies, waits for them, and re-layouts: 1.73 us -> 0.01 us
    ppermute x14, starting transfers between devices: 7.26 us -> 8.96 us  [swapped(): lax.ppermute(value, axis, [(source, source ^ bits) for source in range(co...]
    ppermute x6, waiting for transfers between devices: 0.02 us -> 1.7 us  [shifted(): lax.ppermute(value, axis, [(source, (source + steps) % count) for source...]
    dynamic_slice x1 -> x0, local copies, waits for them, and re-layouts: 0.88 us -> none  [own_slices(): lax.dynamic_slice_in_dim(vectors, head * HEAD_SIZE, HEAD_SIZE, 1)]
    ppermute x14, waiting for transfers between devices: 10.9 us -> 10.3 us  [swapped(): lax.ppermute(value, axis, [(source, source ^ bits) for source in range(co...]
  transfers between devices with their start and end apart: 20 -> 20, of which waited for: 6 -> 10; matrix products, arithmetic and copies ran while one was open for 0% -> 0% of each run, Pallas kernels for 30% -> 14%
where the time goes in v4:
time: 43.7 us; the launch traced here: 43.5 us
  starting transfers between devices  20.7 us (47%)
  waiting for transfers between devices  12 us (27%)
  Pallas kernels  10.7 us (24%)
    ppermute x6, starting transfers between devices, shifted(): lax.ppermute(value, axis, [(source, (source + steps) % count) for source...  11.8 us
    ppermute x14, waiting for transfers between devices, swapped(): lax.ppermute(value, axis, [(source, source ^ bits) for source in range(co...  10.3 us
    ppermute x14, starting transfers between devices, swapped(): lax.ppermute(value, axis, [(source, source ^ bits) for source in range(co...  8.96 us
    pallas_call x5, Pallas kernels, projected(): pl.pallas_call(functools.partial(projection_kernel, places, fresh), out_s...  5.96 us
    pallas_call x1, Pallas kernels, weights_of(): pl.pallas_call(weights_kernel, out_shape=held((blocks_dev, rows, keys)),...  1.86 us
    ppermute x6, waiting for transfers between devices, shifted(): lax.ppermute(value, axis, [(source, (source + steps) % count) for source...  1.7 us
    pallas_call x1, Pallas kernels, prepared(): pl.pallas_call(functools.partial(prepare_kernel, steps, count), out_shape...  1.47 us
    pallas_call x2, Pallas kernels, attended_of(): pl.pallas_call(functools.partial(values_kernel, first, group), out_shape=...  1.43 us
  transfers between devices with their start and end apart: 20, of which 10 were waited for; matrix products, arithmetic and copies ran while one was open for 0% of the time, Pallas kernels for 14%

profile of v4, /device:TPU:0, one launch (start us, length us, event | category | flops | bytes accessed | tf_op | source)
XLA Modules:
  0.0 43.5 jit_solution(10868992020670335464)
XLA Ops:
  0.0 0.0 copy-start
  0.0 1.5 %shard_map.55 = (bf16[256,128]{1,0:T(8,128)(2,1)S(1)}, bf16[256,128]{1,0:T(8,128)(2,1)S(1)}, bf16[2,1024,128]{2,1,0:T(8,128)(2,1)S(1)}, bf16[2,1024,128]{2,1,0:T(8,128)(2,1)S(1)}) custom-call(bf16[256,1024]{1,0:T(8,128)(2,1)} %keys_ref.1, bf16[256,1024]{1,0:T(8,128)(2,1)} %values_ref.1, bf16[256,1024]{1,0:T(8,128)(2,1)} %q_ref.1, s32[8,8]{1,0:T(8,128)} %pattern_ref.1), custom_call_target="tpu_custom_call" | custom-call | bytes 1048576 | tf_op jit(solution)/shard_map/pallas_call | solution.py:95
  1.5 4.1 %collective-permute-start = (bf16[256,128]{1,0:T(8,128)(2,1)S(1)}, bf16[256,128]{1,0:T(8,128)(2,1)S(1)}, u32[]{:S(2)}, u32[]{:S(2)}) collective-permute-start(bf16[256,128]{1,0:T(8,128)(2,1)S(1)} %get-tuple-element.19.refs_0_), channel_id=1, source_target_pairs={{0,16},{8,24},{16,0},{24,8},{1,17},{9,25},{17,1},{25,9},{2,18},{10... | collective-permute-start | bytes 196616 | tf_op jit(solution)/shard_map/ppermute | solution.py:36
  5.6 1.6 %collective-permute-start.1 = (bf16[256,128]{1,0:T(8,128)(2,1)S(1)}, bf16[256,128]{1,0:T(8,128)(2,1)S(1)}, u32[]{:S(2)}, u32[]{:S(2)}) collective-permute-start(bf16[256,128]{1,0:T(8,128)(2,1)S(1)} %get-tuple-element.19.refs_0_), channel_id=1, source_target_pairs={{0,8},{8,16},{16,24},{24,0},{1,9},{9,17},{17,25},{25,1},{2,10},{10... | collective-permute-start | bytes 196616 | tf_op jit(solution)/shard_map/ppermute | solution.py:36
  7.2 2.2 %collective-permute-start.2 = (bf16[256,128]{1,0:T(8,128)(2,1)S(1)}, bf16[256,128]{1,0:T(8,128)(2,1)S(1)}, u32[]{:S(2)}, u32[]{:S(2)}) collective-permute-start(bf16[256,128]{1,0:T(8,128)(2,1)S(1)} %get-tuple-element.19.refs_0_), channel_id=1, source_target_pairs={{0,24},{8,0},{16,8},{24,16},{1,25},{9,1},{17,9},{25,17},{2,26},{10... | collective-permute-start | bytes 196616 | tf_op jit(solution)/shard_map/ppermute | solution.py:36
  9.4 0.0 collective-permute-start.3
  9.4 0.6 %collective-permute-start.4 = (bf16[256,128]{1,0:T(8,128)(2,1)S(1)}, bf16[256,128]{1,0:T(8,128)(2,1)S(1)}, u32[]{:S(2)}, u32[]{:S(2)}) collective-permute-start(bf16[256,128]{1,0:T(8,128)(2,1)S(1)} %get-tuple-element.20.refs_0_), channel_id=1, source_target_pairs={{0,8},{8,16},{16,24},{24,0},{1,9},{9,17},{17,25},{25,1},{2,10},{10... | collective-permute-start | bytes 196616 | tf_op jit(solution)/shard_map/ppermute | solution.py:36
  10.0 0.0 collective-permute-done.refs_1_
  10.0 3.3 %collective-permute-start.5 = (bf16[256,128]{1,0:T(8,128)(2,1)S(1)}, bf16[256,128]{1,0:T(8,128)(2,1)S(1)}, u32[]{:S(2)}, u32[]{:S(2)}) collective-permute-start(bf16[256,128]{1,0:T(8,128)(2,1)S(1)} %get-tuple-element.20.refs_0_), channel_id=1, source_target_pairs={{0,24},{8,0},{16,8},{24,16},{1,25},{9,1},{17,9},{25,17},{2,26},{10... | collective-permute-start | bytes 196616 | tf_op jit(solution)/shard_map/ppermute | solution.py:36
  13.2 0.0 collective-permute-done.1.refs_2_
  13.2 0.0 collective-permute-done.2.refs_3_
  13.2 1.9 %shard_map.56.weights_ref = bf16[2,1024,1024]{2,1,0:T(8,128)(2,1)S(1)} custom-call(bf16[2,1024,128]{2,1,0:T(8,128)(2,1)S(1)} %get-tuple-element.17.q_ref, bf16[2,1024,128]{2,1,0:T(8,128)(2,1)S(1)} %get-tuple-element.18.mask_ref, bf16[256,128]{1,0:T(8,128)(2,1)S(1)} %get-tuple-element.19.refs_0_, bf16[256,128]{1,0:T(8,128)(2,1)S(1)} %collective-permute-done.refs_1_, ...), custom_call_target="tpu_custom_call" | custom-call | flops 2147483648 | bytes 4194304 | tf_op jit(solution)/shard_map/pallas_call | solution.py:143
  15.1 1.6 %collective-permute-done.3.refs_1_ = bf16[256,128]{1,0:T(8,128)(2,1)S(1)} collective-permute-done((bf16[256,128]{1,0:T(8,128)(2,1)S(1)}, bf16[256,128]{1,0:T(8,128)(2,1)S(1)}, u32[]{:S(2)}, u32[]{:S(2)}) %collective-permute-start.3) | collective-permute-done | bytes 65568 | tf_op jit(solution)/shard_map/ppermute | solution.py:36
  16.7 0.0 collective-permute-done.4.refs_2_
  16.7 0.1 collective-permute-done.5.refs_3_
  16.8 0.7 %shard_map.58.refs_1_ = bf16[256,512]{1,0:T(8,128)(2,1)S(1)} custom-call(bf16[2,1024,1024]{2,1,0:T(8,128)(2,1)S(1)} %shard_map.56.weights_ref, bf16[256,128]{1,0:T(8,128)(2,1)S(1)} %get-tuple-element.20.refs_0_, bf16[256,128]{1,0:T(8,128)(2,1)S(1)} %collective-permute-done.3.refs_1_, bf16[256,128]{1,0:T(8,128)(2,1)S(1)} %collective-permute-done.4.refs_2_, ...), custom_call_target="tpu_custom_call" | custom-call | flops 536870912 | bytes 1048576 | tf_op jit(solution)/shard_map/pallas_call | solution.py:172
  17.5 0.7 %shard_map.57.refs_0_ = bf16[256,512]{1,0:T(8,128)(2,1)S(1)} custom-call(bf16[2,1024,1024]{2,1,0:T(8,128)(2,1)S(1)} %shard_map.56.weights_ref, bf16[256,128]{1,0:T(8,128)(2,1)S(1)} %get-tuple-element.20.refs_0_, bf16[256,128]{1,0:T(8,128)(2,1)S(1)} %collective-permute-done.3.refs_1_, bf16[256,128]{1,0:T(8,128)(2,1)S(1)} %collective-permute-done.4.refs_2_, ...), custom_call_target="tpu_custom_call" | custom-call | flops 536870912 | bytes 1048576 | tf_op jit(solution)/shard_map/pallas_call | solution.py:172
  18.2 0.1 collective-permute-start.7
  18.3 0.5 %collective-permute-start.8 = (bf16[256,512]{1,0:T(8,128)(2,1)S(1)}, bf16[256,512]{1,0:T(8,128)(2,1)S(1)}, u32[]{:S(2)}, u32[]{:S(2)}) collective-permute-start(bf16[256,512]{1,0:T(8,128)(2,1)S(1)} %shard_map.58.refs_1_), channel_id=1, source_target_pairs={{0,1},{1,0},{2,3},{3,2},{4,5},{5,4},{6,7},{7,6},{8,9},{9,8},{10,11... | collective-permute-start | bytes 786440 | tf_op jit(solution)/shard_map/ppermute | solution.py:41
  18.8 1.7 %collective-permute-start.6 = (bf16[256,512]{1,0:T(8,128)(2,1)S(1)}, bf16[256,512]{1,0:T(8,128)(2,1)S(1)}, u32[]{:S(2)}, u32[]{:S(2)}) collective-permute-start(bf16[256,512]{1,0:T(8,128)(2,1)S(1)} %shard_map.57.refs_0_), channel_id=1, source_target_pairs={{0,2},{1,3},{2,0},{3,1},{4,6},{5,7},{6,4},{7,5},{8,10},{9,11},{10,... | collective-permute-start | bytes 786440 | tf_op jit(solution)/shard_map/ppermute | solution.py:41
  20.5 1.5 %collective-permute-start.10 = (bf16[256,512]{1,0:T(8,128)(2,1)S(1)}, bf16[256,512]{1,0:T(8,128)(2,1)S(1)}, u32[]{:S(2)}, u32[]{:S(2)}) collective-permute-start(bf16[256,512]{1,0:T(8,128)(2,1)S(1)} %shard_map.58.refs_1_), channel_id=1, source_target_pairs={{0,4},{1,5},{2,6},{3,7},{4,0},{5,1},{6,2},{7,3},{8,12},{9,13},{10,... | collective-permute-start | bytes 786440 | tf_op jit(solution)/shard_map/ppermute | solution.py:41
  22.0 0.5 %collective-permute-start.13 = (bf16[256,512]{1,0:T(8,128)(2,1)S(1)}, bf16[256,512]{1,0:T(8,128)(2,1)S(1)}, u32[]{:S(2)}, u32[]{:S(2)}) collective-permute-start(bf16[256,512]{1,0:T(8,128)(2,1)S(1)} %shard_map.58.refs_1_), channel_id=1, source_target_pairs={{0,2},{1,3},{2,0},{3,1},{4,6},{5,7},{6,4},{7,5},{8,10},{9,11},{10,... | collective-permute-start | bytes 786440 | tf_op jit(solution)/shard_map/ppermute | solution.py:41
  22.6 0.0 collective-permute-done.7.refs_2_
  22.6 0.3 collective-permute-start.15
  22.9 0.0 collective-permute-done.8.refs_3_
  22.9 0.0 copy-done
  22.9 1.2 %shard_map.59.refs_0_ = f32[256,1024]{1,0:T(8,128)S(1)} custom-call(bf16[8192,1024]{1,0:T(8,128)(2,1)S(1)} %copy-done, bf16[256,512]{1,0:T(8,128)(2,1)S(1)} %shard_map.57.refs_0_, bf16[256,512]{1,0:T(8,128)(2,1)S(1)} %shard_map.58.refs_1_, bf16[256,512]{1,0:T(8,128)(2,1)S(1)} %collective-permute-done.7.refs_2_, ...), custom_call_target="tpu_custom_call" | custom-call | flops 4294967296 | bytes 1048576 | tf_op jit(solution)/shard_map/pallas_call | solution.py:202
  24.1 3.8 %collective-permute-done.6.refs_1_ = bf16[256,512]{1,0:T(8,128)(2,1)S(1)} collective-permute-done((bf16[256,512]{1,0:T(8,128)(2,1)S(1)}, bf16[256,512]{1,0:T(8,128)(2,1)S(1)}, u32[]{:S(2)}, u32[]{:S(2)}) %collective-permute-start.6) | collective-permute-done | bytes 262176 | tf_op jit(solution)/shard_map/ppermute | solution.py:41
  28.0 1.7 %collective-permute-done.10.refs_3_ = bf16[256,512]{1,0:T(8,128)(2,1)S(1)} collective-permute-done((bf16[256,512]{1,0:T(8,128)(2,1)S(1)}, bf16[256,512]{1,0:T(8,128)(2,1)S(1)}, u32[]{:S(2)}, u32[]{:S(2)}) %collective-permute-start.10) | collective-permute-done | bytes 262176 | tf_op jit(solution)/shard_map/ppermute | solution.py:41
  29.7 0.0 collective-permute-start.12
  29.7 0.5 %collective-permute-start.11 = (bf16[256,512]{1,0:T(8,128)(2,1)S(1)}, bf16[256,512]{1,0:T(8,128)(2,1)S(1)}, u32[]{:S(2)}, u32[]{:S(2)}) collective-permute-start(bf16[256,512]{1,0:T(8,128)(2,1)S(1)} %collective-permute-done.6.refs_1_), channel_id=1, source_target_pairs={{0,1},{1,0},{2,3},{3,2},{4,5},{5,4},{6,7},{7,6},{8,9},{9,8},{10,11... | collective-permute-start | bytes 786440 | tf_op jit(solution)/shard_map/ppermute | solution.py:41
  30.2 1.5 %collective-permute-start.9 = (bf16[256,512]{1,0:T(8,128)(2,1)S(1)}, bf16[256,512]{1,0:T(8,128)(2,1)S(1)}, u32[]{:S(2)}, u32[]{:S(2)}) collective-permute-start(bf16[256,512]{1,0:T(8,128)(2,1)S(1)} %collective-permute-done.6.refs_1_), channel_id=1, source_target_pairs={{0,4},{1,5},{2,6},{3,7},{4,0},{5,1},{6,2},{7,3},{8,12},{9,13},{10,... | collective-permute-start | bytes 786440 | tf_op jit(solution)/shard_map/ppermute | solution.py:41
  31.8 1.0 %collective-permute-done.13.refs_1_ = bf16[256,512]{1,0:T(8,128)(2,1)S(1)} collective-permute-done((bf16[256,512]{1,0:T(8,128)(2,1)S(1)}, bf16[256,512]{1,0:T(8,128)(2,1)S(1)}, u32[]{:S(2)}, u32[]{:S(2)}) %collective-permute-start.13) | collective-permute-done | bytes 262176 | tf_op jit(solution)/shard_map/ppermute | solution.py:41
  32.7 1.7 %collective-permute-start.18 = (bf16[256,512]{1,0:T(8,128)(2,1)S(1)}, bf16[256,512]{1,0:T(8,128)(2,1)S(1)}, u32[]{:S(2)}, u32[]{:S(2)}) collective-permute-start(bf16[256,512]{1,0:T(8,128)(2,1)S(1)} %collective-permute-done.10.refs_3_), channel_id=1, source_target_pairs={{0,2},{1,3},{2,0},{3,1},{4,6},{5,7},{6,4},{7,5},{8,10},{9,11},{10,... | collective-permute-start | bytes 786440 | tf_op jit(solution)/shard_map/ppermute | solution.py:41
  34.4 0.9 %collective-permute-done.15.refs_3_ = bf16[256,512]{1,0:T(8,128)(2,1)S(1)} collective-permute-done((bf16[256,512]{1,0:T(8,128)(2,1)S(1)}, bf16[256,512]{1,0:T(8,128)(2,1)S(1)}, u32[]{:S(2)}, u32[]{:S(2)}) %collective-permute-start.15) | collective-permute-done | bytes 262176 | tf_op jit(solution)/shard_map/ppermute | solution.py:41
  35.3 0.0 collective-permute-start.14
  35.3 0.0 collective-permute-done.12.refs_4_
  35.4 0.5 %collective-permute-start.16 = (bf16[256,512]{1,0:T(8,128)(2,1)S(1)}, bf16[256,512]{1,0:T(8,128)(2,1)S(1)}, u32[]{:S(2)}, u32[]{:S(2)}) collective-permute-start(bf16[256,512]{1,0:T(8,128)(2,1)S(1)} %collective-permute-done.15.refs_3_), channel_id=1, source_target_pairs={{0,1},{1,0},{2,3},{3,2},{4,5},{5,4},{6,7},{7,6},{8,9},{9,8},{10,11... | collective-permute-start | bytes 786440 | tf_op jit(solution)/shard_map/ppermute | solution.py:41
  35.9 0.0 collective-permute-done.11.refs_2_
  35.9 1.2 %shard_map.60.refs_0_ = f32[256,1024]{1,0:T(8,128)S(1)} custom-call(bf16[8192,1024]{1,0:T(8,128)(2,1)S(1)} %copy-done, f32[256,1024]{1,0:T(8,128)S(1)} %shard_map.59.refs_0_, bf16[256,512]{1,0:T(8,128)(2,1)S(1)} %collective-permute-done.6.refs_1_, bf16[256,512]{1,0:T(8,128)(2,1)S(1)} %collective-permute-done.11.refs_2_, ...), custom_call_target="tpu_custom_call" | custom-call | flops 4294967296 | bytes 1048576 | tf_op jit(solution)/shard_map/pallas_call | solution.py:202
  37.1 0.0 collective-permute-done.14.refs_2_
  37.1 0.1 collective-permute-done.16.refs_4_
  37.3 1.2 %shard_map.61.refs_0_ = f32[256,1024]{1,0:T(8,128)S(1)} custom-call(bf16[8192,1024]{1,0:T(8,128)(2,1)S(1)} %copy-done, f32[256,1024]{1,0:T(8,128)S(1)} %shard_map.60.refs_0_, bf16[256,512]{1,0:T(8,128)(2,1)S(1)} %collective-permute-done.13.refs_1_, bf16[256,512]{1,0:T(8,128)(2,1)S(1)} %collective-permute-done.14.refs_2_, ...), custom_call_target="tpu_custom_call" | custom-call | flops 4294967296 | bytes 1048576 | tf_op jit(solution)/shard_map/pallas_call | solution.py:202
  38.5 1.3 %collective-permute-done.9.refs_1_ = bf16[256,512]{1,0:T(8,128)(2,1)S(1)} collective-permute-done((bf16[256,512]{1,0:T(8,128)(2,1)S(1)}, bf16[256,512]{1,0:T(8,128)(2,1)S(1)}, u32[]{:S(2)}, u32[]{:S(2)}) %collective-permute-start.9) | collective-permute-done | bytes 262176 | tf_op jit(solution)/shard_map/ppermute | solution.py:41
  39.8 0.0 collective-permute-start.17
  39.8 0.4 collective-permute-done.18.refs_1_
  40.2 0.1 collective-permute-start.19
  40.3 1.0 %collective-permute-done.17.refs_2_ = bf16[256,512]{1,0:T(8,128)(2,1)S(1)} collective-permute-done((bf16[256,512]{1,0:T(8,128)(2,1)S(1)}, bf16[256,512]{1,0:T(8,128)(2,1)S(1)}, u32[]{:S(2)}, u32[]{:S(2)}) %collective-permute-start.17) | collective-permute-done | bytes 262176 | tf_op jit(solution)/shard_map/ppermute | solution.py:41
  41.3 0.7 %shard_map.62.refs_0_ = f32[256,1024]{1,0:T(8,128)S(1)} custom-call(bf16[8192,1024]{1,0:T(8,128)(2,1)S(1)} %copy-done, f32[256,1024]{1,0:T(8,128)S(1)} %shard_map.61.refs_0_, bf16[256,512]{1,0:T(8,128)(2,1)S(1)} %collective-permute-done.9.refs_1_, bf16[256,512]{1,0:T(8,128)(2,1)S(1)} %collective-permute-done.17.refs_2_), custom_call_target="tpu_custom_call" | custom-call | flops 2147483648 | bytes 1048576 | tf_op jit(solution)/shard_map/pallas_call | solution.py:202
  42.0 0.0 collective-permute-done.19.refs_2_
  42.0 1.5 %shard_map.63 = bf16[256,1024]{1,0:T(8,128)(2,1)} custom-call(bf16[8192,1024]{1,0:T(8,128)(2,1)S(1)} %copy-done, f32[256,1024]{1,0:T(8,128)S(1)} %shard_map.62.refs_0_, bf16[256,512]{1,0:T(8,128)(2,1)S(1)} %collective-permute-done.18.refs_1_, bf16[256,512]{1,0:T(8,128)(2,1)S(1)} %collective-permute-done.19.refs_2_), custom_call_target="tpu_custom_call" | custom-call | flops 2147483648 | bytes 1048576 | tf_op jit(solution)/shard_map/pallas_call | solution.py:202
Async XLA Ops:
  0.0 22.9 %copy-start = (bf16[8192,1024]{1,0:T(8,128)(2,1)S(1)}, bf16[8192,1024]{1,0:T(8,128)(2,1)}, u32[]{:S(2)}) copy-start(bf16[8192,1024]{1,0:T(8,128)(2,1)} %weight_ref.9) | copy-start | bytes 50331652
  1.5 8.5 %collective-permute-start = (bf16[256,128]{1,0:T(8,128)(2,1)S(1)}, bf16[256,128]{1,0:T(8,128)(2,1)S(1)}, u32[]{:S(2)}, u32[]{:S(2)}) collective-permute-start(bf16[256,128]{1,0:T(8,128)(2,1)S(1)} %get-tuple-element.19.refs_0_), channel_id=1, source_target_pairs={{0,16},{8,24},{16,0},{24,8},{1,17},{9,25},{17,1},{25,9},{2,18},{10... | collective-permute-start | bytes 196616 | tf_op jit(solution)/shard_map/ppermute | solution.py:36
  5.6 7.7 %collective-permute-start.1 = (bf16[256,128]{1,0:T(8,128)(2,1)S(1)}, bf16[256,128]{1,0:T(8,128)(2,1)S(1)}, u32[]{:S(2)}, u32[]{:S(2)}) collective-permute-start(bf16[256,128]{1,0:T(8,128)(2,1)S(1)} %get-tuple-element.19.refs_0_), channel_id=1, source_target_pairs={{0,8},{8,16},{16,24},{24,0},{1,9},{9,17},{17,25},{25,1},{2,10},{10... | collective-permute-start | bytes 196616 | tf_op jit(solution)/shard_map/ppermute | solution.py:36
  7.2 6.1 %collective-permute-start.2 = (bf16[256,128]{1,0:T(8,128)(2,1)S(1)}, bf16[256,128]{1,0:T(8,128)(2,1)S(1)}, u32[]{:S(2)}, u32[]{:S(2)}) collective-permute-start(bf16[256,128]{1,0:T(8,128)(2,1)S(1)} %get-tuple-element.19.refs_0_), channel_id=1, source_target_pairs={{0,24},{8,0},{16,8},{24,16},{1,25},{9,1},{17,9},{25,17},{2,26},{10... | collective-permute-start | bytes 196616 | tf_op jit(solution)/shard_map/ppermute | solution.py:36
  9.4 7.3 %collective-permute-start.3 = (bf16[256,128]{1,0:T(8,128)(2,1)S(1)}, bf16[256,128]{1,0:T(8,128)(2,1)S(1)}, u32[]{:S(2)}, u32[]{:S(2)}) collective-permute-start(bf16[256,128]{1,0:T(8,128)(2,1)S(1)} %get-tuple-element.20.refs_0_), channel_id=1, source_target_pairs={{0,16},{8,24},{16,0},{24,8},{1,17},{9,25},{17,1},{25,9},{2,18},{10... | collective-permute-start | bytes 196616 | tf_op jit(solution)/shard_map/ppermute | solution.py:36
  9.4 7.3 %collective-permute-start.4 = (bf16[256,128]{1,0:T(8,128)(2,1)S(1)}, bf16[256,128]{1,0:T(8,128)(2,1)S(1)}, u32[]{:S(2)}, u32[]{:S(2)}) collective-permute-start(bf16[256,128]{1,0:T(8,128)(2,1)S(1)} %get-tuple-element.20.refs_0_), channel_id=1, source_target_pairs={{0,8},{8,16},{16,24},{24,0},{1,9},{9,17},{17,25},{25,1},{2,10},{10... | collective-permute-start | bytes 196616 | tf_op jit(solution)/shard_map/ppermute | solution.py:36
  10.0 6.8 %collective-permute-start.5 = (bf16[256,128]{1,0:T(8,128)(2,1)S(1)}, bf16[256,128]{1,0:T(8,128)(2,1)S(1)}, u32[]{:S(2)}, u32[]{:S(2)}) collective-permute-start(bf16[256,128]{1,0:T(8,128)(2,1)S(1)} %get-tuple-element.20.refs_0_), channel_id=1, source_target_pairs={{0,24},{8,0},{16,8},{24,16},{1,25},{9,1},{17,9},{25,17},{2,26},{10... | collective-permute-start | bytes 196616 | tf_op jit(solution)/shard_map/ppermute | solution.py:36
  18.2 4.3 %collective-permute-start.7 = (bf16[256,512]{1,0:T(8,128)(2,1)S(1)}, bf16[256,512]{1,0:T(8,128)(2,1)S(1)}, u32[]{:S(2)}, u32[]{:S(2)}) collective-permute-start(bf16[256,512]{1,0:T(8,128)(2,1)S(1)} %shard_map.57.refs_0_), channel_id=1, source_target_pairs={{0,1},{1,0},{2,3},{3,2},{4,5},{5,4},{6,7},{7,6},{8,9},{9,8},{10,11... | collective-permute-start | bytes 786440 | tf_op jit(solution)/shard_map/ppermute | solution.py:41
  18.3 4.6 %collective-permute-start.8 = (bf16[256,512]{1,0:T(8,128)(2,1)S(1)}, bf16[256,512]{1,0:T(8,128)(2,1)S(1)}, u32[]{:S(2)}, u32[]{:S(2)}) collective-permute-start(bf16[256,512]{1,0:T(8,128)(2,1)S(1)} %shard_map.58.refs_1_), channel_id=1, source_target_pairs={{0,1},{1,0},{2,3},{3,2},{4,5},{5,4},{6,7},{7,6},{8,9},{9,8},{10,11... | collective-permute-start | bytes 786440 | tf_op jit(solution)/shard_map/ppermute | solution.py:41
  18.8 9.2 %collective-permute-start.6 = (bf16[256,512]{1,0:T(8,128)(2,1)S(1)}, bf16[256,512]{1,0:T(8,128)(2,1)S(1)}, u32[]{:S(2)}, u32[]{:S(2)}) collective-permute-start(bf16[256,512]{1,0:T(8,128)(2,1)S(1)} %shard_map.57.refs_0_), channel_id=1, source_target_pairs={{0,2},{1,3},{2,0},{3,1},{4,6},{5,7},{6,4},{7,5},{8,10},{9,11},{10,... | collective-permute-start | bytes 786440 | tf_op jit(solution)/shard_map/ppermute | solution.py:41
  20.5 9.2 %collective-permute-start.10 = (bf16[256,512]{1,0:T(8,128)(2,1)S(1)}, bf16[256,512]{1,0:T(8,128)(2,1)S(1)}, u32[]{:S(2)}, u32[]{:S(2)}) collective-permute-start(bf16[256,512]{1,0:T(8,128)(2,1)S(1)} %shard_map.58.refs_1_), channel_id=1, source_target_pairs={{0,4},{1,5},{2,6},{3,7},{4,0},{5,1},{6,2},{7,3},{8,12},{9,13},{10,... | collective-permute-start | bytes 786440 | tf_op jit(solution)/shard_map/ppermute | solution.py:41
  22.0 10.7 %collective-permute-start.13 = (bf16[256,512]{1,0:T(8,128)(2,1)S(1)}, bf16[256,512]{1,0:T(8,128)(2,1)S(1)}, u32[]{:S(2)}, u32[]{:S(2)}) collective-permute-start(bf16[256,512]{1,0:T(8,128)(2,1)S(1)} %shard_map.58.refs_1_), channel_id=1, source_target_pairs={{0,2},{1,3},{2,0},{3,1},{4,6},{5,7},{6,4},{7,5},{8,10},{9,11},{10,... | collective-permute-start | bytes 786440 | tf_op jit(solution)/shard_map/ppermute | solution.py:41
  22.6 12.8 %collective-permute-start.15 = (bf16[256,512]{1,0:T(8,128)(2,1)S(1)}, bf16[256,512]{1,0:T(8,128)(2,1)S(1)}, u32[]{:S(2)}, u32[]{:S(2)}) collective-permute-start(bf16[256,512]{1,0:T(8,128)(2,1)S(1)} %shard_map.57.refs_0_), channel_id=1, source_target_pairs={{0,4},{1,5},{2,6},{3,7},{4,0},{5,1},{6,2},{7,3},{8,12},{9,13},{10,... | collective-permute-start | bytes 786440 | tf_op jit(solution)/shard_map/ppermute | solution.py:41
  29.7 5.6 %collective-permute-start.12 = (bf16[256,512]{1,0:T(8,128)(2,1)S(1)}, bf16[256,512]{1,0:T(8,128)(2,1)S(1)}, u32[]{:S(2)}, u32[]{:S(2)}) collective-permute-start(bf16[256,512]{1,0:T(8,128)(2,1)S(1)} %collective-permute-done.10.refs_3_), channel_id=1, source_target_pairs={{0,1},{1,0},{2,3},{3,2},{4,5},{5,4},{6,7},{7,6},{8,9},{9,8},{10,11... | collective-permute-start | bytes 786440 | tf_op jit(solution)/shard_map/ppermute | solution.py:41
  29.7 6.1 %collective-permute-start.11 = (bf16[256,512]{1,0:T(8,128)(2,1)S(1)}, bf16[256,512]{1,0:T(8,128)(2,1)S(1)}, u32[]{:S(2)}, u32[]{:S(2)}) collective-permute-start(bf16[256,512]{1,0:T(8,128)(2,1)S(1)} %collective-permute-done.6.refs_1_), channel_id=1, source_target_pairs={{0,1},{1,0},{2,3},{3,2},{4,5},{5,4},{6,7},{7,6},{8,9},{9,8},{10,11... | collective-permute-start | bytes 786440 | tf_op jit(solution)/shard_map/ppermute | solution.py:41
  30.2 9.5 %collective-permute-start.9 = (bf16[256,512]{1,0:T(8,128)(2,1)S(1)}, bf16[256,512]{1,0:T(8,128)(2,1)S(1)}, u32[]{:S(2)}, u32[]{:S(2)}) collective-permute-start(bf16[256,512]{1,0:T(8,128)(2,1)S(1)} %collective-permute-done.6.refs_1_), channel_id=1, source_target_pairs={{0,4},{1,5},{2,6},{3,7},{4,0},{5,1},{6,2},{7,3},{8,12},{9,13},{10,... | collective-permute-start | bytes 786440 | tf_op jit(solution)/shard_map/ppermute | solution.py:41
  32.7 7.4 %collective-permute-start.18 = (bf16[256,512]{1,0:T(8,128)(2,1)S(1)}, bf16[256,512]{1,0:T(8,128)(2,1)S(1)}, u32[]{:S(2)}, u32[]{:S(2)}) collective-permute-start(bf16[256,512]{1,0:T(8,128)(2,1)S(1)} %collective-permute-done.10.refs_3_), channel_id=1, source_target_pairs={{0,2},{1,3},{2,0},{3,1},{4,6},{5,7},{6,4},{7,5},{8,10},{9,11},{10,... | collective-permute-start | bytes 786440 | tf_op jit(solution)/shard_map/ppermute | solution.py:41
  35.3 1.8 %collective-permute-start.14 = (bf16[256,512]{1,0:T(8,128)(2,1)S(1)}, bf16[256,512]{1,0:T(8,128)(2,1)S(1)}, u32[]{:S(2)}, u32[]{:S(2)}) collective-permute-start(bf16[256,512]{1,0:T(8,128)(2,1)S(1)} %collective-permute-done.13.refs_1_), channel_id=1, source_target_pairs={{0,1},{1,0},{2,3},{3,2},{4,5},{5,4},{6,7},{7,6},{8,9},{9,8},{10,11... | collective-permute-start | bytes 786440 | tf_op jit(solution)/shard_map/ppermute | solution.py:41
  35.4 1.9 %collective-permute-start.16 = (bf16[256,512]{1,0:T(8,128)(2,1)S(1)}, bf16[256,512]{1,0:T(8,128)(2,1)S(1)}, u32[]{:S(2)}, u32[]{:S(2)}) collective-permute-start(bf16[256,512]{1,0:T(8,128)(2,1)S(1)} %collective-permute-done.15.refs_3_), channel_id=1, source_target_pairs={{0,1},{1,0},{2,3},{3,2},{4,5},{5,4},{6,7},{7,6},{8,9},{9,8},{10,11... | collective-permute-start | bytes 786440 | tf_op jit(solution)/shard_map/ppermute | solution.py:41
  39.8 1.5 %collective-permute-start.17 = (bf16[256,512]{1,0:T(8,128)(2,1)S(1)}, bf16[256,512]{1,0:T(8,128)(2,1)S(1)}, u32[]{:S(2)}, u32[]{:S(2)}) collective-permute-start(bf16[256,512]{1,0:T(8,128)(2,1)S(1)} %collective-permute-done.9.refs_1_), channel_id=1, source_target_pairs={{0,1},{1,0},{2,3},{3,2},{4,5},{5,4},{6,7},{7,6},{8,9},{9,8},{10,11... | collective-permute-start | bytes 786440 | tf_op jit(solution)/shard_map/ppermute | solution.py:41
  40.2 1.8 %collective-permute-start.19 = (bf16[256,512]{1,0:T(8,128)(2,1)S(1)}, bf16[256,512]{1,0:T(8,128)(2,1)S(1)}, u32[]{:S(2)}, u32[]{:S(2)}) collective-permute-start(bf16[256,512]{1,0:T(8,128)(2,1)S(1)} %collective-permute-done.18.refs_1_), channel_id=1, source_target_pairs={{0,1},{1,0},{2,3},{3,2},{4,5},{5,4},{6,7},{7,6},{8,9},{9,8},{10,11... | collective-permute-start | bytes 786440 | tf_op jit(solution)/shard_map/ppermute | solution.py:41

commit v5 on v4

--- a/solution.py
+++ b/solution.py
@@ -27,6 +27,10 @@
     return pltpu.VMEM(shape, dtype)
 
 
+def in_hbm(value):
+    return pltpu.with_memory_space_constraint(value, pltpu.HBM)
+
+
 def cost(flops, moved):
     return pl.CostEstimate(flops=flops, bytes_accessed=moved, transcendentals=0)
 
@@ -45,28 +49,49 @@
     return lax.broadcasted_iota(jnp.int32, shape, 1) == 0
 
 
-def prepare_kernel(steps, count, keys_ref, values_ref, q_ref, pattern_ref, *refs):
-    own_keys_ref, own_values_ref, stacked_ref, mask_ref, table_ref, sems, stack_sems = refs
-    tok_dev, width = q_ref.shape
+def slice_kernel(width, keys_ref, values_ref, own_keys_ref, own_values_ref, sems):
     heads = width // HEAD_SIZE
-    blocks_dev = tok_dev // BLOCK
     head = lax.div(lax.axis_index("head") * heads, QUERY_HEADS // KEY_VALUE_HEADS)
     columns = pl.ds(pl.multiple_of(head * HEAD_SIZE, HEAD_SIZE), HEAD_SIZE)
-    table = pltpu.make_async_copy(pattern_ref, table_ref, sems.at[2])
     copies = [
         pltpu.make_async_copy(keys_ref.at[:, columns], own_keys_ref, sems.at[0]),
         pltpu.make_async_copy(values_ref.at[:, columns], own_values_ref, sems.at[1]),
     ]
+    for copy in copies:
+        copy.start()
+    for copy in copies:
+        copy.wait()
+
+
+def own_slices(key_vectors, value_vectors, width):
+    own = held((key_vectors.shape[0], HEAD_SIZE))
+    return pl.pallas_call(
+        functools.partial(slice_kernel, width),
+        out_shape=[own, own],
+        in_specs=[HBM] * 2,
+        out_specs=[VMEM] * 2,
+        scratch_shapes=[pltpu.SemaphoreType.DMA((2,))],
+        compiler_params=params(8),
+        cost_estimate=cost(0, 1 << 18),
+    )(in_hbm(key_vectors), in_hbm(value_vectors))
+
+
+def stack_kernel(steps, count, q_ref, pattern_ref, *refs):
+    stacked_ref, mask_ref, table_ref, table_sem, sems = refs
+    blocks_dev, rows, _ = stacked_ref.shape
+    heads = rows // BLOCK
+    table = pltpu.make_async_copy(pattern_ref, table_ref, table_sem)
+    table.start()
+    copies = []
     for a in range(blocks_dev):
         for h in range(heads):
             copies.append(
                 pltpu.make_async_copy(
                     q_ref.at[pl.ds(a * BLOCK, BLOCK), pl.ds(h * HEAD_SIZE, HEAD_SIZE)],
                     stacked_ref.at[a, pl.ds(h * BLOCK, BLOCK)],
-                    stack_sems.at[a, h],
+                    sems.at[a, h],
                 )
             )
-    table.start()
     for copy in copies:
         copy.start()
     table.wait()
@@ -88,33 +113,25 @@
         copy.wait()
 
 
-def prepared(key_vectors, value_vectors, queries, block_pattern, steps, count):
+def stacked_of(queries, block_pattern, steps, count):
     tok_dev, width = queries.shape
     blocks_dev, heads = tok_dev // BLOCK, width // HEAD_SIZE
-    own = held((tok_dev, HEAD_SIZE))
-    return pl.pallas_call(
-        functools.partial(prepare_kernel, steps, count),
+    return pl.pallas_call(
+        functools.partial(stack_kernel, steps, count),
         out_shape=[
-            own,
-            own,
             held((blocks_dev, heads * BLOCK, HEAD_SIZE)),
             held((blocks_dev, len(steps) * tok_dev, BLOCK)),
         ],
-        in_specs=[HBM] * 4,
-        out_specs=[VMEM] * 4,
+        in_specs=[HBM] * 2,
+        out_specs=[VMEM] * 2,
         scratch_shapes=[
             pltpu.SMEM(block_pattern.shape, jnp.int32),
-            pltpu.SemaphoreType.DMA((3,)),
+            pltpu.SemaphoreType.DMA(()),
             pltpu.SemaphoreType.DMA((blocks_dev, heads)),
         ],
         compiler_params=params(8),
         cost_estimate=cost(0, 1 << 20),
-    )(
-        *[
-            pltpu.with_memory_space_constraint(operand, pltpu.HBM)
-            for operand in (key_vectors, value_vectors, queries, block_pattern)
-        ]
-    )
+    )(in_hbm(queries), in_hbm(block_pattern))
 
 
 def weights_kernel(q_ref, mask_ref, *refs):
@@ -179,33 +196,57 @@
     )(weights, *value_parts)
 
 
-def projection_kernel(places, fresh, weight_ref, *refs):
-    *parts, out_ref = refs
-    total = None if fresh else parts.pop(0)[...]
+def projection_kernel(places, width, fresh, last, weight_ref, *refs):
+    refs = list(refs)
+    total_ref = None if fresh else refs.pop(0)
+    parts = refs[: len(places)]
+    out_ref = refs[len(places)]
+    columns = weight_ref.shape[1]
+    tile = columns // 4 if last else columns
     me = lax.axis_index("head")
-    for (bits, half), part in zip(places, parts):
-        depth = part.shape[1]
-        row = pl.multiple_of((me ^ bits) * (2 * depth) + half * depth, depth)
-        term = jnp.dot(
-            part[...], weight_ref[pl.ds(row, depth), :], preferred_element_type=jnp.float32
-        )
-        total = term if total is None else total + term
-    out_ref[...] = total.astype(out_ref.dtype)
-
-
-def projected(total, weight, places, parts, last=False):
-    rows, depth = parts[0].shape
+    copies = []
+    for n in range(0, columns, tile):
+        total = None if fresh else total_ref[:, n : n + tile]
+        for (bits, offset), part in zip(places, parts):
+            depth = part.shape[1]
+            row = pl.multiple_of((me ^ bits) * width + offset, depth)
+            term = jnp.dot(
+                part[...],
+                weight_ref[pl.ds(row, depth), n : n + tile],
+                preferred_element_type=jnp.float32,
+            )
+            total = term if total is None else total + term
+        if last:
+            held_ref, sems = refs[len(places) + 1 :]
+            held_ref[:, n : n + tile] = total.astype(held_ref.dtype)
+            copy = pltpu.make_async_copy(
+                held_ref.at[:, pl.ds(n, tile)], out_ref.at[:, pl.ds(n, tile)], sems.at[n // tile]
+            )
+            copy.start()
+            copies.append(copy)
+        else:
+            out_ref[...] = total
+    for copy in copies:
+        copy.wait()
+
+
+def projected(total, weight, width, places, parts, last=False):
+    rows = parts[0].shape[0]
     columns = weight.shape[1]
     fresh = total is None
     operands = ([] if fresh else [total]) + parts
     shape = (rows, columns)
-    return pl.pallas_call(
-        functools.partial(projection_kernel, places, fresh),
+    depth = sum(part.shape[1] for part in parts)
+    return pl.pallas_call(
+        functools.partial(projection_kernel, places, width, fresh, last),
         out_shape=jax.ShapeDtypeStruct(shape, jnp.bfloat16) if last else held(shape, jnp.float32),
         in_specs=[VMEM] * (1 + len(operands)),
-        out_specs=VMEM,
+        out_specs=HBM if last else VMEM,
+        scratch_shapes=[pltpu.VMEM(shape, jnp.bfloat16), pltpu.SemaphoreType.DMA((4,))]
+        if last
+        else [],
         compiler_params=params(8),
-        cost_estimate=cost(8 * rows * depth * columns * len(parts), 1 << 20),
+        cost_estimate=cost(8 * rows * depth * columns, 1 << 20),
     )(weight, *operands)
 
 
@@ -220,16 +261,13 @@
     heads_dev = queries.shape[1] // HEAD_SIZE
     count = lax.axis_size("ctx")
     steps = (0, 2, 1, 3) if count == 4 else tuple(range(count))
-    keys, values, stacked, mask = prepared(
-        key_vectors,
-        value_head_vectors,
-        queries,
-        block_pattern,
-        steps,
-        count if count == 4 else None,
-    )
+    barrier = lax.optimization_barrier
+    keys, values = own_slices(key_vectors, value_head_vectors, queries.shape[1])
     key_parts = gathered_over_ctx(keys, steps)
     value_parts = gathered_over_ctx(values, steps)
+    if count == 4:
+        key_parts[2], queries = barrier((key_parts[2], queries))
+    stacked, mask = stacked_of(queries, block_pattern, steps, count if count == 4 else None)
     weights = weights_of(stacked, mask, key_parts)
     if lax.axis_size("head") != 8:
         att = attended_of(weights, value_parts, 0, heads_dev)
@@ -252,21 +290,27 @@
     a, b = barrier((a, b))
     sa = swapped(a, "head", 1)
     sb = swapped(b, "head", 1)
-    mixed = projected(None, weight, ((0, 0), (0, 1), (1, 0), (1, 1)), [a, b, sa, sb])
+    width, half = heads_dev * HEAD_SIZE, heads_dev * HEAD_SIZE // 2
+    mixed = projected(
+        None, weight, width, ((0, 0), (0, half), (1, 0), (1, half)), [a, b, sa, sb]
+    )
     xa, mixed = barrier((xa, mixed))
     da = swapped(xa, "head", 4)
     yb, mixed = barrier((yb, mixed))
     db = swapped(yb, "head", 2)
     xas, ybs = swapped(xa, "head", 1), swapped(yb, "head", 1)
-    mixed = projected(mixed, weight, ((2, 0), (3, 0), (4, 1), (5, 1)), [xa, xas, yb, ybs])
-
+    mixed = projected(
+        mixed, weight, width, ((2, 0), (3, 0), (4, half), (5, half)), [xa, xas, yb, ybs]
+    )
     xbs, yas = swapped(xb, "head", 1), swapped(ya, "head", 1)
-    mixed = projected(mixed, weight, ((2, 1), (3, 1), (4, 0), (5, 0)), [xb, xbs, ya, yas])
+    mixed = projected(
+        mixed, weight, width, ((2, half), (3, half), (4, 0), (5, 0)), [xb, xbs, ya, yas]
+    )
     da, mixed = barrier((da, mixed))
     das = swapped(da, "head", 1)
-    mixed = projected(mixed, weight, ((6, 0), (7, 0)), [da, das])
+    mixed = projected(mixed, weight, width, ((6, 0), (7, 0)), [da, das])
     dbs = swapped(db, "head", 1)
-    return projected(mixed, weight, ((6, 1), (7, 1)), [db, dbs], True)
+    return projected(mixed, weight, width, ((6, half), (7, half)), [db, dbs], True)
 
 
 def solution(mesh):

time: 43.7 us -> 43.8 us (level)
  Pallas kernels: 10.7 us -> 11.4 us
  starting transfers between devices: 20.7 us -> 20.1 us
    ppermute x6, starting transfers between devices: 11.8 us -> 11 us  [shifted(): lax.ppermute(value, axis, [(source, (source + steps) % count) for source...]
    pallas_call x6 -> x7, Pallas kernels: 7.42 us -> 8.1 us  [the longest x5 5.91 us: projected(): pl.pallas_call(functools.partial(projection_kernel, places, width, fresh,...]
  transfers between devices with their start and end apart: 20 -> 20, of which waited for: 10 -> 9; matrix products, arithmetic and copies ran while one was open for 0% -> 0% of each run, Pallas kernels for 14% -> 17%
where the time goes in v5:
time: 43.8 us; the launch traced here: 43.6 us
  starting transfers between devices  20.1 us (46%)
  waiting for transfers between devices  12 us (27%)
  Pallas kernels  11.4 us (26%)
    ppermute x6, starting transfers between devices, shifted(): lax.ppermute(value, axis, [(source, (source + steps) % count) for source...  11 us
    ppermute x14, waiting for transfers between devices, swapped(): lax.ppermute(value, axis, [(source, source ^ bits) for source in range(co...  10.3 us
    ppermute x14, starting transfers between devices, swapped(): lax.ppermute(value, axis, [(source, source ^ bits) for source in range(co...  9.02 us
    pallas_call x5, Pallas kernels, projected(): pl.pallas_call(functools.partial(projection_kernel, places, width, fresh,...  5.91 us
    pallas_call x1, Pallas kernels, weights_of(): pl.pallas_call(weights_kernel, out_shape=held((blocks_dev, rows, keys)),...  1.84 us
    ppermute x6, waiting for transfers between devices, shifted(): lax.ppermute(value, axis, [(source, (source + steps) % count) for source...  1.72 us
    pallas_call x2, Pallas kernels, attended_of(): pl.pallas_call(functools.partial(values_kernel, first, group), out_shape=...  1.43 us
    pallas_call x1, Pallas kernels, stacked_of(): pl.pallas_call(functools.partial(stack_kernel, steps, count), out_shape=[...  1.15 us
  transfers between devices with their start and end apart: 20, of which 9 were waited for; matrix products, arithmetic and copies ran while one was open for 0% of the time, Pallas kernels for 17%

profile of v5, /device:TPU:0, one launch (start us, length us, event | category | flops | bytes accessed | tf_op | source)
XLA Modules:
  0.0 43.6 jit_solution(17084278296570392587)
XLA Ops:
  0.0 0.0 copy-start
  0.0 1.0 %shard_map.55 = (bf16[256,128]{1,0:T(8,128)(2,1)S(1)}, bf16[256,128]{1,0:T(8,128)(2,1)S(1)}) custom-call(bf16[256,1024]{1,0:T(8,128)(2,1)} %keys_ref.1, bf16[256,1024]{1,0:T(8,128)(2,1)} %values_ref.1), custom_call_target="tpu_custom_call" | custom-call | bytes 262144 | tf_op jit(solution)/shard_map/pallas_call | solution.py:68
  1.0 3.1 %collective-permute-start = (bf16[256,128]{1,0:T(8,128)(2,1)S(1)}, bf16[256,128]{1,0:T(8,128)(2,1)S(1)}, u32[]{:S(2)}, u32[]{:S(2)}) collective-permute-start(bf16[256,128]{1,0:T(8,128)(2,1)S(1)} %get-tuple-element.19.refs_0_), channel_id=1, source_target_pairs={{0,8},{8,16},{16,24},{24,0},{1,9},{9,17},{17,25},{25,1},{2,10},{10... | collective-permute-start | bytes 196616 | tf_op jit(solution)/shard_map/ppermute | solution.py:40
  4.1 2.6 %collective-permute-start.1 = (bf16[256,128]{1,0:T(8,128)(2,1)S(1)}, bf16[256,128]{1,0:T(8,128)(2,1)S(1)}, u32[]{:S(2)}, u32[]{:S(2)}) collective-permute-start(bf16[256,128]{1,0:T(8,128)(2,1)S(1)} %get-tuple-element.19.refs_0_), channel_id=1, source_target_pairs={{0,16},{8,24},{16,0},{24,8},{1,17},{9,25},{17,1},{25,9},{2,18},{10... | collective-permute-start | bytes 196616 | tf_op jit(solution)/shard_map/ppermute | solution.py:40
  6.7 1.3 %collective-permute-start.2 = (bf16[256,128]{1,0:T(8,128)(2,1)S(1)}, bf16[256,128]{1,0:T(8,128)(2,1)S(1)}, u32[]{:S(2)}, u32[]{:S(2)}) collective-permute-start(bf16[256,128]{1,0:T(8,128)(2,1)S(1)} %get-tuple-element.19.refs_0_), channel_id=1, source_target_pairs={{0,24},{8,0},{16,8},{24,16},{1,25},{9,1},{17,9},{25,17},{2,26},{10... | collective-permute-start | bytes 196616 | tf_op jit(solution)/shard_map/ppermute | solution.py:40
  8.1 0.2 collective-permute-start.3
  8.3 0.8 %collective-permute-start.4 = (bf16[256,128]{1,0:T(8,128)(2,1)S(1)}, bf16[256,128]{1,0:T(8,128)(2,1)S(1)}, u32[]{:S(2)}, u32[]{:S(2)}) collective-permute-start(bf16[256,128]{1,0:T(8,128)(2,1)S(1)} %get-tuple-element.24.refs_0_), channel_id=1, source_target_pairs={{0,8},{8,16},{16,24},{24,0},{1,9},{9,17},{17,25},{25,1},{2,10},{10... | collective-permute-start | bytes 196616 | tf_op jit(solution)/shard_map/ppermute | solution.py:40
  9.1 0.0 collective-permute-done.refs_2_
  9.1 3.0 %collective-permute-start.5 = (bf16[256,128]{1,0:T(8,128)(2,1)S(1)}, bf16[256,128]{1,0:T(8,128)(2,1)S(1)}, u32[]{:S(2)}, u32[]{:S(2)}) collective-permute-start(bf16[256,128]{1,0:T(8,128)(2,1)S(1)} %get-tuple-element.24.refs_0_), channel_id=1, source_target_pairs={{0,24},{8,0},{16,8},{24,16},{1,25},{9,1},{17,9},{25,17},{2,26},{10... | collective-permute-start | bytes 196616 | tf_op jit(solution)/shard_map/ppermute | solution.py:40
  12.1 1.2 %shard_map.56 = (bf16[2,1024,128]{2,1,0:T(8,128)(2,1)S(1)}, bf16[2,1024,128]{2,1,0:T(8,128)(2,1)S(1)}) custom-call(bf16[256,1024]{1,0:T(8,128)(2,1)} %q_ref, s32[8,8]{1,0:T(8,128)} %pattern_ref.1), custom_call_target="tpu_custom_call" | custom-call | bytes 1048576 | tf_op jit(solution)/shard_map/pallas_call | solution.py:119
  13.2 0.0 collective-permute-done.1.refs_1_
  13.3 0.0 collective-permute-done.2.refs_3_
  13.3 1.8 %shard_map.57.weights_ref = bf16[2,1024,1024]{2,1,0:T(8,128)(2,1)S(1)} custom-call(bf16[2,1024,128]{2,1,0:T(8,128)(2,1)S(1)} %get-tuple-element.21.q_ref, bf16[2,1024,128]{2,1,0:T(8,128)(2,1)S(1)} %get-tuple-element.22.mask_ref, bf16[256,128]{1,0:T(8,128)(2,1)S(1)} %get-tuple-element.19.refs_0_, bf16[256,128]{1,0:T(8,128)(2,1)S(1)} %collective-permute-done.1.refs_1_, ...), custom_call_target="tpu_custom_call" | custom-call | flops 2147483648 | bytes 4194304 | tf_op jit(solution)/shard_map/pallas_call | solution.py:160
  15.1 1.7 %collective-permute-done.3.refs_1_ = bf16[256,128]{1,0:T(8,128)(2,1)S(1)} collective-permute-done((bf16[256,128]{1,0:T(8,128)(2,1)S(1)}, bf16[256,128]{1,0:T(8,128)(2,1)S(1)}, u32[]{:S(2)}, u32[]{:S(2)}) %collective-permute-start.3) | collective-permute-done | bytes 65568 | tf_op jit(solution)/shard_map/ppermute | solution.py:40
  16.8 0.0 collective-permute-done.4.refs_2_
  16.8 0.0 collective-permute-done.5.refs_3_
  16.8 0.7 %shard_map.59.refs_1_ = bf16[256,512]{1,0:T(8,128)(2,1)S(1)} custom-call(bf16[2,1024,1024]{2,1,0:T(8,128)(2,1)S(1)} %shard_map.57.weights_ref, bf16[256,128]{1,0:T(8,128)(2,1)S(1)} %get-tuple-element.24.refs_0_, bf16[256,128]{1,0:T(8,128)(2,1)S(1)} %collective-permute-done.3.refs_1_, bf16[256,128]{1,0:T(8,128)(2,1)S(1)} %collective-permute-done.4.refs_2_, ...), custom_call_target="tpu_custom_call" | custom-call | flops 536870912 | bytes 1048576 | tf_op jit(solution)/shard_map/pallas_call | solution.py:189
  17.6 0.7 %shard_map.58.refs_0_ = bf16[256,512]{1,0:T(8,128)(2,1)S(1)} custom-call(bf16[2,1024,1024]{2,1,0:T(8,128)(2,1)S(1)} %shard_map.57.weights_ref, bf16[256,128]{1,0:T(8,128)(2,1)S(1)} %get-tuple-element.24.refs_0_, bf16[256,128]{1,0:T(8,128)(2,1)S(1)} %collective-permute-done.3.refs_1_, bf16[256,128]{1,0:T(8,128)(2,1)S(1)} %collective-permute-done.4.refs_2_, ...), custom_call_target="tpu_custom_call" | custom-call | flops 536870912 | bytes 1048576 | tf_op jit(solution)/shard_map/pallas_call | solution.py:189
  18.3 0.1 collective-permute-start.7
  18.4 0.5 %collective-permute-start.8 = (bf16[256,512]{1,0:T(8,128)(2,1)S(1)}, bf16[256,512]{1,0:T(8,128)(2,1)S(1)}, u32[]{:S(2)}, u32[]{:S(2)}) collective-permute-start(bf16[256,512]{1,0:T(8,128)(2,1)S(1)} %shard_map.59.refs_1_), channel_id=1, source_target_pairs={{0,1},{1,0},{2,3},{3,2},{4,5},{5,4},{6,7},{7,6},{8,9},{9,8},{10,11... | collective-permute-start | bytes 786440 | tf_op jit(solution)/shard_map/ppermute | solution.py:45
  18.9 1.8 %collective-permute-start.6 = (bf16[256,512]{1,0:T(8,128)(2,1)S(1)}, bf16[256,512]{1,0:T(8,128)(2,1)S(1)}, u32[]{:S(2)}, u32[]{:S(2)}) collective-permute-start(bf16[256,512]{1,0:T(8,128)(2,1)S(1)} %shard_map.58.refs_0_), channel_id=1, source_target_pairs={{0,2},{1,3},{2,0},{3,1},{4,6},{5,7},{6,4},{7,5},{8,10},{9,11},{10,... | collective-permute-start | bytes 786440 | tf_op jit(solution)/shard_map/ppermute | solution.py:45
  20.6 1.5 %collective-permute-start.10 = (bf16[256,512]{1,0:T(8,128)(2,1)S(1)}, bf16[256,512]{1,0:T(8,128)(2,1)S(1)}, u32[]{:S(2)}, u32[]{:S(2)}) collective-permute-start(bf16[256,512]{1,0:T(8,128)(2,1)S(1)} %shard_map.59.refs_1_), channel_id=1, source_target_pairs={{0,4},{1,5},{2,6},{3,7},{4,0},{5,1},{6,2},{7,3},{8,12},{9,13},{10,... | collective-permute-start | bytes 786440 | tf_op jit(solution)/shard_map/ppermute | solution.py:45
  22.1 0.5 %collective-permute-start.13 = (bf16[256,512]{1,0:T(8,128)(2,1)S(1)}, bf16[256,512]{1,0:T(8,128)(2,1)S(1)}, u32[]{:S(2)}, u32[]{:S(2)}) collective-permute-start(bf16[256,512]{1,0:T(8,128)(2,1)S(1)} %shard_map.59.refs_1_), channel_id=1, source_target_pairs={{0,2},{1,3},{2,0},{3,1},{4,6},{5,7},{6,4},{7,5},{8,10},{9,11},{10,... | collective-permute-start | bytes 786440 | tf_op jit(solution)/shard_map/ppermute | solution.py:45
  22.7 0.0 collective-permute-done.7.refs_2_
  22.7 0.2 collective-permute-start.15
  22.9 0.0 collective-permute-done.8.refs_3_
  22.9 0.0 copy-done
  22.9 1.2 %shard_map.60.refs_0_ = f32[256,1024]{1,0:T(8,128)S(1)} custom-call(bf16[8192,1024]{1,0:T(8,128)(2,1)S(1)} %copy-done, bf16[256,512]{1,0:T(8,128)(2,1)S(1)} %shard_map.58.refs_0_, bf16[256,512]{1,0:T(8,128)(2,1)S(1)} %shard_map.59.refs_1_, bf16[256,512]{1,0:T(8,128)(2,1)S(1)} %collective-permute-done.7.refs_2_, ...), custom_call_target="tpu_custom_call" | custom-call | flops 4294967296 | bytes 1048576 | tf_op jit(solution)/shard_map/pallas_call | solution.py:240
  24.2 3.8 %collective-permute-done.6.refs_1_ = bf16[256,512]{1,0:T(8,128)(2,1)S(1)} collective-permute-done((bf16[256,512]{1,0:T(8,128)(2,1)S(1)}, bf16[256,512]{1,0:T(8,128)(2,1)S(1)}, u32[]{:S(2)}, u32[]{:S(2)}) %collective-permute-start.6) | collective-permute-done | bytes 262176 | tf_op jit(solution)/shard_map/ppermute | solution.py:45
  28.0 1.8 %collective-permute-done.10.refs_3_ = bf16[256,512]{1,0:T(8,128)(2,1)S(1)} collective-permute-done((bf16[256,512]{1,0:T(8,128)(2,1)S(1)}, bf16[256,512]{1,0:T(8,128)(2,1)S(1)}, u32[]{:S(2)}, u32[]{:S(2)}) %collective-permute-start.10) | collective-permute-done | bytes 262176 | tf_op jit(solution)/shard_map/ppermute | solution.py:45
  29.8 0.0 collective-permute-start.12
  29.8 0.5 %collective-permute-start.11 = (bf16[256,512]{1,0:T(8,128)(2,1)S(1)}, bf16[256,512]{1,0:T(8,128)(2,1)S(1)}, u32[]{:S(2)}, u32[]{:S(2)}) collective-permute-start(bf16[256,512]{1,0:T(8,128)(2,1)S(1)} %collective-permute-done.6.refs_1_), channel_id=1, source_target_pairs={{0,1},{1,0},{2,3},{3,2},{4,5},{5,4},{6,7},{7,6},{8,9},{9,8},{10,11... | collective-permute-start | bytes 786440 | tf_op jit(solution)/shard_map/ppermute | solution.py:45
  30.3 1.5 %collective-permute-start.9 = (bf16[256,512]{1,0:T(8,128)(2,1)S(1)}, bf16[256,512]{1,0:T(8,128)(2,1)S(1)}, u32[]{:S(2)}, u32[]{:S(2)}) collective-permute-start(bf16[256,512]{1,0:T(8,128)(2,1)S(1)} %collective-permute-done.6.refs_1_), channel_id=1, source_target_pairs={{0,4},{1,5},{2,6},{3,7},{4,0},{5,1},{6,2},{7,3},{8,12},{9,13},{10,... | collective-permute-start | bytes 786440 | tf_op jit(solution)/shard_map/ppermute | solution.py:45
  31.8 0.9 %collective-permute-done.13.refs_1_ = bf16[256,512]{1,0:T(8,128)(2,1)S(1)} collective-permute-done((bf16[256,512]{1,0:T(8,128)(2,1)S(1)}, bf16[256,512]{1,0:T(8,128)(2,1)S(1)}, u32[]{:S(2)}, u32[]{:S(2)}) %collective-permute-start.13) | collective-permute-done | bytes 262176 | tf_op jit(solution)/shard_map/ppermute | solution.py:45
  32.8 1.7 %collective-permute-start.18 = (bf16[256,512]{1,0:T(8,128)(2,1)S(1)}, bf16[256,512]{1,0:T(8,128)(2,1)S(1)}, u32[]{:S(2)}, u32[]{:S(2)}) collective-permute-start(bf16[256,512]{1,0:T(8,128)(2,1)S(1)} %collective-permute-done.10.refs_3_), channel_id=1, source_target_pairs={{0,2},{1,3},{2,0},{3,1},{4,6},{5,7},{6,4},{7,5},{8,10},{9,11},{10,... | collective-permute-start | bytes 786440 | tf_op jit(solution)/shard_map/ppermute | solution.py:45
  34.5 0.9 %collective-permute-done.15.refs_3_ = bf16[256,512]{1,0:T(8,128)(2,1)S(1)} collective-permute-done((bf16[256,512]{1,0:T(8,128)(2,1)S(1)}, bf16[256,512]{1,0:T(8,128)(2,1)S(1)}, u32[]{:S(2)}, u32[]{:S(2)}) %collective-permute-start.15) | collective-permute-done | bytes 262176 | tf_op jit(solution)/shard_map/ppermute | solution.py:45
  35.4 0.0 collective-permute-start.14
  35.4 0.0 collective-permute-done.12.refs_4_
  35.4 0.5 %collective-permute-start.16 = (bf16[256,512]{1,0:T(8,128)(2,1)S(1)}, bf16[256,512]{1,0:T(8,128)(2,1)S(1)}, u32[]{:S(2)}, u32[]{:S(2)}) collective-permute-start(bf16[256,512]{1,0:T(8,128)(2,1)S(1)} %collective-permute-done.15.refs_3_), channel_id=1, source_target_pairs={{0,1},{1,0},{2,3},{3,2},{4,5},{5,4},{6,7},{7,6},{8,9},{9,8},{10,11... | collective-permute-start | bytes 786440 | tf_op jit(solution)/shard_map/ppermute | solution.py:45
  35.9 0.0 collective-permute-done.11.refs_2_
  36.0 1.2 %shard_map.61.refs_0_ = f32[256,1024]{1,0:T(8,128)S(1)} custom-call(bf16[8192,1024]{1,0:T(8,128)(2,1)S(1)} %copy-done, f32[256,1024]{1,0:T(8,128)S(1)} %shard_map.60.refs_0_, bf16[256,512]{1,0:T(8,128)(2,1)S(1)} %collective-permute-done.6.refs_1_, bf16[256,512]{1,0:T(8,128)(2,1)S(1)} %collective-permute-done.11.refs_2_, ...), custom_call_target="tpu_custom_call" | custom-call | flops 4294967296 | bytes 1048576 | tf_op jit(solution)/shard_map/pallas_call | solution.py:240
  37.2 0.0 collective-permute-done.14.refs_2_
  37.2 0.1 collective-permute-done.16.refs_4_
  37.3 1.2 %shard_map.62.refs_0_ = f32[256,1024]{1,0:T(8,128)S(1)} custom-call(bf16[8192,1024]{1,0:T(8,128)(2,1)S(1)} %copy-done, f32[256,1024]{1,0:T(8,128)S(1)} %shard_map.61.refs_0_, bf16[256,512]{1,0:T(8,128)(2,1)S(1)} %collective-permute-done.13.refs_1_, bf16[256,512]{1,0:T(8,128)(2,1)S(1)} %collective-permute-done.14.refs_2_, ...), custom_call_target="tpu_custom_call" | custom-call | flops 4294967296 | bytes 1048576 | tf_op jit(solution)/shard_map/pallas_call | solution.py:240
  38.6 1.3 %collective-permute-done.9.refs_1_ = bf16[256,512]{1,0:T(8,128)(2,1)S(1)} collective-permute-done((bf16[256,512]{1,0:T(8,128)(2,1)S(1)}, bf16[256,512]{1,0:T(8,128)(2,1)S(1)}, u32[]{:S(2)}, u32[]{:S(2)}) %collective-permute-start.9) | collective-permute-done | bytes 262176 | tf_op jit(solution)/shard_map/ppermute | solution.py:45
  39.9 0.0 collective-permute-start.17
  39.9 0.4 collective-permute-done.18.refs_1_
  40.3 0.1 collective-permute-start.19
  40.4 1.0 %collective-permute-done.17.refs_2_ = bf16[256,512]{1,0:T(8,128)(2,1)S(1)} collective-permute-done((bf16[256,512]{1,0:T(8,128)(2,1)S(1)}, bf16[256,512]{1,0:T(8,128)(2,1)S(1)}, u32[]{:S(2)}, u32[]{:S(2)}) %collective-permute-start.17) | collective-permute-done | bytes 262176 | tf_op jit(solution)/shard_map/ppermute | solution.py:45
  41.4 0.7 %shard_map.63.refs_0_ = f32[256,1024]{1,0:T(8,128)S(1)} custom-call(bf16[8192,1024]{1,0:T(8,128)(2,1)S(1)} %copy-done, f32[256,1024]{1,0:T(8,128)S(1)} %shard_map.62.refs_0_, bf16[256,512]{1,0:T(8,128)(2,1)S(1)} %collective-permute-done.9.refs_1_, bf16[256,512]{1,0:T(8,128)(2,1)S(1)} %collective-permute-done.17.refs_2_), custom_call_target="tpu_custom_call" | custom-call | flops 2147483648 | bytes 1048576 | tf_op jit(solution)/shard_map/pallas_call | solution.py:240
  42.1 0.0 collective-permute-done.19.refs_2_
  42.1 1.5 %shard_map.64 = bf16[256,1024]{1,0:T(8,128)(2,1)} custom-call(bf16[8192,1024]{1,0:T(8,128)(2,1)S(1)} %copy-done, f32[256,1024]{1,0:T(8,128)S(1)} %shard_map.63.refs_0_, bf16[256,512]{1,0:T(8,128)(2,1)S(1)} %collective-permute-done.18.refs_1_, bf16[256,512]{1,0:T(8,128)(2,1)S(1)} %collective-permute-done.19.refs_2_), custom_call_target="tpu_custom_call" | custom-call | flops 2147483648 | bytes 1048576 | tf_op jit(solution)/shard_map/pallas_call | solution.py:240
Async XLA Ops:
  0.0 22.9 %copy-start = (bf16[8192,1024]{1,0:T(8,128)(2,1)S(1)}, bf16[8192,1024]{1,0:T(8,128)(2,1)}, u32[]{:S(2)}) copy-start(bf16[8192,1024]{1,0:T(8,128)(2,1)} %weight_ref.9) | copy-start | bytes 50331652
  1.0 8.0 %collective-permute-start = (bf16[256,128]{1,0:T(8,128)(2,1)S(1)}, bf16[256,128]{1,0:T(8,128)(2,1)S(1)}, u32[]{:S(2)}, u32[]{:S(2)}) collective-permute-start(bf16[256,128]{1,0:T(8,128)(2,1)S(1)} %get-tuple-element.19.refs_0_), channel_id=1, source_target_pairs={{0,8},{8,16},{16,24},{24,0},{1,9},{9,17},{17,25},{25,1},{2,10},{10... | collective-permute-start | bytes 196616 | tf_op jit(solution)/shard_map/ppermute | solution.py:40
  4.1 9.1 %collective-permute-start.1 = (bf16[256,128]{1,0:T(8,128)(2,1)S(1)}, bf16[256,128]{1,0:T(8,128)(2,1)S(1)}, u32[]{:S(2)}, u32[]{:S(2)}) collective-permute-start(bf16[256,128]{1,0:T(8,128)(2,1)S(1)} %get-tuple-element.19.refs_0_), channel_id=1, source_target_pairs={{0,16},{8,24},{16,0},{24,8},{1,17},{9,25},{17,1},{25,9},{2,18},{10... | collective-permute-start | bytes 196616 | tf_op jit(solution)/shard_map/ppermute | solution.py:40
  6.7 6.5 %collective-permute-start.2 = (bf16[256,128]{1,0:T(8,128)(2,1)S(1)}, bf16[256,128]{1,0:T(8,128)(2,1)S(1)}, u32[]{:S(2)}, u32[]{:S(2)}) collective-permute-start(bf16[256,128]{1,0:T(8,128)(2,1)S(1)} %get-tuple-element.19.refs_0_), channel_id=1, source_target_pairs={{0,24},{8,0},{16,8},{24,16},{1,25},{9,1},{17,9},{25,17},{2,26},{10... | collective-permute-start | bytes 196616 | tf_op jit(solution)/shard_map/ppermute | solution.py:40
  8.1 8.8 %collective-permute-start.3 = (bf16[256,128]{1,0:T(8,128)(2,1)S(1)}, bf16[256,128]{1,0:T(8,128)(2,1)S(1)}, u32[]{:S(2)}, u32[]{:S(2)}) collective-permute-start(bf16[256,128]{1,0:T(8,128)(2,1)S(1)} %get-tuple-element.24.refs_0_), channel_id=1, source_target_pairs={{0,16},{8,24},{16,0},{24,8},{1,17},{9,25},{17,1},{25,9},{2,18},{10... | collective-permute-start | bytes 196616 | tf_op jit(solution)/shard_map/ppermute | solution.py:40
  8.3 8.6 %collective-permute-start.4 = (bf16[256,128]{1,0:T(8,128)(2,1)S(1)}, bf16[256,128]{1,0:T(8,128)(2,1)S(1)}, u32[]{:S(2)}, u32[]{:S(2)}) collective-permute-start(bf16[256,128]{1,0:T(8,128)(2,1)S(1)} %get-tuple-element.24.refs_0_), channel_id=1, source_target_pairs={{0,8},{8,16},{16,24},{24,0},{1,9},{9,17},{17,25},{25,1},{2,10},{10... | collective-permute-start | bytes 196616 | tf_op jit(solution)/shard_map/ppermute | solution.py:40
  9.1 7.7 %collective-permute-start.5 = (bf16[256,128]{1,0:T(8,128)(2,1)S(1)}, bf16[256,128]{1,0:T(8,128)(2,1)S(1)}, u32[]{:S(2)}, u32[]{:S(2)}) collective-permute-start(bf16[256,128]{1,0:T(8,128)(2,1)S(1)} %get-tuple-element.24.refs_0_), channel_id=1, source_target_pairs={{0,24},{8,0},{16,8},{24,16},{1,25},{9,1},{17,9},{25,17},{2,26},{10... | collective-permute-start | bytes 196616 | tf_op jit(solution)/shard_map/ppermute | solution.py:40
  18.3 4.4 %collective-permute-start.7 = (bf16[256,512]{1,0:T(8,128)(2,1)S(1)}, bf16[256,512]{1,0:T(8,128)(2,1)S(1)}, u32[]{:S(2)}, u32[]{:S(2)}) collective-permute-start(bf16[256,512]{1,0:T(8,128)(2,1)S(1)} %shard_map.58.refs_0_), channel_id=1, source_target_pairs={{0,1},{1,0},{2,3},{3,2},{4,5},{5,4},{6,7},{7,6},{8,9},{9,8},{10,11... | collective-permute-start | bytes 786440 | tf_op jit(solution)/shard_map/ppermute | solution.py:45
  18.4 4.6 %collective-permute-start.8 = (bf16[256,512]{1,0:T(8,128)(2,1)S(1)}, bf16[256,512]{1,0:T(8,128)(2,1)S(1)}, u32[]{:S(2)}, u32[]{:S(2)}) collective-permute-start(bf16[256,512]{1,0:T(8,128)(2,1)S(1)} %shard_map.59.refs_1_), channel_id=1, source_target_pairs={{0,1},{1,0},{2,3},{3,2},{4,5},{5,4},{6,7},{7,6},{8,9},{9,8},{10,11... | collective-permute-start | bytes 786440 | tf_op jit(solution)/shard_map/ppermute | solution.py:45
  18.9 9.2 %collective-permute-start.6 = (bf16[256,512]{1,0:T(8,128)(2,1)S(1)}, bf16[256,512]{1,0:T(8,128)(2,1)S(1)}, u32[]{:S(2)}, u32[]{:S(2)}) collective-permute-start(bf16[256,512]{1,0:T(8,128)(2,1)S(1)} %shard_map.58.refs_0_), channel_id=1, source_target_pairs={{0,2},{1,3},{2,0},{3,1},{4,6},{5,7},{6,4},{7,5},{8,10},{9,11},{10,... | collective-permute-start | bytes 786440 | tf_op jit(solution)/shard_map/ppermute | solution.py:45
  20.6 9.2 %collective-permute-start.10 = (bf16[256,512]{1,0:T(8,128)(2,1)S(1)}, bf16[256,512]{1,0:T(8,128)(2,1)S(1)}, u32[]{:S(2)}, u32[]{:S(2)}) collective-permute-start(bf16[256,512]{1,0:T(8,128)(2,1)S(1)} %shard_map.59.refs_1_), channel_id=1, source_target_pairs={{0,4},{1,5},{2,6},{3,7},{4,0},{5,1},{6,2},{7,3},{8,12},{9,13},{10,... | collective-permute-start | bytes 786440 | tf_op jit(solution)/shard_map/ppermute | solution.py:45
  22.1 10.6 %collective-permute-start.13 = (bf16[256,512]{1,0:T(8,128)(2,1)S(1)}, bf16[256,512]{1,0:T(8,128)(2,1)S(1)}, u32[]{:S(2)}, u32[]{:S(2)}) collective-permute-start(bf16[256,512]{1,0:T(8,128)(2,1)S(1)} %shard_map.59.refs_1_), channel_id=1, source_target_pairs={{0,2},{1,3},{2,0},{3,1},{4,6},{5,7},{6,4},{7,5},{8,10},{9,11},{10,... | collective-permute-start | bytes 786440 | tf_op jit(solution)/shard_map/ppermute | solution.py:45
  22.7 12.8 %collective-permute-start.15 = (bf16[256,512]{1,0:T(8,128)(2,1)S(1)}, bf16[256,512]{1,0:T(8,128)(2,1)S(1)}, u32[]{:S(2)}, u32[]{:S(2)}) collective-permute-start(bf16[256,512]{1,0:T(8,128)(2,1)S(1)} %shard_map.58.refs_0_), channel_id=1, source_target_pairs={{0,4},{1,5},{2,6},{3,7},{4,0},{5,1},{6,2},{7,3},{8,12},{9,13},{10,... | collective-permute-start | bytes 786440 | tf_op jit(solution)/shard_map/ppermute | solution.py:45
  29.8 5.6 %collective-permute-start.12 = (bf16[256,512]{1,0:T(8,128)(2,1)S(1)}, bf16[256,512]{1,0:T(8,128)(2,1)S(1)}, u32[]{:S(2)}, u32[]{:S(2)}) collective-permute-start(bf16[256,512]{1,0:T(8,128)(2,1)S(1)} %collective-permute-done.10.refs_3_), channel_id=1, source_target_pairs={{0,1},{1,0},{2,3},{3,2},{4,5},{5,4},{6,7},{7,6},{8,9},{9,8},{10,11... | collective-permute-start | bytes 786440 | tf_op jit(solution)/shard_map/ppermute | solution.py:45
  29.8 6.1 %collective-permute-start.11 = (bf16[256,512]{1,0:T(8,128)(2,1)S(1)}, bf16[256,512]{1,0:T(8,128)(2,1)S(1)}, u32[]{:S(2)}, u32[]{:S(2)}) collective-permute-start(bf16[256,512]{1,0:T(8,128)(2,1)S(1)} %collective-permute-done.6.refs_1_), channel_id=1, source_target_pairs={{0,1},{1,0},{2,3},{3,2},{4,5},{5,4},{6,7},{7,6},{8,9},{9,8},{10,11... | collective-permute-start | bytes 786440 | tf_op jit(solution)/shard_map/ppermute | solution.py:45
  30.3 9.5 %collective-permute-start.9 = (bf16[256,512]{1,0:T(8,128)(2,1)S(1)}, bf16[256,512]{1,0:T(8,128)(2,1)S(1)}, u32[]{:S(2)}, u32[]{:S(2)}) collective-permute-start(bf16[256,512]{1,0:T(8,128)(2,1)S(1)} %collective-permute-done.6.refs_1_), channel_id=1, source_target_pairs={{0,4},{1,5},{2,6},{3,7},{4,0},{5,1},{6,2},{7,3},{8,12},{9,13},{10,... | collective-permute-start | bytes 786440 | tf_op jit(solution)/shard_map/ppermute | solution.py:45
  32.8 7.5 %collective-permute-start.18 = (bf16[256,512]{1,0:T(8,128)(2,1)S(1)}, bf16[256,512]{1,0:T(8,128)(2,1)S(1)}, u32[]{:S(2)}, u32[]{:S(2)}) collective-permute-start(bf16[256,512]{1,0:T(8,128)(2,1)S(1)} %collective-permute-done.10.refs_3_), channel_id=1, source_target_pairs={{0,2},{1,3},{2,0},{3,1},{4,6},{5,7},{6,4},{7,5},{8,10},{9,11},{10,... | collective-permute-start | bytes 786440 | tf_op jit(solution)/shard_map/ppermute | solution.py:45
  35.4 1.8 %collective-permute-start.14 = (bf16[256,512]{1,0:T(8,128)(2,1)S(1)}, bf16[256,512]{1,0:T(8,128)(2,1)S(1)}, u32[]{:S(2)}, u32[]{:S(2)}) collective-permute-start(bf16[256,512]{1,0:T(8,128)(2,1)S(1)} %collective-permute-done.13.refs_1_), channel_id=1, source_target_pairs={{0,1},{1,0},{2,3},{3,2},{4,5},{5,4},{6,7},{7,6},{8,9},{9,8},{10,11... | collective-permute-start | bytes 786440 | tf_op jit(solution)/shard_map/ppermute | solution.py:45
  35.4 1.9 %collective-permute-start.16 = (bf16[256,512]{1,0:T(8,128)(2,1)S(1)}, bf16[256,512]{1,0:T(8,128)(2,1)S(1)}, u32[]{:S(2)}, u32[]{:S(2)}) collective-permute-start(bf16[256,512]{1,0:T(8,128)(2,1)S(1)} %collective-permute-done.15.refs_3_), channel_id=1, source_target_pairs={{0,1},{1,0},{2,3},{3,2},{4,5},{5,4},{6,7},{7,6},{8,9},{9,8},{10,11... | collective-permute-start | bytes 786440 | tf_op jit(solution)/shard_map/ppermute | solution.py:45
  39.9 1.5 %collective-permute-start.17 = (bf16[256,512]{1,0:T(8,128)(2,1)S(1)}, bf16[256,512]{1,0:T(8,128)(2,1)S(1)}, u32[]{:S(2)}, u32[]{:S(2)}) collective-permute-start(bf16[256,512]{1,0:T(8,128)(2,1)S(1)} %collective-permute-done.9.refs_1_), channel_id=1, source_target_pairs={{0,1},{1,0},{2,3},{3,2},{4,5},{5,4},{6,7},{7,6},{8,9},{9,8},{10,11... | collective-permute-start | bytes 786440 | tf_op jit(solution)/shard_map/ppermute | solution.py:45
  40.3 1.9 %collective-permute-start.19 = (bf16[256,512]{1,0:T(8,128)(2,1)S(1)}, bf16[256,512]{1,0:T(8,128)(2,1)S(1)}, u32[]{:S(2)}, u32[]{:S(2)}) collective-permute-start(bf16[256,512]{1,0:T(8,128)(2,1)S(1)} %collective-permute-done.18.refs_1_), channel_id=1, source_target_pairs={{0,1},{1,0},{2,3},{3,2},{4,5},{5,4},{6,7},{7,6},{8,9},{9,8},{10,11... | collective-permute-start | bytes 786440 | tf_op jit(solution)/shard_map/ppermute | solution.py:45

commit v6 on v5

--- a/solution.py
+++ b/solution.py
@@ -307,10 +307,9 @@
         mixed, weight, width, ((2, half), (3, half), (4, 0), (5, 0)), [xb, xbs, ya, yas]
     )
     da, mixed = barrier((da, mixed))
-    das = swapped(da, "head", 1)
-    mixed = projected(mixed, weight, width, ((6, 0), (7, 0)), [da, das])
-    dbs = swapped(db, "head", 1)
-    return projected(mixed, weight, width, ((6, half), (7, half)), [db, dbs], True)
+    das, dbs = swapped(da, "head", 1), swapped(db, "head", 1)
+    mixed = projected(mixed, weight, width, ((6, 0), (6, half)), [da, db])
+    return projected(mixed, weight, width, ((7, 0), (7, half)), [das, dbs], True)
 
 
 def solution(mesh):

time: 43.8 us -> 43.4 us (level)
  transfers between devices with their start and end apart: 20 -> 20, of which waited for: 9 -> 10; matrix products, arithmetic and copies ran while one was open for 0% -> 0% of each run, Pallas kernels for 17% -> 17%
where the time goes in v6:
time: 43.4 us; the launch traced here: 43.3 us
  starting transfers between devices  20.1 us (46%)
  waiting for transfers between devices  11.7 us (27%)
  Pallas kernels  11.4 us (26%)
    ppermute x6, starting transfers between devices, shifted(): lax.ppermute(value, axis, [(source, (source + steps) % count) for source...  11 us
    ppermute x14, waiting for transfers between devices, swapped(): lax.ppermute(value, axis, [(source, source ^ bits) for source in range(co...  9.99 us
    ppermute x14, starting transfers between devices, swapped(): lax.ppermute(value, axis, [(source, source ^ bits) for source in range(co...  9.02 us
    pallas_call x5, Pallas kernels, projected(): pl.pallas_call(functools.partial(projection_kernel, places, width, fresh,...  5.9 us
    pallas_call x1, Pallas kernels, weights_of(): pl.pallas_call(weights_kernel, out_shape=held((blocks_dev, rows, keys)),...  1.84 us
    ppermute x6, waiting for transfers between devices, shifted(): lax.ppermute(value, axis, [(source, (source + steps) % count) for source...  1.72 us
    pallas_call x2, Pallas kernels, attended_of(): pl.pallas_call(functools.partial(values_kernel, first, group), out_shape=...  1.43 us
    pallas_call x1, Pallas kernels, stacked_of(): pl.pallas_call(functools.partial(stack_kernel, steps, count), out_shape=[...  1.15 us
  transfers between devices with their start and end apart: 20, of which 10 were waited for; matrix products, arithmetic and copies ran while one was open for 0% of the time, Pallas kernels for 17%

profile of v6, /device:TPU:0, one launch (start us, length us, event | category | flops | bytes accessed | tf_op | source)
XLA Modules:
  0.0 43.3 jit_solution(5770503086784762000)
XLA Ops:
  0.0 0.0 copy-start
  0.0 1.0 %shard_map.55 = (bf16[256,128]{1,0:T(8,128)(2,1)S(1)}, bf16[256,128]{1,0:T(8,128)(2,1)S(1)}) custom-call(bf16[256,1024]{1,0:T(8,128)(2,1)} %keys_ref.1, bf16[256,1024]{1,0:T(8,128)(2,1)} %values_ref.1), custom_call_target="tpu_custom_call" | custom-call | bytes 262144 | tf_op jit(solution)/shard_map/pallas_call | solution.py:68
  1.0 3.1 %collective-permute-start = (bf16[256,128]{1,0:T(8,128)(2,1)S(1)}, bf16[256,128]{1,0:T(8,128)(2,1)S(1)}, u32[]{:S(2)}, u32[]{:S(2)}) collective-permute-start(bf16[256,128]{1,0:T(8,128)(2,1)S(1)} %get-tuple-element.19.refs_0_), channel_id=1, source_target_pairs={{0,8},{8,16},{16,24},{24,0},{1,9},{9,17},{17,25},{25,1},{2,10},{10... | collective-permute-start | bytes 196616 | tf_op jit(solution)/shard_map/ppermute | solution.py:40
  4.1 2.6 %collective-permute-start.1 = (bf16[256,128]{1,0:T(8,128)(2,1)S(1)}, bf16[256,128]{1,0:T(8,128)(2,1)S(1)}, u32[]{:S(2)}, u32[]{:S(2)}) collective-permute-start(bf16[256,128]{1,0:T(8,128)(2,1)S(1)} %get-tuple-element.19.refs_0_), channel_id=1, source_target_pairs={{0,16},{8,24},{16,0},{24,8},{1,17},{9,25},{17,1},{25,9},{2,18},{10... | collective-permute-start | bytes 196616 | tf_op jit(solution)/shard_map/ppermute | solution.py:40
  6.7 1.3 %collective-permute-start.2 = (bf16[256,128]{1,0:T(8,128)(2,1)S(1)}, bf16[256,128]{1,0:T(8,128)(2,1)S(1)}, u32[]{:S(2)}, u32[]{:S(2)}) collective-permute-start(bf16[256,128]{1,0:T(8,128)(2,1)S(1)} %get-tuple-element.19.refs_0_), channel_id=1, source_target_pairs={{0,24},{8,0},{16,8},{24,16},{1,25},{9,1},{17,9},{25,17},{2,26},{10... | collective-permute-start | bytes 196616 | tf_op jit(solution)/shard_map/ppermute | solution.py:40
  8.1 0.2 collective-permute-start.3
  8.3 0.8 %collective-permute-start.4 = (bf16[256,128]{1,0:T(8,128)(2,1)S(1)}, bf16[256,128]{1,0:T(8,128)(2,1)S(1)}, u32[]{:S(2)}, u32[]{:S(2)}) collective-permute-start(bf16[256,128]{1,0:T(8,128)(2,1)S(1)} %get-tuple-element.24.refs_0_), channel_id=1, source_target_pairs={{0,8},{8,16},{16,24},{24,0},{1,9},{9,17},{17,25},{25,1},{2,10},{10... | collective-permute-start | bytes 196616 | tf_op jit(solution)/shard_map/ppermute | solution.py:40
  9.1 0.0 collective-permute-done.refs_2_
  9.1 3.0 %collective-permute-start.5 = (bf16[256,128]{1,0:T(8,128)(2,1)S(1)}, bf16[256,128]{1,0:T(8,128)(2,1)S(1)}, u32[]{:S(2)}, u32[]{:S(2)}) collective-permute-start(bf16[256,128]{1,0:T(8,128)(2,1)S(1)} %get-tuple-element.24.refs_0_), channel_id=1, source_target_pairs={{0,24},{8,0},{16,8},{24,16},{1,25},{9,1},{17,9},{25,17},{2,26},{10... | collective-permute-start | bytes 196616 | tf_op jit(solution)/shard_map/ppermute | solution.py:40
  12.1 1.2 %shard_map.56 = (bf16[2,1024,128]{2,1,0:T(8,128)(2,1)S(1)}, bf16[2,1024,128]{2,1,0:T(8,128)(2,1)S(1)}) custom-call(bf16[256,1024]{1,0:T(8,128)(2,1)} %q_ref, s32[8,8]{1,0:T(8,128)} %pattern_ref.1), custom_call_target="tpu_custom_call" | custom-call | bytes 1048576 | tf_op jit(solution)/shard_map/pallas_call | solution.py:119
  13.2 0.0 collective-permute-done.1.refs_1_
  13.3 0.0 collective-permute-done.2.refs_3_
  13.3 1.8 %shard_map.57.weights_ref = bf16[2,1024,1024]{2,1,0:T(8,128)(2,1)S(1)} custom-call(bf16[2,1024,128]{2,1,0:T(8,128)(2,1)S(1)} %get-tuple-element.21.q_ref, bf16[2,1024,128]{2,1,0:T(8,128)(2,1)S(1)} %get-tuple-element.22.mask_ref, bf16[256,128]{1,0:T(8,128)(2,1)S(1)} %get-tuple-element.19.refs_0_, bf16[256,128]{1,0:T(8,128)(2,1)S(1)} %collective-permute-done.1.refs_1_, ...), custom_call_target="tpu_custom_call" | custom-call | flops 2147483648 | bytes 4194304 | tf_op jit(solution)/shard_map/pallas_call | solution.py:160
  15.1 1.7 %collective-permute-done.3.refs_1_ = bf16[256,128]{1,0:T(8,128)(2,1)S(1)} collective-permute-done((bf16[256,128]{1,0:T(8,128)(2,1)S(1)}, bf16[256,128]{1,0:T(8,128)(2,1)S(1)}, u32[]{:S(2)}, u32[]{:S(2)}) %collective-permute-start.3) | collective-permute-done | bytes 65568 | tf_op jit(solution)/shard_map/ppermute | solution.py:40
  16.8 0.0 collective-permute-done.4.refs_2_
  16.8 0.0 collective-permute-done.5.refs_3_
  16.8 0.7 %shard_map.59.refs_1_ = bf16[256,512]{1,0:T(8,128)(2,1)S(1)} custom-call(bf16[2,1024,1024]{2,1,0:T(8,128)(2,1)S(1)} %shard_map.57.weights_ref, bf16[256,128]{1,0:T(8,128)(2,1)S(1)} %get-tuple-element.24.refs_0_, bf16[256,128]{1,0:T(8,128)(2,1)S(1)} %collective-permute-done.3.refs_1_, bf16[256,128]{1,0:T(8,128)(2,1)S(1)} %collective-permute-done.4.refs_2_, ...), custom_call_target="tpu_custom_call" | custom-call | flops 536870912 | bytes 1048576 | tf_op jit(solution)/shard_map/pallas_call | solution.py:189
  17.6 0.7 %shard_map.58.refs_0_ = bf16[256,512]{1,0:T(8,128)(2,1)S(1)} custom-call(bf16[2,1024,1024]{2,1,0:T(8,128)(2,1)S(1)} %shard_map.57.weights_ref, bf16[256,128]{1,0:T(8,128)(2,1)S(1)} %get-tuple-element.24.refs_0_, bf16[256,128]{1,0:T(8,128)(2,1)S(1)} %collective-permute-done.3.refs_1_, bf16[256,128]{1,0:T(8,128)(2,1)S(1)} %collective-permute-done.4.refs_2_, ...), custom_call_target="tpu_custom_call" | custom-call | flops 536870912 | bytes 1048576 | tf_op jit(solution)/shard_map/pallas_call | solution.py:189
  18.3 0.1 collective-permute-start.7
  18.4 0.5 %collective-permute-start.8 = (bf16[256,512]{1,0:T(8,128)(2,1)S(1)}, bf16[256,512]{1,0:T(8,128)(2,1)S(1)}, u32[]{:S(2)}, u32[]{:S(2)}) collective-permute-start(bf16[256,512]{1,0:T(8,128)(2,1)S(1)} %shard_map.59.refs_1_), channel_id=1, source_target_pairs={{0,1},{1,0},{2,3},{3,2},{4,5},{5,4},{6,7},{7,6},{8,9},{9,8},{10,11... | collective-permute-start | bytes 786440 | tf_op jit(solution)/shard_map/ppermute | solution.py:45
  18.9 1.8 %collective-permute-start.6 = (bf16[256,512]{1,0:T(8,128)(2,1)S(1)}, bf16[256,512]{1,0:T(8,128)(2,1)S(1)}, u32[]{:S(2)}, u32[]{:S(2)}) collective-permute-start(bf16[256,512]{1,0:T(8,128)(2,1)S(1)} %shard_map.58.refs_0_), channel_id=1, source_target_pairs={{0,2},{1,3},{2,0},{3,1},{4,6},{5,7},{6,4},{7,5},{8,10},{9,11},{10,... | collective-permute-start | bytes 786440 | tf_op jit(solution)/shard_map/ppermute | solution.py:45
  20.6 1.5 %collective-permute-start.10 = (bf16[256,512]{1,0:T(8,128)(2,1)S(1)}, bf16[256,512]{1,0:T(8,128)(2,1)S(1)}, u32[]{:S(2)}, u32[]{:S(2)}) collective-permute-start(bf16[256,512]{1,0:T(8,128)(2,1)S(1)} %shard_map.59.refs_1_), channel_id=1, source_target_pairs={{0,4},{1,5},{2,6},{3,7},{4,0},{5,1},{6,2},{7,3},{8,12},{9,13},{10,... | collective-permute-start | bytes 786440 | tf_op jit(solution)/shard_map/ppermute | solution.py:45
  22.1 0.5 %collective-permute-start.13 = (bf16[256,512]{1,0:T(8,128)(2,1)S(1)}, bf16[256,512]{1,0:T(8,128)(2,1)S(1)}, u32[]{:S(2)}, u32[]{:S(2)}) collective-permute-start(bf16[256,512]{1,0:T(8,128)(2,1)S(1)} %shard_map.59.refs_1_), channel_id=1, source_target_pairs={{0,2},{1,3},{2,0},{3,1},{4,6},{5,7},{6,4},{7,5},{8,10},{9,11},{10,... | collective-permute-start | bytes 786440 | tf_op jit(solution)/shard_map/ppermute | solution.py:45
  22.7 0.0 collective-permute-done.7.refs_2_
  22.7 0.2 collective-permute-start.15
  22.9 0.0 collective-permute-done.8.refs_3_
  22.9 0.0 copy-done
  22.9 1.2 %shard_map.60.refs_0_ = f32[256,1024]{1,0:T(8,128)S(1)} custom-call(bf16[8192,1024]{1,0:T(8,128)(2,1)S(1)} %copy-done, bf16[256,512]{1,0:T(8,128)(2,1)S(1)} %shard_map.58.refs_0_, bf16[256,512]{1,0:T(8,128)(2,1)S(1)} %shard_map.59.refs_1_, bf16[256,512]{1,0:T(8,128)(2,1)S(1)} %collective-permute-done.7.refs_2_, ...), custom_call_target="tpu_custom_call" | custom-call | flops 4294967296 | bytes 1048576 | tf_op jit(solution)/shard_map/pallas_call | solution.py:240
  24.2 3.8 %collective-permute-done.6.refs_1_ = bf16[256,512]{1,0:T(8,128)(2,1)S(1)} collective-permute-done((bf16[256,512]{1,0:T(8,128)(2,1)S(1)}, bf16[256,512]{1,0:T(8,128)(2,1)S(1)}, u32[]{:S(2)}, u32[]{:S(2)}) %collective-permute-start.6) | collective-permute-done | bytes 262176 | tf_op jit(solution)/shard_map/ppermute | solution.py:45
  28.0 1.8 %collective-permute-done.10.refs_3_ = bf16[256,512]{1,0:T(8,128)(2,1)S(1)} collective-permute-done((bf16[256,512]{1,0:T(8,128)(2,1)S(1)}, bf16[256,512]{1,0:T(8,128)(2,1)S(1)}, u32[]{:S(2)}, u32[]{:S(2)}) %collective-permute-start.10) | collective-permute-done | bytes 262176 | tf_op jit(solution)/shard_map/ppermute | solution.py:45
  29.8 0.0 collective-permute-start.12
  29.8 0.5 %collective-permute-start.11 = (bf16[256,512]{1,0:T(8,128)(2,1)S(1)}, bf16[256,512]{1,0:T(8,128)(2,1)S(1)}, u32[]{:S(2)}, u32[]{:S(2)}) collective-permute-start(bf16[256,512]{1,0:T(8,128)(2,1)S(1)} %collective-permute-done.6.refs_1_), channel_id=1, source_target_pairs={{0,1},{1,0},{2,3},{3,2},{4,5},{5,4},{6,7},{7,6},{8,9},{9,8},{10,11... | collective-permute-start | bytes 786440 | tf_op jit(solution)/shard_map/ppermute | solution.py:45
  30.3 1.5 %collective-permute-start.9 = (bf16[256,512]{1,0:T(8,128)(2,1)S(1)}, bf16[256,512]{1,0:T(8,128)(2,1)S(1)}, u32[]{:S(2)}, u32[]{:S(2)}) collective-permute-start(bf16[256,512]{1,0:T(8,128)(2,1)S(1)} %collective-permute-done.6.refs_1_), channel_id=1, source_target_pairs={{0,4},{1,5},{2,6},{3,7},{4,0},{5,1},{6,2},{7,3},{8,12},{9,13},{10,... | collective-permute-start | bytes 786440 | tf_op jit(solution)/shard_map/ppermute | solution.py:45
  31.8 0.9 %collective-permute-done.13.refs_1_ = bf16[256,512]{1,0:T(8,128)(2,1)S(1)} collective-permute-done((bf16[256,512]{1,0:T(8,128)(2,1)S(1)}, bf16[256,512]{1,0:T(8,128)(2,1)S(1)}, u32[]{:S(2)}, u32[]{:S(2)}) %collective-permute-start.13) | collective-permute-done | bytes 262176 | tf_op jit(solution)/shard_map/ppermute | solution.py:45
  32.8 1.7 %collective-permute-start.17 = (bf16[256,512]{1,0:T(8,128)(2,1)S(1)}, bf16[256,512]{1,0:T(8,128)(2,1)S(1)}, u32[]{:S(2)}, u32[]{:S(2)}) collective-permute-start(bf16[256,512]{1,0:T(8,128)(2,1)S(1)} %collective-permute-done.10.refs_3_), channel_id=1, source_target_pairs={{0,2},{1,3},{2,0},{3,1},{4,6},{5,7},{6,4},{7,5},{8,10},{9,11},{10,... | collective-permute-start | bytes 786440 | tf_op jit(solution)/shard_map/ppermute | solution.py:45
  34.5 0.9 %collective-permute-done.15.refs_3_ = bf16[256,512]{1,0:T(8,128)(2,1)S(1)} collective-permute-done((bf16[256,512]{1,0:T(8,128)(2,1)S(1)}, bf16[256,512]{1,0:T(8,128)(2,1)S(1)}, u32[]{:S(2)}, u32[]{:S(2)}) %collective-permute-start.15) | collective-permute-done | bytes 262176 | tf_op jit(solution)/shard_map/ppermute | solution.py:45
  35.4 0.0 collective-permute-start.14
  35.4 0.0 collective-permute-done.12.refs_4_
  35.4 0.5 %collective-permute-start.16 = (bf16[256,512]{1,0:T(8,128)(2,1)S(1)}, bf16[256,512]{1,0:T(8,128)(2,1)S(1)}, u32[]{:S(2)}, u32[]{:S(2)}) collective-permute-start(bf16[256,512]{1,0:T(8,128)(2,1)S(1)} %collective-permute-done.15.refs_3_), channel_id=1, source_target_pairs={{0,1},{1,0},{2,3},{3,2},{4,5},{5,4},{6,7},{7,6},{8,9},{9,8},{10,11... | collective-permute-start | bytes 786440 | tf_op jit(solution)/shard_map/ppermute | solution.py:45
  35.9 0.0 collective-permute-done.11.refs_2_
  36.0 1.2 %shard_map.61.refs_0_ = f32[256,1024]{1,0:T(8,128)S(1)} custom-call(bf16[8192,1024]{1,0:T(8,128)(2,1)S(1)} %copy-done, f32[256,1024]{1,0:T(8,128)S(1)} %shard_map.60.refs_0_, bf16[256,512]{1,0:T(8,128)(2,1)S(1)} %collective-permute-done.6.refs_1_, bf16[256,512]{1,0:T(8,128)(2,1)S(1)} %collective-permute-done.11.refs_2_, ...), custom_call_target="tpu_custom_call" | custom-call | flops 4294967296 | bytes 1048576 | tf_op jit(solution)/shard_map/pallas_call | solution.py:240
  37.2 0.0 collective-permute-done.14.refs_2_
  37.2 0.1 collective-permute-done.16.refs_4_
  37.3 1.2 %shard_map.62.refs_0_ = f32[256,1024]{1,0:T(8,128)S(1)} custom-call(bf16[8192,1024]{1,0:T(8,128)(2,1)S(1)} %copy-done, f32[256,1024]{1,0:T(8,128)S(1)} %shard_map.61.refs_0_, bf16[256,512]{1,0:T(8,128)(2,1)S(1)} %collective-permute-done.13.refs_1_, bf16[256,512]{1,0:T(8,128)(2,1)S(1)} %collective-permute-done.14.refs_2_, ...), custom_call_target="tpu_custom_call" | custom-call | flops 4294967296 | bytes 1048576 | tf_op jit(solution)/shard_map/pallas_call | solution.py:240
  38.6 1.3 %collective-permute-done.9.refs_1_ = bf16[256,512]{1,0:T(8,128)(2,1)S(1)} collective-permute-done((bf16[256,512]{1,0:T(8,128)(2,1)S(1)}, bf16[256,512]{1,0:T(8,128)(2,1)S(1)}, u32[]{:S(2)}, u32[]{:S(2)}) %collective-permute-start.9) | collective-permute-done | bytes 262176 | tf_op jit(solution)/shard_map/ppermute | solution.py:45
  39.9 0.0 collective-permute-start.18
  39.9 0.4 collective-permute-done.17.refs_2_
  40.3 0.1 collective-permute-start.19
  40.4 0.7 %shard_map.63.refs_0_ = f32[256,1024]{1,0:T(8,128)S(1)} custom-call(bf16[8192,1024]{1,0:T(8,128)(2,1)S(1)} %copy-done, f32[256,1024]{1,0:T(8,128)S(1)} %shard_map.62.refs_0_, bf16[256,512]{1,0:T(8,128)(2,1)S(1)} %collective-permute-done.9.refs_1_, bf16[256,512]{1,0:T(8,128)(2,1)S(1)} %collective-permute-done.17.refs_2_), custom_call_target="tpu_custom_call" | custom-call | flops 2147483648 | bytes 1048576 | tf_op jit(solution)/shard_map/pallas_call | solution.py:240
  41.1 0.3 collective-permute-done.18.refs_1_
  41.4 0.4 collective-permute-done.19.refs_2_
  41.8 1.5 %shard_map.64 = bf16[256,1024]{1,0:T(8,128)(2,1)} custom-call(bf16[8192,1024]{1,0:T(8,128)(2,1)S(1)} %copy-done, f32[256,1024]{1,0:T(8,128)S(1)} %shard_map.63.refs_0_, bf16[256,512]{1,0:T(8,128)(2,1)S(1)} %collective-permute-done.18.refs_1_, bf16[256,512]{1,0:T(8,128)(2,1)S(1)} %collective-permute-done.19.refs_2_), custom_call_target="tpu_custom_call" | custom-call | flops 2147483648 | bytes 1048576 | tf_op jit(solution)/shard_map/pallas_call | solution.py:240
Async XLA Ops:
  0.0 22.9 %copy-start = (bf16[8192,1024]{1,0:T(8,128)(2,1)S(1)}, bf16[8192,1024]{1,0:T(8,128)(2,1)}, u32[]{:S(2)}) copy-start(bf16[8192,1024]{1,0:T(8,128)(2,1)} %weight_ref.9) | copy-start | bytes 50331652
  1.0 8.0 %collective-permute-start = (bf16[256,128]{1,0:T(8,128)(2,1)S(1)}, bf16[256,128]{1,0:T(8,128)(2,1)S(1)}, u32[]{:S(2)}, u32[]{:S(2)}) collective-permute-start(bf16[256,128]{1,0:T(8,128)(2,1)S(1)} %get-tuple-element.19.refs_0_), channel_id=1, source_target_pairs={{0,8},{8,16},{16,24},{24,0},{1,9},{9,17},{17,25},{25,1},{2,10},{10... | collective-permute-start | bytes 196616 | tf_op jit(solution)/shard_map/ppermute | solution.py:40
  4.1 9.1 %collective-permute-start.1 = (bf16[256,128]{1,0:T(8,128)(2,1)S(1)}, bf16[256,128]{1,0:T(8,128)(2,1)S(1)}, u32[]{:S(2)}, u32[]{:S(2)}) collective-permute-start(bf16[256,128]{1,0:T(8,128)(2,1)S(1)} %get-tuple-element.19.refs_0_), channel_id=1, source_target_pairs={{0,16},{8,24},{16,0},{24,8},{1,17},{9,25},{17,1},{25,9},{2,18},{10... | collective-permute-start | bytes 196616 | tf_op jit(solution)/shard_map/ppermute | solution.py:40
  6.7 6.5 %collective-permute-start.2 = (bf16[256,128]{1,0:T(8,128)(2,1)S(1)}, bf16[256,128]{1,0:T(8,128)(2,1)S(1)}, u32[]{:S(2)}, u32[]{:S(2)}) collective-permute-start(bf16[256,128]{1,0:T(8,128)(2,1)S(1)} %get-tuple-element.19.refs_0_), channel_id=1, source_target_pairs={{0,24},{8,0},{16,8},{24,16},{1,25},{9,1},{17,9},{25,17},{2,26},{10... | collective-permute-start | bytes 196616 | tf_op jit(solution)/shard_map/ppermute | solution.py:40
  8.1 8.8 %collective-permute-start.3 = (bf16[256,128]{1,0:T(8,128)(2,1)S(1)}, bf16[256,128]{1,0:T(8,128)(2,1)S(1)}, u32[]{:S(2)}, u32[]{:S(2)}) collective-permute-start(bf16[256,128]{1,0:T(8,128)(2,1)S(1)} %get-tuple-element.24.refs_0_), channel_id=1, source_target_pairs={{0,16},{8,24},{16,0},{24,8},{1,17},{9,25},{17,1},{25,9},{2,18},{10... | collective-permute-start | bytes 196616 | tf_op jit(solution)/shard_map/ppermute | solution.py:40
  8.3 8.6 %collective-permute-start.4 = (bf16[256,128]{1,0:T(8,128)(2,1)S(1)}, bf16[256,128]{1,0:T(8,128)(2,1)S(1)}, u32[]{:S(2)}, u32[]{:S(2)}) collective-permute-start(bf16[256,128]{1,0:T(8,128)(2,1)S(1)} %get-tuple-element.24.refs_0_), channel_id=1, source_target_pairs={{0,8},{8,16},{16,24},{24,0},{1,9},{9,17},{17,25},{25,1},{2,10},{10... | collective-permute-start | bytes 196616 | tf_op jit(solution)/shard_map/ppermute | solution.py:40
  9.1 7.7 %collective-permute-start.5 = (bf16[256,128]{1,0:T(8,128)(2,1)S(1)}, bf16[256,128]{1,0:T(8,128)(2,1)S(1)}, u32[]{:S(2)}, u32[]{:S(2)}) collective-permute-start(bf16[256,128]{1,0:T(8,128)(2,1)S(1)} %get-tuple-element.24.refs_0_), channel_id=1, source_target_pairs={{0,24},{8,0},{16,8},{24,16},{1,25},{9,1},{17,9},{25,17},{2,26},{10... | collective-permute-start | bytes 196616 | tf_op jit(solution)/shard_map/ppermute | solution.py:40
  18.3 4.4 %collective-permute-start.7 = (bf16[256,512]{1,0:T(8,128)(2,1)S(1)}, bf16[256,512]{1,0:T(8,128)(2,1)S(1)}, u32[]{:S(2)}, u32[]{:S(2)}) collective-permute-start(bf16[256,512]{1,0:T(8,128)(2,1)S(1)} %shard_map.58.refs_0_), channel_id=1, source_target_pairs={{0,1},{1,0},{2,3},{3,2},{4,5},{5,4},{6,7},{7,6},{8,9},{9,8},{10,11... | collective-permute-start | bytes 786440 | tf_op jit(solution)/shard_map/ppermute | solution.py:45
  18.4 4.6 %collective-permute-start.8 = (bf16[256,512]{1,0:T(8,128)(2,1)S(1)}, bf16[256,512]{1,0:T(8,128)(2,1)S(1)}, u32[]{:S(2)}, u32[]{:S(2)}) collective-permute-start(bf16[256,512]{1,0:T(8,128)(2,1)S(1)} %shard_map.59.refs_1_), channel_id=1, source_target_pairs={{0,1},{1,0},{2,3},{3,2},{4,5},{5,4},{6,7},{7,6},{8,9},{9,8},{10,11... | collective-permute-start | bytes 786440 | tf_op jit(solution)/shard_map/ppermute | solution.py:45
  18.9 9.2 %collective-permute-start.6 = (bf16[256,512]{1,0:T(8,128)(2,1)S(1)}, bf16[256,512]{1,0:T(8,128)(2,1)S(1)}, u32[]{:S(2)}, u32[]{:S(2)}) collective-permute-start(bf16[256,512]{1,0:T(8,128)(2,1)S(1)} %shard_map.58.refs_0_), channel_id=1, source_target_pairs={{0,2},{1,3},{2,0},{3,1},{4,6},{5,7},{6,4},{7,5},{8,10},{9,11},{10,... | collective-permute-start | bytes 786440 | tf_op jit(solution)/shard_map/ppermute | solution.py:45
  20.6 9.2 %collective-permute-start.10 = (bf16[256,512]{1,0:T(8,128)(2,1)S(1)}, bf16[256,512]{1,0:T(8,128)(2,1)S(1)}, u32[]{:S(2)}, u32[]{:S(2)}) collective-permute-start(bf16[256,512]{1,0:T(8,128)(2,1)S(1)} %shard_map.59.refs_1_), channel_id=1, source_target_pairs={{0,4},{1,5},{2,6},{3,7},{4,0},{5,1},{6,2},{7,3},{8,12},{9,13},{10,... | collective-permute-start | bytes 786440 | tf_op jit(solution)/shard_map/ppermute | solution.py:45
  22.1 10.6 %collective-permute-start.13 = (bf16[256,512]{1,0:T(8,128)(2,1)S(1)}, bf16[256,512]{1,0:T(8,128)(2,1)S(1)}, u32[]{:S(2)}, u32[]{:S(2)}) collective-permute-start(bf16[256,512]{1,0:T(8,128)(2,1)S(1)} %shard_map.59.refs_1_), channel_id=1, source_target_pairs={{0,2},{1,3},{2,0},{3,1},{4,6},{5,7},{6,4},{7,5},{8,10},{9,11},{10,... | collective-permute-start | bytes 786440 | tf_op jit(solution)/shard_map/ppermute | solution.py:45
  22.7 12.8 %collective-permute-start.15 = (bf16[256,512]{1,0:T(8,128)(2,1)S(1)}, bf16[256,512]{1,0:T(8,128)(2,1)S(1)}, u32[]{:S(2)}, u32[]{:S(2)}) collective-permute-start(bf16[256,512]{1,0:T(8,128)(2,1)S(1)} %shard_map.58.refs_0_), channel_id=1, source_target_pairs={{0,4},{1,5},{2,6},{3,7},{4,0},{5,1},{6,2},{7,3},{8,12},{9,13},{10,... | collective-permute-start | bytes 786440 | tf_op jit(solution)/shard_map/ppermute | solution.py:45
  29.8 5.6 %collective-permute-start.12 = (bf16[256,512]{1,0:T(8,128)(2,1)S(1)}, bf16[256,512]{1,0:T(8,128)(2,1)S(1)}, u32[]{:S(2)}, u32[]{:S(2)}) collective-permute-start(bf16[256,512]{1,0:T(8,128)(2,1)S(1)} %collective-permute-done.10.refs_3_), channel_id=1, source_target_pairs={{0,1},{1,0},{2,3},{3,2},{4,5},{5,4},{6,7},{7,6},{8,9},{9,8},{10,11... | collective-permute-start | bytes 786440 | tf_op jit(solution)/shard_map/ppermute | solution.py:45
  29.8 6.1 %collective-permute-start.11 = (bf16[256,512]{1,0:T(8,128)(2,1)S(1)}, bf16[256,512]{1,0:T(8,128)(2,1)S(1)}, u32[]{:S(2)}, u32[]{:S(2)}) collective-permute-start(bf16[256,512]{1,0:T(8,128)(2,1)S(1)} %collective-permute-done.6.refs_1_), channel_id=1, source_target_pairs={{0,1},{1,0},{2,3},{3,2},{4,5},{5,4},{6,7},{7,6},{8,9},{9,8},{10,11... | collective-permute-start | bytes 786440 | tf_op jit(solution)/shard_map/ppermute | solution.py:45
  30.3 9.5 %collective-permute-start.9 = (bf16[256,512]{1,0:T(8,128)(2,1)S(1)}, bf16[256,512]{1,0:T(8,128)(2,1)S(1)}, u32[]{:S(2)}, u32[]{:S(2)}) collective-permute-start(bf16[256,512]{1,0:T(8,128)(2,1)S(1)} %collective-permute-done.6.refs_1_), channel_id=1, source_target_pairs={{0,4},{1,5},{2,6},{3,7},{4,0},{5,1},{6,2},{7,3},{8,12},{9,13},{10,... | collective-permute-start | bytes 786440 | tf_op jit(solution)/shard_map/ppermute | solution.py:45
  32.8 7.5 %collective-permute-start.17 = (bf16[256,512]{1,0:T(8,128)(2,1)S(1)}, bf16[256,512]{1,0:T(8,128)(2,1)S(1)}, u32[]{:S(2)}, u32[]{:S(2)}) collective-permute-start(bf16[256,512]{1,0:T(8,128)(2,1)S(1)} %collective-permute-done.10.refs_3_), channel_id=1, source_target_pairs={{0,2},{1,3},{2,0},{3,1},{4,6},{5,7},{6,4},{7,5},{8,10},{9,11},{10,... | collective-permute-start | bytes 786440 | tf_op jit(solution)/shard_map/ppermute | solution.py:45
  35.4 1.8 %collective-permute-start.14 = (bf16[256,512]{1,0:T(8,128)(2,1)S(1)}, bf16[256,512]{1,0:T(8,128)(2,1)S(1)}, u32[]{:S(2)}, u32[]{:S(2)}) collective-permute-start(bf16[256,512]{1,0:T(8,128)(2,1)S(1)} %collective-permute-done.13.refs_1_), channel_id=1, source_target_pairs={{0,1},{1,0},{2,3},{3,2},{4,5},{5,4},{6,7},{7,6},{8,9},{9,8},{10,11... | collective-permute-start | bytes 786440 | tf_op jit(solution)/shard_map/ppermute | solution.py:45
  35.4 1.9 %collective-permute-start.16 = (bf16[256,512]{1,0:T(8,128)(2,1)S(1)}, bf16[256,512]{1,0:T(8,128)(2,1)S(1)}, u32[]{:S(2)}, u32[]{:S(2)}) collective-permute-start(bf16[256,512]{1,0:T(8,128)(2,1)S(1)} %collective-permute-done.15.refs_3_), channel_id=1, source_target_pairs={{0,1},{1,0},{2,3},{3,2},{4,5},{5,4},{6,7},{7,6},{8,9},{9,8},{10,11... | collective-permute-start | bytes 786440 | tf_op jit(solution)/shard_map/ppermute | solution.py:45
  39.9 1.5 %collective-permute-start.18 = (bf16[256,512]{1,0:T(8,128)(2,1)S(1)}, bf16[256,512]{1,0:T(8,128)(2,1)S(1)}, u32[]{:S(2)}, u32[]{:S(2)}) collective-permute-start(bf16[256,512]{1,0:T(8,128)(2,1)S(1)} %collective-permute-done.9.refs_1_), channel_id=1, source_target_pairs={{0,1},{1,0},{2,3},{3,2},{4,5},{5,4},{6,7},{7,6},{8,9},{9,8},{10,11... | collective-permute-start | bytes 786440 | tf_op jit(solution)/shard_map/ppermute | solution.py:45
  40.3 1.5 %collective-permute-start.19 = (bf16[256,512]{1,0:T(8,128)(2,1)S(1)}, bf16[256,512]{1,0:T(8,128)(2,1)S(1)}, u32[]{:S(2)}, u32[]{:S(2)}) collective-permute-start(bf16[256,512]{1,0:T(8,128)(2,1)S(1)} %collective-permute-done.17.refs_2_), channel_id=1, source_target_pairs={{0,1},{1,0},{2,3},{3,2},{4,5},{5,4},{6,7},{7,6},{8,9},{9,8},{10,11... | collective-permute-start | bytes 786440 | tf_op jit(solution)/shard_map/ppermute | solution.py:45

commit v7 on v6

--- a/solution.py
+++ b/solution.py
@@ -294,10 +294,10 @@
     mixed = projected(
         None, weight, width, ((0, 0), (0, half), (1, 0), (1, half)), [a, b, sa, sb]
     )
-    xa, mixed = barrier((xa, mixed))
+    xa, yb, mixed = barrier((xa, yb, mixed))
     da = swapped(xa, "head", 4)
-    yb, mixed = barrier((yb, mixed))
-    db = swapped(yb, "head", 2)
+    yb_late, _ = barrier((yb, ya))
+    db = swapped(yb_late, "head", 2)
     xas, ybs = swapped(xa, "head", 1), swapped(yb, "head", 1)
     mixed = projected(
         mixed, weight, width, ((2, 0), (3, 0), (4, half), (5, half)), [xa, xas, yb, ybs]

time: 43.4 us -> 43.9 us (1.012)
  waiting for transfers between devices: 11.7 us -> 13.2 us
  starting transfers between devices: 20.1 us -> 19 us
    ppermute x14, waiting for transfers between devices: 9.99 us -> 11.5 us  [swapped(): lax.ppermute(value, axis, [(source, source ^ bits) for source in range(co...]
    ppermute x14, starting transfers between devices: 9.02 us -> 7.97 us  [swapped(): lax.ppermute(value, axis, [(source, source ^ bits) for source in range(co...]
  transfers between devices with their start and end apart: 20 -> 20, of which waited for: 10 -> 9; matrix products, arithmetic and copies ran while one was open for 0% -> 0% of each run, Pallas kernels for 17% -> 17%
where the time goes in v7:
time: 43.9 us; the launch traced here: 43.7 us
  starting transfers between devices  19 us (43%)
  waiting for transfers between devices  13.2 us (30%)
  Pallas kernels  11.4 us (26%)
    ppermute x14, waiting for transfers between devices, swapped(): lax.ppermute(value, axis, [(source, source ^ bits) for source in range(co...  11.5 us
    ppermute x6, starting transfers between devices, shifted(): lax.ppermute(value, axis, [(source, (source + steps) % count) for source...  11 us
    ppermute x14, starting transfers between devices, swapped(): lax.ppermute(value, axis, [(source, source ^ bits) for source in range(co...  7.97 us
    pallas_call x5, Pallas kernels, projected(): pl.pallas_call(functools.partial(projection_kernel, places, width, fresh,...  5.9 us
    pallas_call x1, Pallas kernels, weights_of(): pl.pallas_call(weights_kernel, out_shape=held((blocks_dev, rows, keys)),...  1.84 us
    ppermute x6, waiting for transfers between devices, shifted(): lax.ppermute(value, axis, [(source, (source + steps) % count) for source...  1.72 us
    pallas_call x2, Pallas kernels, attended_of(): pl.pallas_call(functools.partial(values_kernel, first, group), out_shape=...  1.43 us
    pallas_call x1, Pallas kernels, stacked_of(): pl.pallas_call(functools.partial(stack_kernel, steps, count), out_shape=[...  1.15 us
  transfers between devices with their start and end apart: 20, of which 9 were waited for; matrix products, arithmetic and copies ran while one was open for 0% of the time, Pallas kernels for 17%

profile of v7, /device:TPU:0, one launch (start us, length us, event | category | flops | bytes accessed | tf_op | source)
XLA Modules:
  0.0 43.7 jit_solution(14839554274855527582)
XLA Ops:
  0.0 0.0 copy-start
  0.0 1.0 %shard_map.55 = (bf16[256,128]{1,0:T(8,128)(2,1)S(1)}, bf16[256,128]{1,0:T(8,128)(2,1)S(1)}) custom-call(bf16[256,1024]{1,0:T(8,128)(2,1)} %keys_ref.1, bf16[256,1024]{1,0:T(8,128)(2,1)} %values_ref.1), custom_call_target="tpu_custom_call" | custom-call | bytes 262144 | tf_op jit(solution)/shard_map/pallas_call | solution.py:68
  1.0 3.1 %collective-permute-start = (bf16[256,128]{1,0:T(8,128)(2,1)S(1)}, bf16[256,128]{1,0:T(8,128)(2,1)S(1)}, u32[]{:S(2)}, u32[]{:S(2)}) collective-permute-start(bf16[256,128]{1,0:T(8,128)(2,1)S(1)} %get-tuple-element.19.refs_0_), channel_id=1, source_target_pairs={{0,8},{8,16},{16,24},{24,0},{1,9},{9,17},{17,25},{25,1},{2,10},{10... | collective-permute-start | bytes 196616 | tf_op jit(solution)/shard_map/ppermute | solution.py:40
  4.1 2.6 %collective-permute-start.1 = (bf16[256,128]{1,0:T(8,128)(2,1)S(1)}, bf16[256,128]{1,0:T(8,128)(2,1)S(1)}, u32[]{:S(2)}, u32[]{:S(2)}) collective-permute-start(bf16[256,128]{1,0:T(8,128)(2,1)S(1)} %get-tuple-element.19.refs_0_), channel_id=1, source_target_pairs={{0,16},{8,24},{16,0},{24,8},{1,17},{9,25},{17,1},{25,9},{2,18},{10... | collective-permute-start | bytes 196616 | tf_op jit(solution)/shard_map/ppermute | solution.py:40
  6.7 1.3 %collective-permute-start.2 = (bf16[256,128]{1,0:T(8,128)(2,1)S(1)}, bf16[256,128]{1,0:T(8,128)(2,1)S(1)}, u32[]{:S(2)}, u32[]{:S(2)}) collective-permute-start(bf16[256,128]{1,0:T(8,128)(2,1)S(1)} %get-tuple-element.19.refs_0_), channel_id=1, source_target_pairs={{0,24},{8,0},{16,8},{24,16},{1,25},{9,1},{17,9},{25,17},{2,26},{10... | collective-permute-start | bytes 196616 | tf_op jit(solution)/shard_map/ppermute | solution.py:40
  8.1 0.2 collective-permute-start.3
  8.3 0.8 %collective-permute-start.4 = (bf16[256,128]{1,0:T(8,128)(2,1)S(1)}, bf16[256,128]{1,0:T(8,128)(2,1)S(1)}, u32[]{:S(2)}, u32[]{:S(2)}) collective-permute-start(bf16[256,128]{1,0:T(8,128)(2,1)S(1)} %get-tuple-element.24.refs_0_), channel_id=1, source_target_pairs={{0,8},{8,16},{16,24},{24,0},{1,9},{9,17},{17,25},{25,1},{2,10},{10... | collective-permute-start | bytes 196616 | tf_op jit(solution)/shard_map/ppermute | solution.py:40
  9.1 0.0 collective-permute-done.refs_2_
  9.1 3.0 %collective-permute-start.5 = (bf16[256,128]{1,0:T(8,128)(2,1)S(1)}, bf16[256,128]{1,0:T(8,128)(2,1)S(1)}, u32[]{:S(2)}, u32[]{:S(2)}) collective-permute-start(bf16[256,128]{1,0:T(8,128)(2,1)S(1)} %get-tuple-element.24.refs_0_), channel_id=1, source_target_pairs={{0,24},{8,0},{16,8},{24,16},{1,25},{9,1},{17,9},{25,17},{2,26},{10... | collective-permute-start | bytes 196616 | tf_op jit(solution)/shard_map/ppermute | solution.py:40
  12.1 1.2 %shard_map.56 = (bf16[2,1024,128]{2,1,0:T(8,128)(2,1)S(1)}, bf16[2,1024,128]{2,1,0:T(8,128)(2,1)S(1)}) custom-call(bf16[256,1024]{1,0:T(8,128)(2,1)} %q_ref, s32[8,8]{1,0:T(8,128)} %pattern_ref.1), custom_call_target="tpu_custom_call" | custom-call | bytes 1048576 | tf_op jit(solution)/shard_map/pallas_call | solution.py:119
  13.2 0.0 collective-permute-done.1.refs_1_
  13.3 0.0 collective-permute-done.2.refs_3_
  13.3 1.8 %shard_map.57.weights_ref = bf16[2,1024,1024]{2,1,0:T(8,128)(2,1)S(1)} custom-call(bf16[2,1024,128]{2,1,0:T(8,128)(2,1)S(1)} %get-tuple-element.21.q_ref, bf16[2,1024,128]{2,1,0:T(8,128)(2,1)S(1)} %get-tuple-element.22.mask_ref, bf16[256,128]{1,0:T(8,128)(2,1)S(1)} %get-tuple-element.19.refs_0_, bf16[256,128]{1,0:T(8,128)(2,1)S(1)} %collective-permute-done.1.refs_1_, ...), custom_call_target="tpu_custom_call" | custom-call | flops 2147483648 | bytes 4194304 | tf_op jit(solution)/shard_map/pallas_call | solution.py:160
  15.1 1.7 %collective-permute-done.3.refs_1_ = bf16[256,128]{1,0:T(8,128)(2,1)S(1)} collective-permute-done((bf16[256,128]{1,0:T(8,128)(2,1)S(1)}, bf16[256,128]{1,0:T(8,128)(2,1)S(1)}, u32[]{:S(2)}, u32[]{:S(2)}) %collective-permute-start.3) | collective-permute-done | bytes 65568 | tf_op jit(solution)/shard_map/ppermute | solution.py:40
  16.8 0.0 collective-permute-done.4.refs_2_
  16.8 0.0 collective-permute-done.5.refs_3_
  16.8 0.7 %shard_map.59.refs_1_ = bf16[256,512]{1,0:T(8,128)(2,1)S(1)} custom-call(bf16[2,1024,1024]{2,1,0:T(8,128)(2,1)S(1)} %shard_map.57.weights_ref, bf16[256,128]{1,0:T(8,128)(2,1)S(1)} %get-tuple-element.24.refs_0_, bf16[256,128]{1,0:T(8,128)(2,1)S(1)} %collective-permute-done.3.refs_1_, bf16[256,128]{1,0:T(8,128)(2,1)S(1)} %collective-permute-done.4.refs_2_, ...), custom_call_target="tpu_custom_call" | custom-call | flops 536870912 | bytes 1048576 | tf_op jit(solution)/shard_map/pallas_call | solution.py:189
  17.6 0.7 %shard_map.58.refs_0_ = bf16[256,512]{1,0:T(8,128)(2,1)S(1)} custom-call(bf16[2,1024,1024]{2,1,0:T(8,128)(2,1)S(1)} %shard_map.57.weights_ref, bf16[256,128]{1,0:T(8,128)(2,1)S(1)} %get-tuple-element.24.refs_0_, bf16[256,128]{1,0:T(8,128)(2,1)S(1)} %collective-permute-done.3.refs_1_, bf16[256,128]{1,0:T(8,128)(2,1)S(1)} %collective-permute-done.4.refs_2_, ...), custom_call_target="tpu_custom_call" | custom-call | flops 536870912 | bytes 1048576 | tf_op jit(solution)/shard_map/pallas_call | solution.py:189
  18.3 0.1 collective-permute-start.8
  18.4 0.5 %collective-permute-start.9 = (bf16[256,512]{1,0:T(8,128)(2,1)S(1)}, bf16[256,512]{1,0:T(8,128)(2,1)S(1)}, u32[]{:S(2)}, u32[]{:S(2)}) collective-permute-start(bf16[256,512]{1,0:T(8,128)(2,1)S(1)} %shard_map.59.refs_1_), channel_id=1, source_target_pairs={{0,1},{1,0},{2,3},{3,2},{4,5},{5,4},{6,7},{7,6},{8,9},{9,8},{10,11... | collective-permute-start | bytes 786440 | tf_op jit(solution)/shard_map/ppermute | solution.py:45
  18.9 1.8 %collective-permute-start.7 = (bf16[256,512]{1,0:T(8,128)(2,1)S(1)}, bf16[256,512]{1,0:T(8,128)(2,1)S(1)}, u32[]{:S(2)}, u32[]{:S(2)}) collective-permute-start(bf16[256,512]{1,0:T(8,128)(2,1)S(1)} %shard_map.59.refs_1_), channel_id=1, source_target_pairs={{0,4},{1,5},{2,6},{3,7},{4,0},{5,1},{6,2},{7,3},{8,12},{9,13},{10,... | collective-permute-start | bytes 786440 | tf_op jit(solution)/shard_map/ppermute | solution.py:45
  20.6 1.5 %collective-permute-start.6 = (bf16[256,512]{1,0:T(8,128)(2,1)S(1)}, bf16[256,512]{1,0:T(8,128)(2,1)S(1)}, u32[]{:S(2)}, u32[]{:S(2)}) collective-permute-start(bf16[256,512]{1,0:T(8,128)(2,1)S(1)} %shard_map.58.refs_0_), channel_id=1, source_target_pairs={{0,2},{1,3},{2,0},{3,1},{4,6},{5,7},{6,4},{7,5},{8,10},{9,11},{10,... | collective-permute-start | bytes 786440 | tf_op jit(solution)/shard_map/ppermute | solution.py:45
  22.1 0.5 %collective-permute-start.15 = (bf16[256,512]{1,0:T(8,128)(2,1)S(1)}, bf16[256,512]{1,0:T(8,128)(2,1)S(1)}, u32[]{:S(2)}, u32[]{:S(2)}) collective-permute-start(bf16[256,512]{1,0:T(8,128)(2,1)S(1)} %shard_map.58.refs_0_), channel_id=1, source_target_pairs={{0,4},{1,5},{2,6},{3,7},{4,0},{5,1},{6,2},{7,3},{8,12},{9,13},{10,... | collective-permute-start | bytes 786440 | tf_op jit(solution)/shard_map/ppermute | solution.py:45
  22.6 0.0 collective-permute-done.8.refs_2_
  22.6 0.3 collective-permute-start.13
  22.9 0.0 collective-permute-done.9.refs_3_
  22.9 0.0 copy-done
  22.9 1.2 %shard_map.60.refs_0_ = f32[256,1024]{1,0:T(8,128)S(1)} custom-call(bf16[8192,1024]{1,0:T(8,128)(2,1)S(1)} %copy-done, bf16[256,512]{1,0:T(8,128)(2,1)S(1)} %shard_map.58.refs_0_, bf16[256,512]{1,0:T(8,128)(2,1)S(1)} %shard_map.59.refs_1_, bf16[256,512]{1,0:T(8,128)(2,1)S(1)} %collective-permute-done.8.refs_2_, ...), custom_call_target="tpu_custom_call" | custom-call | flops 4294967296 | bytes 1048576 | tf_op jit(solution)/shard_map/pallas_call | solution.py:240
  24.2 3.8 %collective-permute-done.7.refs_3_ = bf16[256,512]{1,0:T(8,128)(2,1)S(1)} collective-permute-done((bf16[256,512]{1,0:T(8,128)(2,1)S(1)}, bf16[256,512]{1,0:T(8,128)(2,1)S(1)}, u32[]{:S(2)}, u32[]{:S(2)}) %collective-permute-start.7) | collective-permute-done | bytes 262176 | tf_op jit(solution)/shard_map/ppermute | solution.py:45
  28.0 1.8 %collective-permute-done.6.refs_1_ = bf16[256,512]{1,0:T(8,128)(2,1)S(1)} collective-permute-done((bf16[256,512]{1,0:T(8,128)(2,1)S(1)}, bf16[256,512]{1,0:T(8,128)(2,1)S(1)}, u32[]{:S(2)}, u32[]{:S(2)}) %collective-permute-start.6) | collective-permute-done | bytes 262176 | tf_op jit(solution)/shard_map/ppermute | solution.py:45
  29.8 0.0 collective-permute-start.11
  29.8 0.5 %collective-permute-start.12 = (bf16[256,512]{1,0:T(8,128)(2,1)S(1)}, bf16[256,512]{1,0:T(8,128)(2,1)S(1)}, u32[]{:S(2)}, u32[]{:S(2)}) collective-permute-start(bf16[256,512]{1,0:T(8,128)(2,1)S(1)} %collective-permute-done.7.refs_3_), channel_id=1, source_target_pairs={{0,1},{1,0},{2,3},{3,2},{4,5},{5,4},{6,7},{7,6},{8,9},{9,8},{10,11... | collective-permute-start | bytes 786440 | tf_op jit(solution)/shard_map/ppermute | solution.py:45
  30.4 0.2 collective-permute-start.10
  30.6 2.4 %collective-permute-done.15.refs_3_ = bf16[256,512]{1,0:T(8,128)(2,1)S(1)} collective-permute-done((bf16[256,512]{1,0:T(8,128)(2,1)S(1)}, bf16[256,512]{1,0:T(8,128)(2,1)S(1)}, u32[]{:S(2)}, u32[]{:S(2)}) %collective-permute-start.15) | collective-permute-done | bytes 262176 | tf_op jit(solution)/shard_map/ppermute | solution.py:45
  32.9 1.6 %collective-permute-start.17 = (bf16[256,512]{1,0:T(8,128)(2,1)S(1)}, bf16[256,512]{1,0:T(8,128)(2,1)S(1)}, u32[]{:S(2)}, u32[]{:S(2)}) collective-permute-start(bf16[256,512]{1,0:T(8,128)(2,1)S(1)} %collective-permute-done.7.refs_3_), channel_id=1, source_target_pairs={{0,2},{1,3},{2,0},{3,1},{4,6},{5,7},{6,4},{7,5},{8,10},{9,11},{10,... | collective-permute-start | bytes 786440 | tf_op jit(solution)/shard_map/ppermute | solution.py:45
  34.5 0.0 collective-permute-done.13.refs_1_
  34.5 0.0 collective-permute-start.16
  34.5 0.0 collective-permute-done.11.refs_2_
  34.5 0.5 %collective-permute-start.14 = (bf16[256,512]{1,0:T(8,128)(2,1)S(1)}, bf16[256,512]{1,0:T(8,128)(2,1)S(1)}, u32[]{:S(2)}, u32[]{:S(2)}) collective-permute-start(bf16[256,512]{1,0:T(8,128)(2,1)S(1)} %collective-permute-done.13.refs_1_), channel_id=1, source_target_pairs={{0,1},{1,0},{2,3},{3,2},{4,5},{5,4},{6,7},{7,6},{8,9},{9,8},{10,11... | collective-permute-start | bytes 786440 | tf_op jit(solution)/shard_map/ppermute | solution.py:45
  35.1 0.0 collective-permute-done.12.refs_4_
  35.1 1.2 %shard_map.61.refs_0_ = f32[256,1024]{1,0:T(8,128)S(1)} custom-call(bf16[8192,1024]{1,0:T(8,128)(2,1)S(1)} %copy-done, f32[256,1024]{1,0:T(8,128)S(1)} %shard_map.60.refs_0_, bf16[256,512]{1,0:T(8,128)(2,1)S(1)} %collective-permute-done.6.refs_1_, bf16[256,512]{1,0:T(8,128)(2,1)S(1)} %collective-permute-done.11.refs_2_, ...), custom_call_target="tpu_custom_call" | custom-call | flops 4294967296 | bytes 1048576 | tf_op jit(solution)/shard_map/pallas_call | solution.py:240
  36.3 0.0 collective-permute-done.16.refs_4_
  36.3 0.1 collective-permute-done.14.refs_2_
  36.4 1.2 %shard_map.62.refs_0_ = f32[256,1024]{1,0:T(8,128)S(1)} custom-call(bf16[8192,1024]{1,0:T(8,128)(2,1)S(1)} %copy-done, f32[256,1024]{1,0:T(8,128)S(1)} %shard_map.61.refs_0_, bf16[256,512]{1,0:T(8,128)(2,1)S(1)} %collective-permute-done.13.refs_1_, bf16[256,512]{1,0:T(8,128)(2,1)S(1)} %collective-permute-done.14.refs_2_, ...), custom_call_target="tpu_custom_call" | custom-call | flops 4294967296 | bytes 1048576 | tf_op jit(solution)/shard_map/pallas_call | solution.py:240
  37.7 0.9 %collective-permute-done.10.refs_1_ = bf16[256,512]{1,0:T(8,128)(2,1)S(1)} collective-permute-done((bf16[256,512]{1,0:T(8,128)(2,1)S(1)}, bf16[256,512]{1,0:T(8,128)(2,1)S(1)}, u32[]{:S(2)}, u32[]{:S(2)}) %collective-permute-start.10) | collective-permute-done | bytes 262176 | tf_op jit(solution)/shard_map/ppermute | solution.py:45
  38.6 1.7 %collective-permute-done.17.refs_2_ = bf16[256,512]{1,0:T(8,128)(2,1)S(1)} collective-permute-done((bf16[256,512]{1,0:T(8,128)(2,1)S(1)}, bf16[256,512]{1,0:T(8,128)(2,1)S(1)}, u32[]{:S(2)}, u32[]{:S(2)}) %collective-permute-start.17) | collective-permute-done | bytes 262176 | tf_op jit(solution)/shard_map/ppermute | solution.py:45
  40.3 0.0 collective-permute-start.19
  40.3 0.5 %collective-permute-start.18 = (bf16[256,512]{1,0:T(8,128)(2,1)S(1)}, bf16[256,512]{1,0:T(8,128)(2,1)S(1)}, u32[]{:S(2)}, u32[]{:S(2)}) collective-permute-start(bf16[256,512]{1,0:T(8,128)(2,1)S(1)} %collective-permute-done.10.refs_1_), channel_id=1, source_target_pairs={{0,1},{1,0},{2,3},{3,2},{4,5},{5,4},{6,7},{7,6},{8,9},{9,8},{10,11... | collective-permute-start | bytes 786440 | tf_op jit(solution)/shard_map/ppermute | solution.py:45
  40.8 0.7 %shard_map.63.refs_0_ = f32[256,1024]{1,0:T(8,128)S(1)} custom-call(bf16[8192,1024]{1,0:T(8,128)(2,1)S(1)} %copy-done, f32[256,1024]{1,0:T(8,128)S(1)} %shard_map.62.refs_0_, bf16[256,512]{1,0:T(8,128)(2,1)S(1)} %collective-permute-done.10.refs_1_, bf16[256,512]{1,0:T(8,128)(2,1)S(1)} %collective-permute-done.17.refs_2_), custom_call_target="tpu_custom_call" | custom-call | flops 2147483648 | bytes 1048576 | tf_op jit(solution)/shard_map/pallas_call | solution.py:240
  41.5 0.3 collective-permute-done.19.refs_2_
  41.8 0.4 collective-permute-done.18.refs_1_
  42.2 1.5 %shard_map.64 = bf16[256,1024]{1,0:T(8,128)(2,1)} custom-call(bf16[8192,1024]{1,0:T(8,128)(2,1)S(1)} %copy-done, f32[256,1024]{1,0:T(8,128)S(1)} %shard_map.63.refs_0_, bf16[256,512]{1,0:T(8,128)(2,1)S(1)} %collective-permute-done.18.refs_1_, bf16[256,512]{1,0:T(8,128)(2,1)S(1)} %collective-permute-done.19.refs_2_), custom_call_target="tpu_custom_call" | custom-call | flops 2147483648 | bytes 1048576 | tf_op jit(solution)/shard_map/pallas_call | solution.py:240
Async XLA Ops:
  0.0 22.9 %copy-start = (bf16[8192,1024]{1,0:T(8,128)(2,1)S(1)}, bf16[8192,1024]{1,0:T(8,128)(2,1)}, u32[]{:S(2)}) copy-start(bf16[8192,1024]{1,0:T(8,128)(2,1)} %weight_ref.9) | copy-start | bytes 50331652
  1.0 8.0 %collective-permute-start = (bf16[256,128]{1,0:T(8,128)(2,1)S(1)}, bf16[256,128]{1,0:T(8,128)(2,1)S(1)}, u32[]{:S(2)}, u32[]{:S(2)}) collective-permute-start(bf16[256,128]{1,0:T(8,128)(2,1)S(1)} %get-tuple-element.19.refs_0_), channel_id=1, source_target_pairs={{0,8},{8,16},{16,24},{24,0},{1,9},{9,17},{17,25},{25,1},{2,10},{10... | collective-permute-start | bytes 196616 | tf_op jit(solution)/shard_map/ppermute | solution.py:40
  4.1 9.1 %collective-permute-start.1 = (bf16[256,128]{1,0:T(8,128)(2,1)S(1)}, bf16[256,128]{1,0:T(8,128)(2,1)S(1)}, u32[]{:S(2)}, u32[]{:S(2)}) collective-permute-start(bf16[256,128]{1,0:T(8,128)(2,1)S(1)} %get-tuple-element.19.refs_0_), channel_id=1, source_target_pairs={{0,16},{8,24},{16,0},{24,8},{1,17},{9,25},{17,1},{25,9},{2,18},{10... | collective-permute-start | bytes 196616 | tf_op jit(solution)/shard_map/ppermute | solution.py:40
  6.7 6.5 %collective-permute-start.2 = (bf16[256,128]{1,0:T(8,128)(2,1)S(1)}, bf16[256,128]{1,0:T(8,128)(2,1)S(1)}, u32[]{:S(2)}, u32[]{:S(2)}) collective-permute-start(bf16[256,128]{1,0:T(8,128)(2,1)S(1)} %get-tuple-element.19.refs_0_), channel_id=1, source_target_pairs={{0,24},{8,0},{16,8},{24,16},{1,25},{9,1},{17,9},{25,17},{2,26},{10... | collective-permute-start | bytes 196616 | tf_op jit(solution)/shard_map/ppermute | solution.py:40
  8.1 8.8 %collective-permute-start.3 = (bf16[256,128]{1,0:T(8,128)(2,1)S(1)}, bf16[256,128]{1,0:T(8,128)(2,1)S(1)}, u32[]{:S(2)}, u32[]{:S(2)}) collective-permute-start(bf16[256,128]{1,0:T(8,128)(2,1)S(1)} %get-tuple-element.24.refs_0_), channel_id=1, source_target_pairs={{0,16},{8,24},{16,0},{24,8},{1,17},{9,25},{17,1},{25,9},{2,18},{10... | collective-permute-start | bytes 196616 | tf_op jit(solution)/shard_map/ppermute | solution.py:40
  8.3 8.6 %collective-permute-start.4 = (bf16[256,128]{1,0:T(8,128)(2,1)S(1)}, bf16[256,128]{1,0:T(8,128)(2,1)S(1)}, u32[]{:S(2)}, u32[]{:S(2)}) collective-permute-start(bf16[256,128]{1,0:T(8,128)(2,1)S(1)} %get-tuple-element.24.refs_0_), channel_id=1, source_target_pairs={{0,8},{8,16},{16,24},{24,0},{1,9},{9,17},{17,25},{25,1},{2,10},{10... | collective-permute-start | bytes 196616 | tf_op jit(solution)/shard_map/ppermute | solution.py:40
  9.1 7.7 %collective-permute-start.5 = (bf16[256,128]{1,0:T(8,128)(2,1)S(1)}, bf16[256,128]{1,0:T(8,128)(2,1)S(1)}, u32[]{:S(2)}, u32[]{:S(2)}) collective-permute-start(bf16[256,128]{1,0:T(8,128)(2,1)S(1)} %get-tuple-element.24.refs_0_), channel_id=1, source_target_pairs={{0,24},{8,0},{16,8},{24,16},{1,25},{9,1},{17,9},{25,17},{2,26},{10... | collective-permute-start | bytes 196616 | tf_op jit(solution)/shard_map/ppermute | solution.py:40
  18.3 4.4 %collective-permute-start.8 = (bf16[256,512]{1,0:T(8,128)(2,1)S(1)}, bf16[256,512]{1,0:T(8,128)(2,1)S(1)}, u32[]{:S(2)}, u32[]{:S(2)}) collective-permute-start(bf16[256,512]{1,0:T(8,128)(2,1)S(1)} %shard_map.58.refs_0_), channel_id=1, source_target_pairs={{0,1},{1,0},{2,3},{3,2},{4,5},{5,4},{6,7},{7,6},{8,9},{9,8},{10,11... | collective-permute-start | bytes 786440 | tf_op jit(solution)/shard_map/ppermute | solution.py:45
  18.4 4.6 %collective-permute-start.9 = (bf16[256,512]{1,0:T(8,128)(2,1)S(1)}, bf16[256,512]{1,0:T(8,128)(2,1)S(1)}, u32[]{:S(2)}, u32[]{:S(2)}) collective-permute-start(bf16[256,512]{1,0:T(8,128)(2,1)S(1)} %shard_map.59.refs_1_), channel_id=1, source_target_pairs={{0,1},{1,0},{2,3},{3,2},{4,5},{5,4},{6,7},{7,6},{8,9},{9,8},{10,11... | collective-permute-start | bytes 786440 | tf_op jit(solution)/shard_map/ppermute | solution.py:45
  18.9 9.2 %collective-permute-start.7 = (bf16[256,512]{1,0:T(8,128)(2,1)S(1)}, bf16[256,512]{1,0:T(8,128)(2,1)S(1)}, u32[]{:S(2)}, u32[]{:S(2)}) collective-permute-start(bf16[256,512]{1,0:T(8,128)(2,1)S(1)} %shard_map.59.refs_1_), channel_id=1, source_target_pairs={{0,4},{1,5},{2,6},{3,7},{4,0},{5,1},{6,2},{7,3},{8,12},{9,13},{10,... | collective-permute-start | bytes 786440 | tf_op jit(solution)/shard_map/ppermute | solution.py:45
  20.6 9.2 %collective-permute-start.6 = (bf16[256,512]{1,0:T(8,128)(2,1)S(1)}, bf16[256,512]{1,0:T(8,128)(2,1)S(1)}, u32[]{:S(2)}, u32[]{:S(2)}) collective-permute-start(bf16[256,512]{1,0:T(8,128)(2,1)S(1)} %shard_map.58.refs_0_), channel_id=1, source_target_pairs={{0,2},{1,3},{2,0},{3,1},{4,6},{5,7},{6,4},{7,5},{8,10},{9,11},{10,... | collective-permute-start | bytes 786440 | tf_op jit(solution)/shard_map/ppermute | solution.py:45
  22.1 10.8 %collective-permute-start.15 = (bf16[256,512]{1,0:T(8,128)(2,1)S(1)}, bf16[256,512]{1,0:T(8,128)(2,1)S(1)}, u32[]{:S(2)}, u32[]{:S(2)}) collective-permute-start(bf16[256,512]{1,0:T(8,128)(2,1)S(1)} %shard_map.58.refs_0_), channel_id=1, source_target_pairs={{0,4},{1,5},{2,6},{3,7},{4,0},{5,1},{6,2},{7,3},{8,12},{9,13},{10,... | collective-permute-start | bytes 786440 | tf_op jit(solution)/shard_map/ppermute | solution.py:45
  22.6 11.9 %collective-permute-start.13 = (bf16[256,512]{1,0:T(8,128)(2,1)S(1)}, bf16[256,512]{1,0:T(8,128)(2,1)S(1)}, u32[]{:S(2)}, u32[]{:S(2)}) collective-permute-start(bf16[256,512]{1,0:T(8,128)(2,1)S(1)} %shard_map.59.refs_1_), channel_id=1, source_target_pairs={{0,2},{1,3},{2,0},{3,1},{4,6},{5,7},{6,4},{7,5},{8,10},{9,11},{10,... | collective-permute-start | bytes 786440 | tf_op jit(solution)/shard_map/ppermute | solution.py:45
  29.8 4.7 %collective-permute-start.11 = (bf16[256,512]{1,0:T(8,128)(2,1)S(1)}, bf16[256,512]{1,0:T(8,128)(2,1)S(1)}, u32[]{:S(2)}, u32[]{:S(2)}) collective-permute-start(bf16[256,512]{1,0:T(8,128)(2,1)S(1)} %collective-permute-done.6.refs_1_), channel_id=1, source_target_pairs={{0,1},{1,0},{2,3},{3,2},{4,5},{5,4},{6,7},{7,6},{8,9},{9,8},{10,11... | collective-permute-start | bytes 786440 | tf_op jit(solution)/shard_map/ppermute | solution.py:45
  29.8 5.2 %collective-permute-start.12 = (bf16[256,512]{1,0:T(8,128)(2,1)S(1)}, bf16[256,512]{1,0:T(8,128)(2,1)S(1)}, u32[]{:S(2)}, u32[]{:S(2)}) collective-permute-start(bf16[256,512]{1,0:T(8,128)(2,1)S(1)} %collective-permute-done.7.refs_3_), channel_id=1, source_target_pairs={{0,1},{1,0},{2,3},{3,2},{4,5},{5,4},{6,7},{7,6},{8,9},{9,8},{10,11... | collective-permute-start | bytes 786440 | tf_op jit(solution)/shard_map/ppermute | solution.py:45
  30.4 8.2 %collective-permute-start.10 = (bf16[256,512]{1,0:T(8,128)(2,1)S(1)}, bf16[256,512]{1,0:T(8,128)(2,1)S(1)}, u32[]{:S(2)}, u32[]{:S(2)}) collective-permute-start(bf16[256,512]{1,0:T(8,128)(2,1)S(1)} %collective-permute-done.6.refs_1_), channel_id=1, source_target_pairs={{0,4},{1,5},{2,6},{3,7},{4,0},{5,1},{6,2},{7,3},{8,12},{9,13},{10,... | collective-permute-start | bytes 786440 | tf_op jit(solution)/shard_map/ppermute | solution.py:45
  32.9 7.4 %collective-permute-start.17 = (bf16[256,512]{1,0:T(8,128)(2,1)S(1)}, bf16[256,512]{1,0:T(8,128)(2,1)S(1)}, u32[]{:S(2)}, u32[]{:S(2)}) collective-permute-start(bf16[256,512]{1,0:T(8,128)(2,1)S(1)} %collective-permute-done.7.refs_3_), channel_id=1, source_target_pairs={{0,2},{1,3},{2,0},{3,1},{4,6},{5,7},{6,4},{7,5},{8,10},{9,11},{10,... | collective-permute-start | bytes 786440 | tf_op jit(solution)/shard_map/ppermute | solution.py:45
  34.5 1.8 %collective-permute-start.16 = (bf16[256,512]{1,0:T(8,128)(2,1)S(1)}, bf16[256,512]{1,0:T(8,128)(2,1)S(1)}, u32[]{:S(2)}, u32[]{:S(2)}) collective-permute-start(bf16[256,512]{1,0:T(8,128)(2,1)S(1)} %collective-permute-done.15.refs_3_), channel_id=1, source_target_pairs={{0,1},{1,0},{2,3},{3,2},{4,5},{5,4},{6,7},{7,6},{8,9},{9,8},{10,11... | collective-permute-start | bytes 786440 | tf_op jit(solution)/shard_map/ppermute | solution.py:45
  34.5 1.9 %collective-permute-start.14 = (bf16[256,512]{1,0:T(8,128)(2,1)S(1)}, bf16[256,512]{1,0:T(8,128)(2,1)S(1)}, u32[]{:S(2)}, u32[]{:S(2)}) collective-permute-start(bf16[256,512]{1,0:T(8,128)(2,1)S(1)} %collective-permute-done.13.refs_1_), channel_id=1, source_target_pairs={{0,1},{1,0},{2,3},{3,2},{4,5},{5,4},{6,7},{7,6},{8,9},{9,8},{10,11... | collective-permute-start | bytes 786440 | tf_op jit(solution)/shard_map/ppermute | solution.py:45
  40.3 1.5 %collective-permute-start.19 = (bf16[256,512]{1,0:T(8,128)(2,1)S(1)}, bf16[256,512]{1,0:T(8,128)(2,1)S(1)}, u32[]{:S(2)}, u32[]{:S(2)}) collective-permute-start(bf16[256,512]{1,0:T(8,128)(2,1)S(1)} %collective-permute-done.17.refs_2_), channel_id=1, source_target_pairs={{0,1},{1,0},{2,3},{3,2},{4,5},{5,4},{6,7},{7,6},{8,9},{9,8},{10,11... | collective-permute-start | bytes 786440 | tf_op jit(solution)/shard_map/ppermute | solution.py:45
  40.3 1.9 %collective-permute-start.18 = (bf16[256,512]{1,0:T(8,128)(2,1)S(1)}, bf16[256,512]{1,0:T(8,128)(2,1)S(1)}, u32[]{:S(2)}, u32[]{:S(2)}) collective-permute-start(bf16[256,512]{1,0:T(8,128)(2,1)S(1)} %collective-permute-done.10.refs_1_), channel_id=1, source_target_pairs={{0,1},{1,0},{2,3},{3,2},{4,5},{5,4},{6,7},{7,6},{8,9},{9,8},{10,11... | collective-permute-start | bytes 786440 | tf_op jit(solution)/shard_map/ppermute | solution.py:45

commit v8 on v6

--- a/solution.py
+++ b/solution.py
@@ -163,36 +163,48 @@
         in_specs=[VMEM] * (2 + len(key_parts)),
         out_specs=VMEM,
         compiler_params=params(8 + (min(rows, 512) * keys * 16 >> 20)),
-        cost_estimate=cost(8 * blocks_dev * rows * keys * HEAD_SIZE, 4 << 20),
+        cost_estimate=cost(400 * blocks_dev * rows * keys * HEAD_SIZE, 4 << 20),
     )(stacked, mask, *key_parts)
 
 
-def values_kernel(first, group, weights_ref, *refs):
-    value_refs, out_ref = refs[:-1], refs[-1]
-    values = jnp.concatenate([ref[...] for ref in value_refs], axis=0)
+def values_kernel(count, weights_ref, *refs):
+    values = jnp.concatenate([ref[...] for ref in refs[:count]], axis=0)
     values = jnp.concatenate([values, jnp.ones_like(values)], axis=1)
-    for a in range(weights_ref.shape[0]):
-        summed = jnp.dot(
-            weights_ref[a, first * BLOCK : (first + group) * BLOCK, :],
-            values,
-            preferred_element_type=jnp.float32,
-        )
-        result = (summed[:, :HEAD_SIZE] / summed[:, HEAD_SIZE:]).astype(jnp.bfloat16)
-        for i in range(group):
-            out_ref[a * BLOCK : (a + 1) * BLOCK, i * HEAD_SIZE : (i + 1) * HEAD_SIZE] = result[
-                i * BLOCK : (i + 1) * BLOCK
-            ]
-
-
-def attended_of(weights, value_parts, first, group):
-    blocks_dev, _, keys = weights.shape
-    return pl.pallas_call(
-        functools.partial(values_kernel, first, group),
-        out_shape=held((blocks_dev * BLOCK, group * HEAD_SIZE)),
+    whole_ref, *piece_refs = refs[count:]
+    blocks_dev, rows, _ = weights_ref.shape
+    heads = rows // BLOCK
+    pieces = max(1, len(piece_refs))
+    group = heads // pieces
+    for piece in range(pieces):
+        for a in range(blocks_dev):
+            first = piece * group
+            summed = jnp.dot(
+                weights_ref[a, first * BLOCK : (first + group) * BLOCK, :],
+                values,
+                preferred_element_type=jnp.float32,
+            )
+            result = (summed[:, :HEAD_SIZE] / summed[:, HEAD_SIZE:]).astype(jnp.bfloat16)
+            for i in range(group):
+                part = result[i * BLOCK : (i + 1) * BLOCK]
+                tokens = slice(a * BLOCK, (a + 1) * BLOCK)
+                column = (first + i) * HEAD_SIZE
+                whole_ref[tokens, column : column + HEAD_SIZE] = part
+                if piece_refs:
+                    column = i * HEAD_SIZE
+                    piece_refs[piece][tokens, column : column + HEAD_SIZE] = part
+
+
+def attended_of(weights, value_parts, pieces):
+    blocks_dev, rows, keys = weights.shape
+    tokens, width = blocks_dev * BLOCK, rows // BLOCK * HEAD_SIZE
+    shapes = [held((tokens, width))] + [held((tokens, width // 2))] * pieces
+    return pl.pallas_call(
+        functools.partial(values_kernel, len(value_parts)),
+        out_shape=shapes,
         in_specs=[VMEM] * (1 + len(value_parts)),
-        out_specs=VMEM,
+        out_specs=[VMEM] * len(shapes),
         compiler_params=params(16),
-        cost_estimate=cost(4 * blocks_dev * BLOCK * group * keys * HEAD_SIZE, 1 << 20),
+        cost_estimate=cost(400 * tokens * width * keys, 1 << 20),
     )(weights, *value_parts)
 
 
@@ -207,15 +219,18 @@
     copies = []
     for n in range(0, columns, tile):
         total = None if fresh else total_ref[:, n : n + tile]
-        for (bits, offset), part in zip(places, parts):
-            depth = part.shape[1]
-            row = pl.multiple_of((me ^ bits) * width + offset, depth)
-            term = jnp.dot(
-                part[...],
-                weight_ref[pl.ds(row, depth), n : n + tile],
-                preferred_element_type=jnp.float32,
-            )
-            total = term if total is None else total + term
+        for place, part in zip(places, parts):
+            several = place if isinstance(place[0], tuple) else (place,)
+            rows = out_ref.shape[0]
+            for index, (bits, offset) in enumerate(several):
+                depth = part.shape[1]
+                row = pl.multiple_of((me ^ bits) * width + offset, HEAD_SIZE)
+                term = jnp.dot(
+                    part[index * rows : (index + 1) * rows, :],
+                    weight_ref[pl.ds(row, depth), n : n + tile],
+                    preferred_element_type=jnp.float32,
+                )
+                total = term if total is None else total + term
         if last:
             held_ref, sems = refs[len(places) + 1 :]
             held_ref[:, n : n + tile] = total.astype(held_ref.dtype)
@@ -270,7 +285,7 @@
     stacked, mask = stacked_of(queries, block_pattern, steps, count if count == 4 else None)
     weights = weights_of(stacked, mask, key_parts)
     if lax.axis_size("head") != 8:
-        att = attended_of(weights, value_parts, 0, heads_dev)
+        (att,) = attended_of(weights, value_parts, 0)
         mixed = jnp.dot(
             lax.all_gather(att, "head", axis=1, tiled=True),
             out_weight,
@@ -280,36 +295,28 @@
 
     barrier = lax.optimization_barrier
     weight = pltpu.with_memory_space_constraint(out_weight, pltpu.VMEM)
-    half = heads_dev // 2
-    a = attended_of(weights, value_parts, 0, half)
-    b = attended_of(weights, value_parts, half, half)
+    own, a, b = attended_of(weights, value_parts, 2)
+    width, half = heads_dev * HEAD_SIZE, heads_dev * HEAD_SIZE // 2
     xa = swapped(a, "head", 2)
     yb = swapped(b, "head", 4)
     xb = swapped(b, "head", 2)
     ya = swapped(a, "head", 4)
-    a, b = barrier((a, b))
-    sa = swapped(a, "head", 1)
-    sb = swapped(b, "head", 1)
-    width, half = heads_dev * HEAD_SIZE, heads_dev * HEAD_SIZE // 2
-    mixed = projected(
-        None, weight, width, ((0, 0), (0, half), (1, 0), (1, half)), [a, b, sa, sb]
-    )
-    xa, mixed = barrier((xa, mixed))
+    sibling = swapped(own, "head", 1)
+    mixed = projected(None, weight, width, ((0, 0), (1, 0)), [own, sibling])
     da = swapped(xa, "head", 4)
     yb, mixed = barrier((yb, mixed))
     db = swapped(yb, "head", 2)
-    xas, ybs = swapped(xa, "head", 1), swapped(yb, "head", 1)
-    mixed = projected(
-        mixed, weight, width, ((2, 0), (3, 0), (4, half), (5, half)), [xa, xas, yb, ybs]
-    )
-    xbs, yas = swapped(xb, "head", 1), swapped(ya, "head", 1)
-    mixed = projected(
-        mixed, weight, width, ((2, half), (3, half), (4, 0), (5, 0)), [xb, xbs, ya, yas]
-    )
+    xb, ya, mixed = barrier((xb, ya, mixed))
+    xas = swapped(xa, "head", 1)
+    mixed = projected(mixed, weight, width, ((2, 0), (2, half), (3, 0)), [xa, xb, xas])
+    ybs = swapped(yb, "head", 1)
+    xbs = swapped(xb, "head", 1)
+    yas = swapped(ya, "head", 1)
+    mixed = projected(mixed, weight, width, ((4, 0), (4, half), (5, half), (3, half), (5, 0)), [ya, yb, ybs, xbs, yas])
     da, mixed = barrier((da, mixed))
-    das, dbs = swapped(da, "head", 1), swapped(db, "head", 1)
+    da_s, db_s = swapped(da, "head", 1), swapped(db, "head", 1)
     mixed = projected(mixed, weight, width, ((6, 0), (6, half)), [da, db])
-    return projected(mixed, weight, width, ((7, 0), (7, half)), [das, dbs], True)
+    return projected(mixed, weight, width, ((7, 0), (7, half)), [da_s, db_s], True)
 
 
 def solution(mesh):

time: 43.4 us -> 43.5 us (level)
  waiting for transfers between devices: 11.7 us -> 12.5 us
  starting transfers between devices: 20.1 us -> 19.6 us
    ppermute x14 -> x13, waiting for transfers between devices: 9.99 us -> 10.8 us  [swapped(): lax.ppermute(value, axis, [(source, source ^ bits) for source in range(co...]
    ppermute x14 -> x13, starting transfers between devices: 9.02 us -> 8.55 us  [swapped(): lax.ppermute(value, axis, [(source, source ^ bits) for source in range(co...]
    pallas_call x2 -> x1, Pallas kernels: 1.43 us -> 1.27 us  [attended_of(): pl.pallas_call(functools.partial(values_kernel, len(value_parts)), out_sh...]
  transfers between devices with their start and end apart: 20 -> 19, of which waited for: 10 -> 8; matrix products, arithmetic and copies ran while one was open for 0% -> 0% of each run, Pallas kernels for 17% -> 17%
where the time goes in v8:
time: 43.5 us; the launch traced here: 43.3 us
  starting transfers between devices  19.6 us (45%)
  waiting for transfers between devices  12.5 us (29%)
  Pallas kernels  11.1 us (26%)
    ppermute x6, starting transfers between devices, shifted(): lax.ppermute(value, axis, [(source, (source + steps) % count) for source...  11 us
    ppermute x13, waiting for transfers between devices, swapped(): lax.ppermute(value, axis, [(source, source ^ bits) for source in range(co...  10.8 us
    ppermute x13, starting transfers between devices, swapped(): lax.ppermute(value, axis, [(source, source ^ bits) for source in range(co...  8.55 us
    pallas_call x5, Pallas kernels, projected(): pl.pallas_call(functools.partial(projection_kernel, places, width, fresh,...  5.9 us
    pallas_call x1, Pallas kernels, weights_of(): pl.pallas_call(weights_kernel, out_shape=held((blocks_dev, rows, keys)),...  1.84 us
    ppermute x6, waiting for transfers between devices, shifted(): lax.ppermute(value, axis, [(source, (source + steps) % count) for source...  1.71 us
    pallas_call x1, Pallas kernels, attended_of(): pl.pallas_call(functools.partial(values_kernel, len(value_parts)), out_sh...  1.27 us
    pallas_call x1, Pallas kernels, stacked_of(): pl.pallas_call(functools.partial(stack_kernel, steps, count), out_shape=[...  1.15 us
  transfers between devices with their start and end apart: 19, of which 8 were waited for; matrix products, arithmetic and copies ran while one was open for 0% of the time, Pallas kernels for 17%

profile of v8, /device:TPU:0, one launch (start us, length us, event | category | flops | bytes accessed | tf_op | source)
XLA Modules:
  0.0 43.3 jit_solution(1644232139831292625)
XLA Ops:
  0.0 0.9 %shard_map.55 = (bf16[256,128]{1,0:T(8,128)(2,1)S(1)}, bf16[256,128]{1,0:T(8,128)(2,1)S(1)}) custom-call(bf16[256,1024]{1,0:T(8,128)(2,1)} %keys_ref.1, bf16[256,1024]{1,0:T(8,128)(2,1)} %values_ref.1), custom_call_target="tpu_custom_call" | custom-call | bytes 262144 | tf_op jit(solution)/shard_map/pallas_call | solution.py:68
  0.9 3.1 %collective-permute-start = (bf16[256,128]{1,0:T(8,128)(2,1)S(1)}, bf16[256,128]{1,0:T(8,128)(2,1)S(1)}, u32[]{:S(2)}, u32[]{:S(2)}) collective-permute-start(bf16[256,128]{1,0:T(8,128)(2,1)S(1)} %get-tuple-element.21.refs_0_), channel_id=1, source_target_pairs={{0,8},{8,16},{16,24},{24,0},{1,9},{9,17},{17,25},{25,1},{2,10},{10... | collective-permute-start | bytes 196616 | tf_op jit(solution)/shard_map/ppermute | solution.py:40
  4.0 2.6 %collective-permute-start.1 = (bf16[256,128]{1,0:T(8,128)(2,1)S(1)}, bf16[256,128]{1,0:T(8,128)(2,1)S(1)}, u32[]{:S(2)}, u32[]{:S(2)}) collective-permute-start(bf16[256,128]{1,0:T(8,128)(2,1)S(1)} %get-tuple-element.21.refs_0_), channel_id=1, source_target_pairs={{0,16},{8,24},{16,0},{24,8},{1,17},{9,25},{17,1},{25,9},{2,18},{10... | collective-permute-start | bytes 196616 | tf_op jit(solution)/shard_map/ppermute | solution.py:40
  6.6 1.3 %collective-permute-start.2 = (bf16[256,128]{1,0:T(8,128)(2,1)S(1)}, bf16[256,128]{1,0:T(8,128)(2,1)S(1)}, u32[]{:S(2)}, u32[]{:S(2)}) collective-permute-start(bf16[256,128]{1,0:T(8,128)(2,1)S(1)} %get-tuple-element.21.refs_0_), channel_id=1, source_target_pairs={{0,24},{8,0},{16,8},{24,16},{1,25},{9,1},{17,9},{25,17},{2,26},{10... | collective-permute-start | bytes 196616 | tf_op jit(solution)/shard_map/ppermute | solution.py:40
  7.9 0.2 collective-permute-start.3
  8.1 0.8 %collective-permute-start.4 = (bf16[256,128]{1,0:T(8,128)(2,1)S(1)}, bf16[256,128]{1,0:T(8,128)(2,1)S(1)}, u32[]{:S(2)}, u32[]{:S(2)}) collective-permute-start(bf16[256,128]{1,0:T(8,128)(2,1)S(1)} %get-tuple-element.26.refs_0_), channel_id=1, source_target_pairs={{0,8},{8,16},{16,24},{24,0},{1,9},{9,17},{17,25},{25,1},{2,10},{10... | collective-permute-start | bytes 196616 | tf_op jit(solution)/shard_map/ppermute | solution.py:40
  8.9 0.0 collective-permute-done.refs_2_
  8.9 3.0 %collective-permute-start.5 = (bf16[256,128]{1,0:T(8,128)(2,1)S(1)}, bf16[256,128]{1,0:T(8,128)(2,1)S(1)}, u32[]{:S(2)}, u32[]{:S(2)}) collective-permute-start(bf16[256,128]{1,0:T(8,128)(2,1)S(1)} %get-tuple-element.26.refs_0_), channel_id=1, source_target_pairs={{0,24},{8,0},{16,8},{24,16},{1,25},{9,1},{17,9},{25,17},{2,26},{10... | collective-permute-start | bytes 196616 | tf_op jit(solution)/shard_map/ppermute | solution.py:40
  11.9 1.2 %shard_map.56 = (bf16[2,1024,128]{2,1,0:T(8,128)(2,1)S(1)}, bf16[2,1024,128]{2,1,0:T(8,128)(2,1)S(1)}) custom-call(bf16[256,1024]{1,0:T(8,128)(2,1)} %q_ref, s32[8,8]{1,0:T(8,128)} %pattern_ref.1), custom_call_target="tpu_custom_call" | custom-call | bytes 1048576 | tf_op jit(solution)/shard_map/pallas_call | solution.py:119
  13.1 0.0 collective-permute-done.1.refs_1_
  13.1 0.0 collective-permute-done.2.refs_3_
  13.1 1.8 %shard_map.57.weights_ref = bf16[2,1024,1024]{2,1,0:T(8,128)(2,1)S(1)} custom-call(bf16[2,1024,128]{2,1,0:T(8,128)(2,1)S(1)} %get-tuple-element.23.q_ref, bf16[2,1024,128]{2,1,0:T(8,128)(2,1)S(1)} %get-tuple-element.24.mask_ref, bf16[256,128]{1,0:T(8,128)(2,1)S(1)} %get-tuple-element.21.refs_0_, bf16[256,128]{1,0:T(8,128)(2,1)S(1)} %collective-permute-done.1.refs_1_, ...), custom_call_target="tpu_custom_call" | custom-call | flops 107374182400 | bytes 4194304 | tf_op jit(solution)/shard_map/pallas_call | solution.py:160
  15.0 0.0 copy-start
  15.0 1.7 %collective-permute-done.3.refs_1_ = bf16[256,128]{1,0:T(8,128)(2,1)S(1)} collective-permute-done((bf16[256,128]{1,0:T(8,128)(2,1)S(1)}, bf16[256,128]{1,0:T(8,128)(2,1)S(1)}, u32[]{:S(2)}, u32[]{:S(2)}) %collective-permute-start.3) | collective-permute-done | bytes 65568 | tf_op jit(solution)/shard_map/ppermute | solution.py:40
  16.7 0.0 collective-permute-done.4.refs_2_
  16.7 0.0 collective-permute-done.5.refs_3_
  16.7 1.3 %shard_map.58 = (bf16[256,1024]{1,0:T(8,128)(2,1)S(1)}, bf16[256,512]{1,0:T(8,128)(2,1)S(1)}, bf16[256,512]{1,0:T(8,128)(2,1)S(1)}) custom-call(bf16[2,1024,1024]{2,1,0:T(8,128)(2,1)S(1)} %shard_map.57.weights_ref, bf16[256,128]{1,0:T(8,128)(2,1)S(1)} %get-tuple-element.26.refs_0_, bf16[256,128]{1,0:T(8,128)(2,1)S(1)} %collective-permute-done.3.refs_1_, ...), custom_call_target="tpu_custom_call" | custom-call | flops 107374182400 | bytes 1048576 | tf_op jit(solution)/shard_map/pallas_call | solution.py:201
  18.0 0.1 collective-permute-start.11
  18.0 1.8 %collective-permute-start.6 = (bf16[256,512]{1,0:T(8,128)(2,1)S(1)}, bf16[256,512]{1,0:T(8,128)(2,1)S(1)}, u32[]{:S(2)}, u32[]{:S(2)}) collective-permute-start(bf16[256,512]{1,0:T(8,128)(2,1)S(1)} %get-tuple-element.27), channel_id=1, source_target_pairs={{0,2},{1,3},{2,0},{3,1},{4,6},{5,7},{6,4},{7,5},{8,10},{9,11},{10,... | collective-permute-start | bytes 786440 | tf_op jit(solution)/shard_map/ppermute | solution.py:45
  19.9 1.5 %collective-permute-start.10 = (bf16[256,512]{1,0:T(8,128)(2,1)S(1)}, bf16[256,512]{1,0:T(8,128)(2,1)S(1)}, u32[]{:S(2)}, u32[]{:S(2)}) collective-permute-start(bf16[256,512]{1,0:T(8,128)(2,1)S(1)} %get-tuple-element.28), channel_id=1, source_target_pairs={{0,4},{1,5},{2,6},{3,7},{4,0},{5,1},{6,2},{7,3},{8,12},{9,13},{10,... | collective-permute-start | bytes 786440 | tf_op jit(solution)/shard_map/ppermute | solution.py:45
  21.4 0.5 %collective-permute-start.8 = (bf16[256,512]{1,0:T(8,128)(2,1)S(1)}, bf16[256,512]{1,0:T(8,128)(2,1)S(1)}, u32[]{:S(2)}, u32[]{:S(2)}) collective-permute-start(bf16[256,512]{1,0:T(8,128)(2,1)S(1)} %get-tuple-element.28), channel_id=1, source_target_pairs={{0,2},{1,3},{2,0},{3,1},{4,6},{5,7},{6,4},{7,5},{8,10},{9,11},{10,... | collective-permute-start | bytes 786440 | tf_op jit(solution)/shard_map/ppermute | solution.py:45
  21.9 0.2 collective-permute-start.9
  22.1 5.1 %collective-permute-done.6.refs_1_ = bf16[256,512]{1,0:T(8,128)(2,1)S(1)} collective-permute-done((bf16[256,512]{1,0:T(8,128)(2,1)S(1)}, bf16[256,512]{1,0:T(8,128)(2,1)S(1)}, u32[]{:S(2)}, u32[]{:S(2)}) %collective-permute-start.6) | collective-permute-done | bytes 262176 | tf_op jit(solution)/shard_map/ppermute | solution.py:45
  27.2 0.0 collective-permute-start.12
  27.2 0.0 collective-permute-done.11.refs_1_
  27.2 1.8 %collective-permute-start.7 = (bf16[256,512]{1,0:T(8,128)(2,1)S(1)}, bf16[256,512]{1,0:T(8,128)(2,1)S(1)}, u32[]{:S(2)}, u32[]{:S(2)}) collective-permute-start(bf16[256,512]{1,0:T(8,128)(2,1)S(1)} %collective-permute-done.6.refs_1_), channel_id=1, source_target_pairs={{0,4},{1,5},{2,6},{3,7},{4,0},{5,1},{6,2},{7,3},{8,12},{9,13},{10,... | collective-permute-start | bytes 786440 | tf_op jit(solution)/shard_map/ppermute | solution.py:45
  29.0 0.0 copy-done
  29.0 1.2 %shard_map.59.refs_0_ = f32[256,1024]{1,0:T(8,128)S(1)} custom-call(bf16[8192,1024]{1,0:T(8,128)(2,1)S(1)} %copy-done, bf16[256,1024]{1,0:T(8,128)(2,1)S(1)} %get-tuple-element.29.refs_0_, bf16[256,1024]{1,0:T(8,128)(2,1)S(1)} %collective-permute-done.11.refs_1_), custom_call_target="tpu_custom_call" | custom-call | flops 4294967296 | bytes 1048576 | tf_op jit(solution)/shard_map/pallas_call | solution.py:255
  30.3 0.0 collective-permute-done.10.refs_2_
  30.3 0.3 collective-permute-start.13
  30.6 1.8 %collective-permute-done.8.refs_2_ = bf16[256,512]{1,0:T(8,128)(2,1)S(1)} collective-permute-done((bf16[256,512]{1,0:T(8,128)(2,1)S(1)}, bf16[256,512]{1,0:T(8,128)(2,1)S(1)}, u32[]{:S(2)}, u32[]{:S(2)}) %collective-permute-start.8) | collective-permute-done | bytes 262176 | tf_op jit(solution)/shard_map/ppermute | solution.py:45
  32.4 1.8 %collective-permute-start.16 = (bf16[256,512]{1,0:T(8,128)(2,1)S(1)}, bf16[256,512]{1,0:T(8,128)(2,1)S(1)}, u32[]{:S(2)}, u32[]{:S(2)}) collective-permute-start(bf16[256,512]{1,0:T(8,128)(2,1)S(1)} %collective-permute-done.10.refs_2_), channel_id=1, source_target_pairs={{0,2},{1,3},{2,0},{3,1},{4,6},{5,7},{6,4},{7,5},{8,10},{9,11},{10,... | collective-permute-start | bytes 786440 | tf_op jit(solution)/shard_map/ppermute | solution.py:45
  34.1 0.5 %collective-permute-done.9.refs_1_ = bf16[256,512]{1,0:T(8,128)(2,1)S(1)} collective-permute-done((bf16[256,512]{1,0:T(8,128)(2,1)S(1)}, bf16[256,512]{1,0:T(8,128)(2,1)S(1)}, u32[]{:S(2)}, u32[]{:S(2)}) %collective-permute-start.9) | collective-permute-done | bytes 262176 | tf_op jit(solution)/shard_map/ppermute | solution.py:45
  34.6 0.0 collective-permute-start.14
  34.6 0.0 collective-permute-done.12.refs_3_
  34.6 0.5 %collective-permute-start.15 = (bf16[256,512]{1,0:T(8,128)(2,1)S(1)}, bf16[256,512]{1,0:T(8,128)(2,1)S(1)}, u32[]{:S(2)}, u32[]{:S(2)}) collective-permute-start(bf16[256,512]{1,0:T(8,128)(2,1)S(1)} %collective-permute-done.9.refs_1_), channel_id=1, source_target_pairs={{0,1},{1,0},{2,3},{3,2},{4,5},{5,4},{6,7},{7,6},{8,9},{9,8},{10,11... | collective-permute-start | bytes 786440 | tf_op jit(solution)/shard_map/ppermute | solution.py:45
  35.1 1.0 %shard_map.60.refs_0_ = f32[256,1024]{1,0:T(8,128)S(1)} custom-call(bf16[8192,1024]{1,0:T(8,128)(2,1)S(1)} %copy-done, f32[256,1024]{1,0:T(8,128)S(1)} %shard_map.59.refs_0_, bf16[256,512]{1,0:T(8,128)(2,1)S(1)} %collective-permute-done.6.refs_1_, bf16[256,512]{1,0:T(8,128)(2,1)S(1)} %collective-permute-done.8.refs_2_, ...), custom_call_target="tpu_custom_call" | custom-call | flops 3221225472 | bytes 1048576 | tf_op jit(solution)/shard_map/pallas_call | solution.py:255
  36.1 0.0 collective-permute-done.14.refs_4_
  36.2 0.4 collective-permute-done.15.refs_5_
  36.5 0.0 collective-permute-done.13.refs_3_
  36.5 1.5 %shard_map.61.refs_0_ = f32[256,1024]{1,0:T(8,128)S(1)} custom-call(bf16[8192,1024]{1,0:T(8,128)(2,1)S(1)} %copy-done, f32[256,1024]{1,0:T(8,128)S(1)} %shard_map.60.refs_0_, bf16[256,512]{1,0:T(8,128)(2,1)S(1)} %collective-permute-done.9.refs_1_, bf16[256,512]{1,0:T(8,128)(2,1)S(1)} %collective-permute-done.10.refs_2_, ...), custom_call_target="tpu_custom_call" | custom-call | flops 5368709120 | bytes 1048576 | tf_op jit(solution)/shard_map/pallas_call | solution.py:255
  38.1 1.4 %collective-permute-done.7.refs_1_ = bf16[256,512]{1,0:T(8,128)(2,1)S(1)} collective-permute-done((bf16[256,512]{1,0:T(8,128)(2,1)S(1)}, bf16[256,512]{1,0:T(8,128)(2,1)S(1)}, u32[]{:S(2)}, u32[]{:S(2)}) %collective-permute-start.7) | collective-permute-done | bytes 262176 | tf_op jit(solution)/shard_map/ppermute | solution.py:45
  39.5 0.0 collective-permute-start.17
  39.5 0.8 %collective-permute-done.16.refs_2_ = bf16[256,512]{1,0:T(8,128)(2,1)S(1)} collective-permute-done((bf16[256,512]{1,0:T(8,128)(2,1)S(1)}, bf16[256,512]{1,0:T(8,128)(2,1)S(1)}, u32[]{:S(2)}, u32[]{:S(2)}) %collective-permute-start.16) | collective-permute-done | bytes 262176 | tf_op jit(solution)/shard_map/ppermute | solution.py:45
  40.3 0.0 collective-permute-start.18
  40.3 0.7 %shard_map.62.refs_0_ = f32[256,1024]{1,0:T(8,128)S(1)} custom-call(bf16[8192,1024]{1,0:T(8,128)(2,1)S(1)} %copy-done, f32[256,1024]{1,0:T(8,128)S(1)} %shard_map.61.refs_0_, bf16[256,512]{1,0:T(8,128)(2,1)S(1)} %collective-permute-done.7.refs_1_, bf16[256,512]{1,0:T(8,128)(2,1)S(1)} %collective-permute-done.16.refs_2_), custom_call_target="tpu_custom_call" | custom-call | flops 2147483648 | bytes 1048576 | tf_op jit(solution)/shard_map/pallas_call | solution.py:255
  41.0 0.0 collective-permute-done.17.refs_1_
  41.0 0.8 %collective-permute-done.18.refs_2_ = bf16[256,512]{1,0:T(8,128)(2,1)S(1)} collective-permute-done((bf16[256,512]{1,0:T(8,128)(2,1)S(1)}, bf16[256,512]{1,0:T(8,128)(2,1)S(1)}, u32[]{:S(2)}, u32[]{:S(2)}) %collective-permute-start.18) | collective-permute-done | bytes 262176 | tf_op jit(solution)/shard_map/ppermute | solution.py:45
  41.8 1.5 %shard_map.63 = bf16[256,1024]{1,0:T(8,128)(2,1)} custom-call(bf16[8192,1024]{1,0:T(8,128)(2,1)S(1)} %copy-done, f32[256,1024]{1,0:T(8,128)S(1)} %shard_map.62.refs_0_, bf16[256,512]{1,0:T(8,128)(2,1)S(1)} %collective-permute-done.17.refs_1_, bf16[256,512]{1,0:T(8,128)(2,1)S(1)} %collective-permute-done.18.refs_2_), custom_call_target="tpu_custom_call" | custom-call | flops 2147483648 | bytes 1048576 | tf_op jit(solution)/shard_map/pallas_call | solution.py:255
Async XLA Ops:
  0.9 8.0 %collective-permute-start = (bf16[256,128]{1,0:T(8,128)(2,1)S(1)}, bf16[256,128]{1,0:T(8,128)(2,1)S(1)}, u32[]{:S(2)}, u32[]{:S(2)}) collective-permute-start(bf16[256,128]{1,0:T(8,128)(2,1)S(1)} %get-tuple-element.21.refs_0_), channel_id=1, source_target_pairs={{0,8},{8,16},{16,24},{24,0},{1,9},{9,17},{17,25},{25,1},{2,10},{10... | collective-permute-start | bytes 196616 | tf_op jit(solution)/shard_map/ppermute | solution.py:40
  4.0 9.1 %collective-permute-start.1 = (bf16[256,128]{1,0:T(8,128)(2,1)S(1)}, bf16[256,128]{1,0:T(8,128)(2,1)S(1)}, u32[]{:S(2)}, u32[]{:S(2)}) collective-permute-start(bf16[256,128]{1,0:T(8,128)(2,1)S(1)} %get-tuple-element.21.refs_0_), channel_id=1, source_target_pairs={{0,16},{8,24},{16,0},{24,8},{1,17},{9,25},{17,1},{25,9},{2,18},{10... | collective-permute-start | bytes 196616 | tf_op jit(solution)/shard_map/ppermute | solution.py:40
  6.6 6.5 %collective-permute-start.2 = (bf16[256,128]{1,0:T(8,128)(2,1)S(1)}, bf16[256,128]{1,0:T(8,128)(2,1)S(1)}, u32[]{:S(2)}, u32[]{:S(2)}) collective-permute-start(bf16[256,128]{1,0:T(8,128)(2,1)S(1)} %get-tuple-element.21.refs_0_), channel_id=1, source_target_pairs={{0,24},{8,0},{16,8},{24,16},{1,25},{9,1},{17,9},{25,17},{2,26},{10... | collective-permute-start | bytes 196616 | tf_op jit(solution)/shard_map/ppermute | solution.py:40
  7.9 8.8 %collective-permute-start.3 = (bf16[256,128]{1,0:T(8,128)(2,1)S(1)}, bf16[256,128]{1,0:T(8,128)(2,1)S(1)}, u32[]{:S(2)}, u32[]{:S(2)}) collective-permute-start(bf16[256,128]{1,0:T(8,128)(2,1)S(1)} %get-tuple-element.26.refs_0_), channel_id=1, source_target_pairs={{0,16},{8,24},{16,0},{24,8},{1,17},{9,25},{17,1},{25,9},{2,18},{10... | collective-permute-start | bytes 196616 | tf_op jit(solution)/shard_map/ppermute | solution.py:40
  8.1 8.6 %collective-permute-start.4 = (bf16[256,128]{1,0:T(8,128)(2,1)S(1)}, bf16[256,128]{1,0:T(8,128)(2,1)S(1)}, u32[]{:S(2)}, u32[]{:S(2)}) collective-permute-start(bf16[256,128]{1,0:T(8,128)(2,1)S(1)} %get-tuple-element.26.refs_0_), channel_id=1, source_target_pairs={{0,8},{8,16},{16,24},{24,0},{1,9},{9,17},{17,25},{25,1},{2,10},{10... | collective-permute-start | bytes 196616 | tf_op jit(solution)/shard_map/ppermute | solution.py:40
  8.9 7.7 %collective-permute-start.5 = (bf16[256,128]{1,0:T(8,128)(2,1)S(1)}, bf16[256,128]{1,0:T(8,128)(2,1)S(1)}, u32[]{:S(2)}, u32[]{:S(2)}) collective-permute-start(bf16[256,128]{1,0:T(8,128)(2,1)S(1)} %get-tuple-element.26.refs_0_), channel_id=1, source_target_pairs={{0,24},{8,0},{16,8},{24,16},{1,25},{9,1},{17,9},{25,17},{2,26},{10... | collective-permute-start | bytes 196616 | tf_op jit(solution)/shard_map/ppermute | solution.py:40
  15.0 14.0 %copy-start = (bf16[8192,1024]{1,0:T(8,128)(2,1)S(1)}, bf16[8192,1024]{1,0:T(8,128)(2,1)}, u32[]{:S(2)}) copy-start(bf16[8192,1024]{1,0:T(8,128)(2,1)} %weight_ref.9) | copy-start | bytes 50331652
  18.0 9.3 %collective-permute-start.11 = (bf16[256,1024]{1,0:T(8,128)(2,1)S(1)}, bf16[256,1024]{1,0:T(8,128)(2,1)S(1)}, u32[]{:S(2)}, u32[]{:S(2)}) collective-permute-start(bf16[256,1024]{1,0:T(8,128)(2,1)S(1)} %get-tuple-element.29.refs_0_), channel_id=1, source_target_pairs={{0,1},{1,0},{2,3},{3,2},{4,5},{5,4},{6,7},{7,6},{8,9},{9,8},{10,11... | collective-permute-start | bytes 1572872 | tf_op jit(solution)/shard_map/ppermute | solution.py:45
  18.0 9.2 %collective-permute-start.6 = (bf16[256,512]{1,0:T(8,128)(2,1)S(1)}, bf16[256,512]{1,0:T(8,128)(2,1)S(1)}, u32[]{:S(2)}, u32[]{:S(2)}) collective-permute-start(bf16[256,512]{1,0:T(8,128)(2,1)S(1)} %get-tuple-element.27), channel_id=1, source_target_pairs={{0,2},{1,3},{2,0},{3,1},{4,6},{5,7},{6,4},{7,5},{8,10},{9,11},{10,... | collective-permute-start | bytes 786440 | tf_op jit(solution)/shard_map/ppermute | solution.py:45
  19.9 10.4 %collective-permute-start.10 = (bf16[256,512]{1,0:T(8,128)(2,1)S(1)}, bf16[256,512]{1,0:T(8,128)(2,1)S(1)}, u32[]{:S(2)}, u32[]{:S(2)}) collective-permute-start(bf16[256,512]{1,0:T(8,128)(2,1)S(1)} %get-tuple-element.28), channel_id=1, source_target_pairs={{0,4},{1,5},{2,6},{3,7},{4,0},{5,1},{6,2},{7,3},{8,12},{9,13},{10,... | collective-permute-start | bytes 786440 | tf_op jit(solution)/shard_map/ppermute | solution.py:45
  21.4 11.0 %collective-permute-start.8 = (bf16[256,512]{1,0:T(8,128)(2,1)S(1)}, bf16[256,512]{1,0:T(8,128)(2,1)S(1)}, u32[]{:S(2)}, u32[]{:S(2)}) collective-permute-start(bf16[256,512]{1,0:T(8,128)(2,1)S(1)} %get-tuple-element.28), channel_id=1, source_target_pairs={{0,2},{1,3},{2,0},{3,1},{4,6},{5,7},{6,4},{7,5},{8,10},{9,11},{10,... | collective-permute-start | bytes 786440 | tf_op jit(solution)/shard_map/ppermute | solution.py:45
  21.9 12.7 %collective-permute-start.9 = (bf16[256,512]{1,0:T(8,128)(2,1)S(1)}, bf16[256,512]{1,0:T(8,128)(2,1)S(1)}, u32[]{:S(2)}, u32[]{:S(2)}) collective-permute-start(bf16[256,512]{1,0:T(8,128)(2,1)S(1)} %get-tuple-element.27), channel_id=1, source_target_pairs={{0,4},{1,5},{2,6},{3,7},{4,0},{5,1},{6,2},{7,3},{8,12},{9,13},{10,... | collective-permute-start | bytes 786440 | tf_op jit(solution)/shard_map/ppermute | solution.py:45
  27.2 7.4 %collective-permute-start.12 = (bf16[256,512]{1,0:T(8,128)(2,1)S(1)}, bf16[256,512]{1,0:T(8,128)(2,1)S(1)}, u32[]{:S(2)}, u32[]{:S(2)}) collective-permute-start(bf16[256,512]{1,0:T(8,128)(2,1)S(1)} %collective-permute-done.6.refs_1_), channel_id=1, source_target_pairs={{0,1},{1,0},{2,3},{3,2},{4,5},{5,4},{6,7},{7,6},{8,9},{9,8},{10,11... | collective-permute-start | bytes 786440 | tf_op jit(solution)/shard_map/ppermute | solution.py:45
  27.2 12.3 %collective-permute-start.7 = (bf16[256,512]{1,0:T(8,128)(2,1)S(1)}, bf16[256,512]{1,0:T(8,128)(2,1)S(1)}, u32[]{:S(2)}, u32[]{:S(2)}) collective-permute-start(bf16[256,512]{1,0:T(8,128)(2,1)S(1)} %collective-permute-done.6.refs_1_), channel_id=1, source_target_pairs={{0,4},{1,5},{2,6},{3,7},{4,0},{5,1},{6,2},{7,3},{8,12},{9,13},{10,... | collective-permute-start | bytes 786440 | tf_op jit(solution)/shard_map/ppermute | solution.py:45
  30.3 6.3 %collective-permute-start.13 = (bf16[256,512]{1,0:T(8,128)(2,1)S(1)}, bf16[256,512]{1,0:T(8,128)(2,1)S(1)}, u32[]{:S(2)}, u32[]{:S(2)}) collective-permute-start(bf16[256,512]{1,0:T(8,128)(2,1)S(1)} %collective-permute-done.10.refs_2_), channel_id=1, source_target_pairs={{0,1},{1,0},{2,3},{3,2},{4,5},{5,4},{6,7},{7,6},{8,9},{9,8},{10,11... | collective-permute-start | bytes 786440 | tf_op jit(solution)/shard_map/ppermute | solution.py:45
  32.4 7.9 %collective-permute-start.16 = (bf16[256,512]{1,0:T(8,128)(2,1)S(1)}, bf16[256,512]{1,0:T(8,128)(2,1)S(1)}, u32[]{:S(2)}, u32[]{:S(2)}) collective-permute-start(bf16[256,512]{1,0:T(8,128)(2,1)S(1)} %collective-permute-done.10.refs_2_), channel_id=1, source_target_pairs={{0,2},{1,3},{2,0},{3,1},{4,6},{5,7},{6,4},{7,5},{8,10},{9,11},{10,... | collective-permute-start | bytes 786440 | tf_op jit(solution)/shard_map/ppermute | solution.py:45
  34.6 1.5 %collective-permute-start.14 = (bf16[256,512]{1,0:T(8,128)(2,1)S(1)}, bf16[256,512]{1,0:T(8,128)(2,1)S(1)}, u32[]{:S(2)}, u32[]{:S(2)}) collective-permute-start(bf16[256,512]{1,0:T(8,128)(2,1)S(1)} %collective-permute-done.8.refs_2_), channel_id=1, source_target_pairs={{0,1},{1,0},{2,3},{3,2},{4,5},{5,4},{6,7},{7,6},{8,9},{9,8},{10,11... | collective-permute-start | bytes 786440 | tf_op jit(solution)/shard_map/ppermute | solution.py:45
  34.6 1.9 %collective-permute-start.15 = (bf16[256,512]{1,0:T(8,128)(2,1)S(1)}, bf16[256,512]{1,0:T(8,128)(2,1)S(1)}, u32[]{:S(2)}, u32[]{:S(2)}) collective-permute-start(bf16[256,512]{1,0:T(8,128)(2,1)S(1)} %collective-permute-done.9.refs_1_), channel_id=1, source_target_pairs={{0,1},{1,0},{2,3},{3,2},{4,5},{5,4},{6,7},{7,6},{8,9},{9,8},{10,11... | collective-permute-start | bytes 786440 | tf_op jit(solution)/shard_map/ppermute | solution.py:45
  39.5 1.5 %collective-permute-start.17 = (bf16[256,512]{1,0:T(8,128)(2,1)S(1)}, bf16[256,512]{1,0:T(8,128)(2,1)S(1)}, u32[]{:S(2)}, u32[]{:S(2)}) collective-permute-start(bf16[256,512]{1,0:T(8,128)(2,1)S(1)} %collective-permute-done.7.refs_1_), channel_id=1, source_target_pairs={{0,1},{1,0},{2,3},{3,2},{4,5},{5,4},{6,7},{7,6},{8,9},{9,8},{10,11... | collective-permute-start | bytes 786440 | tf_op jit(solution)/shard_map/ppermute | solution.py:45
  40.3 1.5 %collective-permute-start.18 = (bf16[256,512]{1,0:T(8,128)(2,1)S(1)}, bf16[256,512]{1,0:T(8,128)(2,1)S(1)}, u32[]{:S(2)}, u32[]{:S(2)}) collective-permute-start(bf16[256,512]{1,0:T(8,128)(2,1)S(1)} %collective-permute-done.16.refs_2_), channel_id=1, source_target_pairs={{0,1},{1,0},{2,3},{3,2},{4,5},{5,4},{6,7},{7,6},{8,9},{9,8},{10,11... | collective-permute-start | bytes 786440 | tf_op jit(solution)/shard_map/ppermute | solution.py:45

commit v9 on v8

--- a/solution.py
+++ b/solution.py
@@ -301,22 +301,23 @@
     yb = swapped(b, "head", 4)
     xb = swapped(b, "head", 2)
     ya = swapped(a, "head", 4)
-    sibling = swapped(own, "head", 1)
-    mixed = projected(None, weight, width, ((0, 0), (1, 0)), [own, sibling])
+    sa, sb = swapped(a, "head", 1), swapped(b, "head", 1)
+    mixed = projected(None, weight, width, ((0, 0), (0, half), (1, 0), (1, half)), [a, b, sa, sb])
+    xa, mixed = barrier((xa, mixed))
     da = swapped(xa, "head", 4)
     yb, mixed = barrier((yb, mixed))
     db = swapped(yb, "head", 2)
     xb, ya, mixed = barrier((xb, ya, mixed))
     xas = swapped(xa, "head", 1)
-    mixed = projected(mixed, weight, width, ((2, 0), (2, half), (3, 0)), [xa, xb, xas])
     ybs = swapped(yb, "head", 1)
+    mixed = projected(mixed, weight, width, ((2, 0), (3, 0), (4, half), (5, half)), [xa, xas, yb, ybs])
     xbs = swapped(xb, "head", 1)
     yas = swapped(ya, "head", 1)
-    mixed = projected(mixed, weight, width, ((4, 0), (4, half), (5, half), (3, half), (5, 0)), [ya, yb, ybs, xbs, yas])
+    mixed = projected(mixed, weight, width, ((2, half), (4, 0), (3, half), (5, 0)), [xb, ya, xbs, yas])
     da, mixed = barrier((da, mixed))
     da_s, db_s = swapped(da, "head", 1), swapped(db, "head", 1)
-    mixed = projected(mixed, weight, width, ((6, 0), (6, half)), [da, db])
-    return projected(mixed, weight, width, ((7, 0), (7, half)), [da_s, db_s], True)
+    mixed = projected(mixed, weight, width, ((6, 0), (6, half), (7, 0)), [da, db, da_s])
+    return projected(mixed, weight, width, ((7, half),), [db_s], True)
 
 
 def solution(mesh):

time: 43.5 us -> 44.2 us (1.016)
  Pallas kernels: 11.1 us -> 11.9 us
  waiting for transfers between devices: 12.5 us -> 11.9 us
  starting transfers between devices: 19.6 us -> 20.1 us
    pallas_call x1, Pallas kernels: 1.27 us -> 2.07 us  [attended_of(): pl.pallas_call(functools.partial(values_kernel, len(value_parts)), out_sh...]
    ppermute x13 -> x14, waiting for transfers between devices: 10.8 us -> 10.2 us  [swapped(): lax.ppermute(value, axis, [(source, source ^ bits) for source in range(co...]
    ppermute x13 -> x14, starting transfers between devices: 8.55 us -> 9.05 us  [swapped(): lax.ppermute(value, axis, [(source, source ^ bits) for source in range(co...]
  transfers between devices with their start and end apart: 19 -> 20, of which waited for: 8 -> 9; matrix products, arithmetic and copies ran while one was open for 0% -> 0% of each run, Pallas kernels for 17% -> 18%
where the time goes in v9:
time: 44.2 us; the launch traced here: 43.9 us
  starting transfers between devices  20.1 us (45%)
  Pallas kernels  11.9 us (27%)
  waiting for transfers between devices  11.9 us (27%)
    ppermute x6, starting transfers between devices, shifted(): lax.ppermute(value, axis, [(source, (source + steps) % count) for source...  11 us
    ppermute x14, waiting for transfers between devices, swapped(): lax.ppermute(value, axis, [(source, source ^ bits) for source in range(co...  10.2 us
    ppermute x14, starting transfers between devices, swapped(): lax.ppermute(value, axis, [(source, source ^ bits) for source in range(co...  9.05 us
    pallas_call x5, Pallas kernels, projected(): pl.pallas_call(functools.partial(projection_kernel, places, width, fresh,...  5.91 us
    pallas_call x1, Pallas kernels, attended_of(): pl.pallas_call(functools.partial(values_kernel, len(value_parts)), out_sh...  2.07 us
    pallas_call x1, Pallas kernels, weights_of(): pl.pallas_call(weights_kernel, out_shape=held((blocks_dev, rows, keys)),...  1.84 us
    ppermute x6, waiting for transfers between devices, shifted(): lax.ppermute(value, axis, [(source, (source + steps) % count) for source...  1.71 us
    pallas_call x1, Pallas kernels, stacked_of(): pl.pallas_call(functools.partial(stack_kernel, steps, count), out_shape=[...  1.15 us
  transfers between devices with their start and end apart: 20, of which 9 were waited for; matrix products, arithmetic and copies ran while one was open for 0% of the time, Pallas kernels for 18%

profile of v9, /device:TPU:0, one launch (start us, length us, event | category | flops | bytes accessed | tf_op | source)
XLA Modules:
  0.0 43.9 jit_solution(6825788941004089717)
XLA Ops:
  0.0 0.9 %shard_map.55 = (bf16[256,128]{1,0:T(8,128)(2,1)S(1)}, bf16[256,128]{1,0:T(8,128)(2,1)S(1)}) custom-call(bf16[256,1024]{1,0:T(8,128)(2,1)} %keys_ref.1, bf16[256,1024]{1,0:T(8,128)(2,1)} %values_ref.1), custom_call_target="tpu_custom_call" | custom-call | bytes 262144 | tf_op jit(solution)/shard_map/pallas_call | solution.py:68
  0.9 3.1 %collective-permute-start = (bf16[256,128]{1,0:T(8,128)(2,1)S(1)}, bf16[256,128]{1,0:T(8,128)(2,1)S(1)}, u32[]{:S(2)}, u32[]{:S(2)}) collective-permute-start(bf16[256,128]{1,0:T(8,128)(2,1)S(1)} %get-tuple-element.22.refs_0_), channel_id=1, source_target_pairs={{0,8},{8,16},{16,24},{24,0},{1,9},{9,17},{17,25},{25,1},{2,10},{10... | collective-permute-start | bytes 196616 | tf_op jit(solution)/shard_map/ppermute | solution.py:40
  4.0 2.6 %collective-permute-start.1 = (bf16[256,128]{1,0:T(8,128)(2,1)S(1)}, bf16[256,128]{1,0:T(8,128)(2,1)S(1)}, u32[]{:S(2)}, u32[]{:S(2)}) collective-permute-start(bf16[256,128]{1,0:T(8,128)(2,1)S(1)} %get-tuple-element.22.refs_0_), channel_id=1, source_target_pairs={{0,16},{8,24},{16,0},{24,8},{1,17},{9,25},{17,1},{25,9},{2,18},{10... | collective-permute-start | bytes 196616 | tf_op jit(solution)/shard_map/ppermute | solution.py:40
  6.6 1.3 %collective-permute-start.2 = (bf16[256,128]{1,0:T(8,128)(2,1)S(1)}, bf16[256,128]{1,0:T(8,128)(2,1)S(1)}, u32[]{:S(2)}, u32[]{:S(2)}) collective-permute-start(bf16[256,128]{1,0:T(8,128)(2,1)S(1)} %get-tuple-element.22.refs_0_), channel_id=1, source_target_pairs={{0,24},{8,0},{16,8},{24,16},{1,25},{9,1},{17,9},{25,17},{2,26},{10... | collective-permute-start | bytes 196616 | tf_op jit(solution)/shard_map/ppermute | solution.py:40
  7.9 0.2 collective-permute-start.3
  8.1 0.8 %collective-permute-start.4 = (bf16[256,128]{1,0:T(8,128)(2,1)S(1)}, bf16[256,128]{1,0:T(8,128)(2,1)S(1)}, u32[]{:S(2)}, u32[]{:S(2)}) collective-permute-start(bf16[256,128]{1,0:T(8,128)(2,1)S(1)} %get-tuple-element.27.refs_0_), channel_id=1, source_target_pairs={{0,8},{8,16},{16,24},{24,0},{1,9},{9,17},{17,25},{25,1},{2,10},{10... | collective-permute-start | bytes 196616 | tf_op jit(solution)/shard_map/ppermute | solution.py:40
  8.9 0.0 collective-permute-done.refs_2_
  8.9 3.0 %collective-permute-start.5 = (bf16[256,128]{1,0:T(8,128)(2,1)S(1)}, bf16[256,128]{1,0:T(8,128)(2,1)S(1)}, u32[]{:S(2)}, u32[]{:S(2)}) collective-permute-start(bf16[256,128]{1,0:T(8,128)(2,1)S(1)} %get-tuple-element.27.refs_0_), channel_id=1, source_target_pairs={{0,24},{8,0},{16,8},{24,16},{1,25},{9,1},{17,9},{25,17},{2,26},{10... | collective-permute-start | bytes 196616 | tf_op jit(solution)/shard_map/ppermute | solution.py:40
  11.9 1.2 %shard_map.56 = (bf16[2,1024,128]{2,1,0:T(8,128)(2,1)S(1)}, bf16[2,1024,128]{2,1,0:T(8,128)(2,1)S(1)}) custom-call(bf16[256,1024]{1,0:T(8,128)(2,1)} %q_ref, s32[8,8]{1,0:T(8,128)} %pattern_ref.1), custom_call_target="tpu_custom_call" | custom-call | bytes 1048576 | tf_op jit(solution)/shard_map/pallas_call | solution.py:119
  13.1 0.0 collective-permute-done.1.refs_1_
  13.1 0.0 collective-permute-done.2.refs_3_
  13.1 1.8 %shard_map.57.weights_ref = bf16[2,1024,1024]{2,1,0:T(8,128)(2,1)S(1)} custom-call(bf16[2,1024,128]{2,1,0:T(8,128)(2,1)S(1)} %get-tuple-element.24.q_ref, bf16[2,1024,128]{2,1,0:T(8,128)(2,1)S(1)} %get-tuple-element.25.mask_ref, bf16[256,128]{1,0:T(8,128)(2,1)S(1)} %get-tuple-element.22.refs_0_, bf16[256,128]{1,0:T(8,128)(2,1)S(1)} %collective-permute-done.1.refs_1_, ...), custom_call_target="tpu_custom_call" | custom-call | flops 107374182400 | bytes 4194304 | tf_op jit(solution)/shard_map/pallas_call | solution.py:160
  15.0 0.0 copy-start
  15.0 1.7 %collective-permute-done.3.refs_1_ = bf16[256,128]{1,0:T(8,128)(2,1)S(1)} collective-permute-done((bf16[256,128]{1,0:T(8,128)(2,1)S(1)}, bf16[256,128]{1,0:T(8,128)(2,1)S(1)}, u32[]{:S(2)}, u32[]{:S(2)}) %collective-permute-start.3) | collective-permute-done | bytes 65568 | tf_op jit(solution)/shard_map/ppermute | solution.py:40
  16.7 0.0 collective-permute-done.4.refs_2_
  16.7 0.0 collective-permute-done.5.refs_3_
  16.7 2.1 %shard_map.58 = (bf16[256,1024]{1,0:T(8,128)(2,1)}, bf16[256,512]{1,0:T(8,128)(2,1)S(1)}, bf16[256,512]{1,0:T(8,128)(2,1)S(1)}) custom-call(bf16[2,1024,1024]{2,1,0:T(8,128)(2,1)S(1)} %shard_map.57.weights_ref, bf16[256,128]{1,0:T(8,128)(2,1)S(1)} %get-tuple-element.27.refs_0_, bf16[256,128]{1,0:T(8,128)(2,1)S(1)} %collective-permute-done.3.refs_1_, ...), custom_call_target="tpu_custom_call" | custom-call | flops 107374182400 | bytes 1048576 | tf_op jit(solution)/shard_map/pallas_call | solution.py:201
  18.7 0.0 collective-permute-start.7
  18.8 0.5 %collective-permute-start.8 = (bf16[256,512]{1,0:T(8,128)(2,1)S(1)}, bf16[256,512]{1,0:T(8,128)(2,1)S(1)}, u32[]{:S(2)}, u32[]{:S(2)}) collective-permute-start(bf16[256,512]{1,0:T(8,128)(2,1)S(1)} %get-tuple-element.29.refs_1_), channel_id=1, source_target_pairs={{0,1},{1,0},{2,3},{3,2},{4,5},{5,4},{6,7},{7,6},{8,9},{9,8},{10,11... | collective-permute-start | bytes 786440 | tf_op jit(solution)/shard_map/ppermute | solution.py:45
  19.3 1.8 %collective-permute-start.6 = (bf16[256,512]{1,0:T(8,128)(2,1)S(1)}, bf16[256,512]{1,0:T(8,128)(2,1)S(1)}, u32[]{:S(2)}, u32[]{:S(2)}) collective-permute-start(bf16[256,512]{1,0:T(8,128)(2,1)S(1)} %get-tuple-element.28.refs_0_), channel_id=1, source_target_pairs={{0,2},{1,3},{2,0},{3,1},{4,6},{5,7},{6,4},{7,5},{8,10},{9,11},{10,... | collective-permute-start | bytes 786440 | tf_op jit(solution)/shard_map/ppermute | solution.py:45
  21.0 1.5 %collective-permute-start.12 = (bf16[256,512]{1,0:T(8,128)(2,1)S(1)}, bf16[256,512]{1,0:T(8,128)(2,1)S(1)}, u32[]{:S(2)}, u32[]{:S(2)}) collective-permute-start(bf16[256,512]{1,0:T(8,128)(2,1)S(1)} %get-tuple-element.29.refs_1_), channel_id=1, source_target_pairs={{0,4},{1,5},{2,6},{3,7},{4,0},{5,1},{6,2},{7,3},{8,12},{9,13},{10,... | collective-permute-start | bytes 786440 | tf_op jit(solution)/shard_map/ppermute | solution.py:45
  22.5 0.5 %collective-permute-start.10 = (bf16[256,512]{1,0:T(8,128)(2,1)S(1)}, bf16[256,512]{1,0:T(8,128)(2,1)S(1)}, u32[]{:S(2)}, u32[]{:S(2)}) collective-permute-start(bf16[256,512]{1,0:T(8,128)(2,1)S(1)} %get-tuple-element.29.refs_1_), channel_id=1, source_target_pairs={{0,2},{1,3},{2,0},{3,1},{4,6},{5,7},{6,4},{7,5},{8,10},{9,11},{10,... | collective-permute-start | bytes 786440 | tf_op jit(solution)/shard_map/ppermute | solution.py:45
  23.1 0.0 collective-permute-done.7.refs_2_
  23.1 0.2 collective-permute-start.11
  23.3 0.0 collective-permute-done.8.refs_3_
  23.3 0.0 copy-done
  23.3 1.2 %shard_map.59.refs_0_ = f32[256,1024]{1,0:T(8,128)S(1)} custom-call(bf16[8192,1024]{1,0:T(8,128)(2,1)S(1)} %copy-done, bf16[256,512]{1,0:T(8,128)(2,1)S(1)} %get-tuple-element.28.refs_0_, bf16[256,512]{1,0:T(8,128)(2,1)S(1)} %get-tuple-element.29.refs_1_, bf16[256,512]{1,0:T(8,128)(2,1)S(1)} %collective-permute-done.7.refs_2_, ...), custom_call_target="tpu_custom_call" | custom-call | flops 4294967296 | bytes 1048576 | tf_op jit(solution)/shard_map/pallas_call | solution.py:255
  24.6 3.9 %collective-permute-done.6.refs_1_ = bf16[256,512]{1,0:T(8,128)(2,1)S(1)} collective-permute-done((bf16[256,512]{1,0:T(8,128)(2,1)S(1)}, bf16[256,512]{1,0:T(8,128)(2,1)S(1)}, u32[]{:S(2)}, u32[]{:S(2)}) %collective-permute-start.6) | collective-permute-done | bytes 262176 | tf_op jit(solution)/shard_map/ppermute | solution.py:45
  28.4 1.8 %collective-permute-done.12.refs_3_ = bf16[256,512]{1,0:T(8,128)(2,1)S(1)} collective-permute-done((bf16[256,512]{1,0:T(8,128)(2,1)S(1)}, bf16[256,512]{1,0:T(8,128)(2,1)S(1)}, u32[]{:S(2)}, u32[]{:S(2)}) %collective-permute-start.12) | collective-permute-done | bytes 262176 | tf_op jit(solution)/shard_map/ppermute | solution.py:45
  30.2 0.0 collective-permute-start.14
  30.2 0.5 %collective-permute-start.13 = (bf16[256,512]{1,0:T(8,128)(2,1)S(1)}, bf16[256,512]{1,0:T(8,128)(2,1)S(1)}, u32[]{:S(2)}, u32[]{:S(2)}) collective-permute-start(bf16[256,512]{1,0:T(8,128)(2,1)S(1)} %collective-permute-done.6.refs_1_), channel_id=1, source_target_pairs={{0,1},{1,0},{2,3},{3,2},{4,5},{5,4},{6,7},{7,6},{8,9},{9,8},{10,11... | collective-permute-start | bytes 786440 | tf_op jit(solution)/shard_map/ppermute | solution.py:45
  30.7 1.5 %collective-permute-start.9 = (bf16[256,512]{1,0:T(8,128)(2,1)S(1)}, bf16[256,512]{1,0:T(8,128)(2,1)S(1)}, u32[]{:S(2)}, u32[]{:S(2)}) collective-permute-start(bf16[256,512]{1,0:T(8,128)(2,1)S(1)} %collective-permute-done.6.refs_1_), channel_id=1, source_target_pairs={{0,4},{1,5},{2,6},{3,7},{4,0},{5,1},{6,2},{7,3},{8,12},{9,13},{10,... | collective-permute-start | bytes 786440 | tf_op jit(solution)/shard_map/ppermute | solution.py:45
  32.3 0.8 %collective-permute-done.10.refs_1_ = bf16[256,512]{1,0:T(8,128)(2,1)S(1)} collective-permute-done((bf16[256,512]{1,0:T(8,128)(2,1)S(1)}, bf16[256,512]{1,0:T(8,128)(2,1)S(1)}, u32[]{:S(2)}, u32[]{:S(2)}) %collective-permute-start.10) | collective-permute-done | bytes 262176 | tf_op jit(solution)/shard_map/ppermute | solution.py:45
  33.1 1.7 %collective-permute-start.17 = (bf16[256,512]{1,0:T(8,128)(2,1)S(1)}, bf16[256,512]{1,0:T(8,128)(2,1)S(1)}, u32[]{:S(2)}, u32[]{:S(2)}) collective-permute-start(bf16[256,512]{1,0:T(8,128)(2,1)S(1)} %collective-permute-done.12.refs_3_), channel_id=1, source_target_pairs={{0,2},{1,3},{2,0},{3,1},{4,6},{5,7},{6,4},{7,5},{8,10},{9,11},{10,... | collective-permute-start | bytes 786440 | tf_op jit(solution)/shard_map/ppermute | solution.py:45
  34.9 0.9 %collective-permute-done.11.refs_2_ = bf16[256,512]{1,0:T(8,128)(2,1)S(1)} collective-permute-done((bf16[256,512]{1,0:T(8,128)(2,1)S(1)}, bf16[256,512]{1,0:T(8,128)(2,1)S(1)}, u32[]{:S(2)}, u32[]{:S(2)}) %collective-permute-start.11) | collective-permute-done | bytes 262176 | tf_op jit(solution)/shard_map/ppermute | solution.py:45
  35.7 0.0 collective-permute-start.15
  35.7 0.0 collective-permute-done.14.refs_4_
  35.7 0.5 %collective-permute-start.16 = (bf16[256,512]{1,0:T(8,128)(2,1)S(1)}, bf16[256,512]{1,0:T(8,128)(2,1)S(1)}, u32[]{:S(2)}, u32[]{:S(2)}) collective-permute-start(bf16[256,512]{1,0:T(8,128)(2,1)S(1)} %collective-permute-done.11.refs_2_), channel_id=1, source_target_pairs={{0,1},{1,0},{2,3},{3,2},{4,5},{5,4},{6,7},{7,6},{8,9},{9,8},{10,11... | collective-permute-start | bytes 786440 | tf_op jit(solution)/shard_map/ppermute | solution.py:45
  36.3 0.0 collective-permute-done.13.refs_2_
  36.3 1.2 %shard_map.60.refs_0_ = f32[256,1024]{1,0:T(8,128)S(1)} custom-call(bf16[8192,1024]{1,0:T(8,128)(2,1)S(1)} %copy-done, f32[256,1024]{1,0:T(8,128)S(1)} %shard_map.59.refs_0_, bf16[256,512]{1,0:T(8,128)(2,1)S(1)} %collective-permute-done.6.refs_1_, bf16[256,512]{1,0:T(8,128)(2,1)S(1)} %collective-permute-done.13.refs_2_, ...), custom_call_target="tpu_custom_call" | custom-call | flops 4294967296 | bytes 1048576 | tf_op jit(solution)/shard_map/pallas_call | solution.py:255
  37.5 0.0 collective-permute-done.15.refs_3_
  37.5 0.1 collective-permute-done.16.refs_4_
  37.7 1.2 %shard_map.61.refs_0_ = f32[256,1024]{1,0:T(8,128)S(1)} custom-call(bf16[8192,1024]{1,0:T(8,128)(2,1)S(1)} %copy-done, f32[256,1024]{1,0:T(8,128)S(1)} %shard_map.60.refs_0_, bf16[256,512]{1,0:T(8,128)(2,1)S(1)} %collective-permute-done.10.refs_1_, bf16[256,512]{1,0:T(8,128)(2,1)S(1)} %collective-permute-done.11.refs_2_, ...), custom_call_target="tpu_custom_call" | custom-call | flops 4294967296 | bytes 1048576 | tf_op jit(solution)/shard_map/pallas_call | solution.py:255
  38.9 1.3 %collective-permute-done.9.refs_1_ = bf16[256,512]{1,0:T(8,128)(2,1)S(1)} collective-permute-done((bf16[256,512]{1,0:T(8,128)(2,1)S(1)}, bf16[256,512]{1,0:T(8,128)(2,1)S(1)}, u32[]{:S(2)}, u32[]{:S(2)}) %collective-permute-start.9) | collective-permute-done | bytes 262176 | tf_op jit(solution)/shard_map/ppermute | solution.py:45
  40.2 0.0 collective-permute-start.18
  40.2 0.3 collective-permute-done.17.refs_2_
  40.5 0.2 collective-permute-start.19
  40.7 1.0 %collective-permute-done.18.refs_3_ = bf16[256,512]{1,0:T(8,128)(2,1)S(1)} collective-permute-done((bf16[256,512]{1,0:T(8,128)(2,1)S(1)}, bf16[256,512]{1,0:T(8,128)(2,1)S(1)}, u32[]{:S(2)}, u32[]{:S(2)}) %collective-permute-start.18) | collective-permute-done | bytes 262176 | tf_op jit(solution)/shard_map/ppermute | solution.py:45
  41.7 1.0 %shard_map.62.refs_0_ = f32[256,1024]{1,0:T(8,128)S(1)} custom-call(bf16[8192,1024]{1,0:T(8,128)(2,1)S(1)} %copy-done, f32[256,1024]{1,0:T(8,128)S(1)} %shard_map.61.refs_0_, bf16[256,512]{1,0:T(8,128)(2,1)S(1)} %collective-permute-done.9.refs_1_, bf16[256,512]{1,0:T(8,128)(2,1)S(1)} %collective-permute-done.17.refs_2_, ...), custom_call_target="tpu_custom_call" | custom-call | flops 3221225472 | bytes 1048576 | tf_op jit(solution)/shard_map/pallas_call | solution.py:255
  42.7 0.0 collective-permute-done.19.refs_1_
  42.7 1.2 %shard_map.63 = bf16[256,1024]{1,0:T(8,128)(2,1)} custom-call(bf16[8192,1024]{1,0:T(8,128)(2,1)S(1)} %copy-done, f32[256,1024]{1,0:T(8,128)S(1)} %shard_map.62.refs_0_, bf16[256,512]{1,0:T(8,128)(2,1)S(1)} %collective-permute-done.19.refs_1_), custom_call_target="tpu_custom_call" | custom-call | flops 1073741824 | bytes 1048576 | tf_op jit(solution)/shard_map/pallas_call | solution.py:255
Async XLA Ops:
  0.9 8.0 %collective-permute-start = (bf16[256,128]{1,0:T(8,128)(2,1)S(1)}, bf16[256,128]{1,0:T(8,128)(2,1)S(1)}, u32[]{:S(2)}, u32[]{:S(2)}) collective-permute-start(bf16[256,128]{1,0:T(8,128)(2,1)S(1)} %get-tuple-element.22.refs_0_), channel_id=1, source_target_pairs={{0,8},{8,16},{16,24},{24,0},{1,9},{9,17},{17,25},{25,1},{2,10},{10... | collective-permute-start | bytes 196616 | tf_op jit(solution)/shard_map/ppermute | solution.py:40
  4.0 9.1 %collective-permute-start.1 = (bf16[256,128]{1,0:T(8,128)(2,1)S(1)}, bf16[256,128]{1,0:T(8,128)(2,1)S(1)}, u32[]{:S(2)}, u32[]{:S(2)}) collective-permute-start(bf16[256,128]{1,0:T(8,128)(2,1)S(1)} %get-tuple-element.22.refs_0_), channel_id=1, source_target_pairs={{0,16},{8,24},{16,0},{24,8},{1,17},{9,25},{17,1},{25,9},{2,18},{10... | collective-permute-start | bytes 196616 | tf_op jit(solution)/shard_map/ppermute | solution.py:40
  6.6 6.5 %collective-permute-start.2 = (bf16[256,128]{1,0:T(8,128)(2,1)S(1)}, bf16[256,128]{1,0:T(8,128)(2,1)S(1)}, u32[]{:S(2)}, u32[]{:S(2)}) collective-permute-start(bf16[256,128]{1,0:T(8,128)(2,1)S(1)} %get-tuple-element.22.refs_0_), channel_id=1, source_target_pairs={{0,24},{8,0},{16,8},{24,16},{1,25},{9,1},{17,9},{25,17},{2,26},{10... | collective-permute-start | bytes 196616 | tf_op jit(solution)/shard_map/ppermute | solution.py:40
  7.9 8.8 %collective-permute-start.3 = (bf16[256,128]{1,0:T(8,128)(2,1)S(1)}, bf16[256,128]{1,0:T(8,128)(2,1)S(1)}, u32[]{:S(2)}, u32[]{:S(2)}) collective-permute-start(bf16[256,128]{1,0:T(8,128)(2,1)S(1)} %get-tuple-element.27.refs_0_), channel_id=1, source_target_pairs={{0,16},{8,24},{16,0},{24,8},{1,17},{9,25},{17,1},{25,9},{2,18},{10... | collective-permute-start | bytes 196616 | tf_op jit(solution)/shard_map/ppermute | solution.py:40
  8.1 8.6 %collective-permute-start.4 = (bf16[256,128]{1,0:T(8,128)(2,1)S(1)}, bf16[256,128]{1,0:T(8,128)(2,1)S(1)}, u32[]{:S(2)}, u32[]{:S(2)}) collective-permute-start(bf16[256,128]{1,0:T(8,128)(2,1)S(1)} %get-tuple-element.27.refs_0_), channel_id=1, source_target_pairs={{0,8},{8,16},{16,24},{24,0},{1,9},{9,17},{17,25},{25,1},{2,10},{10... | collective-permute-start | bytes 196616 | tf_op jit(solution)/shard_map/ppermute | solution.py:40
  8.9 7.7 %collective-permute-start.5 = (bf16[256,128]{1,0:T(8,128)(2,1)S(1)}, bf16[256,128]{1,0:T(8,128)(2,1)S(1)}, u32[]{:S(2)}, u32[]{:S(2)}) collective-permute-start(bf16[256,128]{1,0:T(8,128)(2,1)S(1)} %get-tuple-element.27.refs_0_), channel_id=1, source_target_pairs={{0,24},{8,0},{16,8},{24,16},{1,25},{9,1},{17,9},{25,17},{2,26},{10... | collective-permute-start | bytes 196616 | tf_op jit(solution)/shard_map/ppermute | solution.py:40
  15.0 8.4 %copy-start = (bf16[8192,1024]{1,0:T(8,128)(2,1)S(1)}, bf16[8192,1024]{1,0:T(8,128)(2,1)}, u32[]{:S(2)}) copy-start(bf16[8192,1024]{1,0:T(8,128)(2,1)} %weight_ref.9) | copy-start | bytes 50331652
  18.7 4.3 %collective-permute-start.7 = (bf16[256,512]{1,0:T(8,128)(2,1)S(1)}, bf16[256,512]{1,0:T(8,128)(2,1)S(1)}, u32[]{:S(2)}, u32[]{:S(2)}) collective-permute-start(bf16[256,512]{1,0:T(8,128)(2,1)S(1)} %get-tuple-element.28.refs_0_), channel_id=1, source_target_pairs={{0,1},{1,0},{2,3},{3,2},{4,5},{5,4},{6,7},{7,6},{8,9},{9,8},{10,11... | collective-permute-start | bytes 786440 | tf_op jit(solution)/shard_map/ppermute | solution.py:45
  18.8 4.6 %collective-permute-start.8 = (bf16[256,512]{1,0:T(8,128)(2,1)S(1)}, bf16[256,512]{1,0:T(8,128)(2,1)S(1)}, u32[]{:S(2)}, u32[]{:S(2)}) collective-permute-start(bf16[256,512]{1,0:T(8,128)(2,1)S(1)} %get-tuple-element.29.refs_1_), channel_id=1, source_target_pairs={{0,1},{1,0},{2,3},{3,2},{4,5},{5,4},{6,7},{7,6},{8,9},{9,8},{10,11... | collective-permute-start | bytes 786440 | tf_op jit(solution)/shard_map/ppermute | solution.py:45
  19.3 9.2 %collective-permute-start.6 = (bf16[256,512]{1,0:T(8,128)(2,1)S(1)}, bf16[256,512]{1,0:T(8,128)(2,1)S(1)}, u32[]{:S(2)}, u32[]{:S(2)}) collective-permute-start(bf16[256,512]{1,0:T(8,128)(2,1)S(1)} %get-tuple-element.28.refs_0_), channel_id=1, source_target_pairs={{0,2},{1,3},{2,0},{3,1},{4,6},{5,7},{6,4},{7,5},{8,10},{9,11},{10,... | collective-permute-start | bytes 786440 | tf_op jit(solution)/shard_map/ppermute | solution.py:45
  21.0 9.2 %collective-permute-start.12 = (bf16[256,512]{1,0:T(8,128)(2,1)S(1)}, bf16[256,512]{1,0:T(8,128)(2,1)S(1)}, u32[]{:S(2)}, u32[]{:S(2)}) collective-permute-start(bf16[256,512]{1,0:T(8,128)(2,1)S(1)} %get-tuple-element.29.refs_1_), channel_id=1, source_target_pairs={{0,4},{1,5},{2,6},{3,7},{4,0},{5,1},{6,2},{7,3},{8,12},{9,13},{10,... | collective-permute-start | bytes 786440 | tf_op jit(solution)/shard_map/ppermute | solution.py:45
  22.5 10.6 %collective-permute-start.10 = (bf16[256,512]{1,0:T(8,128)(2,1)S(1)}, bf16[256,512]{1,0:T(8,128)(2,1)S(1)}, u32[]{:S(2)}, u32[]{:S(2)}) collective-permute-start(bf16[256,512]{1,0:T(8,128)(2,1)S(1)} %get-tuple-element.29.refs_1_), channel_id=1, source_target_pairs={{0,2},{1,3},{2,0},{3,1},{4,6},{5,7},{6,4},{7,5},{8,10},{9,11},{10,... | collective-permute-start | bytes 786440 | tf_op jit(solution)/shard_map/ppermute | solution.py:45
  23.1 12.7 %collective-permute-start.11 = (bf16[256,512]{1,0:T(8,128)(2,1)S(1)}, bf16[256,512]{1,0:T(8,128)(2,1)S(1)}, u32[]{:S(2)}, u32[]{:S(2)}) collective-permute-start(bf16[256,512]{1,0:T(8,128)(2,1)S(1)} %get-tuple-element.28.refs_0_), channel_id=1, source_target_pairs={{0,4},{1,5},{2,6},{3,7},{4,0},{5,1},{6,2},{7,3},{8,12},{9,13},{10,... | collective-permute-start | bytes 786440 | tf_op jit(solution)/shard_map/ppermute | solution.py:45
  30.2 5.5 %collective-permute-start.14 = (bf16[256,512]{1,0:T(8,128)(2,1)S(1)}, bf16[256,512]{1,0:T(8,128)(2,1)S(1)}, u32[]{:S(2)}, u32[]{:S(2)}) collective-permute-start(bf16[256,512]{1,0:T(8,128)(2,1)S(1)} %collective-permute-done.12.refs_3_), channel_id=1, source_target_pairs={{0,1},{1,0},{2,3},{3,2},{4,5},{5,4},{6,7},{7,6},{8,9},{9,8},{10,11... | collective-permute-start | bytes 786440 | tf_op jit(solution)/shard_map/ppermute | solution.py:45
  30.2 6.0 %collective-permute-start.13 = (bf16[256,512]{1,0:T(8,128)(2,1)S(1)}, bf16[256,512]{1,0:T(8,128)(2,1)S(1)}, u32[]{:S(2)}, u32[]{:S(2)}) collective-permute-start(bf16[256,512]{1,0:T(8,128)(2,1)S(1)} %collective-permute-done.6.refs_1_), channel_id=1, source_target_pairs={{0,1},{1,0},{2,3},{3,2},{4,5},{5,4},{6,7},{7,6},{8,9},{9,8},{10,11... | collective-permute-start | bytes 786440 | tf_op jit(solution)/shard_map/ppermute | solution.py:45
  30.7 9.4 %collective-permute-start.9 = (bf16[256,512]{1,0:T(8,128)(2,1)S(1)}, bf16[256,512]{1,0:T(8,128)(2,1)S(1)}, u32[]{:S(2)}, u32[]{:S(2)}) collective-permute-start(bf16[256,512]{1,0:T(8,128)(2,1)S(1)} %collective-permute-done.6.refs_1_), channel_id=1, source_target_pairs={{0,4},{1,5},{2,6},{3,7},{4,0},{5,1},{6,2},{7,3},{8,12},{9,13},{10,... | collective-permute-start | bytes 786440 | tf_op jit(solution)/shard_map/ppermute | solution.py:45
  33.1 7.4 %collective-permute-start.17 = (bf16[256,512]{1,0:T(8,128)(2,1)S(1)}, bf16[256,512]{1,0:T(8,128)(2,1)S(1)}, u32[]{:S(2)}, u32[]{:S(2)}) collective-permute-start(bf16[256,512]{1,0:T(8,128)(2,1)S(1)} %collective-permute-done.12.refs_3_), channel_id=1, source_target_pairs={{0,2},{1,3},{2,0},{3,1},{4,6},{5,7},{6,4},{7,5},{8,10},{9,11},{10,... | collective-permute-start | bytes 786440 | tf_op jit(solution)/shard_map/ppermute | solution.py:45
  35.7 1.8 %collective-permute-start.15 = (bf16[256,512]{1,0:T(8,128)(2,1)S(1)}, bf16[256,512]{1,0:T(8,128)(2,1)S(1)}, u32[]{:S(2)}, u32[]{:S(2)}) collective-permute-start(bf16[256,512]{1,0:T(8,128)(2,1)S(1)} %collective-permute-done.10.refs_1_), channel_id=1, source_target_pairs={{0,1},{1,0},{2,3},{3,2},{4,5},{5,4},{6,7},{7,6},{8,9},{9,8},{10,11... | collective-permute-start | bytes 786440 | tf_op jit(solution)/shard_map/ppermute | solution.py:45
  35.7 1.9 %collective-permute-start.16 = (bf16[256,512]{1,0:T(8,128)(2,1)S(1)}, bf16[256,512]{1,0:T(8,128)(2,1)S(1)}, u32[]{:S(2)}, u32[]{:S(2)}) collective-permute-start(bf16[256,512]{1,0:T(8,128)(2,1)S(1)} %collective-permute-done.11.refs_2_), channel_id=1, source_target_pairs={{0,1},{1,0},{2,3},{3,2},{4,5},{5,4},{6,7},{7,6},{8,9},{9,8},{10,11... | collective-permute-start | bytes 786440 | tf_op jit(solution)/shard_map/ppermute | solution.py:45
  40.2 1.5 %collective-permute-start.18 = (bf16[256,512]{1,0:T(8,128)(2,1)S(1)}, bf16[256,512]{1,0:T(8,128)(2,1)S(1)}, u32[]{:S(2)}, u32[]{:S(2)}) collective-permute-start(bf16[256,512]{1,0:T(8,128)(2,1)S(1)} %collective-permute-done.9.refs_1_), channel_id=1, source_target_pairs={{0,1},{1,0},{2,3},{3,2},{4,5},{5,4},{6,7},{7,6},{8,9},{9,8},{10,11... | collective-permute-start | bytes 786440 | tf_op jit(solution)/shard_map/ppermute | solution.py:45
  40.5 2.2 %collective-permute-start.19 = (bf16[256,512]{1,0:T(8,128)(2,1)S(1)}, bf16[256,512]{1,0:T(8,128)(2,1)S(1)}, u32[]{:S(2)}, u32[]{:S(2)}) collective-permute-start(bf16[256,512]{1,0:T(8,128)(2,1)S(1)} %collective-permute-done.17.refs_2_), channel_id=1, source_target_pairs={{0,1},{1,0},{2,3},{3,2},{4,5},{5,4},{6,7},{7,6},{8,9},{9,8},{10,11... | collective-permute-start | bytes 786440 | tf_op jit(solution)/shard_map/ppermute | solution.py:45

commit v10 on v6

--- a/solution.py
+++ b/solution.py
@@ -163,36 +163,45 @@
         in_specs=[VMEM] * (2 + len(key_parts)),
         out_specs=VMEM,
         compiler_params=params(8 + (min(rows, 512) * keys * 16 >> 20)),
-        cost_estimate=cost(8 * blocks_dev * rows * keys * HEAD_SIZE, 4 << 20),
+        cost_estimate=cost(400 * blocks_dev * rows * keys * HEAD_SIZE, 4 << 20),
     )(stacked, mask, *key_parts)
 
 
-def values_kernel(first, group, weights_ref, *refs):
-    value_refs, out_ref = refs[:-1], refs[-1]
-    values = jnp.concatenate([ref[...] for ref in value_refs], axis=0)
+def values_kernel(count, weights_ref, *refs):
+    values = jnp.concatenate([ref[...] for ref in refs[:count]], axis=0)
     values = jnp.concatenate([values, jnp.ones_like(values)], axis=1)
-    for a in range(weights_ref.shape[0]):
-        summed = jnp.dot(
-            weights_ref[a, first * BLOCK : (first + group) * BLOCK, :],
-            values,
-            preferred_element_type=jnp.float32,
-        )
-        result = (summed[:, :HEAD_SIZE] / summed[:, HEAD_SIZE:]).astype(jnp.bfloat16)
-        for i in range(group):
-            out_ref[a * BLOCK : (a + 1) * BLOCK, i * HEAD_SIZE : (i + 1) * HEAD_SIZE] = result[
-                i * BLOCK : (i + 1) * BLOCK
-            ]
-
-
-def attended_of(weights, value_parts, first, group):
-    blocks_dev, _, keys = weights.shape
-    return pl.pallas_call(
-        functools.partial(values_kernel, first, group),
-        out_shape=held((blocks_dev * BLOCK, group * HEAD_SIZE)),
+    piece_refs = refs[count:]
+    blocks_dev, rows, _ = weights_ref.shape
+    heads = rows // BLOCK
+    pieces = len(piece_refs)
+    group = heads // pieces
+    for piece in range(pieces):
+        for a in range(blocks_dev):
+            first = piece * group
+            summed = jnp.dot(
+                weights_ref[a, first * BLOCK : (first + group) * BLOCK, :],
+                values,
+                preferred_element_type=jnp.float32,
+            )
+            result = (summed[:, :HEAD_SIZE] / summed[:, HEAD_SIZE:]).astype(jnp.bfloat16)
+            for i in range(group):
+                part = result[i * BLOCK : (i + 1) * BLOCK]
+                tokens = slice(a * BLOCK, (a + 1) * BLOCK)
+                column = i * HEAD_SIZE
+                piece_refs[piece][tokens, column : column + HEAD_SIZE] = part
+
+
+def attended_of(weights, value_parts, pieces):
+    blocks_dev, rows, keys = weights.shape
+    tokens, width = blocks_dev * BLOCK, rows // BLOCK * HEAD_SIZE
+    shapes = [held((tokens, width // pieces))] * pieces
+    return pl.pallas_call(
+        functools.partial(values_kernel, len(value_parts)),
+        out_shape=shapes,
         in_specs=[VMEM] * (1 + len(value_parts)),
-        out_specs=VMEM,
+        out_specs=[VMEM] * len(shapes),
         compiler_params=params(16),
-        cost_estimate=cost(4 * blocks_dev * BLOCK * group * keys * HEAD_SIZE, 1 << 20),
+        cost_estimate=cost(400 * tokens * width * keys, 1 << 20),
     )(weights, *value_parts)
 
 
@@ -270,7 +279,7 @@
     stacked, mask = stacked_of(queries, block_pattern, steps, count if count == 4 else None)
     weights = weights_of(stacked, mask, key_parts)
     if lax.axis_size("head") != 8:
-        att = attended_of(weights, value_parts, 0, heads_dev)
+        (att,) = attended_of(weights, value_parts, 1)
         mixed = jnp.dot(
             lax.all_gather(att, "head", axis=1, tiled=True),
             out_weight,
@@ -280,14 +289,11 @@
 
     barrier = lax.optimization_barrier
     weight = pltpu.with_memory_space_constraint(out_weight, pltpu.VMEM)
-    half = heads_dev // 2
-    a = attended_of(weights, value_parts, 0, half)
-    b = attended_of(weights, value_parts, half, half)
+    a, b = attended_of(weights, value_parts, 2)
     xa = swapped(a, "head", 2)
     yb = swapped(b, "head", 4)
     xb = swapped(b, "head", 2)
     ya = swapped(a, "head", 4)
-    a, b = barrier((a, b))
     sa = swapped(a, "head", 1)
     sb = swapped(b, "head", 1)
     width, half = heads_dev * HEAD_SIZE, heads_dev * HEAD_SIZE // 2

time: 43.4 us -> 43.2 us (level)
    pallas_call x2 -> x1, Pallas kernels: 1.43 us -> 1.26 us  [attended_of(): pl.pallas_call(functools.partial(values_kernel, len(value_parts)), out_sh...]
where the time goes in v10:
time: 43.2 us; the launch traced here: 42.9 us
  starting transfers between devices  20.1 us (47%)
  waiting for transfers between devices  11.7 us (27%)
  Pallas kernels  11 us (25%)
    ppermute x6, starting transfers between devices, shifted(): lax.ppermute(value, axis, [(source, (source + steps) % count) for source...  11 us
    ppermute x14, waiting for transfers between devices, swapped(): lax.ppermute(value, axis, [(source, source ^ bits) for source in range(co...  9.99 us
    ppermute x14, starting transfers between devices, swapped(): lax.ppermute(value, axis, [(source, source ^ bits) for source in range(co...  9.02 us
    pallas_call x5, Pallas kernels, projected(): pl.pallas_call(functools.partial(projection_kernel, places, width, fresh,...  5.9 us
    pallas_call x1, Pallas kernels, weights_of(): pl.pallas_call(weights_kernel, out_shape=held((blocks_dev, rows, keys)),...  1.84 us
    ppermute x6, waiting for transfers between devices, shifted(): lax.ppermute(value, axis, [(source, (source + steps) % count) for source...  1.71 us
    pallas_call x1, Pallas kernels, attended_of(): pl.pallas_call(functools.partial(values_kernel, len(value_parts)), out_sh...  1.26 us
    pallas_call x1, Pallas kernels, stacked_of(): pl.pallas_call(functools.partial(stack_kernel, steps, count), out_shape=[...  1.15 us
  transfers between devices with their start and end apart: 20, of which 10 were waited for; matrix products, arithmetic and copies ran while one was open for 0% of the time, Pallas kernels for 17%

profile of v10, /device:TPU:0, one launch (start us, length us, event | category | flops | bytes accessed | tf_op | source)
XLA Modules:
  0.0 42.9 jit_solution(5521971176710544849)
XLA Ops:
  0.0 0.9 %shard_map.55 = (bf16[256,128]{1,0:T(8,128)(2,1)S(1)}, bf16[256,128]{1,0:T(8,128)(2,1)S(1)}) custom-call(bf16[256,1024]{1,0:T(8,128)(2,1)} %keys_ref.1, bf16[256,1024]{1,0:T(8,128)(2,1)} %values_ref.1), custom_call_target="tpu_custom_call" | custom-call | bytes 262144 | tf_op jit(solution)/shard_map/pallas_call | solution.py:68
  0.9 3.1 %collective-permute-start = (bf16[256,128]{1,0:T(8,128)(2,1)S(1)}, bf16[256,128]{1,0:T(8,128)(2,1)S(1)}, u32[]{:S(2)}, u32[]{:S(2)}) collective-permute-start(bf16[256,128]{1,0:T(8,128)(2,1)S(1)} %get-tuple-element.19.refs_0_), channel_id=1, source_target_pairs={{0,8},{8,16},{16,24},{24,0},{1,9},{9,17},{17,25},{25,1},{2,10},{10... | collective-permute-start | bytes 196616 | tf_op jit(solution)/shard_map/ppermute | solution.py:40
  4.0 2.6 %collective-permute-start.1 = (bf16[256,128]{1,0:T(8,128)(2,1)S(1)}, bf16[256,128]{1,0:T(8,128)(2,1)S(1)}, u32[]{:S(2)}, u32[]{:S(2)}) collective-permute-start(bf16[256,128]{1,0:T(8,128)(2,1)S(1)} %get-tuple-element.19.refs_0_), channel_id=1, source_target_pairs={{0,16},{8,24},{16,0},{24,8},{1,17},{9,25},{17,1},{25,9},{2,18},{10... | collective-permute-start | bytes 196616 | tf_op jit(solution)/shard_map/ppermute | solution.py:40
  6.6 1.3 %collective-permute-start.2 = (bf16[256,128]{1,0:T(8,128)(2,1)S(1)}, bf16[256,128]{1,0:T(8,128)(2,1)S(1)}, u32[]{:S(2)}, u32[]{:S(2)}) collective-permute-start(bf16[256,128]{1,0:T(8,128)(2,1)S(1)} %get-tuple-element.19.refs_0_), channel_id=1, source_target_pairs={{0,24},{8,0},{16,8},{24,16},{1,25},{9,1},{17,9},{25,17},{2,26},{10... | collective-permute-start | bytes 196616 | tf_op jit(solution)/shard_map/ppermute | solution.py:40
  7.9 0.2 collective-permute-start.3
  8.1 0.8 %collective-permute-start.4 = (bf16[256,128]{1,0:T(8,128)(2,1)S(1)}, bf16[256,128]{1,0:T(8,128)(2,1)S(1)}, u32[]{:S(2)}, u32[]{:S(2)}) collective-permute-start(bf16[256,128]{1,0:T(8,128)(2,1)S(1)} %get-tuple-element.24.refs_0_), channel_id=1, source_target_pairs={{0,8},{8,16},{16,24},{24,0},{1,9},{9,17},{17,25},{25,1},{2,10},{10... | collective-permute-start | bytes 196616 | tf_op jit(solution)/shard_map/ppermute | solution.py:40
  8.9 0.0 collective-permute-done.refs_2_
  8.9 3.0 %collective-permute-start.5 = (bf16[256,128]{1,0:T(8,128)(2,1)S(1)}, bf16[256,128]{1,0:T(8,128)(2,1)S(1)}, u32[]{:S(2)}, u32[]{:S(2)}) collective-permute-start(bf16[256,128]{1,0:T(8,128)(2,1)S(1)} %get-tuple-element.24.refs_0_), channel_id=1, source_target_pairs={{0,24},{8,0},{16,8},{24,16},{1,25},{9,1},{17,9},{25,17},{2,26},{10... | collective-permute-start | bytes 196616 | tf_op jit(solution)/shard_map/ppermute | solution.py:40
  11.9 1.2 %shard_map.56 = (bf16[2,1024,128]{2,1,0:T(8,128)(2,1)S(1)}, bf16[2,1024,128]{2,1,0:T(8,128)(2,1)S(1)}) custom-call(bf16[256,1024]{1,0:T(8,128)(2,1)} %q_ref, s32[8,8]{1,0:T(8,128)} %pattern_ref.1), custom_call_target="tpu_custom_call" | custom-call | bytes 1048576 | tf_op jit(solution)/shard_map/pallas_call | solution.py:119
  13.1 0.0 collective-permute-done.1.refs_1_
  13.1 0.0 collective-permute-done.2.refs_3_
  13.1 1.8 %shard_map.57.weights_ref = bf16[2,1024,1024]{2,1,0:T(8,128)(2,1)S(1)} custom-call(bf16[2,1024,128]{2,1,0:T(8,128)(2,1)S(1)} %get-tuple-element.21.q_ref, bf16[2,1024,128]{2,1,0:T(8,128)(2,1)S(1)} %get-tuple-element.22.mask_ref, bf16[256,128]{1,0:T(8,128)(2,1)S(1)} %get-tuple-element.19.refs_0_, bf16[256,128]{1,0:T(8,128)(2,1)S(1)} %collective-permute-done.1.refs_1_, ...), custom_call_target="tpu_custom_call" | custom-call | flops 107374182400 | bytes 4194304 | tf_op jit(solution)/shard_map/pallas_call | solution.py:160
  15.0 0.0 copy-start
  15.0 1.7 %collective-permute-done.3.refs_1_ = bf16[256,128]{1,0:T(8,128)(2,1)S(1)} collective-permute-done((bf16[256,128]{1,0:T(8,128)(2,1)S(1)}, bf16[256,128]{1,0:T(8,128)(2,1)S(1)}, u32[]{:S(2)}, u32[]{:S(2)}) %collective-permute-start.3) | collective-permute-done | bytes 65568 | tf_op jit(solution)/shard_map/ppermute | solution.py:40
  16.7 0.0 collective-permute-done.4.refs_2_
  16.7 0.0 collective-permute-done.5.refs_3_
  16.7 1.3 %shard_map.58 = (bf16[256,512]{1,0:T(8,128)(2,1)S(1)}, bf16[256,512]{1,0:T(8,128)(2,1)S(1)}) custom-call(bf16[2,1024,1024]{2,1,0:T(8,128)(2,1)S(1)} %shard_map.57.weights_ref, bf16[256,128]{1,0:T(8,128)(2,1)S(1)} %get-tuple-element.24.refs_0_, bf16[256,128]{1,0:T(8,128)(2,1)S(1)} %collective-permute-done.3.refs_1_, ...), custom_call_target="tpu_custom_call" | custom-call | flops 107374182400 | bytes 1048576 | tf_op jit(solution)/shard_map/pallas_call | solution.py:198
  17.9 0.1 collective-permute-start.7
  18.0 0.5 %collective-permute-start.8 = (bf16[256,512]{1,0:T(8,128)(2,1)S(1)}, bf16[256,512]{1,0:T(8,128)(2,1)S(1)}, u32[]{:S(2)}, u32[]{:S(2)}) collective-permute-start(bf16[256,512]{1,0:T(8,128)(2,1)S(1)} %get-tuple-element.26.refs_1_), channel_id=1, source_target_pairs={{0,1},{1,0},{2,3},{3,2},{4,5},{5,4},{6,7},{7,6},{8,9},{9,8},{10,11... | collective-permute-start | bytes 786440 | tf_op jit(solution)/shard_map/ppermute | solution.py:45
  18.5 1.8 %collective-permute-start.6 = (bf16[256,512]{1,0:T(8,128)(2,1)S(1)}, bf16[256,512]{1,0:T(8,128)(2,1)S(1)}, u32[]{:S(2)}, u32[]{:S(2)}) collective-permute-start(bf16[256,512]{1,0:T(8,128)(2,1)S(1)} %get-tuple-element.25.refs_0_), channel_id=1, source_target_pairs={{0,2},{1,3},{2,0},{3,1},{4,6},{5,7},{6,4},{7,5},{8,10},{9,11},{10,... | collective-permute-start | bytes 786440 | tf_op jit(solution)/shard_map/ppermute | solution.py:45
  20.3 1.5 %collective-permute-start.10 = (bf16[256,512]{1,0:T(8,128)(2,1)S(1)}, bf16[256,512]{1,0:T(8,128)(2,1)S(1)}, u32[]{:S(2)}, u32[]{:S(2)}) collective-permute-start(bf16[256,512]{1,0:T(8,128)(2,1)S(1)} %get-tuple-element.26.refs_1_), channel_id=1, source_target_pairs={{0,4},{1,5},{2,6},{3,7},{4,0},{5,1},{6,2},{7,3},{8,12},{9,13},{10,... | collective-permute-start | bytes 786440 | tf_op jit(solution)/shard_map/ppermute | solution.py:45
  21.8 0.5 %collective-permute-start.13 = (bf16[256,512]{1,0:T(8,128)(2,1)S(1)}, bf16[256,512]{1,0:T(8,128)(2,1)S(1)}, u32[]{:S(2)}, u32[]{:S(2)}) collective-permute-start(bf16[256,512]{1,0:T(8,128)(2,1)S(1)} %get-tuple-element.26.refs_1_), channel_id=1, source_target_pairs={{0,2},{1,3},{2,0},{3,1},{4,6},{5,7},{6,4},{7,5},{8,10},{9,11},{10,... | collective-permute-start | bytes 786440 | tf_op jit(solution)/shard_map/ppermute | solution.py:45
  22.3 0.0 collective-permute-done.7.refs_2_
  22.3 0.2 collective-permute-start.15
  22.6 0.0 collective-permute-done.8.refs_3_
  22.6 0.0 copy-done
  22.6 1.2 %shard_map.59.refs_0_ = f32[256,1024]{1,0:T(8,128)S(1)} custom-call(bf16[8192,1024]{1,0:T(8,128)(2,1)S(1)} %copy-done, bf16[256,512]{1,0:T(8,128)(2,1)S(1)} %get-tuple-element.25.refs_0_, bf16[256,512]{1,0:T(8,128)(2,1)S(1)} %get-tuple-element.26.refs_1_, bf16[256,512]{1,0:T(8,128)(2,1)S(1)} %collective-permute-done.7.refs_2_, ...), custom_call_target="tpu_custom_call" | custom-call | flops 4294967296 | bytes 1048576 | tf_op jit(solution)/shard_map/pallas_call | solution.py:249
  23.8 3.8 %collective-permute-done.6.refs_1_ = bf16[256,512]{1,0:T(8,128)(2,1)S(1)} collective-permute-done((bf16[256,512]{1,0:T(8,128)(2,1)S(1)}, bf16[256,512]{1,0:T(8,128)(2,1)S(1)}, u32[]{:S(2)}, u32[]{:S(2)}) %collective-permute-start.6) | collective-permute-done | bytes 262176 | tf_op jit(solution)/shard_map/ppermute | solution.py:45
  27.7 1.8 %collective-permute-done.10.refs_3_ = bf16[256,512]{1,0:T(8,128)(2,1)S(1)} collective-permute-done((bf16[256,512]{1,0:T(8,128)(2,1)S(1)}, bf16[256,512]{1,0:T(8,128)(2,1)S(1)}, u32[]{:S(2)}, u32[]{:S(2)}) %collective-permute-start.10) | collective-permute-done | bytes 262176 | tf_op jit(solution)/shard_map/ppermute | solution.py:45
  29.5 0.0 collective-permute-start.12
  29.5 0.5 %collective-permute-start.11 = (bf16[256,512]{1,0:T(8,128)(2,1)S(1)}, bf16[256,512]{1,0:T(8,128)(2,1)S(1)}, u32[]{:S(2)}, u32[]{:S(2)}) collective-permute-start(bf16[256,512]{1,0:T(8,128)(2,1)S(1)} %collective-permute-done.6.refs_1_), channel_id=1, source_target_pairs={{0,1},{1,0},{2,3},{3,2},{4,5},{5,4},{6,7},{7,6},{8,9},{9,8},{10,11... | collective-permute-start | bytes 786440 | tf_op jit(solution)/shard_map/ppermute | solution.py:45
  30.0 1.5 %collective-permute-start.9 = (bf16[256,512]{1,0:T(8,128)(2,1)S(1)}, bf16[256,512]{1,0:T(8,128)(2,1)S(1)}, u32[]{:S(2)}, u32[]{:S(2)}) collective-permute-start(bf16[256,512]{1,0:T(8,128)(2,1)S(1)} %collective-permute-done.6.refs_1_), channel_id=1, source_target_pairs={{0,4},{1,5},{2,6},{3,7},{4,0},{5,1},{6,2},{7,3},{8,12},{9,13},{10,... | collective-permute-start | bytes 786440 | tf_op jit(solution)/shard_map/ppermute | solution.py:45
  31.5 0.9 %collective-permute-done.13.refs_1_ = bf16[256,512]{1,0:T(8,128)(2,1)S(1)} collective-permute-done((bf16[256,512]{1,0:T(8,128)(2,1)S(1)}, bf16[256,512]{1,0:T(8,128)(2,1)S(1)}, u32[]{:S(2)}, u32[]{:S(2)}) %collective-permute-start.13) | collective-permute-done | bytes 262176 | tf_op jit(solution)/shard_map/ppermute | solution.py:45
  32.4 1.7 %collective-permute-start.17 = (bf16[256,512]{1,0:T(8,128)(2,1)S(1)}, bf16[256,512]{1,0:T(8,128)(2,1)S(1)}, u32[]{:S(2)}, u32[]{:S(2)}) collective-permute-start(bf16[256,512]{1,0:T(8,128)(2,1)S(1)} %collective-permute-done.10.refs_3_), channel_id=1, source_target_pairs={{0,2},{1,3},{2,0},{3,1},{4,6},{5,7},{6,4},{7,5},{8,10},{9,11},{10,... | collective-permute-start | bytes 786440 | tf_op jit(solution)/shard_map/ppermute | solution.py:45
  34.2 0.9 %collective-permute-done.15.refs_3_ = bf16[256,512]{1,0:T(8,128)(2,1)S(1)} collective-permute-done((bf16[256,512]{1,0:T(8,128)(2,1)S(1)}, bf16[256,512]{1,0:T(8,128)(2,1)S(1)}, u32[]{:S(2)}, u32[]{:S(2)}) %collective-permute-start.15) | collective-permute-done | bytes 262176 | tf_op jit(solution)/shard_map/ppermute | solution.py:45
  35.1 0.0 collective-permute-start.14
  35.1 0.0 collective-permute-done.12.refs_4_
  35.1 0.5 %collective-permute-start.16 = (bf16[256,512]{1,0:T(8,128)(2,1)S(1)}, bf16[256,512]{1,0:T(8,128)(2,1)S(1)}, u32[]{:S(2)}, u32[]{:S(2)}) collective-permute-start(bf16[256,512]{1,0:T(8,128)(2,1)S(1)} %collective-permute-done.15.refs_3_), channel_id=1, source_target_pairs={{0,1},{1,0},{2,3},{3,2},{4,5},{5,4},{6,7},{7,6},{8,9},{9,8},{10,11... | collective-permute-start | bytes 786440 | tf_op jit(solution)/shard_map/ppermute | solution.py:45
  35.6 0.0 collective-permute-done.11.refs_2_
  35.6 1.2 %shard_map.60.refs_0_ = f32[256,1024]{1,0:T(8,128)S(1)} custom-call(bf16[8192,1024]{1,0:T(8,128)(2,1)S(1)} %copy-done, f32[256,1024]{1,0:T(8,128)S(1)} %shard_map.59.refs_0_, bf16[256,512]{1,0:T(8,128)(2,1)S(1)} %collective-permute-done.6.refs_1_, bf16[256,512]{1,0:T(8,128)(2,1)S(1)} %collective-permute-done.11.refs_2_, ...), custom_call_target="tpu_custom_call" | custom-call | flops 4294967296 | bytes 1048576 | tf_op jit(solution)/shard_map/pallas_call | solution.py:249
  36.9 0.0 collective-permute-done.14.refs_2_
  36.9 0.1 collective-permute-done.16.refs_4_
  37.0 1.2 %shard_map.61.refs_0_ = f32[256,1024]{1,0:T(8,128)S(1)} custom-call(bf16[8192,1024]{1,0:T(8,128)(2,1)S(1)} %copy-done, f32[256,1024]{1,0:T(8,128)S(1)} %shard_map.60.refs_0_, bf16[256,512]{1,0:T(8,128)(2,1)S(1)} %collective-permute-done.13.refs_1_, bf16[256,512]{1,0:T(8,128)(2,1)S(1)} %collective-permute-done.14.refs_2_, ...), custom_call_target="tpu_custom_call" | custom-call | flops 4294967296 | bytes 1048576 | tf_op jit(solution)/shard_map/pallas_call | solution.py:249
  38.3 1.3 %collective-permute-done.9.refs_1_ = bf16[256,512]{1,0:T(8,128)(2,1)S(1)} collective-permute-done((bf16[256,512]{1,0:T(8,128)(2,1)S(1)}, bf16[256,512]{1,0:T(8,128)(2,1)S(1)}, u32[]{:S(2)}, u32[]{:S(2)}) %collective-permute-start.9) | collective-permute-done | bytes 262176 | tf_op jit(solution)/shard_map/ppermute | solution.py:45
  39.5 0.0 collective-permute-start.18
  39.5 0.4 collective-permute-done.17.refs_2_
  39.9 0.1 collective-permute-start.19
  40.0 0.7 %shard_map.62.refs_0_ = f32[256,1024]{1,0:T(8,128)S(1)} custom-call(bf16[8192,1024]{1,0:T(8,128)(2,1)S(1)} %copy-done, f32[256,1024]{1,0:T(8,128)S(1)} %shard_map.61.refs_0_, bf16[256,512]{1,0:T(8,128)(2,1)S(1)} %collective-permute-done.9.refs_1_, bf16[256,512]{1,0:T(8,128)(2,1)S(1)} %collective-permute-done.17.refs_2_), custom_call_target="tpu_custom_call" | custom-call | flops 2147483648 | bytes 1048576 | tf_op jit(solution)/shard_map/pallas_call | solution.py:249
  40.8 0.3 collective-permute-done.18.refs_1_
  41.1 0.4 collective-permute-done.19.refs_2_
  41.5 1.5 %shard_map.63 = bf16[256,1024]{1,0:T(8,128)(2,1)} custom-call(bf16[8192,1024]{1,0:T(8,128)(2,1)S(1)} %copy-done, f32[256,1024]{1,0:T(8,128)S(1)} %shard_map.62.refs_0_, bf16[256,512]{1,0:T(8,128)(2,1)S(1)} %collective-permute-done.18.refs_1_, bf16[256,512]{1,0:T(8,128)(2,1)S(1)} %collective-permute-done.19.refs_2_), custom_call_target="tpu_custom_call" | custom-call | flops 2147483648 | bytes 1048576 | tf_op jit(solution)/shard_map/pallas_call | solution.py:249
Async XLA Ops:
  0.9 8.0 %collective-permute-start = (bf16[256,128]{1,0:T(8,128)(2,1)S(1)}, bf16[256,128]{1,0:T(8,128)(2,1)S(1)}, u32[]{:S(2)}, u32[]{:S(2)}) collective-permute-start(bf16[256,128]{1,0:T(8,128)(2,1)S(1)} %get-tuple-element.19.refs_0_), channel_id=1, source_target_pairs={{0,8},{8,16},{16,24},{24,0},{1,9},{9,17},{17,25},{25,1},{2,10},{10... | collective-permute-start | bytes 196616 | tf_op jit(solution)/shard_map/ppermute | solution.py:40
  4.0 9.1 %collective-permute-start.1 = (bf16[256,128]{1,0:T(8,128)(2,1)S(1)}, bf16[256,128]{1,0:T(8,128)(2,1)S(1)}, u32[]{:S(2)}, u32[]{:S(2)}) collective-permute-start(bf16[256,128]{1,0:T(8,128)(2,1)S(1)} %get-tuple-element.19.refs_0_), channel_id=1, source_target_pairs={{0,16},{8,24},{16,0},{24,8},{1,17},{9,25},{17,1},{25,9},{2,18},{10... | collective-permute-start | bytes 196616 | tf_op jit(solution)/shard_map/ppermute | solution.py:40
  6.6 6.5 %collective-permute-start.2 = (bf16[256,128]{1,0:T(8,128)(2,1)S(1)}, bf16[256,128]{1,0:T(8,128)(2,1)S(1)}, u32[]{:S(2)}, u32[]{:S(2)}) collective-permute-start(bf16[256,128]{1,0:T(8,128)(2,1)S(1)} %get-tuple-element.19.refs_0_), channel_id=1, source_target_pairs={{0,24},{8,0},{16,8},{24,16},{1,25},{9,1},{17,9},{25,17},{2,26},{10... | collective-permute-start | bytes 196616 | tf_op jit(solution)/shard_map/ppermute | solution.py:40
  7.9 8.8 %collective-permute-start.3 = (bf16[256,128]{1,0:T(8,128)(2,1)S(1)}, bf16[256,128]{1,0:T(8,128)(2,1)S(1)}, u32[]{:S(2)}, u32[]{:S(2)}) collective-permute-start(bf16[256,128]{1,0:T(8,128)(2,1)S(1)} %get-tuple-element.24.refs_0_), channel_id=1, source_target_pairs={{0,16},{8,24},{16,0},{24,8},{1,17},{9,25},{17,1},{25,9},{2,18},{10... | collective-permute-start | bytes 196616 | tf_op jit(solution)/shard_map/ppermute | solution.py:40
  8.1 8.6 %collective-permute-start.4 = (bf16[256,128]{1,0:T(8,128)(2,1)S(1)}, bf16[256,128]{1,0:T(8,128)(2,1)S(1)}, u32[]{:S(2)}, u32[]{:S(2)}) collective-permute-start(bf16[256,128]{1,0:T(8,128)(2,1)S(1)} %get-tuple-element.24.refs_0_), channel_id=1, source_target_pairs={{0,8},{8,16},{16,24},{24,0},{1,9},{9,17},{17,25},{25,1},{2,10},{10... | collective-permute-start | bytes 196616 | tf_op jit(solution)/shard_map/ppermute | solution.py:40
  8.9 7.7 %collective-permute-start.5 = (bf16[256,128]{1,0:T(8,128)(2,1)S(1)}, bf16[256,128]{1,0:T(8,128)(2,1)S(1)}, u32[]{:S(2)}, u32[]{:S(2)}) collective-permute-start(bf16[256,128]{1,0:T(8,128)(2,1)S(1)} %get-tuple-element.24.refs_0_), channel_id=1, source_target_pairs={{0,24},{8,0},{16,8},{24,16},{1,25},{9,1},{17,9},{25,17},{2,26},{10... | collective-permute-start | bytes 196616 | tf_op jit(solution)/shard_map/ppermute | solution.py:40
  15.0 7.6 %copy-start = (bf16[8192,1024]{1,0:T(8,128)(2,1)S(1)}, bf16[8192,1024]{1,0:T(8,128)(2,1)}, u32[]{:S(2)}) copy-start(bf16[8192,1024]{1,0:T(8,128)(2,1)} %weight_ref.9) | copy-start | bytes 50331652
  17.9 4.4 %collective-permute-start.7 = (bf16[256,512]{1,0:T(8,128)(2,1)S(1)}, bf16[256,512]{1,0:T(8,128)(2,1)S(1)}, u32[]{:S(2)}, u32[]{:S(2)}) collective-permute-start(bf16[256,512]{1,0:T(8,128)(2,1)S(1)} %get-tuple-element.25.refs_0_), channel_id=1, source_target_pairs={{0,1},{1,0},{2,3},{3,2},{4,5},{5,4},{6,7},{7,6},{8,9},{9,8},{10,11... | collective-permute-start | bytes 786440 | tf_op jit(solution)/shard_map/ppermute | solution.py:45
  18.0 4.6 %collective-permute-start.8 = (bf16[256,512]{1,0:T(8,128)(2,1)S(1)}, bf16[256,512]{1,0:T(8,128)(2,1)S(1)}, u32[]{:S(2)}, u32[]{:S(2)}) collective-permute-start(bf16[256,512]{1,0:T(8,128)(2,1)S(1)} %get-tuple-element.26.refs_1_), channel_id=1, source_target_pairs={{0,1},{1,0},{2,3},{3,2},{4,5},{5,4},{6,7},{7,6},{8,9},{9,8},{10,11... | collective-permute-start | bytes 786440 | tf_op jit(solution)/shard_map/ppermute | solution.py:45
  18.5 9.2 %collective-permute-start.6 = (bf16[256,512]{1,0:T(8,128)(2,1)S(1)}, bf16[256,512]{1,0:T(8,128)(2,1)S(1)}, u32[]{:S(2)}, u32[]{:S(2)}) collective-permute-start(bf16[256,512]{1,0:T(8,128)(2,1)S(1)} %get-tuple-element.25.refs_0_), channel_id=1, source_target_pairs={{0,2},{1,3},{2,0},{3,1},{4,6},{5,7},{6,4},{7,5},{8,10},{9,11},{10,... | collective-permute-start | bytes 786440 | tf_op jit(solution)/shard_map/ppermute | solution.py:45
  20.3 9.2 %collective-permute-start.10 = (bf16[256,512]{1,0:T(8,128)(2,1)S(1)}, bf16[256,512]{1,0:T(8,128)(2,1)S(1)}, u32[]{:S(2)}, u32[]{:S(2)}) collective-permute-start(bf16[256,512]{1,0:T(8,128)(2,1)S(1)} %get-tuple-element.26.refs_1_), channel_id=1, source_target_pairs={{0,4},{1,5},{2,6},{3,7},{4,0},{5,1},{6,2},{7,3},{8,12},{9,13},{10,... | collective-permute-start | bytes 786440 | tf_op jit(solution)/shard_map/ppermute | solution.py:45
  21.8 10.6 %collective-permute-start.13 = (bf16[256,512]{1,0:T(8,128)(2,1)S(1)}, bf16[256,512]{1,0:T(8,128)(2,1)S(1)}, u32[]{:S(2)}, u32[]{:S(2)}) collective-permute-start(bf16[256,512]{1,0:T(8,128)(2,1)S(1)} %get-tuple-element.26.refs_1_), channel_id=1, source_target_pairs={{0,2},{1,3},{2,0},{3,1},{4,6},{5,7},{6,4},{7,5},{8,10},{9,11},{10,... | collective-permute-start | bytes 786440 | tf_op jit(solution)/shard_map/ppermute | solution.py:45
  22.3 12.8 %collective-permute-start.15 = (bf16[256,512]{1,0:T(8,128)(2,1)S(1)}, bf16[256,512]{1,0:T(8,128)(2,1)S(1)}, u32[]{:S(2)}, u32[]{:S(2)}) collective-permute-start(bf16[256,512]{1,0:T(8,128)(2,1)S(1)} %get-tuple-element.25.refs_0_), channel_id=1, source_target_pairs={{0,4},{1,5},{2,6},{3,7},{4,0},{5,1},{6,2},{7,3},{8,12},{9,13},{10,... | collective-permute-start | bytes 786440 | tf_op jit(solution)/shard_map/ppermute | solution.py:45
  29.5 5.6 %collective-permute-start.12 = (bf16[256,512]{1,0:T(8,128)(2,1)S(1)}, bf16[256,512]{1,0:T(8,128)(2,1)S(1)}, u32[]{:S(2)}, u32[]{:S(2)}) collective-permute-start(bf16[256,512]{1,0:T(8,128)(2,1)S(1)} %collective-permute-done.10.refs_3_), channel_id=1, source_target_pairs={{0,1},{1,0},{2,3},{3,2},{4,5},{5,4},{6,7},{7,6},{8,9},{9,8},{10,11... | collective-permute-start | bytes 786440 | tf_op jit(solution)/shard_map/ppermute | solution.py:45
  29.5 6.1 %collective-permute-start.11 = (bf16[256,512]{1,0:T(8,128)(2,1)S(1)}, bf16[256,512]{1,0:T(8,128)(2,1)S(1)}, u32[]{:S(2)}, u32[]{:S(2)}) collective-permute-start(bf16[256,512]{1,0:T(8,128)(2,1)S(1)} %collective-permute-done.6.refs_1_), channel_id=1, source_target_pairs={{0,1},{1,0},{2,3},{3,2},{4,5},{5,4},{6,7},{7,6},{8,9},{9,8},{10,11... | collective-permute-start | bytes 786440 | tf_op jit(solution)/shard_map/ppermute | solution.py:45
  30.0 9.5 %collective-permute-start.9 = (bf16[256,512]{1,0:T(8,128)(2,1)S(1)}, bf16[256,512]{1,0:T(8,128)(2,1)S(1)}, u32[]{:S(2)}, u32[]{:S(2)}) collective-permute-start(bf16[256,512]{1,0:T(8,128)(2,1)S(1)} %collective-permute-done.6.refs_1_), channel_id=1, source_target_pairs={{0,4},{1,5},{2,6},{3,7},{4,0},{5,1},{6,2},{7,3},{8,12},{9,13},{10,... | collective-permute-start | bytes 786440 | tf_op jit(solution)/shard_map/ppermute | solution.py:45
  32.4 7.5 %collective-permute-start.17 = (bf16[256,512]{1,0:T(8,128)(2,1)S(1)}, bf16[256,512]{1,0:T(8,128)(2,1)S(1)}, u32[]{:S(2)}, u32[]{:S(2)}) collective-permute-start(bf16[256,512]{1,0:T(8,128)(2,1)S(1)} %collective-permute-done.10.refs_3_), channel_id=1, source_target_pairs={{0,2},{1,3},{2,0},{3,1},{4,6},{5,7},{6,4},{7,5},{8,10},{9,11},{10,... | collective-permute-start | bytes 786440 | tf_op jit(solution)/shard_map/ppermute | solution.py:45
  35.1 1.8 %collective-permute-start.14 = (bf16[256,512]{1,0:T(8,128)(2,1)S(1)}, bf16[256,512]{1,0:T(8,128)(2,1)S(1)}, u32[]{:S(2)}, u32[]{:S(2)}) collective-permute-start(bf16[256,512]{1,0:T(8,128)(2,1)S(1)} %collective-permute-done.13.refs_1_), channel_id=1, source_target_pairs={{0,1},{1,0},{2,3},{3,2},{4,5},{5,4},{6,7},{7,6},{8,9},{9,8},{10,11... | collective-permute-start | bytes 786440 | tf_op jit(solution)/shard_map/ppermute | solution.py:45
  35.1 1.9 %collective-permute-start.16 = (bf16[256,512]{1,0:T(8,128)(2,1)S(1)}, bf16[256,512]{1,0:T(8,128)(2,1)S(1)}, u32[]{:S(2)}, u32[]{:S(2)}) collective-permute-start(bf16[256,512]{1,0:T(8,128)(2,1)S(1)} %collective-permute-done.15.refs_3_), channel_id=1, source_target_pairs={{0,1},{1,0},{2,3},{3,2},{4,5},{5,4},{6,7},{7,6},{8,9},{9,8},{10,11... | collective-permute-start | bytes 786440 | tf_op jit(solution)/shard_map/ppermute | solution.py:45
  39.5 1.5 %collective-permute-start.18 = (bf16[256,512]{1,0:T(8,128)(2,1)S(1)}, bf16[256,512]{1,0:T(8,128)(2,1)S(1)}, u32[]{:S(2)}, u32[]{:S(2)}) collective-permute-start(bf16[256,512]{1,0:T(8,128)(2,1)S(1)} %collective-permute-done.9.refs_1_), channel_id=1, source_target_pairs={{0,1},{1,0},{2,3},{3,2},{4,5},{5,4},{6,7},{7,6},{8,9},{9,8},{10,11... | collective-permute-start | bytes 786440 | tf_op jit(solution)/shard_map/ppermute | solution.py:45
  39.9 1.5 %collective-permute-start.19 = (bf16[256,512]{1,0:T(8,128)(2,1)S(1)}, bf16[256,512]{1,0:T(8,128)(2,1)S(1)}, u32[]{:S(2)}, u32[]{:S(2)}) collective-permute-start(bf16[256,512]{1,0:T(8,128)(2,1)S(1)} %collective-permute-done.17.refs_2_), channel_id=1, source_target_pairs={{0,1},{1,0},{2,3},{3,2},{4,5},{5,4},{6,7},{7,6},{8,9},{9,8},{10,11... | collective-permute-start | bytes 786440 | tf_op jit(solution)/shard_map/ppermute | solution.py:45

commit v11 on v10

--- a/solution.py
+++ b/solution.py
@@ -298,7 +298,7 @@
     sb = swapped(b, "head", 1)
     width, half = heads_dev * HEAD_SIZE, heads_dev * HEAD_SIZE // 2
     mixed = projected(
-        None, weight, width, ((0, 0), (0, half), (1, 0), (1, half)), [a, b, sa, sb]
+        None, weight, width, ((0, 0), (0, half), (1, 0)), [a, b, sa]
     )
     xa, mixed = barrier((xa, mixed))
     da = swapped(xa, "head", 4)
@@ -306,7 +306,7 @@
     db = swapped(yb, "head", 2)
     xas, ybs = swapped(xa, "head", 1), swapped(yb, "head", 1)
     mixed = projected(
-        mixed, weight, width, ((2, 0), (3, 0), (4, half), (5, half)), [xa, xas, yb, ybs]
+        mixed, weight, width, ((2, 0), (3, 0), (4, half), (5, half), (1, half)), [xa, xas, yb, ybs, sb]
     )
     xbs, yas = swapped(xb, "head", 1), swapped(ya, "head", 1)
     mixed = projected(

time: 43.2 us -> 43.5 us (level)
  waiting for transfers between devices: 11.7 us -> 12.5 us
  starting transfers between devices: 20.1 us -> 19.5 us
    ppermute x14, waiting for transfers between devices: 9.99 us -> 10.8 us  [swapped(): lax.ppermute(value, axis, [(source, source ^ bits) for source in range(co...]
    ppermute x14, starting transfers between devices: 9.02 us -> 8.49 us  [swapped(): lax.ppermute(value, axis, [(source, source ^ bits) for source in range(co...]
  transfers between devices with their start and end apart: 20 -> 20, of which waited for: 10 -> 8; matrix products, arithmetic and copies ran while one was open for 0% -> 0% of each run, Pallas kernels for 17% -> 17%
where the time goes in v11:
time: 43.5 us; the launch traced here: 43.3 us
  starting transfers between devices  19.5 us (45%)
  waiting for transfers between devices  12.5 us (29%)
  Pallas kernels  11.1 us (26%)
    ppermute x6, starting transfers between devices, shifted(): lax.ppermute(value, axis, [(source, (source + steps) % count) for source...  11 us
    ppermute x14, waiting for transfers between devices, swapped(): lax.ppermute(value, axis, [(source, source ^ bits) for source in range(co...  10.8 us
    ppermute x14, starting transfers between devices, swapped(): lax.ppermute(value, axis, [(source, source ^ bits) for source in range(co...  8.49 us
    pallas_call x5, Pallas kernels, projected(): pl.pallas_call(functools.partial(projection_kernel, places, width, fresh,...  5.91 us
    pallas_call x1, Pallas kernels, weights_of(): pl.pallas_call(weights_kernel, out_shape=held((blocks_dev, rows, keys)),...  1.84 us
    ppermute x6, waiting for transfers between devices, shifted(): lax.ppermute(value, axis, [(source, (source + steps) % count) for source...  1.71 us
    pallas_call x1, Pallas kernels, attended_of(): pl.pallas_call(functools.partial(values_kernel, len(value_parts)), out_sh...  1.26 us
    pallas_call x1, Pallas kernels, stacked_of(): pl.pallas_call(functools.partial(stack_kernel, steps, count), out_shape=[...  1.15 us
  transfers between devices with their start and end apart: 20, of which 8 were waited for; matrix products, arithmetic and copies ran while one was open for 0% of the time, Pallas kernels for 17%

profile of v11, /device:TPU:0, one launch (start us, length us, event | category | flops | bytes accessed | tf_op | source)
XLA Modules:
  0.0 43.3 jit_solution(4819724195197520774)
XLA Ops:
  0.0 0.9 %shard_map.55 = (bf16[256,128]{1,0:T(8,128)(2,1)S(1)}, bf16[256,128]{1,0:T(8,128)(2,1)S(1)}) custom-call(bf16[256,1024]{1,0:T(8,128)(2,1)} %keys_ref.1, bf16[256,1024]{1,0:T(8,128)(2,1)} %values_ref.1), custom_call_target="tpu_custom_call" | custom-call | bytes 262144 | tf_op jit(solution)/shard_map/pallas_call | solution.py:68
  0.9 3.1 %collective-permute-start = (bf16[256,128]{1,0:T(8,128)(2,1)S(1)}, bf16[256,128]{1,0:T(8,128)(2,1)S(1)}, u32[]{:S(2)}, u32[]{:S(2)}) collective-permute-start(bf16[256,128]{1,0:T(8,128)(2,1)S(1)} %get-tuple-element.19.refs_0_), channel_id=1, source_target_pairs={{0,8},{8,16},{16,24},{24,0},{1,9},{9,17},{17,25},{25,1},{2,10},{10... | collective-permute-start | bytes 196616 | tf_op jit(solution)/shard_map/ppermute | solution.py:40
  4.0 2.6 %collective-permute-start.1 = (bf16[256,128]{1,0:T(8,128)(2,1)S(1)}, bf16[256,128]{1,0:T(8,128)(2,1)S(1)}, u32[]{:S(2)}, u32[]{:S(2)}) collective-permute-start(bf16[256,128]{1,0:T(8,128)(2,1)S(1)} %get-tuple-element.19.refs_0_), channel_id=1, source_target_pairs={{0,16},{8,24},{16,0},{24,8},{1,17},{9,25},{17,1},{25,9},{2,18},{10... | collective-permute-start | bytes 196616 | tf_op jit(solution)/shard_map/ppermute | solution.py:40
  6.6 1.3 %collective-permute-start.2 = (bf16[256,128]{1,0:T(8,128)(2,1)S(1)}, bf16[256,128]{1,0:T(8,128)(2,1)S(1)}, u32[]{:S(2)}, u32[]{:S(2)}) collective-permute-start(bf16[256,128]{1,0:T(8,128)(2,1)S(1)} %get-tuple-element.19.refs_0_), channel_id=1, source_target_pairs={{0,24},{8,0},{16,8},{24,16},{1,25},{9,1},{17,9},{25,17},{2,26},{10... | collective-permute-start | bytes 196616 | tf_op jit(solution)/shard_map/ppermute | solution.py:40
  7.9 0.2 collective-permute-start.3
  8.1 0.8 %collective-permute-start.4 = (bf16[256,128]{1,0:T(8,128)(2,1)S(1)}, bf16[256,128]{1,0:T(8,128)(2,1)S(1)}, u32[]{:S(2)}, u32[]{:S(2)}) collective-permute-start(bf16[256,128]{1,0:T(8,128)(2,1)S(1)} %get-tuple-element.24.refs_0_), channel_id=1, source_target_pairs={{0,8},{8,16},{16,24},{24,0},{1,9},{9,17},{17,25},{25,1},{2,10},{10... | collective-permute-start | bytes 196616 | tf_op jit(solution)/shard_map/ppermute | solution.py:40
  8.9 0.0 collective-permute-done.refs_2_
  8.9 3.0 %collective-permute-start.5 = (bf16[256,128]{1,0:T(8,128)(2,1)S(1)}, bf16[256,128]{1,0:T(8,128)(2,1)S(1)}, u32[]{:S(2)}, u32[]{:S(2)}) collective-permute-start(bf16[256,128]{1,0:T(8,128)(2,1)S(1)} %get-tuple-element.24.refs_0_), channel_id=1, source_target_pairs={{0,24},{8,0},{16,8},{24,16},{1,25},{9,1},{17,9},{25,17},{2,26},{10... | collective-permute-start | bytes 196616 | tf_op jit(solution)/shard_map/ppermute | solution.py:40
  11.9 1.2 %shard_map.56 = (bf16[2,1024,128]{2,1,0:T(8,128)(2,1)S(1)}, bf16[2,1024,128]{2,1,0:T(8,128)(2,1)S(1)}) custom-call(bf16[256,1024]{1,0:T(8,128)(2,1)} %q_ref, s32[8,8]{1,0:T(8,128)} %pattern_ref.1), custom_call_target="tpu_custom_call" | custom-call | bytes 1048576 | tf_op jit(solution)/shard_map/pallas_call | solution.py:119
  13.1 0.0 collective-permute-done.1.refs_1_
  13.1 0.0 collective-permute-done.2.refs_3_
  13.1 1.8 %shard_map.57.weights_ref = bf16[2,1024,1024]{2,1,0:T(8,128)(2,1)S(1)} custom-call(bf16[2,1024,128]{2,1,0:T(8,128)(2,1)S(1)} %get-tuple-element.21.q_ref, bf16[2,1024,128]{2,1,0:T(8,128)(2,1)S(1)} %get-tuple-element.22.mask_ref, bf16[256,128]{1,0:T(8,128)(2,1)S(1)} %get-tuple-element.19.refs_0_, bf16[256,128]{1,0:T(8,128)(2,1)S(1)} %collective-permute-done.1.refs_1_, ...), custom_call_target="tpu_custom_call" | custom-call | flops 107374182400 | bytes 4194304 | tf_op jit(solution)/shard_map/pallas_call | solution.py:160
  15.0 0.0 copy-start
  15.0 1.7 %collective-permute-done.3.refs_1_ = bf16[256,128]{1,0:T(8,128)(2,1)S(1)} collective-permute-done((bf16[256,128]{1,0:T(8,128)(2,1)S(1)}, bf16[256,128]{1,0:T(8,128)(2,1)S(1)}, u32[]{:S(2)}, u32[]{:S(2)}) %collective-permute-start.3) | collective-permute-done | bytes 65568 | tf_op jit(solution)/shard_map/ppermute | solution.py:40
  16.7 0.0 collective-permute-done.4.refs_2_
  16.7 0.0 collective-permute-done.5.refs_3_
  16.7 1.3 %shard_map.58 = (bf16[256,512]{1,0:T(8,128)(2,1)S(1)}, bf16[256,512]{1,0:T(8,128)(2,1)S(1)}) custom-call(bf16[2,1024,1024]{2,1,0:T(8,128)(2,1)S(1)} %shard_map.57.weights_ref, bf16[256,128]{1,0:T(8,128)(2,1)S(1)} %get-tuple-element.24.refs_0_, bf16[256,128]{1,0:T(8,128)(2,1)S(1)} %collective-permute-done.3.refs_1_, ...), custom_call_target="tpu_custom_call" | custom-call | flops 107374182400 | bytes 1048576 | tf_op jit(solution)/shard_map/pallas_call | solution.py:198
  17.9 0.1 collective-permute-start.7
  18.0 1.8 %collective-permute-start.6 = (bf16[256,512]{1,0:T(8,128)(2,1)S(1)}, bf16[256,512]{1,0:T(8,128)(2,1)S(1)}, u32[]{:S(2)}, u32[]{:S(2)}) collective-permute-start(bf16[256,512]{1,0:T(8,128)(2,1)S(1)} %get-tuple-element.25.refs_0_), channel_id=1, source_target_pairs={{0,2},{1,3},{2,0},{3,1},{4,6},{5,7},{6,4},{7,5},{8,10},{9,11},{10,... | collective-permute-start | bytes 786440 | tf_op jit(solution)/shard_map/ppermute | solution.py:45
  19.9 1.5 %collective-permute-start.9 = (bf16[256,512]{1,0:T(8,128)(2,1)S(1)}, bf16[256,512]{1,0:T(8,128)(2,1)S(1)}, u32[]{:S(2)}, u32[]{:S(2)}) collective-permute-start(bf16[256,512]{1,0:T(8,128)(2,1)S(1)} %get-tuple-element.26.refs_1_), channel_id=1, source_target_pairs={{0,4},{1,5},{2,6},{3,7},{4,0},{5,1},{6,2},{7,3},{8,12},{9,13},{10,... | collective-permute-start | bytes 786440 | tf_op jit(solution)/shard_map/ppermute | solution.py:45
  21.4 0.0 collective-permute-start.12
  21.4 0.5 %collective-permute-start.13 = (bf16[256,512]{1,0:T(8,128)(2,1)S(1)}, bf16[256,512]{1,0:T(8,128)(2,1)S(1)}, u32[]{:S(2)}, u32[]{:S(2)}) collective-permute-start(bf16[256,512]{1,0:T(8,128)(2,1)S(1)} %get-tuple-element.26.refs_1_), channel_id=1, source_target_pairs={{0,2},{1,3},{2,0},{3,1},{4,6},{5,7},{6,4},{7,5},{8,10},{9,11},{10,... | collective-permute-start | bytes 786440 | tf_op jit(solution)/shard_map/ppermute | solution.py:45
  21.9 0.0 collective-permute-done.7.refs_2_
  21.9 0.2 collective-permute-start.15
  22.1 0.0 copy-done
  22.1 1.0 %shard_map.59.refs_0_ = f32[256,1024]{1,0:T(8,128)S(1)} custom-call(bf16[8192,1024]{1,0:T(8,128)(2,1)S(1)} %copy-done, bf16[256,512]{1,0:T(8,128)(2,1)S(1)} %get-tuple-element.25.refs_0_, bf16[256,512]{1,0:T(8,128)(2,1)S(1)} %get-tuple-element.26.refs_1_, bf16[256,512]{1,0:T(8,128)(2,1)S(1)} %collective-permute-done.7.refs_2_), custom_call_target="tpu_custom_call" | custom-call | flops 3221225472 | bytes 1048576 | tf_op jit(solution)/shard_map/pallas_call | solution.py:249
  23.1 4.1 %collective-permute-done.6.refs_1_ = bf16[256,512]{1,0:T(8,128)(2,1)S(1)} collective-permute-done((bf16[256,512]{1,0:T(8,128)(2,1)S(1)}, bf16[256,512]{1,0:T(8,128)(2,1)S(1)}, u32[]{:S(2)}, u32[]{:S(2)}) %collective-permute-start.6) | collective-permute-done | bytes 262176 | tf_op jit(solution)/shard_map/ppermute | solution.py:45
  27.2 1.8 %collective-permute-done.9.refs_3_ = bf16[256,512]{1,0:T(8,128)(2,1)S(1)} collective-permute-done((bf16[256,512]{1,0:T(8,128)(2,1)S(1)}, bf16[256,512]{1,0:T(8,128)(2,1)S(1)}, u32[]{:S(2)}, u32[]{:S(2)}) %collective-permute-start.9) | collective-permute-done | bytes 262176 | tf_op jit(solution)/shard_map/ppermute | solution.py:45
  29.0 0.0 collective-permute-start.11
  29.0 0.5 %collective-permute-start.10 = (bf16[256,512]{1,0:T(8,128)(2,1)S(1)}, bf16[256,512]{1,0:T(8,128)(2,1)S(1)}, u32[]{:S(2)}, u32[]{:S(2)}) collective-permute-start(bf16[256,512]{1,0:T(8,128)(2,1)S(1)} %collective-permute-done.6.refs_1_), channel_id=1, source_target_pairs={{0,1},{1,0},{2,3},{3,2},{4,5},{5,4},{6,7},{7,6},{8,9},{9,8},{10,11... | collective-permute-start | bytes 786440 | tf_op jit(solution)/shard_map/ppermute | solution.py:45
  29.5 0.0 collective-permute-done.12.refs_5_
  29.5 1.5 %collective-permute-start.8 = (bf16[256,512]{1,0:T(8,128)(2,1)S(1)}, bf16[256,512]{1,0:T(8,128)(2,1)S(1)}, u32[]{:S(2)}, u32[]{:S(2)}) collective-permute-start(bf16[256,512]{1,0:T(8,128)(2,1)S(1)} %collective-permute-done.6.refs_1_), channel_id=1, source_target_pairs={{0,4},{1,5},{2,6},{3,7},{4,0},{5,1},{6,2},{7,3},{8,12},{9,13},{10,... | collective-permute-start | bytes 786440 | tf_op jit(solution)/shard_map/ppermute | solution.py:45
  31.0 1.3 %collective-permute-done.13.refs_1_ = bf16[256,512]{1,0:T(8,128)(2,1)S(1)} collective-permute-done((bf16[256,512]{1,0:T(8,128)(2,1)S(1)}, bf16[256,512]{1,0:T(8,128)(2,1)S(1)}, u32[]{:S(2)}, u32[]{:S(2)}) %collective-permute-start.13) | collective-permute-done | bytes 262176 | tf_op jit(solution)/shard_map/ppermute | solution.py:45
  32.4 1.8 %collective-permute-start.17 = (bf16[256,512]{1,0:T(8,128)(2,1)S(1)}, bf16[256,512]{1,0:T(8,128)(2,1)S(1)}, u32[]{:S(2)}, u32[]{:S(2)}) collective-permute-start(bf16[256,512]{1,0:T(8,128)(2,1)S(1)} %collective-permute-done.9.refs_3_), channel_id=1, source_target_pairs={{0,2},{1,3},{2,0},{3,1},{4,6},{5,7},{6,4},{7,5},{8,10},{9,11},{10,... | collective-permute-start | bytes 786440 | tf_op jit(solution)/shard_map/ppermute | solution.py:45
  34.1 0.5 %collective-permute-done.15.refs_3_ = bf16[256,512]{1,0:T(8,128)(2,1)S(1)} collective-permute-done((bf16[256,512]{1,0:T(8,128)(2,1)S(1)}, bf16[256,512]{1,0:T(8,128)(2,1)S(1)}, u32[]{:S(2)}, u32[]{:S(2)}) %collective-permute-start.15) | collective-permute-done | bytes 262176 | tf_op jit(solution)/shard_map/ppermute | solution.py:45
  34.6 0.0 collective-permute-start.14
  34.6 0.0 collective-permute-done.11.refs_4_
  34.6 0.5 %collective-permute-start.16 = (bf16[256,512]{1,0:T(8,128)(2,1)S(1)}, bf16[256,512]{1,0:T(8,128)(2,1)S(1)}, u32[]{:S(2)}, u32[]{:S(2)}) collective-permute-start(bf16[256,512]{1,0:T(8,128)(2,1)S(1)} %collective-permute-done.15.refs_3_), channel_id=1, source_target_pairs={{0,1},{1,0},{2,3},{3,2},{4,5},{5,4},{6,7},{7,6},{8,9},{9,8},{10,11... | collective-permute-start | bytes 786440 | tf_op jit(solution)/shard_map/ppermute | solution.py:45
  35.1 0.0 collective-permute-done.10.refs_2_
  35.1 1.5 %shard_map.60.refs_0_ = f32[256,1024]{1,0:T(8,128)S(1)} custom-call(bf16[8192,1024]{1,0:T(8,128)(2,1)S(1)} %copy-done, f32[256,1024]{1,0:T(8,128)S(1)} %shard_map.59.refs_0_, bf16[256,512]{1,0:T(8,128)(2,1)S(1)} %collective-permute-done.6.refs_1_, bf16[256,512]{1,0:T(8,128)(2,1)S(1)} %collective-permute-done.10.refs_2_, ...), custom_call_target="tpu_custom_call" | custom-call | flops 5368709120 | bytes 1048576 | tf_op jit(solution)/shard_map/pallas_call | solution.py:249
  36.7 0.0 collective-permute-done.14.refs_2_
  36.7 0.0 collective-permute-done.16.refs_4_
  36.7 1.3 %shard_map.61.refs_0_ = f32[256,1024]{1,0:T(8,128)S(1)} custom-call(bf16[8192,1024]{1,0:T(8,128)(2,1)S(1)} %copy-done, f32[256,1024]{1,0:T(8,128)S(1)} %shard_map.60.refs_0_, bf16[256,512]{1,0:T(8,128)(2,1)S(1)} %collective-permute-done.13.refs_1_, bf16[256,512]{1,0:T(8,128)(2,1)S(1)} %collective-permute-done.14.refs_2_, ...), custom_call_target="tpu_custom_call" | custom-call | flops 4294967296 | bytes 1048576 | tf_op jit(solution)/shard_map/pallas_call | solution.py:249
  37.9 1.5 %collective-permute-done.8.refs_1_ = bf16[256,512]{1,0:T(8,128)(2,1)S(1)} collective-permute-done((bf16[256,512]{1,0:T(8,128)(2,1)S(1)}, bf16[256,512]{1,0:T(8,128)(2,1)S(1)}, u32[]{:S(2)}, u32[]{:S(2)}) %collective-permute-start.8) | collective-permute-done | bytes 262176 | tf_op jit(solution)/shard_map/ppermute | solution.py:45
  39.5 0.0 collective-permute-start.18
  39.5 0.8 %collective-permute-done.17.refs_2_ = bf16[256,512]{1,0:T(8,128)(2,1)S(1)} collective-permute-done((bf16[256,512]{1,0:T(8,128)(2,1)S(1)}, bf16[256,512]{1,0:T(8,128)(2,1)S(1)}, u32[]{:S(2)}, u32[]{:S(2)}) %collective-permute-start.17) | collective-permute-done | bytes 262176 | tf_op jit(solution)/shard_map/ppermute | solution.py:45
  40.3 0.0 collective-permute-start.19
  40.3 0.7 %shard_map.62.refs_0_ = f32[256,1024]{1,0:T(8,128)S(1)} custom-call(bf16[8192,1024]{1,0:T(8,128)(2,1)S(1)} %copy-done, f32[256,1024]{1,0:T(8,128)S(1)} %shard_map.61.refs_0_, bf16[256,512]{1,0:T(8,128)(2,1)S(1)} %collective-permute-done.8.refs_1_, bf16[256,512]{1,0:T(8,128)(2,1)S(1)} %collective-permute-done.17.refs_2_), custom_call_target="tpu_custom_call" | custom-call | flops 2147483648 | bytes 1048576 | tf_op jit(solution)/shard_map/pallas_call | solution.py:249
  41.0 0.0 collective-permute-done.18.refs_1_
  41.0 0.8 %collective-permute-done.19.refs_2_ = bf16[256,512]{1,0:T(8,128)(2,1)S(1)} collective-permute-done((bf16[256,512]{1,0:T(8,128)(2,1)S(1)}, bf16[256,512]{1,0:T(8,128)(2,1)S(1)}, u32[]{:S(2)}, u32[]{:S(2)}) %collective-permute-start.19) | collective-permute-done | bytes 262176 | tf_op jit(solution)/shard_map/ppermute | solution.py:45
  41.8 1.5 %shard_map.63 = bf16[256,1024]{1,0:T(8,128)(2,1)} custom-call(bf16[8192,1024]{1,0:T(8,128)(2,1)S(1)} %copy-done, f32[256,1024]{1,0:T(8,128)S(1)} %shard_map.62.refs_0_, bf16[256,512]{1,0:T(8,128)(2,1)S(1)} %collective-permute-done.18.refs_1_, bf16[256,512]{1,0:T(8,128)(2,1)S(1)} %collective-permute-done.19.refs_2_), custom_call_target="tpu_custom_call" | custom-call | flops 2147483648 | bytes 1048576 | tf_op jit(solution)/shard_map/pallas_call | solution.py:249
Async XLA Ops:
  0.9 8.0 %collective-permute-start = (bf16[256,128]{1,0:T(8,128)(2,1)S(1)}, bf16[256,128]{1,0:T(8,128)(2,1)S(1)}, u32[]{:S(2)}, u32[]{:S(2)}) collective-permute-start(bf16[256,128]{1,0:T(8,128)(2,1)S(1)} %get-tuple-element.19.refs_0_), channel_id=1, source_target_pairs={{0,8},{8,16},{16,24},{24,0},{1,9},{9,17},{17,25},{25,1},{2,10},{10... | collective-permute-start | bytes 196616 | tf_op jit(solution)/shard_map/ppermute | solution.py:40
  4.0 9.1 %collective-permute-start.1 = (bf16[256,128]{1,0:T(8,128)(2,1)S(1)}, bf16[256,128]{1,0:T(8,128)(2,1)S(1)}, u32[]{:S(2)}, u32[]{:S(2)}) collective-permute-start(bf16[256,128]{1,0:T(8,128)(2,1)S(1)} %get-tuple-element.19.refs_0_), channel_id=1, source_target_pairs={{0,16},{8,24},{16,0},{24,8},{1,17},{9,25},{17,1},{25,9},{2,18},{10... | collective-permute-start | bytes 196616 | tf_op jit(solution)/shard_map/ppermute | solution.py:40
  6.6 6.5 %collective-permute-start.2 = (bf16[256,128]{1,0:T(8,128)(2,1)S(1)}, bf16[256,128]{1,0:T(8,128)(2,1)S(1)}, u32[]{:S(2)}, u32[]{:S(2)}) collective-permute-start(bf16[256,128]{1,0:T(8,128)(2,1)S(1)} %get-tuple-element.19.refs_0_), channel_id=1, source_target_pairs={{0,24},{8,0},{16,8},{24,16},{1,25},{9,1},{17,9},{25,17},{2,26},{10... | collective-permute-start | bytes 196616 | tf_op jit(solution)/shard_map/ppermute | solution.py:40
  7.9 8.8 %collective-permute-start.3 = (bf16[256,128]{1,0:T(8,128)(2,1)S(1)}, bf16[256,128]{1,0:T(8,128)(2,1)S(1)}, u32[]{:S(2)}, u32[]{:S(2)}) collective-permute-start(bf16[256,128]{1,0:T(8,128)(2,1)S(1)} %get-tuple-element.24.refs_0_), channel_id=1, source_target_pairs={{0,16},{8,24},{16,0},{24,8},{1,17},{9,25},{17,1},{25,9},{2,18},{10... | collective-permute-start | bytes 196616 | tf_op jit(solution)/shard_map/ppermute | solution.py:40
  8.1 8.6 %collective-permute-start.4 = (bf16[256,128]{1,0:T(8,128)(2,1)S(1)}, bf16[256,128]{1,0:T(8,128)(2,1)S(1)}, u32[]{:S(2)}, u32[]{:S(2)}) collective-permute-start(bf16[256,128]{1,0:T(8,128)(2,1)S(1)} %get-tuple-element.24.refs_0_), channel_id=1, source_target_pairs={{0,8},{8,16},{16,24},{24,0},{1,9},{9,17},{17,25},{25,1},{2,10},{10... | collective-permute-start | bytes 196616 | tf_op jit(solution)/shard_map/ppermute | solution.py:40
  8.9 7.7 %collective-permute-start.5 = (bf16[256,128]{1,0:T(8,128)(2,1)S(1)}, bf16[256,128]{1,0:T(8,128)(2,1)S(1)}, u32[]{:S(2)}, u32[]{:S(2)}) collective-permute-start(bf16[256,128]{1,0:T(8,128)(2,1)S(1)} %get-tuple-element.24.refs_0_), channel_id=1, source_target_pairs={{0,24},{8,0},{16,8},{24,16},{1,25},{9,1},{17,9},{25,17},{2,26},{10... | collective-permute-start | bytes 196616 | tf_op jit(solution)/shard_map/ppermute | solution.py:40
  15.0 7.2 %copy-start = (bf16[8192,1024]{1,0:T(8,128)(2,1)S(1)}, bf16[8192,1024]{1,0:T(8,128)(2,1)}, u32[]{:S(2)}) copy-start(bf16[8192,1024]{1,0:T(8,128)(2,1)} %weight_ref.9) | copy-start | bytes 50331652
  17.9 4.0 %collective-permute-start.7 = (bf16[256,512]{1,0:T(8,128)(2,1)S(1)}, bf16[256,512]{1,0:T(8,128)(2,1)S(1)}, u32[]{:S(2)}, u32[]{:S(2)}) collective-permute-start(bf16[256,512]{1,0:T(8,128)(2,1)S(1)} %get-tuple-element.25.refs_0_), channel_id=1, source_target_pairs={{0,1},{1,0},{2,3},{3,2},{4,5},{5,4},{6,7},{7,6},{8,9},{9,8},{10,11... | collective-permute-start | bytes 786440 | tf_op jit(solution)/shard_map/ppermute | solution.py:45
  18.0 9.2 %collective-permute-start.6 = (bf16[256,512]{1,0:T(8,128)(2,1)S(1)}, bf16[256,512]{1,0:T(8,128)(2,1)S(1)}, u32[]{:S(2)}, u32[]{:S(2)}) collective-permute-start(bf16[256,512]{1,0:T(8,128)(2,1)S(1)} %get-tuple-element.25.refs_0_), channel_id=1, source_target_pairs={{0,2},{1,3},{2,0},{3,1},{4,6},{5,7},{6,4},{7,5},{8,10},{9,11},{10,... | collective-permute-start | bytes 786440 | tf_op jit(solution)/shard_map/ppermute | solution.py:45
  19.9 9.2 %collective-permute-start.9 = (bf16[256,512]{1,0:T(8,128)(2,1)S(1)}, bf16[256,512]{1,0:T(8,128)(2,1)S(1)}, u32[]{:S(2)}, u32[]{:S(2)}) collective-permute-start(bf16[256,512]{1,0:T(8,128)(2,1)S(1)} %get-tuple-element.26.refs_1_), channel_id=1, source_target_pairs={{0,4},{1,5},{2,6},{3,7},{4,0},{5,1},{6,2},{7,3},{8,12},{9,13},{10,... | collective-permute-start | bytes 786440 | tf_op jit(solution)/shard_map/ppermute | solution.py:45
  21.4 8.1 %collective-permute-start.12 = (bf16[256,512]{1,0:T(8,128)(2,1)S(1)}, bf16[256,512]{1,0:T(8,128)(2,1)S(1)}, u32[]{:S(2)}, u32[]{:S(2)}) collective-permute-start(bf16[256,512]{1,0:T(8,128)(2,1)S(1)} %get-tuple-element.26.refs_1_), channel_id=1, source_target_pairs={{0,1},{1,0},{2,3},{3,2},{4,5},{5,4},{6,7},{7,6},{8,9},{9,8},{10,11... | collective-permute-start | bytes 786440 | tf_op jit(solution)/shard_map/ppermute | solution.py:45
  21.4 11.0 %collective-permute-start.13 = (bf16[256,512]{1,0:T(8,128)(2,1)S(1)}, bf16[256,512]{1,0:T(8,128)(2,1)S(1)}, u32[]{:S(2)}, u32[]{:S(2)}) collective-permute-start(bf16[256,512]{1,0:T(8,128)(2,1)S(1)} %get-tuple-element.26.refs_1_), channel_id=1, source_target_pairs={{0,2},{1,3},{2,0},{3,1},{4,6},{5,7},{6,4},{7,5},{8,10},{9,11},{10,... | collective-permute-start | bytes 786440 | tf_op jit(solution)/shard_map/ppermute | solution.py:45
  21.9 12.7 %collective-permute-start.15 = (bf16[256,512]{1,0:T(8,128)(2,1)S(1)}, bf16[256,512]{1,0:T(8,128)(2,1)S(1)}, u32[]{:S(2)}, u32[]{:S(2)}) collective-permute-start(bf16[256,512]{1,0:T(8,128)(2,1)S(1)} %get-tuple-element.25.refs_0_), channel_id=1, source_target_pairs={{0,4},{1,5},{2,6},{3,7},{4,0},{5,1},{6,2},{7,3},{8,12},{9,13},{10,... | collective-permute-start | bytes 786440 | tf_op jit(solution)/shard_map/ppermute | solution.py:45
  29.0 5.6 %collective-permute-start.11 = (bf16[256,512]{1,0:T(8,128)(2,1)S(1)}, bf16[256,512]{1,0:T(8,128)(2,1)S(1)}, u32[]{:S(2)}, u32[]{:S(2)}) collective-permute-start(bf16[256,512]{1,0:T(8,128)(2,1)S(1)} %collective-permute-done.9.refs_3_), channel_id=1, source_target_pairs={{0,1},{1,0},{2,3},{3,2},{4,5},{5,4},{6,7},{7,6},{8,9},{9,8},{10,11... | collective-permute-start | bytes 786440 | tf_op jit(solution)/shard_map/ppermute | solution.py:45
  29.0 6.1 %collective-permute-start.10 = (bf16[256,512]{1,0:T(8,128)(2,1)S(1)}, bf16[256,512]{1,0:T(8,128)(2,1)S(1)}, u32[]{:S(2)}, u32[]{:S(2)}) collective-permute-start(bf16[256,512]{1,0:T(8,128)(2,1)S(1)} %collective-permute-done.6.refs_1_), channel_id=1, source_target_pairs={{0,1},{1,0},{2,3},{3,2},{4,5},{5,4},{6,7},{7,6},{8,9},{9,8},{10,11... | collective-permute-start | bytes 786440 | tf_op jit(solution)/shard_map/ppermute | solution.py:45
  29.5 9.9 %collective-permute-start.8 = (bf16[256,512]{1,0:T(8,128)(2,1)S(1)}, bf16[256,512]{1,0:T(8,128)(2,1)S(1)}, u32[]{:S(2)}, u32[]{:S(2)}) collective-permute-start(bf16[256,512]{1,0:T(8,128)(2,1)S(1)} %collective-permute-done.6.refs_1_), channel_id=1, source_target_pairs={{0,4},{1,5},{2,6},{3,7},{4,0},{5,1},{6,2},{7,3},{8,12},{9,13},{10,... | collective-permute-start | bytes 786440 | tf_op jit(solution)/shard_map/ppermute | solution.py:45
  32.4 7.9 %collective-permute-start.17 = (bf16[256,512]{1,0:T(8,128)(2,1)S(1)}, bf16[256,512]{1,0:T(8,128)(2,1)S(1)}, u32[]{:S(2)}, u32[]{:S(2)}) collective-permute-start(bf16[256,512]{1,0:T(8,128)(2,1)S(1)} %collective-permute-done.9.refs_3_), channel_id=1, source_target_pairs={{0,2},{1,3},{2,0},{3,1},{4,6},{5,7},{6,4},{7,5},{8,10},{9,11},{10,... | collective-permute-start | bytes 786440 | tf_op jit(solution)/shard_map/ppermute | solution.py:45
  34.6 2.0 %collective-permute-start.14 = (bf16[256,512]{1,0:T(8,128)(2,1)S(1)}, bf16[256,512]{1,0:T(8,128)(2,1)S(1)}, u32[]{:S(2)}, u32[]{:S(2)}) collective-permute-start(bf16[256,512]{1,0:T(8,128)(2,1)S(1)} %collective-permute-done.13.refs_1_), channel_id=1, source_target_pairs={{0,1},{1,0},{2,3},{3,2},{4,5},{5,4},{6,7},{7,6},{8,9},{9,8},{10,11... | collective-permute-start | bytes 786440 | tf_op jit(solution)/shard_map/ppermute | solution.py:45
  34.6 2.0 %collective-permute-start.16 = (bf16[256,512]{1,0:T(8,128)(2,1)S(1)}, bf16[256,512]{1,0:T(8,128)(2,1)S(1)}, u32[]{:S(2)}, u32[]{:S(2)}) collective-permute-start(bf16[256,512]{1,0:T(8,128)(2,1)S(1)} %collective-permute-done.15.refs_3_), channel_id=1, source_target_pairs={{0,1},{1,0},{2,3},{3,2},{4,5},{5,4},{6,7},{7,6},{8,9},{9,8},{10,11... | collective-permute-start | bytes 786440 | tf_op jit(solution)/shard_map/ppermute | solution.py:45
  39.5 1.5 %collective-permute-start.18 = (bf16[256,512]{1,0:T(8,128)(2,1)S(1)}, bf16[256,512]{1,0:T(8,128)(2,1)S(1)}, u32[]{:S(2)}, u32[]{:S(2)}) collective-permute-start(bf16[256,512]{1,0:T(8,128)(2,1)S(1)} %collective-permute-done.8.refs_1_), channel_id=1, source_target_pairs={{0,1},{1,0},{2,3},{3,2},{4,5},{5,4},{6,7},{7,6},{8,9},{9,8},{10,11... | collective-permute-start | bytes 786440 | tf_op jit(solution)/shard_map/ppermute | solution.py:45
  40.3 1.5 %collective-permute-start.19 = (bf16[256,512]{1,0:T(8,128)(2,1)S(1)}, bf16[256,512]{1,0:T(8,128)(2,1)S(1)}, u32[]{:S(2)}, u32[]{:S(2)}) collective-permute-start(bf16[256,512]{1,0:T(8,128)(2,1)S(1)} %collective-permute-done.17.refs_2_), channel_id=1, source_target_pairs={{0,1},{1,0},{2,3},{3,2},{4,5},{5,4},{6,7},{7,6},{8,9},{9,8},{10,11... | collective-permute-start | bytes 786440 | tf_op jit(solution)/shard_map/ppermute | solution.py:45

commit v12 on v10

--- a/solution.py
+++ b/solution.py
@@ -211,7 +211,7 @@
     parts = refs[: len(places)]
     out_ref = refs[len(places)]
     columns = weight_ref.shape[1]
-    tile = columns // 4 if last else columns
+    tile = columns // 2 if last else columns
     me = lax.axis_index("head")
     copies = []
     for n in range(0, columns, tile):

time: 43.2 us -> 43.2 us (level)
  no operation moved by 1% of the time
where the time goes in v12:
time: 43.2 us; the launch traced here: 42.9 us
  starting transfers between devices  20.1 us (47%)
  waiting for transfers between devices  11.7 us (27%)
  Pallas kernels  11 us (25%)
    ppermute x6, starting transfers between devices, shifted(): lax.ppermute(value, axis, [(source, (source + steps) % count) for source...  11 us
    ppermute x14, waiting for transfers between devices, swapped(): lax.ppermute(value, axis, [(source, source ^ bits) for source in range(co...  9.99 us
    ppermute x14, starting transfers between devices, swapped(): lax.ppermute(value, axis, [(source, source ^ bits) for source in range(co...  9.02 us
    pallas_call x5, Pallas kernels, projected(): pl.pallas_call(functools.partial(projection_kernel, places, width, fresh,...  5.89 us
    pallas_call x1, Pallas kernels, weights_of(): pl.pallas_call(weights_kernel, out_shape=held((blocks_dev, rows, keys)),...  1.84 us
    ppermute x6, waiting for transfers between devices, shifted(): lax.ppermute(value, axis, [(source, (source + steps) % count) for source...  1.71 us
    pallas_call x1, Pallas kernels, attended_of(): pl.pallas_call(functools.partial(values_kernel, len(value_parts)), out_sh...  1.26 us
    pallas_call x1, Pallas kernels, stacked_of(): pl.pallas_call(functools.partial(stack_kernel, steps, count), out_shape=[...  1.15 us
  transfers between devices with their start and end apart: 20, of which 10 were waited for; matrix products, arithmetic and copies ran while one was open for 0% of the time, Pallas kernels for 17%

profile of v12, /device:TPU:0, one launch (start us, length us, event | category | flops | bytes accessed | tf_op | source)
XLA Modules:
  0.0 42.9 jit_solution(16065143511150053482)
XLA Ops:
  0.0 0.9 %shard_map.55 = (bf16[256,128]{1,0:T(8,128)(2,1)S(1)}, bf16[256,128]{1,0:T(8,128)(2,1)S(1)}) custom-call(bf16[256,1024]{1,0:T(8,128)(2,1)} %keys_ref.1, bf16[256,1024]{1,0:T(8,128)(2,1)} %values_ref.1), custom_call_target="tpu_custom_call" | custom-call | bytes 262144 | tf_op jit(solution)/shard_map/pallas_call | solution.py:68
  0.9 3.1 %collective-permute-start = (bf16[256,128]{1,0:T(8,128)(2,1)S(1)}, bf16[256,128]{1,0:T(8,128)(2,1)S(1)}, u32[]{:S(2)}, u32[]{:S(2)}) collective-permute-start(bf16[256,128]{1,0:T(8,128)(2,1)S(1)} %get-tuple-element.19.refs_0_), channel_id=1, source_target_pairs={{0,8},{8,16},{16,24},{24,0},{1,9},{9,17},{17,25},{25,1},{2,10},{10... | collective-permute-start | bytes 196616 | tf_op jit(solution)/shard_map/ppermute | solution.py:40
  4.0 2.6 %collective-permute-start.1 = (bf16[256,128]{1,0:T(8,128)(2,1)S(1)}, bf16[256,128]{1,0:T(8,128)(2,1)S(1)}, u32[]{:S(2)}, u32[]{:S(2)}) collective-permute-start(bf16[256,128]{1,0:T(8,128)(2,1)S(1)} %get-tuple-element.19.refs_0_), channel_id=1, source_target_pairs={{0,16},{8,24},{16,0},{24,8},{1,17},{9,25},{17,1},{25,9},{2,18},{10... | collective-permute-start | bytes 196616 | tf_op jit(solution)/shard_map/ppermute | solution.py:40
  6.6 1.3 %collective-permute-start.2 = (bf16[256,128]{1,0:T(8,128)(2,1)S(1)}, bf16[256,128]{1,0:T(8,128)(2,1)S(1)}, u32[]{:S(2)}, u32[]{:S(2)}) collective-permute-start(bf16[256,128]{1,0:T(8,128)(2,1)S(1)} %get-tuple-element.19.refs_0_), channel_id=1, source_target_pairs={{0,24},{8,0},{16,8},{24,16},{1,25},{9,1},{17,9},{25,17},{2,26},{10... | collective-permute-start | bytes 196616 | tf_op jit(solution)/shard_map/ppermute | solution.py:40
  7.9 0.2 collective-permute-start.3
  8.1 0.8 %collective-permute-start.4 = (bf16[256,128]{1,0:T(8,128)(2,1)S(1)}, bf16[256,128]{1,0:T(8,128)(2,1)S(1)}, u32[]{:S(2)}, u32[]{:S(2)}) collective-permute-start(bf16[256,128]{1,0:T(8,128)(2,1)S(1)} %get-tuple-element.24.refs_0_), channel_id=1, source_target_pairs={{0,8},{8,16},{16,24},{24,0},{1,9},{9,17},{17,25},{25,1},{2,10},{10... | collective-permute-start | bytes 196616 | tf_op jit(solution)/shard_map/ppermute | solution.py:40
  8.9 0.0 collective-permute-done.refs_2_
  8.9 3.0 %collective-permute-start.5 = (bf16[256,128]{1,0:T(8,128)(2,1)S(1)}, bf16[256,128]{1,0:T(8,128)(2,1)S(1)}, u32[]{:S(2)}, u32[]{:S(2)}) collective-permute-start(bf16[256,128]{1,0:T(8,128)(2,1)S(1)} %get-tuple-element.24.refs_0_), channel_id=1, source_target_pairs={{0,24},{8,0},{16,8},{24,16},{1,25},{9,1},{17,9},{25,17},{2,26},{10... | collective-permute-start | bytes 196616 | tf_op jit(solution)/shard_map/ppermute | solution.py:40
  11.9 1.2 %shard_map.56 = (bf16[2,1024,128]{2,1,0:T(8,128)(2,1)S(1)}, bf16[2,1024,128]{2,1,0:T(8,128)(2,1)S(1)}) custom-call(bf16[256,1024]{1,0:T(8,128)(2,1)} %q_ref, s32[8,8]{1,0:T(8,128)} %pattern_ref.1), custom_call_target="tpu_custom_call" | custom-call | bytes 1048576 | tf_op jit(solution)/shard_map/pallas_call | solution.py:119
  13.1 0.0 collective-permute-done.1.refs_1_
  13.1 0.0 collective-permute-done.2.refs_3_
  13.1 1.8 %shard_map.57.weights_ref = bf16[2,1024,1024]{2,1,0:T(8,128)(2,1)S(1)} custom-call(bf16[2,1024,128]{2,1,0:T(8,128)(2,1)S(1)} %get-tuple-element.21.q_ref, bf16[2,1024,128]{2,1,0:T(8,128)(2,1)S(1)} %get-tuple-element.22.mask_ref, bf16[256,128]{1,0:T(8,128)(2,1)S(1)} %get-tuple-element.19.refs_0_, bf16[256,128]{1,0:T(8,128)(2,1)S(1)} %collective-permute-done.1.refs_1_, ...), custom_call_target="tpu_custom_call" | custom-call | flops 107374182400 | bytes 4194304 | tf_op jit(solution)/shard_map/pallas_call | solution.py:160
  15.0 0.0 copy-start
  15.0 1.7 %collective-permute-done.3.refs_1_ = bf16[256,128]{1,0:T(8,128)(2,1)S(1)} collective-permute-done((bf16[256,128]{1,0:T(8,128)(2,1)S(1)}, bf16[256,128]{1,0:T(8,128)(2,1)S(1)}, u32[]{:S(2)}, u32[]{:S(2)}) %collective-permute-start.3) | collective-permute-done | bytes 65568 | tf_op jit(solution)/shard_map/ppermute | solution.py:40
  16.7 0.0 collective-permute-done.4.refs_2_
  16.7 0.0 collective-permute-done.5.refs_3_
  16.7 1.3 %shard_map.58 = (bf16[256,512]{1,0:T(8,128)(2,1)S(1)}, bf16[256,512]{1,0:T(8,128)(2,1)S(1)}) custom-call(bf16[2,1024,1024]{2,1,0:T(8,128)(2,1)S(1)} %shard_map.57.weights_ref, bf16[256,128]{1,0:T(8,128)(2,1)S(1)} %get-tuple-element.24.refs_0_, bf16[256,128]{1,0:T(8,128)(2,1)S(1)} %collective-permute-done.3.refs_1_, ...), custom_call_target="tpu_custom_call" | custom-call | flops 107374182400 | bytes 1048576 | tf_op jit(solution)/shard_map/pallas_call | solution.py:198
  17.9 0.1 collective-permute-start.7
  18.0 0.5 %collective-permute-start.8 = (bf16[256,512]{1,0:T(8,128)(2,1)S(1)}, bf16[256,512]{1,0:T(8,128)(2,1)S(1)}, u32[]{:S(2)}, u32[]{:S(2)}) collective-permute-start(bf16[256,512]{1,0:T(8,128)(2,1)S(1)} %get-tuple-element.26.refs_1_), channel_id=1, source_target_pairs={{0,1},{1,0},{2,3},{3,2},{4,5},{5,4},{6,7},{7,6},{8,9},{9,8},{10,11... | collective-permute-start | bytes 786440 | tf_op jit(solution)/shard_map/ppermute | solution.py:45
  18.5 1.8 %collective-permute-start.6 = (bf16[256,512]{1,0:T(8,128)(2,1)S(1)}, bf16[256,512]{1,0:T(8,128)(2,1)S(1)}, u32[]{:S(2)}, u32[]{:S(2)}) collective-permute-start(bf16[256,512]{1,0:T(8,128)(2,1)S(1)} %get-tuple-element.25.refs_0_), channel_id=1, source_target_pairs={{0,2},{1,3},{2,0},{3,1},{4,6},{5,7},{6,4},{7,5},{8,10},{9,11},{10,... | collective-permute-start | bytes 786440 | tf_op jit(solution)/shard_map/ppermute | solution.py:45
  20.3 1.5 %collective-permute-start.10 = (bf16[256,512]{1,0:T(8,128)(2,1)S(1)}, bf16[256,512]{1,0:T(8,128)(2,1)S(1)}, u32[]{:S(2)}, u32[]{:S(2)}) collective-permute-start(bf16[256,512]{1,0:T(8,128)(2,1)S(1)} %get-tuple-element.26.refs_1_), channel_id=1, source_target_pairs={{0,4},{1,5},{2,6},{3,7},{4,0},{5,1},{6,2},{7,3},{8,12},{9,13},{10,... | collective-permute-start | bytes 786440 | tf_op jit(solution)/shard_map/ppermute | solution.py:45
  21.8 0.5 %collective-permute-start.13 = (bf16[256,512]{1,0:T(8,128)(2,1)S(1)}, bf16[256,512]{1,0:T(8,128)(2,1)S(1)}, u32[]{:S(2)}, u32[]{:S(2)}) collective-permute-start(bf16[256,512]{1,0:T(8,128)(2,1)S(1)} %get-tuple-element.26.refs_1_), channel_id=1, source_target_pairs={{0,2},{1,3},{2,0},{3,1},{4,6},{5,7},{6,4},{7,5},{8,10},{9,11},{10,... | collective-permute-start | bytes 786440 | tf_op jit(solution)/shard_map/ppermute | solution.py:45
  22.3 0.0 collective-permute-done.7.refs_2_
  22.3 0.2 collective-permute-start.15
  22.6 0.0 collective-permute-done.8.refs_3_
  22.6 0.0 copy-done
  22.6 1.2 %shard_map.59.refs_0_ = f32[256,1024]{1,0:T(8,128)S(1)} custom-call(bf16[8192,1024]{1,0:T(8,128)(2,1)S(1)} %copy-done, bf16[256,512]{1,0:T(8,128)(2,1)S(1)} %get-tuple-element.25.refs_0_, bf16[256,512]{1,0:T(8,128)(2,1)S(1)} %get-tuple-element.26.refs_1_, bf16[256,512]{1,0:T(8,128)(2,1)S(1)} %collective-permute-done.7.refs_2_, ...), custom_call_target="tpu_custom_call" | custom-call | flops 4294967296 | bytes 1048576 | tf_op jit(solution)/shard_map/pallas_call | solution.py:249
  23.8 3.8 %collective-permute-done.6.refs_1_ = bf16[256,512]{1,0:T(8,128)(2,1)S(1)} collective-permute-done((bf16[256,512]{1,0:T(8,128)(2,1)S(1)}, bf16[256,512]{1,0:T(8,128)(2,1)S(1)}, u32[]{:S(2)}, u32[]{:S(2)}) %collective-permute-start.6) | collective-permute-done | bytes 262176 | tf_op jit(solution)/shard_map/ppermute | solution.py:45
  27.7 1.8 %collective-permute-done.10.refs_3_ = bf16[256,512]{1,0:T(8,128)(2,1)S(1)} collective-permute-done((bf16[256,512]{1,0:T(8,128)(2,1)S(1)}, bf16[256,512]{1,0:T(8,128)(2,1)S(1)}, u32[]{:S(2)}, u32[]{:S(2)}) %collective-permute-start.10) | collective-permute-done | bytes 262176 | tf_op jit(solution)/shard_map/ppermute | solution.py:45
  29.5 0.0 collective-permute-start.12
  29.5 0.5 %collective-permute-start.11 = (bf16[256,512]{1,0:T(8,128)(2,1)S(1)}, bf16[256,512]{1,0:T(8,128)(2,1)S(1)}, u32[]{:S(2)}, u32[]{:S(2)}) collective-permute-start(bf16[256,512]{1,0:T(8,128)(2,1)S(1)} %collective-permute-done.6.refs_1_), channel_id=1, source_target_pairs={{0,1},{1,0},{2,3},{3,2},{4,5},{5,4},{6,7},{7,6},{8,9},{9,8},{10,11... | collective-permute-start | bytes 786440 | tf_op jit(solution)/shard_map/ppermute | solution.py:45
  30.0 1.5 %collective-permute-start.9 = (bf16[256,512]{1,0:T(8,128)(2,1)S(1)}, bf16[256,512]{1,0:T(8,128)(2,1)S(1)}, u32[]{:S(2)}, u32[]{:S(2)}) collective-permute-start(bf16[256,512]{1,0:T(8,128)(2,1)S(1)} %collective-permute-done.6.refs_1_), channel_id=1, source_target_pairs={{0,4},{1,5},{2,6},{3,7},{4,0},{5,1},{6,2},{7,3},{8,12},{9,13},{10,... | collective-permute-start | bytes 786440 | tf_op jit(solution)/shard_map/ppermute | solution.py:45
  31.5 0.9 %collective-permute-done.13.refs_1_ = bf16[256,512]{1,0:T(8,128)(2,1)S(1)} collective-permute-done((bf16[256,512]{1,0:T(8,128)(2,1)S(1)}, bf16[256,512]{1,0:T(8,128)(2,1)S(1)}, u32[]{:S(2)}, u32[]{:S(2)}) %collective-permute-start.13) | collective-permute-done | bytes 262176 | tf_op jit(solution)/shard_map/ppermute | solution.py:45
  32.4 1.7 %collective-permute-start.17 = (bf16[256,512]{1,0:T(8,128)(2,1)S(1)}, bf16[256,512]{1,0:T(8,128)(2,1)S(1)}, u32[]{:S(2)}, u32[]{:S(2)}) collective-permute-start(bf16[256,512]{1,0:T(8,128)(2,1)S(1)} %collective-permute-done.10.refs_3_), channel_id=1, source_target_pairs={{0,2},{1,3},{2,0},{3,1},{4,6},{5,7},{6,4},{7,5},{8,10},{9,11},{10,... | collective-permute-start | bytes 786440 | tf_op jit(solution)/shard_map/ppermute | solution.py:45
  34.2 0.9 %collective-permute-done.15.refs_3_ = bf16[256,512]{1,0:T(8,128)(2,1)S(1)} collective-permute-done((bf16[256,512]{1,0:T(8,128)(2,1)S(1)}, bf16[256,512]{1,0:T(8,128)(2,1)S(1)}, u32[]{:S(2)}, u32[]{:S(2)}) %collective-permute-start.15) | collective-permute-done | bytes 262176 | tf_op jit(solution)/shard_map/ppermute | solution.py:45
  35.1 0.0 collective-permute-start.14
  35.1 0.0 collective-permute-done.12.refs_4_
  35.1 0.5 %collective-permute-start.16 = (bf16[256,512]{1,0:T(8,128)(2,1)S(1)}, bf16[256,512]{1,0:T(8,128)(2,1)S(1)}, u32[]{:S(2)}, u32[]{:S(2)}) collective-permute-start(bf16[256,512]{1,0:T(8,128)(2,1)S(1)} %collective-permute-done.15.refs_3_), channel_id=1, source_target_pairs={{0,1},{1,0},{2,3},{3,2},{4,5},{5,4},{6,7},{7,6},{8,9},{9,8},{10,11... | collective-permute-start | bytes 786440 | tf_op jit(solution)/shard_map/ppermute | solution.py:45
  35.6 0.0 collective-permute-done.11.refs_2_
  35.6 1.2 %shard_map.60.refs_0_ = f32[256,1024]{1,0:T(8,128)S(1)} custom-call(bf16[8192,1024]{1,0:T(8,128)(2,1)S(1)} %copy-done, f32[256,1024]{1,0:T(8,128)S(1)} %shard_map.59.refs_0_, bf16[256,512]{1,0:T(8,128)(2,1)S(1)} %collective-permute-done.6.refs_1_, bf16[256,512]{1,0:T(8,128)(2,1)S(1)} %collective-permute-done.11.refs_2_, ...), custom_call_target="tpu_custom_call" | custom-call | flops 4294967296 | bytes 1048576 | tf_op jit(solution)/shard_map/pallas_call | solution.py:249
  36.9 0.0 collective-permute-done.14.refs_2_
  36.9 0.1 collective-permute-done.16.refs_4_
  37.0 1.2 %shard_map.61.refs_0_ = f32[256,1024]{1,0:T(8,128)S(1)} custom-call(bf16[8192,1024]{1,0:T(8,128)(2,1)S(1)} %copy-done, f32[256,1024]{1,0:T(8,128)S(1)} %shard_map.60.refs_0_, bf16[256,512]{1,0:T(8,128)(2,1)S(1)} %collective-permute-done.13.refs_1_, bf16[256,512]{1,0:T(8,128)(2,1)S(1)} %collective-permute-done.14.refs_2_, ...), custom_call_target="tpu_custom_call" | custom-call | flops 4294967296 | bytes 1048576 | tf_op jit(solution)/shard_map/pallas_call | solution.py:249
  38.3 1.3 %collective-permute-done.9.refs_1_ = bf16[256,512]{1,0:T(8,128)(2,1)S(1)} collective-permute-done((bf16[256,512]{1,0:T(8,128)(2,1)S(1)}, bf16[256,512]{1,0:T(8,128)(2,1)S(1)}, u32[]{:S(2)}, u32[]{:S(2)}) %collective-permute-start.9) | collective-permute-done | bytes 262176 | tf_op jit(solution)/shard_map/ppermute | solution.py:45
  39.5 0.0 collective-permute-start.18
  39.5 0.4 collective-permute-done.17.refs_2_
  39.9 0.1 collective-permute-start.19
  40.0 0.7 %shard_map.62.refs_0_ = f32[256,1024]{1,0:T(8,128)S(1)} custom-call(bf16[8192,1024]{1,0:T(8,128)(2,1)S(1)} %copy-done, f32[256,1024]{1,0:T(8,128)S(1)} %shard_map.61.refs_0_, bf16[256,512]{1,0:T(8,128)(2,1)S(1)} %collective-permute-done.9.refs_1_, bf16[256,512]{1,0:T(8,128)(2,1)S(1)} %collective-permute-done.17.refs_2_), custom_call_target="tpu_custom_call" | custom-call | flops 2147483648 | bytes 1048576 | tf_op jit(solution)/shard_map/pallas_call | solution.py:249
  40.8 0.3 collective-permute-done.18.refs_1_
  41.1 0.4 collective-permute-done.19.refs_2_
  41.5 1.4 %shard_map.63 = bf16[256,1024]{1,0:T(8,128)(2,1)} custom-call(bf16[8192,1024]{1,0:T(8,128)(2,1)S(1)} %copy-done, f32[256,1024]{1,0:T(8,128)S(1)} %shard_map.62.refs_0_, bf16[256,512]{1,0:T(8,128)(2,1)S(1)} %collective-permute-done.18.refs_1_, bf16[256,512]{1,0:T(8,128)(2,1)S(1)} %collective-permute-done.19.refs_2_), custom_call_target="tpu_custom_call" | custom-call | flops 2147483648 | bytes 1048576 | tf_op jit(solution)/shard_map/pallas_call | solution.py:249
Async XLA Ops:
  0.9 8.0 %collective-permute-start = (bf16[256,128]{1,0:T(8,128)(2,1)S(1)}, bf16[256,128]{1,0:T(8,128)(2,1)S(1)}, u32[]{:S(2)}, u32[]{:S(2)}) collective-permute-start(bf16[256,128]{1,0:T(8,128)(2,1)S(1)} %get-tuple-element.19.refs_0_), channel_id=1, source_target_pairs={{0,8},{8,16},{16,24},{24,0},{1,9},{9,17},{17,25},{25,1},{2,10},{10... | collective-permute-start | bytes 196616 | tf_op jit(solution)/shard_map/ppermute | solution.py:40
  4.0 9.1 %collective-permute-start.1 = (bf16[256,128]{1,0:T(8,128)(2,1)S(1)}, bf16[256,128]{1,0:T(8,128)(2,1)S(1)}, u32[]{:S(2)}, u32[]{:S(2)}) collective-permute-start(bf16[256,128]{1,0:T(8,128)(2,1)S(1)} %get-tuple-element.19.refs_0_), channel_id=1, source_target_pairs={{0,16},{8,24},{16,0},{24,8},{1,17},{9,25},{17,1},{25,9},{2,18},{10... | collective-permute-start | bytes 196616 | tf_op jit(solution)/shard_map/ppermute | solution.py:40
  6.6 6.5 %collective-permute-start.2 = (bf16[256,128]{1,0:T(8,128)(2,1)S(1)}, bf16[256,128]{1,0:T(8,128)(2,1)S(1)}, u32[]{:S(2)}, u32[]{:S(2)}) collective-permute-start(bf16[256,128]{1,0:T(8,128)(2,1)S(1)} %get-tuple-element.19.refs_0_), channel_id=1, source_target_pairs={{0,24},{8,0},{16,8},{24,16},{1,25},{9,1},{17,9},{25,17},{2,26},{10... | collective-permute-start | bytes 196616 | tf_op jit(solution)/shard_map/ppermute | solution.py:40
  7.9 8.8 %collective-permute-start.3 = (bf16[256,128]{1,0:T(8,128)(2,1)S(1)}, bf16[256,128]{1,0:T(8,128)(2,1)S(1)}, u32[]{:S(2)}, u32[]{:S(2)}) collective-permute-start(bf16[256,128]{1,0:T(8,128)(2,1)S(1)} %get-tuple-element.24.refs_0_), channel_id=1, source_target_pairs={{0,16},{8,24},{16,0},{24,8},{1,17},{9,25},{17,1},{25,9},{2,18},{10... | collective-permute-start | bytes 196616 | tf_op jit(solution)/shard_map/ppermute | solution.py:40
  8.1 8.6 %collective-permute-start.4 = (bf16[256,128]{1,0:T(8,128)(2,1)S(1)}, bf16[256,128]{1,0:T(8,128)(2,1)S(1)}, u32[]{:S(2)}, u32[]{:S(2)}) collective-permute-start(bf16[256,128]{1,0:T(8,128)(2,1)S(1)} %get-tuple-element.24.refs_0_), channel_id=1, source_target_pairs={{0,8},{8,16},{16,24},{24,0},{1,9},{9,17},{17,25},{25,1},{2,10},{10... | collective-permute-start | bytes 196616 | tf_op jit(solution)/shard_map/ppermute | solution.py:40
  8.9 7.7 %collective-permute-start.5 = (bf16[256,128]{1,0:T(8,128)(2,1)S(1)}, bf16[256,128]{1,0:T(8,128)(2,1)S(1)}, u32[]{:S(2)}, u32[]{:S(2)}) collective-permute-start(bf16[256,128]{1,0:T(8,128)(2,1)S(1)} %get-tuple-element.24.refs_0_), channel_id=1, source_target_pairs={{0,24},{8,0},{16,8},{24,16},{1,25},{9,1},{17,9},{25,17},{2,26},{10... | collective-permute-start | bytes 196616 | tf_op jit(solution)/shard_map/ppermute | solution.py:40
  15.0 7.6 %copy-start = (bf16[8192,1024]{1,0:T(8,128)(2,1)S(1)}, bf16[8192,1024]{1,0:T(8,128)(2,1)}, u32[]{:S(2)}) copy-start(bf16[8192,1024]{1,0:T(8,128)(2,1)} %weight_ref.9) | copy-start | bytes 50331652
  17.9 4.4 %collective-permute-start.7 = (bf16[256,512]{1,0:T(8,128)(2,1)S(1)}, bf16[256,512]{1,0:T(8,128)(2,1)S(1)}, u32[]{:S(2)}, u32[]{:S(2)}) collective-permute-start(bf16[256,512]{1,0:T(8,128)(2,1)S(1)} %get-tuple-element.25.refs_0_), channel_id=1, source_target_pairs={{0,1},{1,0},{2,3},{3,2},{4,5},{5,4},{6,7},{7,6},{8,9},{9,8},{10,11... | collective-permute-start | bytes 786440 | tf_op jit(solution)/shard_map/ppermute | solution.py:45
  18.0 4.6 %collective-permute-start.8 = (bf16[256,512]{1,0:T(8,128)(2,1)S(1)}, bf16[256,512]{1,0:T(8,128)(2,1)S(1)}, u32[]{:S(2)}, u32[]{:S(2)}) collective-permute-start(bf16[256,512]{1,0:T(8,128)(2,1)S(1)} %get-tuple-element.26.refs_1_), channel_id=1, source_target_pairs={{0,1},{1,0},{2,3},{3,2},{4,5},{5,4},{6,7},{7,6},{8,9},{9,8},{10,11... | collective-permute-start | bytes 786440 | tf_op jit(solution)/shard_map/ppermute | solution.py:45
  18.5 9.2 %collective-permute-start.6 = (bf16[256,512]{1,0:T(8,128)(2,1)S(1)}, bf16[256,512]{1,0:T(8,128)(2,1)S(1)}, u32[]{:S(2)}, u32[]{:S(2)}) collective-permute-start(bf16[256,512]{1,0:T(8,128)(2,1)S(1)} %get-tuple-element.25.refs_0_), channel_id=1, source_target_pairs={{0,2},{1,3},{2,0},{3,1},{4,6},{5,7},{6,4},{7,5},{8,10},{9,11},{10,... | collective-permute-start | bytes 786440 | tf_op jit(solution)/shard_map/ppermute | solution.py:45
  20.3 9.2 %collective-permute-start.10 = (bf16[256,512]{1,0:T(8,128)(2,1)S(1)}, bf16[256,512]{1,0:T(8,128)(2,1)S(1)}, u32[]{:S(2)}, u32[]{:S(2)}) collective-permute-start(bf16[256,512]{1,0:T(8,128)(2,1)S(1)} %get-tuple-element.26.refs_1_), channel_id=1, source_target_pairs={{0,4},{1,5},{2,6},{3,7},{4,0},{5,1},{6,2},{7,3},{8,12},{9,13},{10,... | collective-permute-start | bytes 786440 | tf_op jit(solution)/shard_map/ppermute | solution.py:45
  21.8 10.6 %collective-permute-start.13 = (bf16[256,512]{1,0:T(8,128)(2,1)S(1)}, bf16[256,512]{1,0:T(8,128)(2,1)S(1)}, u32[]{:S(2)}, u32[]{:S(2)}) collective-permute-start(bf16[256,512]{1,0:T(8,128)(2,1)S(1)} %get-tuple-element.26.refs_1_), channel_id=1, source_target_pairs={{0,2},{1,3},{2,0},{3,1},{4,6},{5,7},{6,4},{7,5},{8,10},{9,11},{10,... | collective-permute-start | bytes 786440 | tf_op jit(solution)/shard_map/ppermute | solution.py:45
  22.3 12.8 %collective-permute-start.15 = (bf16[256,512]{1,0:T(8,128)(2,1)S(1)}, bf16[256,512]{1,0:T(8,128)(2,1)S(1)}, u32[]{:S(2)}, u32[]{:S(2)}) collective-permute-start(bf16[256,512]{1,0:T(8,128)(2,1)S(1)} %get-tuple-element.25.refs_0_), channel_id=1, source_target_pairs={{0,4},{1,5},{2,6},{3,7},{4,0},{5,1},{6,2},{7,3},{8,12},{9,13},{10,... | collective-permute-start | bytes 786440 | tf_op jit(solution)/shard_map/ppermute | solution.py:45
  29.5 5.6 %collective-permute-start.12 = (bf16[256,512]{1,0:T(8,128)(2,1)S(1)}, bf16[256,512]{1,0:T(8,128)(2,1)S(1)}, u32[]{:S(2)}, u32[]{:S(2)}) collective-permute-start(bf16[256,512]{1,0:T(8,128)(2,1)S(1)} %collective-permute-done.10.refs_3_), channel_id=1, source_target_pairs={{0,1},{1,0},{2,3},{3,2},{4,5},{5,4},{6,7},{7,6},{8,9},{9,8},{10,11... | collective-permute-start | bytes 786440 | tf_op jit(solution)/shard_map/ppermute | solution.py:45
  29.5 6.1 %collective-permute-start.11 = (bf16[256,512]{1,0:T(8,128)(2,1)S(1)}, bf16[256,512]{1,0:T(8,128)(2,1)S(1)}, u32[]{:S(2)}, u32[]{:S(2)}) collective-permute-start(bf16[256,512]{1,0:T(8,128)(2,1)S(1)} %collective-permute-done.6.refs_1_), channel_id=1, source_target_pairs={{0,1},{1,0},{2,3},{3,2},{4,5},{5,4},{6,7},{7,6},{8,9},{9,8},{10,11... | collective-permute-start | bytes 786440 | tf_op jit(solution)/shard_map/ppermute | solution.py:45
  30.0 9.5 %collective-permute-start.9 = (bf16[256,512]{1,0:T(8,128)(2,1)S(1)}, bf16[256,512]{1,0:T(8,128)(2,1)S(1)}, u32[]{:S(2)}, u32[]{:S(2)}) collective-permute-start(bf16[256,512]{1,0:T(8,128)(2,1)S(1)} %collective-permute-done.6.refs_1_), channel_id=1, source_target_pairs={{0,4},{1,5},{2,6},{3,7},{4,0},{5,1},{6,2},{7,3},{8,12},{9,13},{10,... | collective-permute-start | bytes 786440 | tf_op jit(solution)/shard_map/ppermute | solution.py:45
  32.4 7.5 %collective-permute-start.17 = (bf16[256,512]{1,0:T(8,128)(2,1)S(1)}, bf16[256,512]{1,0:T(8,128)(2,1)S(1)}, u32[]{:S(2)}, u32[]{:S(2)}) collective-permute-start(bf16[256,512]{1,0:T(8,128)(2,1)S(1)} %collective-permute-done.10.refs_3_), channel_id=1, source_target_pairs={{0,2},{1,3},{2,0},{3,1},{4,6},{5,7},{6,4},{7,5},{8,10},{9,11},{10,... | collective-permute-start | bytes 786440 | tf_op jit(solution)/shard_map/ppermute | solution.py:45
  35.1 1.8 %collective-permute-start.14 = (bf16[256,512]{1,0:T(8,128)(2,1)S(1)}, bf16[256,512]{1,0:T(8,128)(2,1)S(1)}, u32[]{:S(2)}, u32[]{:S(2)}) collective-permute-start(bf16[256,512]{1,0:T(8,128)(2,1)S(1)} %collective-permute-done.13.refs_1_), channel_id=1, source_target_pairs={{0,1},{1,0},{2,3},{3,2},{4,5},{5,4},{6,7},{7,6},{8,9},{9,8},{10,11... | collective-permute-start | bytes 786440 | tf_op jit(solution)/shard_map/ppermute | solution.py:45
  35.1 1.9 %collective-permute-start.16 = (bf16[256,512]{1,0:T(8,128)(2,1)S(1)}, bf16[256,512]{1,0:T(8,128)(2,1)S(1)}, u32[]{:S(2)}, u32[]{:S(2)}) collective-permute-start(bf16[256,512]{1,0:T(8,128)(2,1)S(1)} %collective-permute-done.15.refs_3_), channel_id=1, source_target_pairs={{0,1},{1,0},{2,3},{3,2},{4,5},{5,4},{6,7},{7,6},{8,9},{9,8},{10,11... | collective-permute-start | bytes 786440 | tf_op jit(solution)/shard_map/ppermute | solution.py:45
  39.5 1.5 %collective-permute-start.18 = (bf16[256,512]{1,0:T(8,128)(2,1)S(1)}, bf16[256,512]{1,0:T(8,128)(2,1)S(1)}, u32[]{:S(2)}, u32[]{:S(2)}) collective-permute-start(bf16[256,512]{1,0:T(8,128)(2,1)S(1)} %collective-permute-done.9.refs_1_), channel_id=1, source_target_pairs={{0,1},{1,0},{2,3},{3,2},{4,5},{5,4},{6,7},{7,6},{8,9},{9,8},{10,11... | collective-permute-start | bytes 786440 | tf_op jit(solution)/shard_map/ppermute | solution.py:45
  39.9 1.5 %collective-permute-start.19 = (bf16[256,512]{1,0:T(8,128)(2,1)S(1)}, bf16[256,512]{1,0:T(8,128)(2,1)S(1)}, u32[]{:S(2)}, u32[]{:S(2)}) collective-permute-start(bf16[256,512]{1,0:T(8,128)(2,1)S(1)} %collective-permute-done.17.refs_2_), channel_id=1, source_target_pairs={{0,1},{1,0},{2,3},{3,2},{4,5},{5,4},{6,7},{7,6},{8,9},{9,8},{10,11... | collective-permute-start | bytes 786440 | tf_op jit(solution)/shard_map/ppermute | solution.py:45
